TPU v7x, 32 devices: a whole 2x2x4 slice. The times are simulated.
32 devices in a mesh: grp: 4 (over y, x), seq: 8 (over z, core).
Axes of the slice: x: 2, y: 2, z: 4, core: 2. Of those that a mesh axis runs over, the one named last changes fastest.
Arguments:
- resid_in: bfloat16 [4, 1024, 2048], P('grp', 'seq'), may hold values from -8 to 8
- lin_query: bfloat16 [4, 1024, 2048], P('grp', 'seq'), may hold values from -6 to 6
- lin_key: bfloat16 [4, 1024, 2048], P('grp', 'seq'), may hold values from -6 to 6
- lin_value: bfloat16 [4, 1024, 2048], P('grp', 'seq'), may hold values from -40 to 40
- lin_gain: float32 [2048], replicated, may hold values from 0.5 to 1.5
- out_proj: bfloat16 [2048, 2048], replicated, may hold values from -0.125 to 0.125
- moe_gain: float32 [2048], replicated, may hold values from 0.5 to 1.5
- expert_ids: int32 [4, 1024, 8], P('grp', 'seq'), may hold values from 0 to 31, all different within a row; in each aligned block of 128 rows (0 to 127, 128 to 255, ..., all dimensions but the last counted through in order) at most 40 rows name the same one
- route_scores: float32 [4, 1024, 8], P('grp', 'seq'), may hold values from 0.01 to 1
- gate_weight: bfloat16 [32, 2048, 768], P(('grp', 'seq')), may hold values from -0.125 to 0.125
- up_weight: bfloat16 [32, 2048, 768], P(('grp', 'seq')), may hold values from -0.125 to 0.125
- down_weight: bfloat16 [32, 768, 2048], P(('grp', 'seq')), may hold values from -0.875 to 0.875
Outputs:
- layer_out: bfloat16 [4, 1024, 2048], P('grp', 'seq')
Inputs may be any that keep to these rules, and one draw needn't show every extreme that they name: `expert_ids`: in each aligned block of 128 rows (the rows of one device) no expert is named by more than 40 rows, a bound that some block reaches.
All inputs are finite; a program needn't handle non-finite values.
Results may differ from a plain program's by a relative error of at most 0.015.
Values may be sent and summed in bfloat16 or wider, within the bound.
No kernel may reach another device: no remote copies, remote signals or barrier semaphores. Data moves between devices by JAX's collectives and lax.ppermute only.
A program may use at most 128 MiB of HBM per device.

v0:
```python
import functools

import jax
import jax.numpy as jnp
from jax import lax
from jax.experimental import pallas as pl
from jax.experimental.pallas import tpu as pltpu
from jax.sharding import PartitionSpec as P


HEAD = 128
TOP = 8
epsilon = 1e-06
BF = jnp.bfloat16
F32 = jnp.float32


def dot(a, b, ca=1, cb=0):
    return lax.dot_general(a, b, (((ca,), (cb,)), ((), ())), preferred_element_type=F32)


def whole(shape):
    return pl.BlockSpec(shape, lambda *_: (0,) * len(shape))


def state_kernel(k_ref, v_ref, s_ref):
    heads = k_ref.shape[1] // HEAD
    for h in range(heads):
        cols = slice(h * HEAD, (h + 1) * HEAD)
        s_ref[cols, :] = dot(k_ref[:, cols], v_ref[:, cols], 0, 0).astype(BF)


def local_states(keys, values):
    return pl.pallas_call(
        state_kernel,
        out_shape=jax.ShapeDtypeStruct((keys.shape[1], HEAD), BF),
        name="states",
    )(keys, values)


def inside_kernel(q_ref, k_ref, v_ref, o_ref):
    tokens = q_ref.shape[0]
    heads = q_ref.shape[1] // HEAD
    rows = lax.broadcasted_iota(jnp.int32, (tokens, tokens), 0)
    cols = lax.broadcasted_iota(jnp.int32, (tokens, tokens), 1)
    causal = rows >= cols
    for h in range(heads):
        part = slice(h * HEAD, (h + 1) * HEAD)
        scores = dot(q_ref[:, part], k_ref[:, part], 1, 1)
        scores = jnp.where(causal, scores, 0.0).astype(BF)
        o_ref[:, part] = dot(scores, v_ref[:, part])


def inside_block(queries, keys, values):
    return pl.pallas_call(
        inside_kernel,
        out_shape=jax.ShapeDtypeStruct(queries.shape, F32),
        name="inside",
    )(queries, keys, values)


def project_kernel(
    core_ref, in_ref, q_ref, mine_ref, other_ref, pair_ref, gain_ref, resid_ref, w_ref, mgain_ref,
    res_ref, moe_ref, normed_ref, square_ref,
):
    step = pl.program_id(0)
    core = core_ref[0]
    heads = q_ref.shape[1] // HEAD
    half = heads // 2

    @pl.when(step == 0)
    def _():
        low = core == 0
        second = jnp.where(low, 0.0, 1.0)
        for h in range(heads):
            part = slice(h * HEAD, (h + 1) * HEAD)
            at = slice((h % half) * HEAD, (h % half + 1) * HEAD)
            first = low if h < half else jnp.logical_not(low)
            prefix = jnp.where(first, mine_ref[at, :].astype(F32), other_ref[at, :].astype(F32))
            carried = (prefix + second * pair_ref[part, :].astype(F32)).astype(BF)
            attended = in_ref[:, part] + dot(q_ref[:, part], carried)
            mean = jnp.mean(attended * attended, axis=1, keepdims=True)
            normed_ref[:, part] = (
                attended * lax.rsqrt(mean + epsilon) * gain_ref[:, part]
            ).astype(BF)
        square_ref[...] = jnp.zeros_like(square_ref)

    width = w_ref.shape[1]
    at = pl.ds(pl.multiple_of(step * width, width), width)
    added = resid_ref[:, at].astype(F32) + dot(normed_ref[...], w_ref[...])
    rounded = added.astype(BF)
    res_ref[:, at] = rounded
    wide = rounded.astype(F32)
    square_ref[...] += jnp.sum(wide * wide, axis=1, keepdims=True)

    @pl.when(step == pl.num_programs(0) - 1)
    def _():
        features = res_ref.shape[1]
        scale = lax.rsqrt(square_ref[...] / features + epsilon)
        moe_ref[...] = (res_ref[...].astype(F32) * scale * mgain_ref[...]).astype(BF)


def attend_project(core, inside, queries, mine, other, pair, gain, resid, weight, moe_gain):
    tokens, features = resid.shape
    inner = queries.shape[1]
    steps = 4
    width = features // steps
    return pl.pallas_call(
        project_kernel,
        grid_spec=pltpu.PrefetchScalarGridSpec(
            num_scalar_prefetch=1,
            grid=(steps,),
            in_specs=[
                whole(inside.shape), whole(queries.shape), whole(mine.shape), whole(other.shape),
                whole(pair.shape), whole(gain.shape), whole(resid.shape),
                pl.BlockSpec((inner, width), lambda i, *_: (0, i)),
                whole(moe_gain.shape),
            ],
            out_specs=[whole(resid.shape), whole(resid.shape)],
            scratch_shapes=[pltpu.VMEM((tokens, inner), BF), pltpu.VMEM((tokens, 1), F32)],
        ),
        out_shape=[jax.ShapeDtypeStruct(resid.shape, BF)] * 2,
        compiler_params=pltpu.CompilerParams(dimension_semantics=("arbitrary",)),
        name="project",
    )(core, inside, queries, mine, other, pair, gain, resid, weight, moe_gain)


def slots_of(rank_ref, weight_ref, row, slots, weighted):
    rank = rank_ref[row : row + 1, :]
    weight = weight_ref[row : row + 1, :]
    number = lax.broadcasted_iota(jnp.int32, (slots, rank.shape[1]), 0).astype(F32)
    hit = jnp.logical_and(number == rank, weight > 0.0)
    return jnp.where(hit, weight if weighted else 1.0, 0.0)


def select_kernel(slots, own_ref, par_ref, rank_ref, weight_ref, *outs):
    groups = len(outs)
    picks = []
    for block in range(2):
        rows = [
            slots_of(rank_ref, weight_ref, block * groups + k, slots, False) for k in range(groups)
        ]
        picks.append(jnp.concatenate(rows, axis=0).astype(BF))
    first = dot(picks[0], own_ref[...])
    second = dot(picks[1], par_ref[...])
    for k in range(groups):
        at = slice(k * slots, (k + 1) * slots)
        outs[k][...] = jnp.concatenate([first[at], second[at]], axis=0).astype(BF)


def select(slots, groups, own, par, rank, weight):
    shape = jax.ShapeDtypeStruct((2 * slots, own.shape[1]), BF)
    return pl.pallas_call(
        functools.partial(select_kernel, slots), out_shape=[shape] * groups, name="select"
    )(own, par, rank, weight)


def combine_kernel(slots, groups, *refs):
    backs = refs[:groups]
    rank_ref, weight_ref, own_ref, par_ref = refs[groups:]
    rows = jnp.concatenate([r[...] for r in backs], axis=0)
    zero = jnp.zeros((slots, rank_ref.shape[1]), F32)
    sides = []
    for block in range(2):
        parts = []
        for k in range(groups):
            mine = slots_of(rank_ref, weight_ref, block * groups + k, slots, True)
            parts += [mine, zero] if block == 0 else [zero, mine]
        sides.append(jnp.concatenate(parts, axis=0).astype(BF))
    own_ref[...] = dot(sides[0], rows, 0, 0).astype(BF)
    par_ref[...] = dot(sides[1], rows, 0, 0).astype(BF)


def combine(slots, backs, rank, weight):
    tokens = rank.shape[1]
    shape = jax.ShapeDtypeStruct((tokens, backs[0].shape[1]), BF)
    return pl.pallas_call(
        functools.partial(combine_kernel, slots, len(backs)), out_shape=[shape] * 2, name="combine"
    )(*backs, rank, weight)


def expert_kernel(groups, *refs):
    xs = refs[:groups]
    gate_ref, up_ref, down_ref = refs[groups : groups + 3]
    outs = refs[groups + 3 : 2 * groups + 3]
    x_ref, acc_ref = refs[2 * groups + 3 :]
    step = pl.program_id(0)
    rows = xs[0].shape[0]

    @pl.when(step == 0)
    def _():
        for k in range(groups):
            x_ref[k * rows : (k + 1) * rows, :] = xs[k][...]

    x = x_ref[...]
    gate = dot(x, gate_ref[0])
    up = dot(x, up_ref[0])
    hidden = (gate / (1.0 + jnp.exp(-gate)) * up).astype(BF)
    out = dot(hidden, down_ref[0])

    @pl.when(step == 0)
    def _():
        acc_ref[...] = out

    @pl.when(jnp.logical_and(step > 0, step < pl.num_programs(0) - 1))
    def _():
        acc_ref[...] += out

    @pl.when(step == pl.num_programs(0) - 1)
    def _():
        for k in range(groups):
            at = slice(k * rows, (k + 1) * rows)
            outs[k][...] = (acc_ref[at, :] + out[at, :]).astype(BF)


def experts(xs, gate, up, down):
    groups = len(xs)
    rows, features = xs[0].shape
    width = 256
    steps = gate.shape[2] // width
    return pl.pallas_call(
        functools.partial(expert_kernel, groups),
        grid=(steps,),
        in_specs=[whole(xs[0].shape)] * groups
        + [
            pl.BlockSpec((1, features, width), lambda i: (0, 0, i)),
            pl.BlockSpec((1, features, width), lambda i: (0, 0, i)),
            pl.BlockSpec((1, width, features), lambda i: (0, i, 0)),
        ],
        out_specs=[whole(xs[0].shape)] * groups,
        out_shape=[jax.ShapeDtypeStruct(xs[0].shape, BF)] * groups,
        scratch_shapes=[
            pltpu.VMEM((groups * rows, features), BF),
            pltpu.VMEM((groups * rows, features), F32),
        ],
        compiler_params=pltpu.CompilerParams(dimension_semantics=("arbitrary",)),
        name="experts",
    )(*xs, gate, up, down)


def on_device(
    resid_in,
    lin_query,
    lin_key,
    lin_value,
    lin_gain,
    out_proj,
    moe_gain,
    expert_ids,
    route_scores,
    gate_weight,
    up_weight,
    down_weight,
):
    tokens = resid_in.shape[1]
    features = resid_in.shape[2]
    groups = lax.axis_size("grp")
    length = lax.axis_size("seq")
    stages = length // 2
    group = lax.axis_index("grp")
    place = lax.axis_index("seq")
    core = place % 2
    expert_count = gate_weight.shape[0] * groups * length
    capacity = tokens * TOP * 5 // (4 * expert_count)
    slots = -(-capacity // 8) * 8

    def swap(x):
        return lax.ppermute(x, "seq", [(s, s ^ 1) for s in range(length)])

    def along(x, m):
        return lax.ppermute(x, "seq", [(s, s ^ (2 * m)) for s in range(length)])

    def across(x, m):
        if m == 0:
            return x
        return lax.ppermute(x, "grp", [(g, g ^ m) for g in range(groups)])

    def later(x, m):
        return lax.ppermute(x, "seq", [(s, s + 2 * m) for s in range(length - 2 * m)])

    queries = lin_query.reshape(tokens, -1)
    keys = lin_key.reshape(tokens, -1)
    values = lin_value.reshape(tokens, -1)
    inner = queries.shape[1]
    half = inner // 2

    states = local_states(keys, values)
    pair = swap(states)
    summed = (states.astype(F32) + pair.astype(F32)).astype(BF)
    summed = lax.dynamic_slice_in_dim(summed, core * half, half, axis=0)
    arrived = [later(summed, m) for m in range(1, stages)]

    chosen = expert_ids.reshape(tokens, TOP).T
    scores = route_scores.reshape(tokens, TOP)
    shares = (scores / jnp.sum(scores, axis=1, keepdims=True)).T
    hit = chosen[None] == jnp.arange(expert_count, dtype=jnp.int32)[:, None, None]
    dense = jnp.sum(jnp.where(hit, shares[None], 0.0), axis=1)
    both = jnp.stack([dense, swap(dense)])
    routes = jnp.stack([both] + [along(both, m) for m in range(1, stages)])
    routes = routes.reshape(stages, 2, groups, length, tokens)
    routes = lax.dynamic_index_in_dim(routes, place, axis=3, keepdims=False)
    routes = jnp.stack(
        [
            lax.dynamic_index_in_dim(routes, group ^ k, axis=2, keepdims=False)
            for k in range(groups)
        ],
        axis=2,
    ).reshape(stages, 2 * groups, tokens)
    earlier = (jnp.arange(tokens)[:, None] < jnp.arange(tokens)[None, :]).astype(BF)
    ranks = jnp.einsum(
        "srt,tu->sru", (routes > 0.0).astype(BF), earlier, preferred_element_type=F32
    )

    inside = inside_block(queries, keys, values)
    total = arrived[0].astype(F32)
    for more in arrived[1:]:
        total = total + more.astype(F32)
    mine = total.astype(BF)
    other = swap(mine)
    residual, moe_in = attend_project(
        core.reshape(1),
        inside,
        queries,
        mine,
        other,
        pair,
        lin_gain.reshape(1, inner),
        resid_in.reshape(tokens, features),
        out_proj,
        moe_gain.reshape(1, features),
    )

    order = visits(stages)
    blocks = {0: moe_in}
    for m in order[1:]:
        blocks[m] = along(moe_in, m)
    outs = {}
    for m in order:
        partner = swap(blocks[m])
        picked = select(slots, groups, blocks[m], partner, ranks[m], routes[m])
        taken = [across(picked[k], k) for k in range(groups)]
        outs[m] = experts(taken, gate_weight, up_weight, down_weight)
    combined = residual.astype(F32)
    for m in order[2:] + [1, 0]:
        backs = [across(outs[m][k], k) for k in range(groups)]
        own, par = combine(slots, backs, ranks[m], routes[m])
        part = own.astype(F32) + swap(par).astype(F32)
        if m:
            part = along(part.astype(BF), m).astype(F32)
        combined = combined + part
    return combined.astype(BF).reshape(1, tokens, features)


def visits(stages):
    return [0, 1] + list(range(stages - 1, 1, -1))


def solution(mesh):
    rows = P("grp", "seq", None)
    held = P(("grp", "seq"), None, None)
    in_specs = (rows, rows, rows, rows, P(), P(), P(), rows, rows, held, held, held)

    return jax.shard_map(on_device, mesh=mesh, in_specs=in_specs, out_specs=rows, check_vma=False)
```

profile of v0, /device:TPU:0, one launch (start us, length us, event | category | flops | bytes accessed | tf_op | source)
XLA Modules:
  0.0 271.5 jit_solution(1032769891569238842)
XLA Ops:
  0.0 2.3 states.1
  2.8 0.7 reduce_sum.18
  3.5 1.0 collective-permute-done.pair_ref
  4.6 1.2 add_convert_fusion.5
  5.8 4.9 %collective-permute-start.1 = (bf16[1024,128]{1,0:T(8,128)(2,1)S(1)}, bf16[1024,128]{1,0:T(8,128)(2,1)S(1)}, u32[]{:S(2)}, u32[]{:S(2)}) collective-permute-start(bf16[1024,128]{1,0:T(8,128)(2,1)S(1)} %add_convert_fusion.5), channel_id=1, source_target_pairs={{0,2},{1,3},{2,4},{3,5},{4,6},{5,7},{8,10},{9,11},{10,12},{11,13},... | collective-permute-start | bytes 786440 | tf_op jit(solution)/shard_map/ppermute | solution.py:279
  10.6 4.5 %collective-permute-start.2 = (bf16[1024,128]{1,0:T(8,128)(2,1)S(1)}, bf16[1024,128]{1,0:T(8,128)(2,1)S(1)}, u32[]{:S(2)}, u32[]{:S(2)}) collective-permute-start(bf16[1024,128]{1,0:T(8,128)(2,1)S(1)} %add_convert_fusion.5), channel_id=1, source_target_pairs={{0,4},{1,5},{2,6},{3,7},{8,12},{9,13},{10,14},{11,15},{16,20},{17,... | collective-permute-start | bytes 786440 | tf_op jit(solution)/shard_map/ppermute | solution.py:279
  15.1 1.3 collective-permute-start.3
  17.1 0.7 select_reduce_fusion
  18.0 4.9 %inside.1.in_ref = f32[128,2048]{1,0:T(8,128)} custom-call(bf16[128,2048]{1,0:T(8,128)(2,1)} %bitcast.54, bf16[128,2048]{1,0:T(8,128)(2,1)} %bitcast.51, bf16[128,2048]{1,0:T(8,128)(2,1)} %bitcast.53), custom_call_target="tpu_custom_call" | custom-call | tf_op jit(solution)/shard_map/inside/pallas_call | solution.py:55
  23.0 4.3 %collective-permute-start.10 = (f32[2,32,128]{2,1,0:T(8,128)S(1)}, f32[2,32,128]{2,1,0:T(8,128)S(1)}, u32[]{:S(2)}, u32[]{:S(2)}) collective-permute-start(f32[2,32,128]{2,1,0:T(8,128)S(1)} %pad_maximum_fusion.1), channel_id=1, source_target_pairs={{0,6},{1,7},{2,4},{3,5},{4,2},{5,3},{6,0},{7,1},{8,14},{9,15},{10,... | collective-permute-start | bytes 98312 | tf_op jit(solution)/shard_map/ppermute | solution.py:271
  27.3 1.2 collective-permute-done.3
  30.3 0.7 copy-done.33
  31.0 7.8 %project.1 = (bf16[128,2048]{1,0:T(8,128)(2,1)}, bf16[128,2048]{1,0:T(8,128)(2,1)}) custom-call(s32[1]{0:T(128)} %bitcast.core_ref, f32[128,2048]{1,0:T(8,128)} %inside.1.in_ref, bf16[128,2048]{1,0:T(8,128)(2,1)} %bitcast.55, bf16[1024,128]{1,0:T(8,128)(2,1)} %copy-done.1, bf16[1024,128]{1,0:T(8,128)(2,1)} %copy-done.33, bf16[2048,128]{1,0:T(8,128)(2,1)} %copy-done, ...), custom_call_target="tpu_custom_call" | custom-call | tf_op jit(solution)/shard_map/project/pallas_call | solution.py:108
  38.8 11.3 %collective-permute-start.5 = (bf16[128,2048]{1,0:T(8,128)(2,1)}, bf16[128,2048]{1,0:T(8,128)(2,1)S(1)}, u32[]{:S(2)}, u32[]{:S(2)}) collective-permute-start(bf16[128,2048]{1,0:T(8,128)(2,1)} %get-tuple-element.48.own_ref), channel_id=1, source_target_pairs={{0,6},{1,7},{2,4},{3,5},{4,2},{5,3},{6,0},{7,1},{8,14},{9,15},{10,... | collective-permute-start | bytes 1572872 | tf_op jit(solution)/shard_map/ppermute | solution.py:271
  50.2 0.7 collective-permute-start.29
  52.2 0.8 copy-done.13
  53.0 2.7 %select.9 = (bf16[80,2048]{1,0:T(8,128)(2,1)}, bf16[80,2048]{1,0:T(8,128)(2,1)}, bf16[80,2048]{1,0:T(8,128)(2,1)}, bf16[80,2048]{1,0:T(8,128)(2,1)}) custom-call(bf16[128,2048]{1,0:T(8,128)(2,1)} %get-tuple-element.48.own_ref, bf16[128,2048]{1,0:T(8,128)(2,1)} %copy-done.13, f32[8,128]{1,0:T(8,128)} %get-tuple-element.100.rank_ref.refs_4_, f32[8,128]{1,0:T(8,128)} %bitcast.63), custom_call_target="tpu_custom_call" | custom-call | tf_op jit(solution)/shard_map/select/pallas_call | solution.py:153
  55.7 1.5 collective-permute-start.40
  57.2 6.0 %collective-permute-done.5.own_ref = bf16[128,2048]{1,0:T(8,128)(2,1)S(1)} collective-permute-done((bf16[128,2048]{1,0:T(8,128)(2,1)}, bf16[128,2048]{1,0:T(8,128)(2,1)S(1)}, u32[]{:S(2)}, u32[]{:S(2)}) %collective-permute-start.5) | collective-permute-done | bytes 524320 | tf_op jit(solution)/shard_map/ppermute | solution.py:271
  63.2 1.5 collective-permute-start.41
  64.7 29.8 %collective-permute-done.19.own_ref = bf16[128,2048]{1,0:T(8,128)(2,1)S(1)} collective-permute-done((bf16[128,2048]{1,0:T(8,128)(2,1)}, bf16[128,2048]{1,0:T(8,128)(2,1)S(1)}, u32[]{:S(2)}, u32[]{:S(2)}) %collective-permute-start.19) | collective-permute-done | bytes 524320 | tf_op jit(solution)/shard_map/ppermute | solution.py:271
  94.5 2.4 collective-permute-start.42
  97.5 7.1 %collective-permute-done.42.refs_3_ = bf16[80,2048]{1,0:T(8,128)(2,1)} collective-permute-done((bf16[80,2048]{1,0:T(8,128)(2,1)}, bf16[80,2048]{1,0:T(8,128)(2,1)}, u32[]{:S(2)}, u32[]{:S(2)}) %collective-permute-start.42) | collective-permute-done | bytes 327712 | tf_op jit(solution)/shard_map/ppermute | solution.py:276
  104.7 8.6 %experts.7 = (bf16[80,2048]{1,0:T(8,128)(2,1)}, bf16[80,2048]{1,0:T(8,128)(2,1)}, bf16[80,2048]{1,0:T(8,128)(2,1)}, bf16[80,2048]{1,0:T(8,128)(2,1)}) custom-call(bf16[80,2048]{1,0:T(8,128)(2,1)} %get-tuple-element.79.refs_0_, bf16[80,2048]{1,0:T(8,128)(2,1)} %copy-done.32, bf16[80,2048]{1,0:T(8,128)(2,1)} %collective-permute-done.41.refs_2_, ...), custom_call_target="tpu_custom_call" | custom-call | tf_op jit(solution)/shard_map/experts/pallas_call | solution.py:221
  113.3 1.5 collective-permute-start.43
  114.8 0.8 copy-done.12
  115.6 2.8 %select.6 = (bf16[80,2048]{1,0:T(8,128)(2,1)}, bf16[80,2048]{1,0:T(8,128)(2,1)}, bf16[80,2048]{1,0:T(8,128)(2,1)}, bf16[80,2048]{1,0:T(8,128)(2,1)}) custom-call(bf16[128,2048]{1,0:T(8,128)(2,1)} %copy-done.9, bf16[128,2048]{1,0:T(8,128)(2,1)} %copy-done.12, f32[8,128]{1,0:T(8,128)} %get-tuple-element.99.rank_ref.refs_4_, f32[8,128]{1,0:T(8,128)} %bitcast.67), custom_call_target="tpu_custom_call" | custom-call | tf_op jit(solution)/shard_map/select/pallas_call | solution.py:153
  118.9 1.5 collective-permute-start.12
  120.5 1.4 collective-permute-start.13
  121.9 2.7 %select.7 = (bf16[80,2048]{1,0:T(8,128)(2,1)}, bf16[80,2048]{1,0:T(8,128)(2,1)}, bf16[80,2048]{1,0:T(8,128)(2,1)}, bf16[80,2048]{1,0:T(8,128)(2,1)}) custom-call(bf16[128,2048]{1,0:T(8,128)(2,1)} %copy-done.8, bf16[128,2048]{1,0:T(8,128)(2,1)} %copy-done.11, f32[8,128]{1,0:T(8,128)} %get-tuple-element.102.rank_ref.refs_4_, f32[8,128]{1,0:T(8,128)} %bitcast.65), custom_call_target="tpu_custom_call" | custom-call | tf_op jit(solution)/shard_map/select/pallas_call | solution.py:153
  124.6 1.6 collective-permute-start.44
  126.8 4.1 %collective-permute-done.11.refs_1_ = bf16[80,2048]{1,0:T(8,128)(2,1)S(1)} collective-permute-done((bf16[80,2048]{1,0:T(8,128)(2,1)}, bf16[80,2048]{1,0:T(8,128)(2,1)S(1)}, u32[]{:S(2)}, u32[]{:S(2)}) %collective-permute-start.11) | collective-permute-done | bytes 327712 | tf_op jit(solution)/shard_map/ppermute | solution.py:276
  130.9 0.8 copy-done.28
  131.7 1.5 collective-permute-start.22
  133.2 4.0 %collective-permute-start.23 = (bf16[80,2048]{1,0:T(8,128)(2,1)}, bf16[80,2048]{1,0:T(8,128)(2,1)}, u32[]{:S(2)}, u32[]{:S(2)}) collective-permute-start(bf16[80,2048]{1,0:T(8,128)(2,1)} %get-tuple-element.62), channel_id=1, source_target_pairs={{0,24},{8,16},{16,8},{24,0},{1,25},{9,17},{17,9},{25,1},{2,26},{10... | collective-permute-start | bytes 983048 | tf_op jit(solution)/shard_map/ppermute | solution.py:276
  137.2 2.7 %select.8 = (bf16[80,2048]{1,0:T(8,128)(2,1)}, bf16[80,2048]{1,0:T(8,128)(2,1)}, bf16[80,2048]{1,0:T(8,128)(2,1)}, bf16[80,2048]{1,0:T(8,128)(2,1)}) custom-call(bf16[128,2048]{1,0:T(8,128)(2,1)} %copy-done.7, bf16[128,2048]{1,0:T(8,128)(2,1)} %copy-done.10, f32[8,128]{1,0:T(8,128)} %get-tuple-element.101.rank_ref.refs_4_, f32[8,128]{1,0:T(8,128)} %bitcast.61), custom_call_target="tpu_custom_call" | custom-call | tf_op jit(solution)/shard_map/select/pallas_call | solution.py:153
  139.9 0.8 collective-permute-start.31
  140.7 8.7 %experts.4 = (bf16[80,2048]{1,0:T(8,128)(2,1)}, bf16[80,2048]{1,0:T(8,128)(2,1)}, bf16[80,2048]{1,0:T(8,128)(2,1)}, bf16[80,2048]{1,0:T(8,128)(2,1)}) custom-call(bf16[80,2048]{1,0:T(8,128)(2,1)} %get-tuple-element.49.refs_0_, bf16[80,2048]{1,0:T(8,128)(2,1)} %copy-done.28, bf16[80,2048]{1,0:T(8,128)(2,1)} %copy-done.29, bf16[80,2048]{1,0:T(8,128)(2,1)} %copy-done.31, ...), custom_call_target="tpu_custom_call" | custom-call | tf_op jit(solution)/shard_map/experts/pallas_call | solution.py:221
  149.4 1.4 collective-permute-start.14
  150.8 1.0 collective-permute-start.15
  151.7 4.8 %collective-permute-done.22.refs_2_ = bf16[80,2048]{1,0:T(8,128)(2,1)S(1)} collective-permute-done((bf16[80,2048]{1,0:T(8,128)(2,1)}, bf16[80,2048]{1,0:T(8,128)(2,1)S(1)}, u32[]{:S(2)}, u32[]{:S(2)}) %collective-permute-start.22) | collective-permute-done | bytes 327712 | tf_op jit(solution)/shard_map/ppermute | solution.py:276
  156.6 0.7 copy-done.26
  157.3 3.4 %collective-permute-start.16 = (bf16[80,2048]{1,0:T(8,128)(2,1)}, bf16[80,2048]{1,0:T(8,128)(2,1)S(1)}, u32[]{:S(2)}, u32[]{:S(2)}) collective-permute-start(bf16[80,2048]{1,0:T(8,128)(2,1)} %get-tuple-element.56), channel_id=1, source_target_pairs={{0,24},{8,16},{16,8},{24,0},{1,25},{9,17},{17,9},{25,1},{2,26},{10... | collective-permute-start | bytes 983048 | tf_op jit(solution)/shard_map/ppermute | solution.py:276
  160.7 1.1 collective-permute-start.33
  161.8 8.6 %experts.5 = (bf16[80,2048]{1,0:T(8,128)(2,1)}, bf16[80,2048]{1,0:T(8,128)(2,1)}, bf16[80,2048]{1,0:T(8,128)(2,1)}, bf16[80,2048]{1,0:T(8,128)(2,1)}) custom-call(bf16[80,2048]{1,0:T(8,128)(2,1)} %get-tuple-element.59.refs_0_, bf16[80,2048]{1,0:T(8,128)(2,1)} %copy-done.25, bf16[80,2048]{1,0:T(8,128)(2,1)} %copy-done.26, ...), custom_call_target="tpu_custom_call" | custom-call | tf_op jit(solution)/shard_map/experts/pallas_call | solution.py:221
  170.4 2.5 collective-permute-start.24
  172.9 1.2 collective-permute-done.16.refs_3_
  174.1 5.1 %collective-permute-start.26 = (bf16[80,2048]{1,0:T(8,128)(2,1)}, bf16[80,2048]{1,0:T(8,128)(2,1)S(1)}, u32[]{:S(2)}, u32[]{:S(2)}) collective-permute-start(bf16[80,2048]{1,0:T(8,128)(2,1)} %get-tuple-element.66), channel_id=1, source_target_pairs={{0,24},{8,16},{16,8},{24,0},{1,25},{9,17},{17,9},{25,1},{2,26},{10... | collective-permute-start | bytes 983048 | tf_op jit(solution)/shard_map/ppermute | solution.py:276
  179.3 2.8 %combine.4 = (bf16[128,2048]{1,0:T(8,128)(2,1)}, bf16[128,2048]{1,0:T(8,128)(2,1)}) custom-call(bf16[80,2048]{1,0:T(8,128)(2,1)} %get-tuple-element.53.refs_0_, bf16[80,2048]{1,0:T(8,128)(2,1)} %copy-done.18, bf16[80,2048]{1,0:T(8,128)(2,1)} %copy-done.21, bf16[80,2048]{1,0:T(8,128)(2,1)} %copy-done.23, f32[8,128]{1,0:T(8,128)} %get-tuple-element.99.rank_ref.refs_4_, ...), custom_call_target="tpu_custom_call" | custom-call | tf_op jit(solution)/shard_map/combine/pallas_call | solution.py:177
  182.1 3.5 %collective-permute-done.32.refs_2_ = bf16[80,2048]{1,0:T(8,128)(2,1)S(1)} collective-permute-done((bf16[80,2048]{1,0:T(8,128)(2,1)}, bf16[80,2048]{1,0:T(8,128)(2,1)S(1)}, u32[]{:S(2)}, u32[]{:S(2)}) %collective-permute-start.32) | collective-permute-done | bytes 327712 | tf_op jit(solution)/shard_map/ppermute | solution.py:276
  185.7 9.5 %collective-permute-start.45 = (bf16[80,2048]{1,0:T(8,128)(2,1)}, bf16[80,2048]{1,0:T(8,128)(2,1)S(1)}, u32[]{:S(2)}, u32[]{:S(2)}) collective-permute-start(bf16[80,2048]{1,0:T(8,128)(2,1)} %get-tuple-element.86), channel_id=1, source_target_pairs={{0,24},{8,16},{16,8},{24,0},{1,25},{9,17},{17,9},{25,1},{2,26},{10... | collective-permute-start | bytes 983048 | tf_op jit(solution)/shard_map/ppermute | solution.py:276
  195.1 8.8 %experts.6 = (bf16[80,2048]{1,0:T(8,128)(2,1)}, bf16[80,2048]{1,0:T(8,128)(2,1)}, bf16[80,2048]{1,0:T(8,128)(2,1)}, bf16[80,2048]{1,0:T(8,128)(2,1)}) custom-call(bf16[80,2048]{1,0:T(8,128)(2,1)} %get-tuple-element.69.refs_0_, bf16[80,2048]{1,0:T(8,128)(2,1)} %copy-done.24, bf16[80,2048]{1,0:T(8,128)(2,1)} %copy-done.27, bf16[80,2048]{1,0:T(8,128)(2,1)} %copy-done.30, ...), custom_call_target="tpu_custom_call" | custom-call | tf_op jit(solution)/shard_map/experts/pallas_call | solution.py:221
  204.0 1.4 collective-permute-start.35
  205.4 2.1 collective-permute-start.36
  207.5 2.8 %combine.5 = (bf16[128,2048]{1,0:T(8,128)(2,1)}, bf16[128,2048]{1,0:T(8,128)(2,1)}) custom-call(bf16[80,2048]{1,0:T(8,128)(2,1)} %get-tuple-element.63.refs_0_, bf16[80,2048]{1,0:T(8,128)(2,1)} %copy-done.16, bf16[80,2048]{1,0:T(8,128)(2,1)} %copy-done.17, bf16[80,2048]{1,0:T(8,128)(2,1)} %copy-done.19, f32[8,128]{1,0:T(8,128)} %get-tuple-element.102.rank_ref.refs_4_, ...), custom_call_target="tpu_custom_call" | custom-call | tf_op jit(solution)/shard_map/combine/pallas_call | solution.py:177
  211.1 2.8 %combine.7 = (bf16[128,2048]{1,0:T(8,128)(2,1)}, bf16[128,2048]{1,0:T(8,128)(2,1)}) custom-call(bf16[80,2048]{1,0:T(8,128)(2,1)} %get-tuple-element.83.refs_0_, bf16[80,2048]{1,0:T(8,128)(2,1)} %copy-done.14, bf16[80,2048]{1,0:T(8,128)(2,1)} %copy-done.15, bf16[80,2048]{1,0:T(8,128)(2,1)} %copy-done.22, f32[8,128]{1,0:T(8,128)} %get-tuple-element.100.rank_ref.refs_4_, ...), custom_call_target="tpu_custom_call" | custom-call | tf_op jit(solution)/shard_map/combine/pallas_call | solution.py:177
  213.9 0.9 collective-permute-done.34.refs_1_
  214.8 6.4 %collective-permute-done.35.refs_2_ = bf16[80,2048]{1,0:T(8,128)(2,1)} collective-permute-done((bf16[80,2048]{1,0:T(8,128)(2,1)}, bf16[80,2048]{1,0:T(8,128)(2,1)}, u32[]{:S(2)}, u32[]{:S(2)}) %collective-permute-start.35) | collective-permute-done | bytes 327712 | tf_op jit(solution)/shard_map/ppermute | solution.py:276
  221.2 2.8 %combine.6 = (bf16[128,2048]{1,0:T(8,128)(2,1)}, bf16[128,2048]{1,0:T(8,128)(2,1)}) custom-call(bf16[80,2048]{1,0:T(8,128)(2,1)} %get-tuple-element.73.refs_0_, bf16[80,2048]{1,0:T(8,128)(2,1)} %copy-done.20, bf16[80,2048]{1,0:T(8,128)(2,1)} %collective-permute-done.35.refs_2_, bf16[80,2048]{1,0:T(8,128)(2,1)} %collective-permute-done.36.refs_3_, ...), custom_call_target="tpu_custom_call" | custom-call | tf_op jit(solution)/shard_map/combine/pallas_call | solution.py:177
  224.7 1.2 add_convert_fusion.2
  226.3 3.8 %collective-permute-start.38 = (bf16[128,2048]{1,0:T(8,128)(2,1)S(1)}, bf16[128,2048]{1,0:T(8,128)(2,1)S(1)}, u32[]{:S(2)}, u32[]{:S(2)}) collective-permute-start(bf16[128,2048]{1,0:T(8,128)(2,1)S(1)} %add_convert_fusion.1), channel_id=1, source_target_pairs={{0,2},{1,3},{2,0},{3,1},{4,6},{5,7},{6,4},{7,5},{8,10},{9,11},{10,... | collective-permute-start | bytes 1572872 | tf_op jit(solution)/shard_map/ppermute | solution.py:271
  230.1 10.9 %collective-permute-done.18 = bf16[128,2048]{1,0:T(8,128)(2,1)S(1)} collective-permute-done((bf16[128,2048]{1,0:T(8,128)(2,1)S(1)}, bf16[128,2048]{1,0:T(8,128)(2,1)S(1)}, u32[]{:S(2)}, u32[]{:S(2)}) %collective-permute-start.18) | collective-permute-done | bytes 524320 | tf_op jit(solution)/shard_map/ppermute | solution.py:271
  241.0 29.2 %collective-permute-done.28 = bf16[128,2048]{1,0:T(8,128)(2,1)S(1)} collective-permute-done((bf16[128,2048]{1,0:T(8,128)(2,1)S(1)}, bf16[128,2048]{1,0:T(8,128)(2,1)S(1)}, u32[]{:S(2)}, u32[]{:S(2)}) %collective-permute-start.28) | collective-permute-done | bytes 524320 | tf_op jit(solution)/shard_map/ppermute | solution.py:271
  270.2 1.3 fusion
  (131 shorter events, 8.1 us)
Async XLA Ops:
  2.3 2.2 collective-permute-start
  4.6 25.7 %copy-start = (bf16[2048,128]{1,0:T(8,128)(2,1)}, bf16[2048,128]{1,0:T(8,128)(2,1)S(1)}, u32[]{:S(2)}) copy-start(bf16[2048,128]{1,0:T(8,128)(2,1)S(1)} %collective-permute-done.pair_ref) | copy-start | bytes 1572868
  5.8 17.3 %collective-permute-start.1 = (bf16[1024,128]{1,0:T(8,128)(2,1)S(1)}, bf16[1024,128]{1,0:T(8,128)(2,1)S(1)}, u32[]{:S(2)}, u32[]{:S(2)}) collective-permute-start(bf16[1024,128]{1,0:T(8,128)(2,1)S(1)} %add_convert_fusion.5), channel_id=1, source_target_pairs={{0,2},{1,3},{2,4},{3,5},{4,6},{5,7},{8,10},{9,11},{10,12},{11,13},... | collective-permute-start | bytes 786440 | tf_op jit(solution)/shard_map/ppermute | solution.py:279
  10.6 16.7 %collective-permute-start.2 = (bf16[1024,128]{1,0:T(8,128)(2,1)S(1)}, bf16[1024,128]{1,0:T(8,128)(2,1)S(1)}, u32[]{:S(2)}, u32[]{:S(2)}) collective-permute-start(bf16[1024,128]{1,0:T(8,128)(2,1)S(1)} %add_convert_fusion.5), channel_id=1, source_target_pairs={{0,4},{1,5},{2,6},{3,7},{8,12},{9,13},{10,14},{11,15},{16,20},{17,... | collective-permute-start | bytes 786440 | tf_op jit(solution)/shard_map/ppermute | solution.py:279
  15.1 13.4 %collective-permute-start.3 = (bf16[1024,128]{1,0:T(8,128)(2,1)S(1)}, bf16[1024,128]{1,0:T(8,128)(2,1)S(1)}, u32[]{:S(2)}, u32[]{:S(2)}) collective-permute-start(bf16[1024,128]{1,0:T(8,128)(2,1)S(1)} %add_convert_fusion.5), channel_id=1, source_target_pairs={{0,6},{1,7},{8,14},{9,15},{16,22},{17,23},{24,30},{25,31}} | collective-permute-start | bytes 786440 | tf_op jit(solution)/shard_map/ppermute | solution.py:279
  17.9 5.0 %collective-permute-start.7 = (f32[32,128]{1,0:T(8,128)S(1)}, f32[32,128]{1,0:T(8,128)S(1)}, u32[]{:S(2)}, u32[]{:S(2)}) collective-permute-start(f32[32,128]{1,0:T(8,128)S(1)} %select_reduce_fusion), channel_id=1, source_target_pairs={{0,1},{1,0},{2,3},{3,2},{4,5},{5,4},{6,7},{7,6},{8,9},{9,8},{10,11... | collective-permute-start | bytes 49160 | tf_op jit(solution)/shard_map/ppermute | solution.py:268
  22.9 6.3 %collective-permute-start.8 = (f32[2,32,128]{2,1,0:T(8,128)S(1)}, f32[2,32,128]{2,1,0:T(8,128)S(1)}, u32[]{:S(2)}, u32[]{:S(2)}) collective-permute-start(f32[2,32,128]{2,1,0:T(8,128)S(1)} %pad_maximum_fusion.1), channel_id=1, source_target_pairs={{0,2},{1,3},{2,0},{3,1},{4,6},{5,7},{6,4},{7,5},{8,10},{9,11},{10,... | collective-permute-start | bytes 98312 | tf_op jit(solution)/shard_map/ppermute | solution.py:271
  22.9 6.6 %collective-permute-start.9 = (f32[2,32,128]{2,1,0:T(8,128)S(1)}, f32[2,32,128]{2,1,0:T(8,128)S(1)}, u32[]{:S(2)}, u32[]{:S(2)}) collective-permute-start(f32[2,32,128]{2,1,0:T(8,128)S(1)} %pad_maximum_fusion.1), channel_id=1, source_target_pairs={{0,4},{1,5},{2,6},{3,7},{4,0},{5,1},{6,2},{7,3},{8,12},{9,13},{10,... | collective-permute-start | bytes 98312 | tf_op jit(solution)/shard_map/ppermute | solution.py:271
  23.0 6.8 %collective-permute-start.10 = (f32[2,32,128]{2,1,0:T(8,128)S(1)}, f32[2,32,128]{2,1,0:T(8,128)S(1)}, u32[]{:S(2)}, u32[]{:S(2)}) collective-permute-start(f32[2,32,128]{2,1,0:T(8,128)S(1)} %pad_maximum_fusion.1), channel_id=1, source_target_pairs={{0,6},{1,7},{2,4},{3,5},{4,2},{5,3},{6,0},{7,1},{8,14},{9,15},{10,... | collective-permute-start | bytes 98312 | tf_op jit(solution)/shard_map/ppermute | solution.py:271
  28.7 1.6 collective-permute-start.4
  38.8 24.4 %collective-permute-start.5 = (bf16[128,2048]{1,0:T(8,128)(2,1)}, bf16[128,2048]{1,0:T(8,128)(2,1)S(1)}, u32[]{:S(2)}, u32[]{:S(2)}) collective-permute-start(bf16[128,2048]{1,0:T(8,128)(2,1)} %get-tuple-element.48.own_ref), channel_id=1, source_target_pairs={{0,6},{1,7},{2,4},{3,5},{4,2},{5,3},{6,0},{7,1},{8,14},{9,15},{10,... | collective-permute-start | bytes 1572872 | tf_op jit(solution)/shard_map/ppermute | solution.py:271
  50.0 2.1 collective-permute-start.39
  50.2 44.4 %collective-permute-start.19 = (bf16[128,2048]{1,0:T(8,128)(2,1)}, bf16[128,2048]{1,0:T(8,128)(2,1)S(1)}, u32[]{:S(2)}, u32[]{:S(2)}) collective-permute-start(bf16[128,2048]{1,0:T(8,128)(2,1)} %get-tuple-element.48.own_ref), channel_id=1, source_target_pairs={{0,4},{1,5},{2,6},{3,7},{4,0},{5,1},{6,2},{7,3},{8,12},{9,13},{10,... | collective-permute-start | bytes 1572872 | tf_op jit(solution)/shard_map/ppermute | solution.py:271
  50.2 46.8 %collective-permute-start.29 = (bf16[128,2048]{1,0:T(8,128)(2,1)}, bf16[128,2048]{1,0:T(8,128)(2,1)S(1)}, u32[]{:S(2)}, u32[]{:S(2)}) collective-permute-start(bf16[128,2048]{1,0:T(8,128)(2,1)} %get-tuple-element.48.own_ref), channel_id=1, source_target_pairs={{0,2},{1,3},{2,0},{3,1},{4,6},{5,7},{6,4},{7,5},{8,10},{9,11},{10,... | collective-permute-start | bytes 1572872 | tf_op jit(solution)/shard_map/ppermute | solution.py:271
  55.7 41.3 %collective-permute-start.40 = (bf16[80,2048]{1,0:T(8,128)(2,1)}, bf16[80,2048]{1,0:T(8,128)(2,1)S(1)}, u32[]{:S(2)}, u32[]{:S(2)}) collective-permute-start(bf16[80,2048]{1,0:T(8,128)(2,1)} %get-tuple-element.80), channel_id=1, source_target_pairs={{0,8},{8,0},{16,24},{24,16},{1,9},{9,1},{17,25},{25,17},{2,10},{10... | collective-permute-start | bytes 983048 | tf_op jit(solution)/shard_map/ppermute | solution.py:276
  63.2 50.1 %copy-start.9 = (bf16[128,2048]{1,0:T(8,128)(2,1)}, bf16[128,2048]{1,0:T(8,128)(2,1)S(1)}, u32[]{:S(2)}) copy-start(bf16[128,2048]{1,0:T(8,128)(2,1)S(1)} %collective-permute-done.5.own_ref) | copy-start | bytes 1572868
  63.2 51.6 %collective-permute-start.6 = (bf16[128,2048]{1,0:T(8,128)(2,1)S(1)}, bf16[128,2048]{1,0:T(8,128)(2,1)S(1)}, u32[]{:S(2)}, u32[]{:S(2)}) collective-permute-start(bf16[128,2048]{1,0:T(8,128)(2,1)S(1)} %collective-permute-done.5.own_ref), channel_id=1, source_target_pairs={{0,1},{1,0},{2,3},{3,2},{4,5},{5,4},{6,7},{7,6},{8,9},{9,8},{10,11... | collective-permute-start | bytes 1572872 | tf_op jit(solution)/shard_map/ppermute | solution.py:268
  63.2 34.3 %collective-permute-start.41 = (bf16[80,2048]{1,0:T(8,128)(2,1)}, bf16[80,2048]{1,0:T(8,128)(2,1)}, u32[]{:S(2)}, u32[]{:S(2)}) collective-permute-start(bf16[80,2048]{1,0:T(8,128)(2,1)} %get-tuple-element.81), channel_id=1, source_target_pairs={{0,16},{8,24},{16,0},{24,8},{1,17},{9,25},{17,1},{25,9},{2,18},{10... | collective-permute-start | bytes 983048 | tf_op jit(solution)/shard_map/ppermute | solution.py:276
  94.5 18.7 %copy-start.8 = (bf16[128,2048]{1,0:T(8,128)(2,1)}, bf16[128,2048]{1,0:T(8,128)(2,1)S(1)}, u32[]{:S(2)}) copy-start(bf16[128,2048]{1,0:T(8,128)(2,1)S(1)} %collective-permute-done.19.own_ref) | copy-start | bytes 1572868
  94.5 10.1 %collective-permute-start.42 = (bf16[80,2048]{1,0:T(8,128)(2,1)}, bf16[80,2048]{1,0:T(8,128)(2,1)}, u32[]{:S(2)}, u32[]{:S(2)}) collective-permute-start(bf16[80,2048]{1,0:T(8,128)(2,1)} %get-tuple-element.82), channel_id=1, source_target_pairs={{0,24},{8,16},{16,8},{24,0},{1,25},{9,17},{17,9},{25,1},{2,26},{10... | collective-permute-start | bytes 983048 | tf_op jit(solution)/shard_map/ppermute | solution.py:276
  97.0 16.3 %copy-start.7 = (bf16[128,2048]{1,0:T(8,128)(2,1)}, bf16[128,2048]{1,0:T(8,128)(2,1)S(1)}, u32[]{:S(2)}) copy-start(bf16[128,2048]{1,0:T(8,128)(2,1)S(1)} %collective-permute-done.29.own_ref) | copy-start | bytes 1572868
  97.0 23.5 %collective-permute-start.20 = (bf16[128,2048]{1,0:T(8,128)(2,1)S(1)}, bf16[128,2048]{1,0:T(8,128)(2,1)S(1)}, u32[]{:S(2)}, u32[]{:S(2)}) collective-permute-start(bf16[128,2048]{1,0:T(8,128)(2,1)S(1)} %collective-permute-done.19.own_ref), channel_id=1, source_target_pairs={{0,1},{1,0},{2,3},{3,2},{4,5},{5,4},{6,7},{7,6},{8,9},{9,8},{10,11... | collective-permute-start | bytes 1572872 | tf_op jit(solution)/shard_map/ppermute | solution.py:268
  97.0 27.6 %collective-permute-start.30 = (bf16[128,2048]{1,0:T(8,128)(2,1)S(1)}, bf16[128,2048]{1,0:T(8,128)(2,1)S(1)}, u32[]{:S(2)}, u32[]{:S(2)}) collective-permute-start(bf16[128,2048]{1,0:T(8,128)(2,1)S(1)} %collective-permute-done.29.own_ref), channel_id=1, source_target_pairs={{0,1},{1,0},{2,3},{3,2},{4,5},{5,4},{6,7},{7,6},{8,9},{9,8},{10,11... | collective-permute-start | bytes 1572872 | tf_op jit(solution)/shard_map/ppermute | solution.py:268
  113.3 13.0 %collective-permute-start.43 = (bf16[80,2048]{1,0:T(8,128)(2,1)}, bf16[80,2048]{1,0:T(8,128)(2,1)S(1)}, u32[]{:S(2)}, u32[]{:S(2)}) collective-permute-start(bf16[80,2048]{1,0:T(8,128)(2,1)} %get-tuple-element.84), channel_id=1, source_target_pairs={{0,8},{8,0},{16,24},{24,16},{1,9},{9,1},{17,25},{25,17},{2,10},{10... | collective-permute-start | bytes 983048 | tf_op jit(solution)/shard_map/ppermute | solution.py:276
  118.4 12.5 %collective-permute-start.11 = (bf16[80,2048]{1,0:T(8,128)(2,1)}, bf16[80,2048]{1,0:T(8,128)(2,1)S(1)}, u32[]{:S(2)}, u32[]{:S(2)}) collective-permute-start(bf16[80,2048]{1,0:T(8,128)(2,1)} %get-tuple-element.50), channel_id=1, source_target_pairs={{0,8},{8,0},{16,24},{24,16},{1,9},{9,1},{17,25},{25,17},{2,10},{10... | collective-permute-start | bytes 983048 | tf_op jit(solution)/shard_map/ppermute | solution.py:276
  118.9 14.2 %collective-permute-start.12 = (bf16[80,2048]{1,0:T(8,128)(2,1)}, bf16[80,2048]{1,0:T(8,128)(2,1)S(1)}, u32[]{:S(2)}, u32[]{:S(2)}) collective-permute-start(bf16[80,2048]{1,0:T(8,128)(2,1)} %get-tuple-element.51), channel_id=1, source_target_pairs={{0,16},{8,24},{16,0},{24,8},{1,17},{9,25},{17,1},{25,9},{2,18},{10... | collective-permute-start | bytes 983048 | tf_op jit(solution)/shard_map/ppermute | solution.py:276
  120.5 19.4 %collective-permute-start.13 = (bf16[80,2048]{1,0:T(8,128)(2,1)}, bf16[80,2048]{1,0:T(8,128)(2,1)S(1)}, u32[]{:S(2)}, u32[]{:S(2)}) collective-permute-start(bf16[80,2048]{1,0:T(8,128)(2,1)} %get-tuple-element.52), channel_id=1, source_target_pairs={{0,24},{8,16},{16,8},{24,0},{1,25},{9,17},{17,9},{25,1},{2,26},{10... | collective-permute-start | bytes 983048 | tf_op jit(solution)/shard_map/ppermute | solution.py:276
  124.6 12.5 %copy-start.10 = (bf16[128,2048]{1,0:T(8,128)(2,1)}, bf16[128,2048]{1,0:T(8,128)(2,1)S(1)}, u32[]{:S(2)}) copy-start(bf16[128,2048]{1,0:T(8,128)(2,1)S(1)} %collective-permute-done.30.par_ref) | copy-start | bytes 1572868
  124.6 24.7 %collective-permute-start.44 = (bf16[80,2048]{1,0:T(8,128)(2,1)}, bf16[80,2048]{1,0:T(8,128)(2,1)S(1)}, u32[]{:S(2)}, u32[]{:S(2)}) collective-permute-start(bf16[80,2048]{1,0:T(8,128)(2,1)} %get-tuple-element.85), channel_id=1, source_target_pairs={{0,16},{8,24},{16,0},{24,8},{1,17},{9,25},{17,1},{25,9},{2,18},{10... | collective-permute-start | bytes 983048 | tf_op jit(solution)/shard_map/ppermute | solution.py:276
  126.2 23.1 %copy-start.14 = (bf16[80,2048]{1,0:T(8,128)(2,1)}, bf16[80,2048]{1,0:T(8,128)(2,1)S(1)}, u32[]{:S(2)}) copy-start(bf16[80,2048]{1,0:T(8,128)(2,1)S(1)} %collective-permute-done.43.refs_1_) | copy-start | bytes 983044
  126.2 24.5 %collective-permute-start.21 = (bf16[80,2048]{1,0:T(8,128)(2,1)}, bf16[80,2048]{1,0:T(8,128)(2,1)S(1)}, u32[]{:S(2)}, u32[]{:S(2)}) collective-permute-start(bf16[80,2048]{1,0:T(8,128)(2,1)} %get-tuple-element.60), channel_id=1, source_target_pairs={{0,8},{8,0},{16,24},{24,16},{1,9},{9,1},{17,25},{25,17},{2,10},{10... | collective-permute-start | bytes 983048 | tf_op jit(solution)/shard_map/ppermute | solution.py:276
  131.7 24.9 %collective-permute-start.22 = (bf16[80,2048]{1,0:T(8,128)(2,1)}, bf16[80,2048]{1,0:T(8,128)(2,1)S(1)}, u32[]{:S(2)}, u32[]{:S(2)}) collective-permute-start(bf16[80,2048]{1,0:T(8,128)(2,1)} %get-tuple-element.61), channel_id=1, source_target_pairs={{0,16},{8,24},{16,0},{24,8},{1,17},{9,25},{17,1},{25,9},{2,18},{10... | collective-permute-start | bytes 983048 | tf_op jit(solution)/shard_map/ppermute | solution.py:276
  133.2 27.5 %collective-permute-start.23 = (bf16[80,2048]{1,0:T(8,128)(2,1)}, bf16[80,2048]{1,0:T(8,128)(2,1)}, u32[]{:S(2)}, u32[]{:S(2)}) collective-permute-start(bf16[80,2048]{1,0:T(8,128)(2,1)} %get-tuple-element.62), channel_id=1, source_target_pairs={{0,24},{8,16},{16,8},{24,0},{1,25},{9,17},{17,9},{25,1},{2,26},{10... | collective-permute-start | bytes 983048 | tf_op jit(solution)/shard_map/ppermute | solution.py:276
  139.9 20.8 %collective-permute-start.31 = (bf16[80,2048]{1,0:T(8,128)(2,1)}, bf16[80,2048]{1,0:T(8,128)(2,1)S(1)}, u32[]{:S(2)}, u32[]{:S(2)}) collective-permute-start(bf16[80,2048]{1,0:T(8,128)(2,1)} %get-tuple-element.70), channel_id=1, source_target_pairs={{0,8},{8,0},{16,24},{24,16},{1,9},{9,1},{17,25},{25,17},{2,10},{10... | collective-permute-start | bytes 983048 | tf_op jit(solution)/shard_map/ppermute | solution.py:276
  140.7 20.0 %copy-start.34 = (bf16[80,2048]{1,0:T(8,128)(2,1)S(1)}, bf16[80,2048]{1,0:T(8,128)(2,1)}, u32[]{:S(2)}) copy-start(bf16[80,2048]{1,0:T(8,128)(2,1)} %get-tuple-element.72) | copy-start | bytes 983044
  149.3 21.0 %copy-start.15 = (bf16[80,2048]{1,0:T(8,128)(2,1)}, bf16[80,2048]{1,0:T(8,128)(2,1)S(1)}, u32[]{:S(2)}) copy-start(bf16[80,2048]{1,0:T(8,128)(2,1)S(1)} %collective-permute-done.44.refs_2_) | copy-start | bytes 983044
  149.4 21.0 %collective-permute-start.14 = (bf16[80,2048]{1,0:T(8,128)(2,1)}, bf16[80,2048]{1,0:T(8,128)(2,1)S(1)}, u32[]{:S(2)}, u32[]{:S(2)}) collective-permute-start(bf16[80,2048]{1,0:T(8,128)(2,1)} %get-tuple-element.54), channel_id=1, source_target_pairs={{0,8},{8,0},{16,24},{24,16},{1,9},{9,1},{17,25},{25,17},{2,10},{10... | collective-permute-start | bytes 983048 | tf_op jit(solution)/shard_map/ppermute | solution.py:276
  150.8 11.0 %copy-start.25 = (bf16[80,2048]{1,0:T(8,128)(2,1)}, bf16[80,2048]{1,0:T(8,128)(2,1)S(1)}, u32[]{:S(2)}) copy-start(bf16[80,2048]{1,0:T(8,128)(2,1)S(1)} %collective-permute-done.21.refs_1_) | copy-start | bytes 983044
  150.8 22.1 %collective-permute-start.15 = (bf16[80,2048]{1,0:T(8,128)(2,1)}, bf16[80,2048]{1,0:T(8,128)(2,1)S(1)}, u32[]{:S(2)}, u32[]{:S(2)}) collective-permute-start(bf16[80,2048]{1,0:T(8,128)(2,1)} %get-tuple-element.55), channel_id=1, source_target_pairs={{0,16},{8,24},{16,0},{24,8},{1,17},{9,25},{17,1},{25,9},{2,18},{10... | collective-permute-start | bytes 983048 | tf_op jit(solution)/shard_map/ppermute | solution.py:276
  157.3 16.9 %collective-permute-start.16 = (bf16[80,2048]{1,0:T(8,128)(2,1)}, bf16[80,2048]{1,0:T(8,128)(2,1)S(1)}, u32[]{:S(2)}, u32[]{:S(2)}) collective-permute-start(bf16[80,2048]{1,0:T(8,128)(2,1)} %get-tuple-element.56), channel_id=1, source_target_pairs={{0,24},{8,16},{16,8},{24,0},{1,25},{9,17},{17,9},{25,1},{2,26},{10... | collective-permute-start | bytes 983048 | tf_op jit(solution)/shard_map/ppermute | solution.py:276
  160.7 25.0 %collective-permute-start.32 = (bf16[80,2048]{1,0:T(8,128)(2,1)}, bf16[80,2048]{1,0:T(8,128)(2,1)S(1)}, u32[]{:S(2)}, u32[]{:S(2)}) collective-permute-start(bf16[80,2048]{1,0:T(8,128)(2,1)} %get-tuple-element.71), channel_id=1, source_target_pairs={{0,16},{8,24},{16,0},{24,8},{1,17},{9,25},{17,1},{25,9},{2,18},{10... | collective-permute-start | bytes 983048 | tf_op jit(solution)/shard_map/ppermute | solution.py:276
  160.7 9.7 %copy-start.24 = (bf16[80,2048]{1,0:T(8,128)(2,1)}, bf16[80,2048]{1,0:T(8,128)(2,1)S(1)}, u32[]{:S(2)}) copy-start(bf16[80,2048]{1,0:T(8,128)(2,1)S(1)} %collective-permute-done.31.refs_1_) | copy-start | bytes 983044
  160.7 25.0 %collective-permute-start.33 = (bf16[80,2048]{1,0:T(8,128)(2,1)S(1)}, bf16[80,2048]{1,0:T(8,128)(2,1)S(1)}, u32[]{:S(2)}, u32[]{:S(2)}) collective-permute-start(bf16[80,2048]{1,0:T(8,128)(2,1)S(1)} %copy-done.34), channel_id=1, source_target_pairs={{0,24},{8,16},{16,8},{24,0},{1,25},{9,17},{17,9},{25,1},{2,26},{10... | collective-permute-start | bytes 983048 | tf_op jit(solution)/shard_map/ppermute | solution.py:276
  170.4 8.9 %copy-start.18 = (bf16[80,2048]{1,0:T(8,128)(2,1)}, bf16[80,2048]{1,0:T(8,128)(2,1)S(1)}, u32[]{:S(2)}) copy-start(bf16[80,2048]{1,0:T(8,128)(2,1)S(1)} %collective-permute-done.14.refs_1_) | copy-start | bytes 983044
  170.4 33.6 %collective-permute-start.24 = (bf16[80,2048]{1,0:T(8,128)(2,1)}, bf16[80,2048]{1,0:T(8,128)(2,1)S(1)}, u32[]{:S(2)}, u32[]{:S(2)}) collective-permute-start(bf16[80,2048]{1,0:T(8,128)(2,1)} %get-tuple-element.64), channel_id=1, source_target_pairs={{0,8},{8,0},{16,24},{24,16},{1,9},{9,1},{17,25},{25,17},{2,10},{10... | collective-permute-start | bytes 983048 | tf_op jit(solution)/shard_map/ppermute | solution.py:276
  172.9 31.1 %collective-permute-start.25 = (bf16[80,2048]{1,0:T(8,128)(2,1)}, bf16[80,2048]{1,0:T(8,128)(2,1)S(1)}, u32[]{:S(2)}, u32[]{:S(2)}) collective-permute-start(bf16[80,2048]{1,0:T(8,128)(2,1)} %get-tuple-element.65), channel_id=1, source_target_pairs={{0,16},{8,24},{16,0},{24,8},{1,17},{9,25},{17,1},{25,9},{2,18},{10... | collective-permute-start | bytes 983048 | tf_op jit(solution)/shard_map/ppermute | solution.py:276
  174.1 31.3 %collective-permute-start.26 = (bf16[80,2048]{1,0:T(8,128)(2,1)}, bf16[80,2048]{1,0:T(8,128)(2,1)S(1)}, u32[]{:S(2)}, u32[]{:S(2)}) collective-permute-start(bf16[80,2048]{1,0:T(8,128)(2,1)} %get-tuple-element.66), channel_id=1, source_target_pairs={{0,24},{8,16},{16,8},{24,0},{1,25},{9,17},{17,9},{25,1},{2,26},{10... | collective-permute-start | bytes 983048 | tf_op jit(solution)/shard_map/ppermute | solution.py:276
  185.6 9.5 %copy-start.27 = (bf16[80,2048]{1,0:T(8,128)(2,1)}, bf16[80,2048]{1,0:T(8,128)(2,1)S(1)}, u32[]{:S(2)}) copy-start(bf16[80,2048]{1,0:T(8,128)(2,1)S(1)} %collective-permute-done.32.refs_2_) | copy-start | bytes 983044
  185.6 38.4 %collective-permute-start.17 = (bf16[128,2048]{1,0:T(8,128)(2,1)}, bf16[128,2048]{1,0:T(8,128)(2,1)S(1)}, u32[]{:S(2)}, u32[]{:S(2)}) collective-permute-start(bf16[128,2048]{1,0:T(8,128)(2,1)} %get-tuple-element.58), channel_id=1, source_target_pairs={{0,1},{1,0},{2,3},{3,2},{4,5},{5,4},{6,7},{7,6},{8,9},{9,8},{10,11... | collective-permute-start | bytes 1572872 | tf_op jit(solution)/shard_map/ppermute | solution.py:268
  185.6 9.5 %copy-start.30 = (bf16[80,2048]{1,0:T(8,128)(2,1)}, bf16[80,2048]{1,0:T(8,128)(2,1)S(1)}, u32[]{:S(2)}) copy-start(bf16[80,2048]{1,0:T(8,128)(2,1)S(1)} %collective-permute-done.33.refs_3_) | copy-start | bytes 983044
  185.7 24.7 %collective-permute-start.45 = (bf16[80,2048]{1,0:T(8,128)(2,1)}, bf16[80,2048]{1,0:T(8,128)(2,1)S(1)}, u32[]{:S(2)}, u32[]{:S(2)}) collective-permute-start(bf16[80,2048]{1,0:T(8,128)(2,1)} %get-tuple-element.86), channel_id=1, source_target_pairs={{0,24},{8,16},{16,8},{24,0},{1,25},{9,17},{17,9},{25,1},{2,26},{10... | collective-permute-start | bytes 983048 | tf_op jit(solution)/shard_map/ppermute | solution.py:276
  203.9 20.1 %copy-start.3 = (bf16[128,2048]{1,0:T(8,128)(2,1)S(1)}, bf16[128,2048]{1,0:T(8,128)(2,1)}, u32[]{:S(2)}) copy-start(bf16[128,2048]{1,0:T(8,128)(2,1)} %get-tuple-element.57) | copy-start | bytes 1572868
  203.9 10.9 %collective-permute-start.34 = (bf16[80,2048]{1,0:T(8,128)(2,1)}, bf16[80,2048]{1,0:T(8,128)(2,1)S(1)}, u32[]{:S(2)}, u32[]{:S(2)}) collective-permute-start(bf16[80,2048]{1,0:T(8,128)(2,1)} %get-tuple-element.74), channel_id=1, source_target_pairs={{0,8},{8,0},{16,24},{24,16},{1,9},{9,1},{17,25},{25,17},{2,10},{10... | collective-permute-start | bytes 983048 | tf_op jit(solution)/shard_map/ppermute | solution.py:276
  204.0 17.2 %collective-permute-start.35 = (bf16[80,2048]{1,0:T(8,128)(2,1)}, bf16[80,2048]{1,0:T(8,128)(2,1)}, u32[]{:S(2)}, u32[]{:S(2)}) collective-permute-start(bf16[80,2048]{1,0:T(8,128)(2,1)} %get-tuple-element.75), channel_id=1, source_target_pairs={{0,16},{8,24},{16,0},{24,8},{1,17},{9,25},{17,1},{25,9},{2,18},{10... | collective-permute-start | bytes 983048 | tf_op jit(solution)/shard_map/ppermute | solution.py:276
  205.4 15.8 %collective-permute-start.36 = (bf16[80,2048]{1,0:T(8,128)(2,1)}, bf16[80,2048]{1,0:T(8,128)(2,1)}, u32[]{:S(2)}, u32[]{:S(2)}) collective-permute-start(bf16[80,2048]{1,0:T(8,128)(2,1)} %get-tuple-element.76), channel_id=1, source_target_pairs={{0,24},{8,16},{16,8},{24,0},{1,25},{9,17},{17,9},{25,1},{2,26},{10... | collective-permute-start | bytes 983048 | tf_op jit(solution)/shard_map/ppermute | solution.py:276
  210.3 14.4 %copy-start.5 = (bf16[128,2048]{1,0:T(8,128)(2,1)S(1)}, bf16[128,2048]{1,0:T(8,128)(2,1)}, u32[]{:S(2)}) copy-start(bf16[128,2048]{1,0:T(8,128)(2,1)} %get-tuple-element.67) | copy-start | bytes 1572868
  210.3 14.4 %collective-permute-start.27 = (bf16[128,2048]{1,0:T(8,128)(2,1)}, bf16[128,2048]{1,0:T(8,128)(2,1)}, u32[]{:S(2)}, u32[]{:S(2)}) collective-permute-start(bf16[128,2048]{1,0:T(8,128)(2,1)} %get-tuple-element.68), channel_id=1, source_target_pairs={{0,1},{1,0},{2,3},{3,2},{4,5},{5,4},{6,7},{7,6},{8,9},{9,8},{10,11... | collective-permute-start | bytes 1572872 | tf_op jit(solution)/shard_map/ppermute | solution.py:268
  213.9 56.3 %copy-start.2 = (bf16[128,2048]{1,0:T(8,128)(2,1)S(1)}, bf16[128,2048]{1,0:T(8,128)(2,1)}, u32[]{:S(2)}) copy-start(bf16[128,2048]{1,0:T(8,128)(2,1)} %get-tuple-element.47) | copy-start | bytes 1572868
  213.9 56.3 %copy-start.4 = (bf16[128,2048]{1,0:T(8,128)(2,1)S(1)}, bf16[128,2048]{1,0:T(8,128)(2,1)}, u32[]{:S(2)}) copy-start(bf16[128,2048]{1,0:T(8,128)(2,1)} %get-tuple-element.87) | copy-start | bytes 1572868
  214.8 15.3 %collective-permute-start.46 = (bf16[128,2048]{1,0:T(8,128)(2,1)}, bf16[128,2048]{1,0:T(8,128)(2,1)S(1)}, u32[]{:S(2)}, u32[]{:S(2)}) collective-permute-start(bf16[128,2048]{1,0:T(8,128)(2,1)} %get-tuple-element.88), channel_id=1, source_target_pairs={{0,1},{1,0},{2,3},{3,2},{4,5},{5,4},{6,7},{7,6},{8,9},{9,8},{10,11... | collective-permute-start | bytes 1572872 | tf_op jit(solution)/shard_map/ppermute | solution.py:268
  224.0 2.1 collective-permute-start.37
  224.2 16.8 %collective-permute-start.18 = (bf16[128,2048]{1,0:T(8,128)(2,1)S(1)}, bf16[128,2048]{1,0:T(8,128)(2,1)S(1)}, u32[]{:S(2)}, u32[]{:S(2)}) collective-permute-start(bf16[128,2048]{1,0:T(8,128)(2,1)S(1)} %add_convert_fusion.3), channel_id=1, source_target_pairs={{0,6},{1,7},{2,4},{3,5},{4,2},{5,3},{6,0},{7,1},{8,14},{9,15},{10,... | collective-permute-start | bytes 1572872 | tf_op jit(solution)/shard_map/ppermute | solution.py:271
  225.9 44.3 %collective-permute-start.28 = (bf16[128,2048]{1,0:T(8,128)(2,1)S(1)}, bf16[128,2048]{1,0:T(8,128)(2,1)S(1)}, u32[]{:S(2)}, u32[]{:S(2)}) collective-permute-start(bf16[128,2048]{1,0:T(8,128)(2,1)S(1)} %add_convert_fusion.2), channel_id=1, source_target_pairs={{0,4},{1,5},{2,6},{3,7},{4,0},{5,1},{6,2},{7,3},{8,12},{9,13},{10,... | collective-permute-start | bytes 1572872 | tf_op jit(solution)/shard_map/ppermute | solution.py:271
  226.3 43.9 %collective-permute-start.38 = (bf16[128,2048]{1,0:T(8,128)(2,1)S(1)}, bf16[128,2048]{1,0:T(8,128)(2,1)S(1)}, u32[]{:S(2)}, u32[]{:S(2)}) collective-permute-start(bf16[128,2048]{1,0:T(8,128)(2,1)S(1)} %add_convert_fusion.1), channel_id=1, source_target_pairs={{0,2},{1,3},{2,0},{3,1},{4,6},{5,7},{6,4},{7,5},{8,10},{9,11},{10,... | collective-permute-start | bytes 1572872 | tf_op jit(solution)/shard_map/ppermute | solution.py:271
  (18 other events, 52.0 us)
where the time goes:
time: 272 us; the launch traced here: 271 us
  waiting for transfers between devices  108 us (40%)
  starting transfers between devices  79 us (29%)
  Pallas kernels  71.8 us (26%)
  other arithmetic  6.17 us (2%)
  local copies, waits for them, and re-layouts  5.86 us (2%)
    ppermute x9, waiting for transfers between devices, along(): return lax.ppermute(x, 'seq', [(s, s ^ 2 * m) for s in range(length)])  77 us
    ppermute x24, starting transfers between devices, across(): return lax.ppermute(x, 'grp', [(g, g ^ m) for g in range(groups)])  46.4 us
    pallas_call x4, Pallas kernels, experts(): pl.pallas_call(functools.partial(expert_kernel, groups), grid=(steps,), i...  34.6 us
    ppermute x24, waiting for transfers between devices, across(): return lax.ppermute(x, 'grp', [(g, g ^ m) for g in range(groups)])  28.2 us
    ppermute x9, starting transfers between devices, along(): return lax.ppermute(x, 'seq', [(s, s ^ 2 * m) for s in range(length)])  20.8 us
    pallas_call x4, Pallas kernels, combine(): pl.pallas_call(functools.partial(combine_kernel, slots, len(backs)), out_...  11.2 us
    pallas_call x4, Pallas kernels, select(): pl.pallas_call(functools.partial(select_kernel, slots), out_shape=[shape]...  11 us
    ppermute x3, starting transfers between devices, later(): lax.ppermute(x, 'seq', [(s, s + 2 * m) for s in range(length - 2 * m)])  10.7 us
  transfers between devices with their start and end apart: 47, of which 19 were waited for; matrix products, arithmetic and copies ran while one was open for 2% of the time, Pallas kernels for 23%

commit v1 on v0

v1 whole, which is shorter than its diff:
```python
import functools

import jax
import jax.numpy as jnp
from jax import lax
from jax.experimental import pallas as pl
from jax.experimental.pallas import tpu as pltpu
from jax.sharding import PartitionSpec as P


HEAD = 128
TOP = 8
epsilon = 1e-06
BF = jnp.bfloat16
F32 = jnp.float32


def dot(a, b, ca=1, cb=0):
    return lax.dot_general(a, b, (((ca,), (cb,)), ((), ())), preferred_element_type=F32)


def call(body, outs, scratch=(), limit=24):
    def run(*args):
        specs = []
        placed = []
        for x in args:
            space = pltpu.SMEM if x.size == 1 else pltpu.VMEM
            specs.append(pl.BlockSpec(memory_space=space))
            placed.append(pltpu.with_memory_space_constraint(x, space))
        return pl.pallas_call(
            body,
            in_specs=specs,
            out_specs=[pl.BlockSpec(memory_space=pltpu.VMEM)] * len(outs),
            out_shape=[pltpu.VMEM(shape, dtype) for shape, dtype in outs],
            scratch_shapes=list(scratch),
            compiler_params=pltpu.CompilerParams(vmem_limit_bytes=limit << 20),
        )(*placed)

    return run


def state_kernel(k_ref, v_ref, s_ref):
    heads = k_ref.shape[1] // HEAD
    for h in range(heads):
        cols = slice(h * HEAD, (h + 1) * HEAD)
        s_ref[cols, :] = dot(k_ref[:, cols], v_ref[:, cols], 0, 0).astype(BF)


def inside_kernel(q_ref, k_ref, v_ref, o_ref):
    tokens = q_ref.shape[0]
    heads = q_ref.shape[1] // HEAD
    rows = lax.broadcasted_iota(jnp.int32, (tokens, tokens), 0)
    cols = lax.broadcasted_iota(jnp.int32, (tokens, tokens), 1)
    causal = rows >= cols
    for h in range(heads):
        part = slice(h * HEAD, (h + 1) * HEAD)
        scores = dot(q_ref[:, part], k_ref[:, part], 1, 1)
        scores = jnp.where(causal, scores, 0.0).astype(BF)
        o_ref[:, part] = dot(scores, v_ref[:, part])


def project_kernel(
    core_ref, in_ref, q_ref, mine_ref, other_ref, pair_ref, gain_ref, resid_ref, w_ref, mgain_ref,
    res_ref, moe_ref, normed_ref,
):
    core = core_ref[0]
    heads = q_ref.shape[1] // HEAD
    half = heads // 2
    low = core == 0
    second = jnp.where(low, 0.0, 1.0)
    for h in range(heads):
        part = slice(h * HEAD, (h + 1) * HEAD)
        at = slice((h % half) * HEAD, (h % half + 1) * HEAD)
        first = low if h < half else jnp.logical_not(low)
        prefix = jnp.where(first, mine_ref[at, :].astype(F32), other_ref[at, :].astype(F32))
        carried = (prefix + second * pair_ref[part, :].astype(F32)).astype(BF)
        attended = in_ref[:, part] + dot(q_ref[:, part], carried)
        mean = jnp.mean(attended * attended, axis=1, keepdims=True)
        normed_ref[:, part] = (attended * lax.rsqrt(mean + epsilon) * gain_ref[:, part]).astype(BF)
    features = res_ref.shape[1]
    width = features // 4
    square = jnp.zeros((res_ref.shape[0], 1), F32)
    for i in range(4):
        at = slice(i * width, (i + 1) * width)
        added = resid_ref[:, at].astype(F32) + dot(normed_ref[...], w_ref[:, at])
        rounded = added.astype(BF)
        res_ref[:, at] = rounded
        wide = rounded.astype(F32)
        square = square + jnp.sum(wide * wide, axis=1, keepdims=True)
    scale = lax.rsqrt(square / features + epsilon)
    moe_ref[...] = (res_ref[...].astype(F32) * scale * mgain_ref[...]).astype(BF)


def rank_kernel(route_ref, rank_ref):
    tokens = route_ref.shape[1]
    rows = lax.broadcasted_iota(jnp.int32, (tokens, tokens), 0)
    cols = lax.broadcasted_iota(jnp.int32, (tokens, tokens), 1)
    earlier = jnp.where(rows < cols, 1.0, 0.0).astype(BF)
    named = route_ref[...] > 0.0
    rank = dot(jnp.where(named, 1.0, 0.0).astype(BF), earlier)
    rank_ref[...] = jnp.where(named, rank, -1.0)


def slots_of(rank_ref, value, row, slots):
    rank = rank_ref[row : row + 1, :]
    number = lax.broadcasted_iota(jnp.int32, (slots, rank.shape[1]), 0).astype(F32)
    return jnp.where(number == rank, value, 0.0)


def select_kernel(slots, base, own_ref, par_ref, rank_ref, *outs):
    groups = len(outs)
    picks = []
    for block in range(2):
        rows = [slots_of(rank_ref, 1.0, base + block * groups + k, slots) for k in range(groups)]
        picks.append(jnp.concatenate(rows, axis=0).astype(BF))
    first = dot(picks[0], own_ref[...])
    second = dot(picks[1], par_ref[...])
    for k in range(groups):
        at = slice(k * slots, (k + 1) * slots)
        outs[k][...] = jnp.concatenate([first[at], second[at]], axis=0).astype(BF)


def select(slots, groups, base, own, par, rank):
    shape = ((2 * slots, own.shape[1]), BF)
    body = functools.partial(select_kernel, slots, base)
    return call(body, [shape] * groups)(own, par, rank)


def combine_kernel(slots, groups, base, *refs):
    backs = refs[:groups]
    rank_ref, weight_ref, own_ref, par_ref = refs[groups:]
    rows = jnp.concatenate([r[...] for r in backs], axis=0)
    zero = jnp.zeros((slots, rank_ref.shape[1]), F32)
    sides = []
    for block in range(2):
        parts = []
        for k in range(groups):
            row = base + block * groups + k
            mine = slots_of(rank_ref, weight_ref[row : row + 1, :], row, slots)
            parts += [mine, zero] if block == 0 else [zero, mine]
        sides.append(jnp.concatenate(parts, axis=0).astype(BF))
    own_ref[...] = dot(sides[0], rows, 0, 0).astype(BF)
    par_ref[...] = dot(sides[1], rows, 0, 0).astype(BF)


def combine(slots, base, backs, rank, weight):
    shape = ((rank.shape[1], backs[0].shape[1]), BF)
    body = functools.partial(combine_kernel, slots, len(backs), base)
    return call(body, [shape] * 2)(*backs, rank, weight)


def expert_kernel(groups, *refs):
    xs = refs[:groups]
    gate_ref, up_ref, down_ref = refs[groups : groups + 3]
    outs = refs[groups + 3 : 2 * groups + 3]
    hidden_ref = refs[2 * groups + 3]
    rows, features = xs[0].shape
    units = gate_ref.shape[2]
    x = jnp.concatenate([r[...] for r in xs], axis=0)
    width = 256
    for j in range(units // width):
        at = slice(j * width, (j + 1) * width)
        gate = dot(x, gate_ref[0, :, at])
        up = dot(x, up_ref[0, :, at])
        hidden_ref[:, at] = (gate / (1.0 + jnp.exp(-gate)) * up).astype(BF)
    hidden = hidden_ref[...]
    width = 512
    for j in range(features // width):
        at = slice(j * width, (j + 1) * width)
        out = dot(hidden, down_ref[0, :, at]).astype(BF)
        for k in range(groups):
            outs[k][:, at] = out[k * rows : (k + 1) * rows]


def experts(xs, gate, up, down):
    groups = len(xs)
    body = functools.partial(expert_kernel, groups)
    scratch = [pltpu.VMEM((groups * xs[0].shape[0], gate.shape[2]), BF)]
    outs = [(xs[0].shape, BF)] * groups
    return call(body, outs, scratch)(*xs, gate, up, down)


def on_device(
    resid_in,
    lin_query,
    lin_key,
    lin_value,
    lin_gain,
    out_proj,
    moe_gain,
    expert_ids,
    route_scores,
    gate_weight,
    up_weight,
    down_weight,
):
    tokens = resid_in.shape[1]
    features = resid_in.shape[2]
    groups = lax.axis_size("grp")
    length = lax.axis_size("seq")
    stages = length // 2
    group = lax.axis_index("grp")
    place = lax.axis_index("seq")
    core = place % 2
    expert_count = gate_weight.shape[0] * groups * length
    capacity = tokens * TOP * 5 // (4 * expert_count)
    slots = -(-capacity // 8) * 8

    def swap(x):
        return lax.ppermute(x, "seq", [(s, s ^ 1) for s in range(length)])

    def along(x, m):
        return lax.ppermute(x, "seq", [(s, s ^ (2 * m)) for s in range(length)])

    def across(x, m):
        if m == 0:
            return x
        return lax.ppermute(x, "grp", [(g, g ^ m) for g in range(groups)])

    def later(x, m):
        return lax.ppermute(x, "seq", [(s, s + 2 * m) for s in range(length - 2 * m)])

    queries = lin_query.reshape(tokens, -1)
    keys = lin_key.reshape(tokens, -1)
    values = lin_value.reshape(tokens, -1)
    inner = queries.shape[1]
    half = inner // 2

    states = call(state_kernel, [((inner, HEAD), BF)])(keys, values)[0]
    pair = swap(states)
    summed = (states.astype(F32) + pair.astype(F32)).astype(BF)
    summed = lax.dynamic_slice_in_dim(summed, core * half, half, axis=0)
    arrived = [later(summed, m) for m in range(1, stages)]

    chosen = expert_ids.reshape(tokens, TOP).T
    scores = route_scores.reshape(tokens, TOP)
    shares = (scores / jnp.sum(scores, axis=1, keepdims=True)).T
    hit = chosen[None] == jnp.arange(expert_count, dtype=jnp.int32)[:, None, None]
    dense = jnp.sum(jnp.where(hit, shares[None], 0.0), axis=1)
    both = jnp.stack([dense, swap(dense)])
    routes = jnp.stack([both] + [along(both, m) for m in range(1, stages)])
    routes = routes.reshape(stages, 2, groups, length, tokens)
    routes = lax.dynamic_index_in_dim(routes, place, axis=3, keepdims=False)
    routes = jnp.stack(
        [
            lax.dynamic_index_in_dim(routes, group ^ k, axis=2, keepdims=False)
            for k in range(groups)
        ],
        axis=2,
    ).reshape(stages * 2 * groups, tokens)

    inside = call(inside_kernel, [((tokens, inner), F32)])(queries, keys, values)[0]
    ranks = call(rank_kernel, [(routes.shape, F32)])(routes)[0]
    total = arrived[0].astype(F32)
    for more in arrived[1:]:
        total = total + more.astype(F32)
    mine = total.astype(BF)
    other = swap(mine)
    residual, moe_in = call(
        project_kernel, [((tokens, features), BF)] * 2, [pltpu.VMEM((tokens, inner), BF)]
    )(
        core.reshape(1),
        inside,
        queries,
        mine,
        other,
        pair,
        lin_gain.reshape(1, inner),
        resid_in.reshape(tokens, features),
        out_proj,
        moe_gain.reshape(1, features),
    )

    routing = sending(stages)
    returning = homing(stages)
    blocks = {0: moe_in}
    outs = {}
    partners = {0: swap(moe_in)}
    for m in range(1, stages):
        source, shift = routing[m]
        blocks[m] = along(blocks[source], shift)
    for m in range(stages):
        base = m * 2 * groups
        partner = swap(blocks[m]) if m else partners[0]
        picked = select(slots, groups, base, blocks[m], partner, ranks)
        taken = [across(picked[k], k) for k in range(groups)]
        outs[m] = experts(taken, gate_weight, up_weight, down_weight)
    sums = {m: [] for m in range(stages)}
    for m in back_order(stages):
        base = m * 2 * groups
        backs = [across(outs[m][k], k) for k in range(groups)]
        own, par = combine(slots, base, backs, ranks, routes)
        part = own.astype(F32) + swap(par).astype(F32)
        for more in sums[m]:
            part = part + more.astype(F32)
        if m:
            into, shift = returning[m]
            sums[into].append(along(part.astype(BF), shift))
    combined = residual.astype(F32) + part
    return combined.astype(BF).reshape(1, tokens, features)


def sending(stages):
    if stages == 4:
        return {1: (0, 1), 2: (0, 2), 3: (2, 1)}
    return {m: (0, m) for m in range(1, stages)}


def homing(stages):
    if stages == 4:
        return {2: (3, 1), 3: (0, 3), 1: (0, 1)}
    return {m: (0, m) for m in range(1, stages)}


def back_order(stages):
    return list(range(2, stages)) + [1, 0]


def solution(mesh):
    rows = P("grp", "seq", None)
    held = P(("grp", "seq"), None, None)
    in_specs = (rows, rows, rows, rows, P(), P(), P(), rows, rows, held, held, held)

    return jax.shard_map(on_device, mesh=mesh, in_specs=in_specs, out_specs=rows, check_vma=False)
```

time: 272 us -> 247 us (0.908)
  Pallas kernels: 71.8 us -> 28.4 us
  waiting for transfers between devices: 108 us -> 149 us
  starting transfers between devices: 79 us -> 56.9 us
  local copies, waits for them, and re-layouts: 5.86 us -> 10.1 us
  other arithmetic: 6.17 us -> 2 us
    pallas_call x15 -> x16, Pallas kernels: 71.8 us -> 28.4 us  [run(): pl.pallas_call(body, in_specs=specs, out_specs=[pl.BlockSpec(memory_space...]
    ppermute x24, waiting for transfers between devices: 28.2 us -> 62.7 us  [across(): return lax.ppermute(x, 'grp', [(g, g ^ m) for g in range(groups)])]
    ppermute x24, starting transfers between devices: 46.4 us -> 31.2 us  [across(): return lax.ppermute(x, 'grp', [(g, g ^ m) for g in range(groups)])]
    ppermute x3, waiting for transfers between devices: 1.25 us -> 13.4 us  [later(): lax.ppermute(x, 'seq', [(s, s + 2 * m) for s in range(length - 2 * m)])]
    ppermute x9, starting transfers between devices: 20.8 us -> 13.6 us  [along(): return lax.ppermute(x, 'seq', [(s, s ^ 2 * m) for s in range(length)])]
    unnamed x70 -> x34, local copies, waits for them, and re-layouts: 4.62 us -> 10.1 us
    ppermute x9, waiting for transfers between devices: 77 us -> 71.6 us  [along(): return lax.ppermute(x, 'seq', [(s, s ^ 2 * m) for s in range(length)])]
  transfers between devices with their start and end apart: 47 -> 47, of which waited for: 19 -> 24; matrix products, arithmetic and copies ran while one was open for 2% -> 0% of each run, Pallas kernels for 23% -> 10%
where the time goes in v1:
time: 247 us
  waiting for transfers between devices  149 us (60%)
  starting transfers between devices  56.9 us (23%)
  Pallas kernels  28.4 us (11%)
  local copies, waits for them, and re-layouts  10.1 us (4%)
    ppermute x9, waiting for transfers between devices, along(): return lax.ppermute(x, 'seq', [(s, s ^ 2 * m) for s in range(length)])  71.6 us
    ppermute x24, waiting for transfers between devices, across(): return lax.ppermute(x, 'grp', [(g, g ^ m) for g in range(groups)])  62.7 us
    ppermute x24, starting transfers between devices, across(): return lax.ppermute(x, 'grp', [(g, g ^ m) for g in range(groups)])  31.2 us
    pallas_call x16, Pallas kernels, run(): pl.pallas_call(body, in_specs=specs, out_specs=[pl.BlockSpec(memory_space...  28.4 us
    ppermute x9, starting transfers between devices, along(): return lax.ppermute(x, 'seq', [(s, s ^ 2 * m) for s in range(length)])  13.6 us
    ppermute x3, waiting for transfers between devices, later(): lax.ppermute(x, 'seq', [(s, s + 2 * m) for s in range(length - 2 * m)])  13.4 us
    ppermute x3, starting transfers between devices, later(): lax.ppermute(x, 'seq', [(s, s + 2 * m) for s in range(length - 2 * m)])  10.7 us
    unnamed x34, local copies, waits for them, and re-layouts  10.1 us
  transfers between devices with their start and end apart: 47, of which 24 were waited for; matrix products, arithmetic and copies ran while one was open for 0% of the time, Pallas kernels for 10%

profile of v1, /device:TPU:0, one launch (start us, length us, event | category | flops | bytes accessed | tf_op | source)
XLA Modules:
  0.0 247.0 jit_solution(14075668842003596476)
XLA Ops:
  0.0 1.0 copy-done.5
  1.0 1.0 copy-done.7
  3.0 1.5 collective-permute-done.pair_ref
  4.6 6.9 %collective-permute-start.3 = (bf16[1024,128]{1,0:T(8,128)(2,1)S(1)}, bf16[1024,128]{1,0:T(8,128)(2,1)S(1)}, u32[]{:S(2)}, u32[]{:S(2)}) collective-permute-start(bf16[1024,128]{1,0:T(8,128)(2,1)S(1)} %add_convert_fusion.5), channel_id=1, source_target_pairs={{0,6},{1,7},{8,14},{9,15},{16,22},{17,23},{24,30},{25,31}} | collective-permute-start | bytes 786440 | tf_op jit(solution)/shard_map/ppermute | solution.py:221
  11.5 1.3 collective-permute-start.2
  12.8 2.5 %collective-permute-start.1 = (bf16[1024,128]{1,0:T(8,128)(2,1)S(1)}, bf16[1024,128]{1,0:T(8,128)(2,1)S(1)}, u32[]{:S(2)}, u32[]{:S(2)}) collective-permute-start(bf16[1024,128]{1,0:T(8,128)(2,1)S(1)} %add_convert_fusion.5), channel_id=1, source_target_pairs={{0,2},{1,3},{2,4},{3,5},{4,6},{5,7},{8,10},{9,11},{10,12},{11,13},... | collective-permute-start | bytes 786440 | tf_op jit(solution)/shard_map/ppermute | solution.py:221
  15.3 3.0 %collective-permute-done.3 = bf16[1024,128]{1,0:T(8,128)(2,1)S(1)} collective-permute-done((bf16[1024,128]{1,0:T(8,128)(2,1)S(1)}, bf16[1024,128]{1,0:T(8,128)(2,1)S(1)}, u32[]{:S(2)}, u32[]{:S(2)}) %collective-permute-start.3) | collective-permute-done | bytes 262176 | tf_op jit(solution)/shard_map/ppermute | solution.py:221
  18.3 5.6 %collective-permute-done.2 = bf16[1024,128]{1,0:T(8,128)(2,1)S(1)} collective-permute-done((bf16[1024,128]{1,0:T(8,128)(2,1)S(1)}, bf16[1024,128]{1,0:T(8,128)(2,1)S(1)}, u32[]{:S(2)}, u32[]{:S(2)}) %collective-permute-start.2) | collective-permute-done | bytes 262176 | tf_op jit(solution)/shard_map/ppermute | solution.py:221
  23.9 4.8 %collective-permute-done.1 = bf16[1024,128]{1,0:T(8,128)(2,1)S(1)} collective-permute-done((bf16[1024,128]{1,0:T(8,128)(2,1)S(1)}, bf16[1024,128]{1,0:T(8,128)(2,1)S(1)}, u32[]{:S(2)}, u32[]{:S(2)}) %collective-permute-start.1) | collective-permute-done | bytes 262176 | tf_op jit(solution)/shard_map/ppermute | solution.py:221
  28.9 2.6 %shard_map.118.in_ref = f32[128,2048]{1,0:T(8,128)S(1)} custom-call(bf16[128,2048]{1,0:T(8,128)(2,1)S(1)} %bitcast.38, bf16[128,2048]{1,0:T(8,128)(2,1)S(1)} %bitcast.35, bf16[128,2048]{1,0:T(8,128)(2,1)S(1)} %bitcast.37), custom_call_target="tpu_custom_call" | custom-call | tf_op jit(solution)/shard_map/pallas_call | solution.py:30
  31.5 3.4 %copy-done.4 = bf16[2048,2048]{1,0:T(8,128)(2,1)S(1)} copy-done((bf16[2048,2048]{1,0:T(8,128)(2,1)S(1)}, bf16[2048,2048]{1,0:T(8,128)(2,1)}, u32[]{:S(2)}) %copy-start.4) | copy-done | bytes 8388632
  34.9 2.9 %shard_map.120 = (bf16[128,2048]{1,0:T(8,128)(2,1)S(1)}, bf16[128,2048]{1,0:T(8,128)(2,1)}) custom-call(s32[1]{0:T(128)} %bitcast.core_ref, f32[128,2048]{1,0:T(8,128)S(1)} %shard_map.118.in_ref, bf16[128,2048]{1,0:T(8,128)(2,1)S(1)} %bitcast.39, bf16[1024,128]{1,0:T(8,128)(2,1)S(1)} %add_convert_fusion.4.mine_ref, ...), custom_call_target="tpu_custom_call" | custom-call | tf_op jit(solution)/shard_map/pallas_call | solution.py:30
  37.8 0.8 copy-done.11
  38.6 9.0 %collective-permute-start.17 = (bf16[128,2048]{1,0:T(8,128)(2,1)}, bf16[128,2048]{1,0:T(8,128)(2,1)}, u32[]{:S(2)}, u32[]{:S(2)}) collective-permute-start(bf16[128,2048]{1,0:T(8,128)(2,1)} %get-tuple-element.48.own_ref), channel_id=1, source_target_pairs={{0,4},{1,5},{2,6},{3,7},{4,0},{5,1},{6,2},{7,3},{8,12},{9,13},{10,... | collective-permute-start | bytes 1572872 | tf_op jit(solution)/shard_map/ppermute | solution.py:213
  48.0 23.8 %collective-permute-done.17.own_ref = bf16[128,2048]{1,0:T(8,128)(2,1)} collective-permute-done((bf16[128,2048]{1,0:T(8,128)(2,1)}, bf16[128,2048]{1,0:T(8,128)(2,1)}, u32[]{:S(2)}, u32[]{:S(2)}) %collective-permute-start.17) | collective-permute-done | bytes 524320 | tf_op jit(solution)/shard_map/ppermute | solution.py:213
  72.4 5.4 %collective-permute-done.9 = f32[2,32,128]{2,1,0:T(8,128)S(1)} collective-permute-done((f32[2,32,128]{2,1,0:T(8,128)S(1)}, f32[2,32,128]{2,1,0:T(8,128)S(1)}, u32[]{:S(2)}, u32[]{:S(2)}) %collective-permute-start.9) | collective-permute-done | bytes 32800 | tf_op jit(solution)/shard_map/ppermute | solution.py:213
  78.4 1.4 collective-permute-start.7
  79.8 11.8 %collective-permute-done.7 = f32[2,32,128]{2,1,0:T(8,128)S(1)} collective-permute-done((f32[2,32,128]{2,1,0:T(8,128)S(1)}, f32[2,32,128]{2,1,0:T(8,128)S(1)}, u32[]{:S(2)}, u32[]{:S(2)}) %collective-permute-start.7) | collective-permute-done | bytes 32800 | tf_op jit(solution)/shard_map/ppermute | solution.py:213
  92.0 1.7 shard_map.128
  93.7 1.6 collective-permute-start.28
  95.2 1.5 collective-permute-start.29
  97.2 1.7 shard_map.122
  98.9 1.6 collective-permute-start.10
  100.5 3.8 %collective-permute-done.28.refs_1_ = bf16[80,2048]{1,0:T(8,128)(2,1)S(1)} collective-permute-done((bf16[80,2048]{1,0:T(8,128)(2,1)S(1)}, bf16[80,2048]{1,0:T(8,128)(2,1)S(1)}, u32[]{:S(2)}, u32[]{:S(2)}) %collective-permute-start.28) | collective-permute-done | bytes 327712 | tf_op jit(solution)/shard_map/ppermute | solution.py:218
  104.3 1.5 collective-permute-start.11
  105.8 1.5 shard_map.131
  107.4 4.7 %collective-permute-done.29.refs_2_ = bf16[80,2048]{1,0:T(8,128)(2,1)S(1)} collective-permute-done((bf16[80,2048]{1,0:T(8,128)(2,1)S(1)}, bf16[80,2048]{1,0:T(8,128)(2,1)S(1)}, u32[]{:S(2)}, u32[]{:S(2)}) %collective-permute-start.29) | collective-permute-done | bytes 327712 | tf_op jit(solution)/shard_map/ppermute | solution.py:218
  112.3 2.0 collective-permute-start.40
  114.4 1.9 copy-done.1
  116.3 1.9 copy-done.3
  118.2 3.2 %shard_map.129 = (bf16[80,2048]{1,0:T(8,128)(2,1)S(1)}, bf16[80,2048]{1,0:T(8,128)(2,1)S(1)}, bf16[80,2048]{1,0:T(8,128)(2,1)S(1)}, bf16[80,2048]{1,0:T(8,128)(2,1)S(1)}) custom-call(bf16[80,2048]{1,0:T(8,128)(2,1)S(1)} %get-tuple-element.69.refs_0_, bf16[80,2048]{1,0:T(8,128)(2,1)S(1)} %collective-permute-done.28.refs_1_, ...), custom_call_target="tpu_custom_call" | custom-call | tf_op jit(solution)/shard_map/pallas_call | solution.py:30
  121.4 1.5 collective-permute-start.41
  123.6 1.9 collective-permute-done.39.refs_1_
  125.4 1.5 collective-permute-start.32
  127.0 1.4 collective-permute-start.33
  128.4 1.5 shard_map.125
  129.9 3.1 %collective-permute-done.40.refs_2_ = bf16[80,2048]{1,0:T(8,128)(2,1)S(1)} collective-permute-done((bf16[80,2048]{1,0:T(8,128)(2,1)S(1)}, bf16[80,2048]{1,0:T(8,128)(2,1)S(1)}, u32[]{:S(2)}, u32[]{:S(2)}) %collective-permute-start.40) | collective-permute-done | bytes 327712 | tf_op jit(solution)/shard_map/ppermute | solution.py:218
  133.5 2.0 collective-permute-start.21
  135.4 4.1 %collective-permute-done.31.refs_1_ = bf16[80,2048]{1,0:T(8,128)(2,1)S(1)} collective-permute-done((bf16[80,2048]{1,0:T(8,128)(2,1)S(1)}, bf16[80,2048]{1,0:T(8,128)(2,1)S(1)}, u32[]{:S(2)}, u32[]{:S(2)}) %collective-permute-start.31) | collective-permute-done | bytes 327712 | tf_op jit(solution)/shard_map/ppermute | solution.py:218
  139.5 2.5 %collective-permute-start.22 = (bf16[80,2048]{1,0:T(8,128)(2,1)S(1)}, bf16[80,2048]{1,0:T(8,128)(2,1)S(1)}, u32[]{:S(2)}, u32[]{:S(2)}) collective-permute-start(bf16[80,2048]{1,0:T(8,128)(2,1)S(1)} %get-tuple-element.62), channel_id=1, source_target_pairs={{0,24},{8,16},{16,8},{24,0},{1,25},{9,17},{17,9},{25,1},{2,26},{10... | collective-permute-start | bytes 983048 | tf_op jit(solution)/shard_map/ppermute | solution.py:218
  142.0 3.2 %shard_map.132 = (bf16[80,2048]{1,0:T(8,128)(2,1)S(1)}, bf16[80,2048]{1,0:T(8,128)(2,1)S(1)}, bf16[80,2048]{1,0:T(8,128)(2,1)S(1)}, bf16[80,2048]{1,0:T(8,128)(2,1)S(1)}) custom-call(bf16[80,2048]{1,0:T(8,128)(2,1)S(1)} %get-tuple-element.79.refs_0_, bf16[80,2048]{1,0:T(8,128)(2,1)S(1)} %collective-permute-done.39.refs_1_, ...), custom_call_target="tpu_custom_call" | custom-call | tf_op jit(solution)/shard_map/pallas_call | solution.py:30
  145.3 1.8 collective-permute-done.32.refs_2_
  147.0 1.7 collective-permute-start.12
  148.7 2.2 collective-permute-start.42
  150.9 0.7 shard_map.130
  151.7 1.9 collective-permute-done.20.refs_1_
  153.6 14.2 %collective-permute-done.21.refs_2_ = bf16[80,2048]{1,0:T(8,128)(2,1)S(1)} collective-permute-done((bf16[80,2048]{1,0:T(8,128)(2,1)S(1)}, bf16[80,2048]{1,0:T(8,128)(2,1)S(1)}, u32[]{:S(2)}, u32[]{:S(2)}) %collective-permute-start.21) | collective-permute-done | bytes 327712 | tf_op jit(solution)/shard_map/ppermute | solution.py:218
  167.9 1.9 collective-permute-start.43
  169.8 3.4 %shard_map.126 = (bf16[80,2048]{1,0:T(8,128)(2,1)S(1)}, bf16[80,2048]{1,0:T(8,128)(2,1)S(1)}, bf16[80,2048]{1,0:T(8,128)(2,1)S(1)}, bf16[80,2048]{1,0:T(8,128)(2,1)S(1)}) custom-call(bf16[80,2048]{1,0:T(8,128)(2,1)S(1)} %get-tuple-element.59.refs_0_, bf16[80,2048]{1,0:T(8,128)(2,1)S(1)} %collective-permute-done.20.refs_1_, ...), custom_call_target="tpu_custom_call" | custom-call | tf_op jit(solution)/shard_map/pallas_call | solution.py:30
  173.2 1.6 collective-permute-start.23
  174.8 1.9 collective-permute-start.24
  176.8 3.2 %shard_map.123 = (bf16[80,2048]{1,0:T(8,128)(2,1)S(1)}, bf16[80,2048]{1,0:T(8,128)(2,1)S(1)}, bf16[80,2048]{1,0:T(8,128)(2,1)S(1)}, bf16[80,2048]{1,0:T(8,128)(2,1)S(1)}) custom-call(bf16[80,2048]{1,0:T(8,128)(2,1)S(1)} %get-tuple-element.49.refs_0_, bf16[80,2048]{1,0:T(8,128)(2,1)S(1)} %collective-permute-done.10.refs_1_, ...), custom_call_target="tpu_custom_call" | custom-call | tf_op jit(solution)/shard_map/pallas_call | solution.py:30
  180.0 5.4 %collective-permute-done.43.refs_2_ = bf16[80,2048]{1,0:T(8,128)(2,1)S(1)} collective-permute-done((bf16[80,2048]{1,0:T(8,128)(2,1)S(1)}, bf16[80,2048]{1,0:T(8,128)(2,1)S(1)}, u32[]{:S(2)}, u32[]{:S(2)}) %collective-permute-start.43) | collective-permute-done | bytes 327712 | tf_op jit(solution)/shard_map/ppermute | solution.py:218
  185.4 2.0 collective-permute-start.14
  187.4 0.7 shard_map.133
  188.1 1.5 collective-permute-start.15
  189.7 2.7 %collective-permute-done.24.refs_2_ = bf16[80,2048]{1,0:T(8,128)(2,1)S(1)} collective-permute-done((bf16[80,2048]{1,0:T(8,128)(2,1)S(1)}, bf16[80,2048]{1,0:T(8,128)(2,1)S(1)}, u32[]{:S(2)}, u32[]{:S(2)}) %collective-permute-start.24) | collective-permute-done | bytes 327712 | tf_op jit(solution)/shard_map/ppermute | solution.py:218
  192.5 17.9 %collective-permute-done.25.refs_3_ = bf16[80,2048]{1,0:T(8,128)(2,1)S(1)} collective-permute-done((bf16[80,2048]{1,0:T(8,128)(2,1)S(1)}, bf16[80,2048]{1,0:T(8,128)(2,1)S(1)}, u32[]{:S(2)}, u32[]{:S(2)}) %collective-permute-start.25) | collective-permute-done | bytes 327712 | tf_op jit(solution)/shard_map/ppermute | solution.py:218
  210.7 0.7 shard_map.127
  211.9 0.7 shard_map.124
  213.0 1.8 collective-permute-start.46
  214.8 10.4 %collective-permute-done.35 = bf16[128,2048]{1,0:T(8,128)(2,1)S(1)} collective-permute-done((bf16[128,2048]{1,0:T(8,128)(2,1)S(1)}, bf16[128,2048]{1,0:T(8,128)(2,1)S(1)}, u32[]{:S(2)}, u32[]{:S(2)}) %collective-permute-start.35) | collective-permute-done | bytes 524320 | tf_op jit(solution)/shard_map/ppermute | solution.py:213
  226.2 19.6 %collective-permute-done.46 = bf16[128,2048]{1,0:T(8,128)(2,1)S(1)} collective-permute-done((bf16[128,2048]{1,0:T(8,128)(2,1)S(1)}, bf16[128,2048]{1,0:T(8,128)(2,1)S(1)}, u32[]{:S(2)}, u32[]{:S(2)}) %collective-permute-start.46) | collective-permute-done | bytes 524320 | tf_op jit(solution)/shard_map/ppermute | solution.py:213
  245.7 1.2 fusion
  (93 shorter events, 7.0 us)
Async XLA Ops:
  0.0 1.0 copy-start.5
  1.0 1.0 copy-start.7
  2.1 26.8 %copy-start.6 = (bf16[1,128,2048]{2,1,0:T(8,128)(2,1)S(1)}, bf16[1,128,2048]{2,1,0:T(8,128)(2,1)}, u32[]{:S(2)}) copy-start(bf16[1,128,2048]{2,1,0:T(8,128)(2,1)} %param.14) | copy-start | bytes 1572868
  2.1 26.8 %copy-start.8 = (bf16[1,128,2048]{2,1,0:T(8,128)(2,1)S(1)}, bf16[1,128,2048]{2,1,0:T(8,128)(2,1)}, u32[]{:S(2)}) copy-start(bf16[1,128,2048]{2,1,0:T(8,128)(2,1)} %param.15) | copy-start | bytes 1572868
  2.1 26.8 %copy-start.9 = (bf16[1,128,2048]{2,1,0:T(8,128)(2,1)S(1)}, bf16[1,128,2048]{2,1,0:T(8,128)(2,1)}, u32[]{:S(2)}) copy-start(bf16[1,128,2048]{2,1,0:T(8,128)(2,1)} %param.13) | copy-start | bytes 1572868
  2.1 29.4 %copy-start.10 = (bf16[1,128,2048]{2,1,0:T(8,128)(2,1)S(1)}, bf16[1,128,2048]{2,1,0:T(8,128)(2,1)}, u32[]{:S(2)}) copy-start(bf16[1,128,2048]{2,1,0:T(8,128)(2,1)} %param.12) | copy-start | bytes 1572868
  2.1 29.4 %copy-start.13 = (f32[2048]{0:T(1024)S(1)}, f32[2048]{0:T(1024)}, u32[]{:S(2)}) copy-start(f32[2048]{0:T(1024)} %param.16) | copy-start | bytes 24580
  2.1 29.4 %copy-start.14 = (f32[2048]{0:T(1024)S(1)}, f32[2048]{0:T(1024)}, u32[]{:S(2)}) copy-start(f32[2048]{0:T(1024)} %param.18) | copy-start | bytes 24580
  2.5 2.1 collective-permute-start
  4.6 13.6 %collective-permute-start.3 = (bf16[1024,128]{1,0:T(8,128)(2,1)S(1)}, bf16[1024,128]{1,0:T(8,128)(2,1)S(1)}, u32[]{:S(2)}, u32[]{:S(2)}) collective-permute-start(bf16[1024,128]{1,0:T(8,128)(2,1)S(1)} %add_convert_fusion.5), channel_id=1, source_target_pairs={{0,6},{1,7},{8,14},{9,15},{16,22},{17,23},{24,30},{25,31}} | collective-permute-start | bytes 786440 | tf_op jit(solution)/shard_map/ppermute | solution.py:221
  11.5 12.4 %collective-permute-start.2 = (bf16[1024,128]{1,0:T(8,128)(2,1)S(1)}, bf16[1024,128]{1,0:T(8,128)(2,1)S(1)}, u32[]{:S(2)}, u32[]{:S(2)}) collective-permute-start(bf16[1024,128]{1,0:T(8,128)(2,1)S(1)} %add_convert_fusion.5), channel_id=1, source_target_pairs={{0,4},{1,5},{2,6},{3,7},{8,12},{9,13},{10,14},{11,15},{16,20},{17,... | collective-permute-start | bytes 786440 | tf_op jit(solution)/shard_map/ppermute | solution.py:221
  12.8 15.8 %collective-permute-start.1 = (bf16[1024,128]{1,0:T(8,128)(2,1)S(1)}, bf16[1024,128]{1,0:T(8,128)(2,1)S(1)}, u32[]{:S(2)}, u32[]{:S(2)}) collective-permute-start(bf16[1024,128]{1,0:T(8,128)(2,1)S(1)} %add_convert_fusion.5), channel_id=1, source_target_pairs={{0,2},{1,3},{2,4},{3,5},{4,6},{5,7},{8,10},{9,11},{10,12},{11,13},... | collective-permute-start | bytes 786440 | tf_op jit(solution)/shard_map/ppermute | solution.py:221
  28.8 2.7 %collective-permute-start.4 = (bf16[1024,128]{1,0:T(8,128)(2,1)S(1)}, bf16[1024,128]{1,0:T(8,128)(2,1)S(1)}, u32[]{:S(2)}, u32[]{:S(2)}) collective-permute-start(bf16[1024,128]{1,0:T(8,128)(2,1)S(1)} %add_convert_fusion.4.mine_ref), channel_id=1, source_target_pairs={{0,1},{1,0},{2,3},{3,2},{4,5},{5,4},{6,7},{7,6},{8,9},{9,8},{10,11... | collective-permute-start | bytes 786440 | tf_op jit(solution)/shard_map/ppermute | solution.py:210
  31.5 3.4 %copy-start.4 = (bf16[2048,2048]{1,0:T(8,128)(2,1)S(1)}, bf16[2048,2048]{1,0:T(8,128)(2,1)}, u32[]{:S(2)}) copy-start(bf16[2048,2048]{1,0:T(8,128)(2,1)} %w_ref.1) | copy-start | bytes 25165828
  34.9 12.7 %copy-start.15 = (f32[1,128,8]{1,2,0:T(8,128)S(1)}, f32[1,128,8]{1,2,0:T(8,128)}, u32[]{:S(2)}) copy-start(f32[1,128,8]{1,2,0:T(8,128)} %param.20) | copy-start | bytes 12292
  34.9 12.8 %copy-start.16 = (s32[1,128,8]{1,2,0:T(8,128)S(1)}, s32[1,128,8]{1,2,0:T(8,128)}, u32[]{:S(2)}) copy-start(s32[1,128,8]{1,2,0:T(8,128)} %param.19) | copy-start | bytes 12292
  37.8 0.8 copy-start.11
  38.6 75.8 %copy-start = (bf16[1,2048,768]{2,1,0:T(8,128)(2,1)S(1)}, bf16[1,2048,768]{2,1,0:T(8,128)(2,1)}, u32[]{:S(2)}) copy-start(bf16[1,2048,768]{2,1,0:T(8,128)(2,1)} %refs_4_.7) | copy-start | bytes 9437188
  38.6 33.2 %collective-permute-start.17 = (bf16[128,2048]{1,0:T(8,128)(2,1)}, bf16[128,2048]{1,0:T(8,128)(2,1)}, u32[]{:S(2)}, u32[]{:S(2)}) collective-permute-start(bf16[128,2048]{1,0:T(8,128)(2,1)} %get-tuple-element.48.own_ref), channel_id=1, source_target_pairs={{0,4},{1,5},{2,6},{3,7},{4,0},{5,1},{6,2},{7,3},{8,12},{9,13},{10,... | collective-permute-start | bytes 1572872 | tf_op jit(solution)/shard_map/ppermute | solution.py:213
  47.6 44.1 %collective-permute-start.37 = (bf16[128,2048]{1,0:T(8,128)(2,1)}, bf16[128,2048]{1,0:T(8,128)(2,1)}, u32[]{:S(2)}, u32[]{:S(2)}) collective-permute-start(bf16[128,2048]{1,0:T(8,128)(2,1)} %get-tuple-element.48.own_ref), channel_id=1, source_target_pairs={{0,2},{1,3},{2,0},{3,1},{4,6},{5,7},{6,4},{7,5},{8,10},{9,11},{10,... | collective-permute-start | bytes 1572872 | tf_op jit(solution)/shard_map/ppermute | solution.py:213
  47.7 24.1 %collective-permute-start.6 = (f32[32,128]{1,0:T(8,128)S(1)}, f32[32,128]{1,0:T(8,128)S(1)}, u32[]{:S(2)}, u32[]{:S(2)}) collective-permute-start(f32[32,128]{1,0:T(8,128)S(1)} %select_reduce_fusion), channel_id=1, source_target_pairs={{0,1},{1,0},{2,3},{3,2},{4,5},{5,4},{6,7},{7,6},{8,9},{9,8},{10,11... | collective-permute-start | bytes 49160 | tf_op jit(solution)/shard_map/ppermute | solution.py:210
  71.8 20.2 %collective-permute-start.27 = (bf16[128,2048]{1,0:T(8,128)(2,1)}, bf16[128,2048]{1,0:T(8,128)(2,1)}, u32[]{:S(2)}, u32[]{:S(2)}) collective-permute-start(bf16[128,2048]{1,0:T(8,128)(2,1)} %collective-permute-done.17.own_ref), channel_id=1, source_target_pairs={{0,1},{1,0},{2,3},{3,2},{4,5},{5,4},{6,7},{7,6},{8,9},{9,8},{10,11... | collective-permute-start | bytes 1572872 | tf_op jit(solution)/shard_map/ppermute | solution.py:210
  71.8 6.0 %collective-permute-start.9 = (f32[2,32,128]{2,1,0:T(8,128)S(1)}, f32[2,32,128]{2,1,0:T(8,128)S(1)}, u32[]{:S(2)}, u32[]{:S(2)}) collective-permute-start(f32[2,32,128]{2,1,0:T(8,128)S(1)} %pad_maximum_fusion.1), channel_id=1, source_target_pairs={{0,6},{1,7},{2,4},{3,5},{4,2},{5,3},{6,0},{7,1},{8,14},{9,15},{10,... | collective-permute-start | bytes 98312 | tf_op jit(solution)/shard_map/ppermute | solution.py:213
  72.2 6.2 %collective-permute-start.8 = (f32[2,32,128]{2,1,0:T(8,128)S(1)}, f32[2,32,128]{2,1,0:T(8,128)S(1)}, u32[]{:S(2)}, u32[]{:S(2)}) collective-permute-start(f32[2,32,128]{2,1,0:T(8,128)S(1)} %pad_maximum_fusion.1), channel_id=1, source_target_pairs={{0,4},{1,5},{2,6},{3,7},{4,0},{5,1},{6,2},{7,3},{8,12},{9,13},{10,... | collective-permute-start | bytes 98312 | tf_op jit(solution)/shard_map/ppermute | solution.py:213
  72.2 24.6 %collective-permute-start.5 = (bf16[128,2048]{1,0:T(8,128)(2,1)}, bf16[128,2048]{1,0:T(8,128)(2,1)}, u32[]{:S(2)}, u32[]{:S(2)}) collective-permute-start(bf16[128,2048]{1,0:T(8,128)(2,1)} %get-tuple-element.48.own_ref), channel_id=1, source_target_pairs={{0,1},{1,0},{2,3},{3,2},{4,5},{5,4},{6,7},{7,6},{8,9},{9,8},{10,11... | collective-permute-start | bytes 1572872 | tf_op jit(solution)/shard_map/ppermute | solution.py:210
  77.8 19.4 %collective-permute-start.18 = (bf16[128,2048]{1,0:T(8,128)(2,1)}, bf16[128,2048]{1,0:T(8,128)(2,1)}, u32[]{:S(2)}, u32[]{:S(2)}) collective-permute-start(bf16[128,2048]{1,0:T(8,128)(2,1)} %collective-permute-done.17.own_ref), channel_id=1, source_target_pairs={{0,2},{1,3},{2,0},{3,1},{4,6},{5,7},{6,4},{7,5},{8,10},{9,11},{10,... | collective-permute-start | bytes 1572872 | tf_op jit(solution)/shard_map/ppermute | solution.py:213
  78.4 13.3 %collective-permute-start.7 = (f32[2,32,128]{2,1,0:T(8,128)S(1)}, f32[2,32,128]{2,1,0:T(8,128)S(1)}, u32[]{:S(2)}, u32[]{:S(2)}) collective-permute-start(f32[2,32,128]{2,1,0:T(8,128)S(1)} %pad_maximum_fusion.1), channel_id=1, source_target_pairs={{0,2},{1,3},{2,0},{3,1},{4,6},{5,7},{6,4},{7,5},{8,10},{9,11},{10,... | collective-permute-start | bytes 98312 | tf_op jit(solution)/shard_map/ppermute | solution.py:213
  91.7 7.2 %collective-permute-start.38 = (bf16[128,2048]{1,0:T(8,128)(2,1)}, bf16[128,2048]{1,0:T(8,128)(2,1)S(1)}, u32[]{:S(2)}, u32[]{:S(2)}) collective-permute-start(bf16[128,2048]{1,0:T(8,128)(2,1)} %collective-permute-done.37.own_ref), channel_id=1, source_target_pairs={{0,1},{1,0},{2,3},{3,2},{4,5},{5,4},{6,7},{7,6},{8,9},{9,8},{10,11... | collective-permute-start | bytes 1572872 | tf_op jit(solution)/shard_map/ppermute | solution.py:210
  93.7 10.6 %collective-permute-start.28 = (bf16[80,2048]{1,0:T(8,128)(2,1)S(1)}, bf16[80,2048]{1,0:T(8,128)(2,1)S(1)}, u32[]{:S(2)}, u32[]{:S(2)}) collective-permute-start(bf16[80,2048]{1,0:T(8,128)(2,1)S(1)} %get-tuple-element.70), channel_id=1, source_target_pairs={{0,8},{8,0},{16,24},{24,16},{1,9},{9,1},{17,25},{25,17},{2,10},{10... | collective-permute-start | bytes 983048 | tf_op jit(solution)/shard_map/ppermute | solution.py:218
  95.2 16.9 %collective-permute-start.29 = (bf16[80,2048]{1,0:T(8,128)(2,1)S(1)}, bf16[80,2048]{1,0:T(8,128)(2,1)S(1)}, u32[]{:S(2)}, u32[]{:S(2)}) collective-permute-start(bf16[80,2048]{1,0:T(8,128)(2,1)S(1)} %get-tuple-element.71), channel_id=1, source_target_pairs={{0,16},{8,24},{16,0},{24,8},{1,17},{9,25},{17,1},{25,9},{2,18},{10... | collective-permute-start | bytes 983048 | tf_op jit(solution)/shard_map/ppermute | solution.py:218
  96.8 15.6 %collective-permute-start.30 = (bf16[80,2048]{1,0:T(8,128)(2,1)S(1)}, bf16[80,2048]{1,0:T(8,128)(2,1)S(1)}, u32[]{:S(2)}, u32[]{:S(2)}) collective-permute-start(bf16[80,2048]{1,0:T(8,128)(2,1)S(1)} %get-tuple-element.72), channel_id=1, source_target_pairs={{0,24},{8,16},{16,8},{24,0},{1,25},{9,17},{17,9},{25,1},{2,26},{10... | collective-permute-start | bytes 983048 | tf_op jit(solution)/shard_map/ppermute | solution.py:218
  97.2 29.7 %collective-permute-start.19 = (bf16[128,2048]{1,0:T(8,128)(2,1)}, bf16[128,2048]{1,0:T(8,128)(2,1)S(1)}, u32[]{:S(2)}, u32[]{:S(2)}) collective-permute-start(bf16[128,2048]{1,0:T(8,128)(2,1)} %collective-permute-done.18.own_ref), channel_id=1, source_target_pairs={{0,1},{1,0},{2,3},{3,2},{4,5},{5,4},{6,7},{7,6},{8,9},{9,8},{10,11... | collective-permute-start | bytes 1572872 | tf_op jit(solution)/shard_map/ppermute | solution.py:210
  98.9 22.4 %collective-permute-start.10 = (bf16[80,2048]{1,0:T(8,128)(2,1)S(1)}, bf16[80,2048]{1,0:T(8,128)(2,1)S(1)}, u32[]{:S(2)}, u32[]{:S(2)}) collective-permute-start(bf16[80,2048]{1,0:T(8,128)(2,1)S(1)} %get-tuple-element.50), channel_id=1, source_target_pairs={{0,8},{8,0},{16,24},{24,16},{1,9},{9,1},{17,25},{25,17},{2,10},{10... | collective-permute-start | bytes 983048 | tf_op jit(solution)/shard_map/ppermute | solution.py:218
  104.3 18.6 %collective-permute-start.11 = (bf16[80,2048]{1,0:T(8,128)(2,1)S(1)}, bf16[80,2048]{1,0:T(8,128)(2,1)S(1)}, u32[]{:S(2)}, u32[]{:S(2)}) collective-permute-start(bf16[80,2048]{1,0:T(8,128)(2,1)S(1)} %get-tuple-element.51), channel_id=1, source_target_pairs={{0,16},{8,24},{16,0},{24,8},{1,17},{9,25},{17,1},{25,9},{2,18},{10... | collective-permute-start | bytes 983048 | tf_op jit(solution)/shard_map/ppermute | solution.py:218
  112.1 13.3 %collective-permute-start.39 = (bf16[80,2048]{1,0:T(8,128)(2,1)S(1)}, bf16[80,2048]{1,0:T(8,128)(2,1)S(1)}, u32[]{:S(2)}, u32[]{:S(2)}) collective-permute-start(bf16[80,2048]{1,0:T(8,128)(2,1)S(1)} %get-tuple-element.80), channel_id=1, source_target_pairs={{0,8},{8,0},{16,24},{24,16},{1,9},{9,1},{17,25},{25,17},{2,10},{10... | collective-permute-start | bytes 983048 | tf_op jit(solution)/shard_map/ppermute | solution.py:218
  112.3 20.7 %collective-permute-start.40 = (bf16[80,2048]{1,0:T(8,128)(2,1)S(1)}, bf16[80,2048]{1,0:T(8,128)(2,1)S(1)}, u32[]{:S(2)}, u32[]{:S(2)}) collective-permute-start(bf16[80,2048]{1,0:T(8,128)(2,1)S(1)} %get-tuple-element.81), channel_id=1, source_target_pairs={{0,16},{8,24},{16,0},{24,8},{1,17},{9,25},{17,1},{25,9},{2,18},{10... | collective-permute-start | bytes 983048 | tf_op jit(solution)/shard_map/ppermute | solution.py:218
  114.4 1.9 copy-start.1
  116.3 1.9 copy-start.3
  118.1 23.9 %copy-start.2 = (bf16[1,2048,768]{2,1,0:T(8,128)(2,1)S(1)}, bf16[1,2048,768]{2,1,0:T(8,128)(2,1)}, u32[]{:S(2)}) copy-start(bf16[1,2048,768]{2,1,0:T(8,128)(2,1)} %refs_5_.7) | copy-start | bytes 9437188
  121.4 12.1 %collective-permute-start.41 = (bf16[80,2048]{1,0:T(8,128)(2,1)S(1)}, bf16[80,2048]{1,0:T(8,128)(2,1)S(1)}, u32[]{:S(2)}, u32[]{:S(2)}) collective-permute-start(bf16[80,2048]{1,0:T(8,128)(2,1)S(1)} %get-tuple-element.82), channel_id=1, source_target_pairs={{0,24},{8,16},{16,8},{24,0},{1,25},{9,17},{17,9},{25,1},{2,26},{10... | collective-permute-start | bytes 983048 | tf_op jit(solution)/shard_map/ppermute | solution.py:218
  122.9 16.6 %collective-permute-start.31 = (bf16[80,2048]{1,0:T(8,128)(2,1)S(1)}, bf16[80,2048]{1,0:T(8,128)(2,1)S(1)}, u32[]{:S(2)}, u32[]{:S(2)}) collective-permute-start(bf16[80,2048]{1,0:T(8,128)(2,1)S(1)} %get-tuple-element.74), channel_id=1, source_target_pairs={{0,8},{8,0},{16,24},{24,16},{1,9},{9,1},{17,25},{25,17},{2,10},{10... | collective-permute-start | bytes 983048 | tf_op jit(solution)/shard_map/ppermute | solution.py:218
  125.4 21.6 %collective-permute-start.32 = (bf16[80,2048]{1,0:T(8,128)(2,1)S(1)}, bf16[80,2048]{1,0:T(8,128)(2,1)S(1)}, u32[]{:S(2)}, u32[]{:S(2)}) collective-permute-start(bf16[80,2048]{1,0:T(8,128)(2,1)S(1)} %get-tuple-element.75), channel_id=1, source_target_pairs={{0,16},{8,24},{16,0},{24,8},{1,17},{9,25},{17,1},{25,9},{2,18},{10... | collective-permute-start | bytes 983048 | tf_op jit(solution)/shard_map/ppermute | solution.py:218
  127.0 21.8 %collective-permute-start.33 = (bf16[80,2048]{1,0:T(8,128)(2,1)S(1)}, bf16[80,2048]{1,0:T(8,128)(2,1)S(1)}, u32[]{:S(2)}, u32[]{:S(2)}) collective-permute-start(bf16[80,2048]{1,0:T(8,128)(2,1)S(1)} %get-tuple-element.76), channel_id=1, source_target_pairs={{0,24},{8,16},{16,8},{24,0},{1,25},{9,17},{17,9},{25,1},{2,26},{10... | collective-permute-start | bytes 983048 | tf_op jit(solution)/shard_map/ppermute | solution.py:218
  133.0 20.6 %collective-permute-start.20 = (bf16[80,2048]{1,0:T(8,128)(2,1)S(1)}, bf16[80,2048]{1,0:T(8,128)(2,1)S(1)}, u32[]{:S(2)}, u32[]{:S(2)}) collective-permute-start(bf16[80,2048]{1,0:T(8,128)(2,1)S(1)} %get-tuple-element.60), channel_id=1, source_target_pairs={{0,8},{8,0},{16,24},{24,16},{1,9},{9,1},{17,25},{25,17},{2,10},{10... | collective-permute-start | bytes 983048 | tf_op jit(solution)/shard_map/ppermute | solution.py:218
  133.5 34.4 %collective-permute-start.21 = (bf16[80,2048]{1,0:T(8,128)(2,1)S(1)}, bf16[80,2048]{1,0:T(8,128)(2,1)S(1)}, u32[]{:S(2)}, u32[]{:S(2)}) collective-permute-start(bf16[80,2048]{1,0:T(8,128)(2,1)S(1)} %get-tuple-element.61), channel_id=1, source_target_pairs={{0,16},{8,24},{16,0},{24,8},{1,17},{9,25},{17,1},{25,9},{2,18},{10... | collective-permute-start | bytes 983048 | tf_op jit(solution)/shard_map/ppermute | solution.py:218
  139.5 30.3 %collective-permute-start.22 = (bf16[80,2048]{1,0:T(8,128)(2,1)S(1)}, bf16[80,2048]{1,0:T(8,128)(2,1)S(1)}, u32[]{:S(2)}, u32[]{:S(2)}) collective-permute-start(bf16[80,2048]{1,0:T(8,128)(2,1)S(1)} %get-tuple-element.62), channel_id=1, source_target_pairs={{0,24},{8,16},{16,8},{24,0},{1,25},{9,17},{17,9},{25,1},{2,26},{10... | collective-permute-start | bytes 983048 | tf_op jit(solution)/shard_map/ppermute | solution.py:218
  147.0 26.2 %collective-permute-start.12 = (bf16[80,2048]{1,0:T(8,128)(2,1)S(1)}, bf16[80,2048]{1,0:T(8,128)(2,1)S(1)}, u32[]{:S(2)}, u32[]{:S(2)}) collective-permute-start(bf16[80,2048]{1,0:T(8,128)(2,1)S(1)} %get-tuple-element.52), channel_id=1, source_target_pairs={{0,24},{8,16},{16,8},{24,0},{1,25},{9,17},{17,9},{25,1},{2,26},{10... | collective-permute-start | bytes 983048 | tf_op jit(solution)/shard_map/ppermute | solution.py:218
  148.7 26.1 %collective-permute-start.42 = (bf16[80,2048]{1,0:T(8,128)(2,1)S(1)}, bf16[80,2048]{1,0:T(8,128)(2,1)S(1)}, u32[]{:S(2)}, u32[]{:S(2)}) collective-permute-start(bf16[80,2048]{1,0:T(8,128)(2,1)S(1)} %get-tuple-element.84), channel_id=1, source_target_pairs={{0,8},{8,0},{16,24},{24,16},{1,9},{9,1},{17,25},{25,17},{2,10},{10... | collective-permute-start | bytes 983048 | tf_op jit(solution)/shard_map/ppermute | solution.py:218
  153.6 34.5 %collective-permute-start.34 = (bf16[128,2048]{1,0:T(8,128)(2,1)S(1)}, bf16[128,2048]{1,0:T(8,128)(2,1)S(1)}, u32[]{:S(2)}, u32[]{:S(2)}) collective-permute-start(bf16[128,2048]{1,0:T(8,128)(2,1)S(1)} %get-tuple-element.78), channel_id=1, source_target_pairs={{0,1},{1,0},{2,3},{3,2},{4,5},{5,4},{6,7},{7,6},{8,9},{9,8},{10,11... | collective-permute-start | bytes 1572872 | tf_op jit(solution)/shard_map/ppermute | solution.py:210
  167.9 17.5 %collective-permute-start.43 = (bf16[80,2048]{1,0:T(8,128)(2,1)S(1)}, bf16[80,2048]{1,0:T(8,128)(2,1)S(1)}, u32[]{:S(2)}, u32[]{:S(2)}) collective-permute-start(bf16[80,2048]{1,0:T(8,128)(2,1)S(1)} %get-tuple-element.85), channel_id=1, source_target_pairs={{0,16},{8,24},{16,0},{24,8},{1,17},{9,25},{17,1},{25,9},{2,18},{10... | collective-permute-start | bytes 983048 | tf_op jit(solution)/shard_map/ppermute | solution.py:218
  169.8 15.6 %collective-permute-start.44 = (bf16[80,2048]{1,0:T(8,128)(2,1)S(1)}, bf16[80,2048]{1,0:T(8,128)(2,1)S(1)}, u32[]{:S(2)}, u32[]{:S(2)}) collective-permute-start(bf16[80,2048]{1,0:T(8,128)(2,1)S(1)} %get-tuple-element.86), channel_id=1, source_target_pairs={{0,24},{8,16},{16,8},{24,0},{1,25},{9,17},{17,9},{25,1},{2,26},{10... | collective-permute-start | bytes 983048 | tf_op jit(solution)/shard_map/ppermute | solution.py:218
  173.2 16.5 %collective-permute-start.23 = (bf16[80,2048]{1,0:T(8,128)(2,1)S(1)}, bf16[80,2048]{1,0:T(8,128)(2,1)S(1)}, u32[]{:S(2)}, u32[]{:S(2)}) collective-permute-start(bf16[80,2048]{1,0:T(8,128)(2,1)S(1)} %get-tuple-element.64), channel_id=1, source_target_pairs={{0,8},{8,0},{16,24},{24,16},{1,9},{9,1},{17,25},{25,17},{2,10},{10... | collective-permute-start | bytes 983048 | tf_op jit(solution)/shard_map/ppermute | solution.py:218
  174.8 17.5 %collective-permute-start.24 = (bf16[80,2048]{1,0:T(8,128)(2,1)S(1)}, bf16[80,2048]{1,0:T(8,128)(2,1)S(1)}, u32[]{:S(2)}, u32[]{:S(2)}) collective-permute-start(bf16[80,2048]{1,0:T(8,128)(2,1)S(1)} %get-tuple-element.65), channel_id=1, source_target_pairs={{0,16},{8,24},{16,0},{24,8},{1,17},{9,25},{17,1},{25,9},{2,18},{10... | collective-permute-start | bytes 983048 | tf_op jit(solution)/shard_map/ppermute | solution.py:218
  185.4 26.1 %collective-permute-start.13 = (bf16[80,2048]{1,0:T(8,128)(2,1)S(1)}, bf16[80,2048]{1,0:T(8,128)(2,1)S(1)}, u32[]{:S(2)}, u32[]{:S(2)}) collective-permute-start(bf16[80,2048]{1,0:T(8,128)(2,1)S(1)} %get-tuple-element.54), channel_id=1, source_target_pairs={{0,8},{8,0},{16,24},{24,16},{1,9},{9,1},{17,25},{25,17},{2,10},{10... | collective-permute-start | bytes 983048 | tf_op jit(solution)/shard_map/ppermute | solution.py:218
  185.4 26.6 %collective-permute-start.14 = (bf16[80,2048]{1,0:T(8,128)(2,1)S(1)}, bf16[80,2048]{1,0:T(8,128)(2,1)S(1)}, u32[]{:S(2)}, u32[]{:S(2)}) collective-permute-start(bf16[80,2048]{1,0:T(8,128)(2,1)S(1)} %get-tuple-element.55), channel_id=1, source_target_pairs={{0,16},{8,24},{16,0},{24,8},{1,17},{9,25},{17,1},{25,9},{2,18},{10... | collective-permute-start | bytes 983048 | tf_op jit(solution)/shard_map/ppermute | solution.py:218
  188.1 23.8 %collective-permute-start.15 = (bf16[80,2048]{1,0:T(8,128)(2,1)S(1)}, bf16[80,2048]{1,0:T(8,128)(2,1)S(1)}, u32[]{:S(2)}, u32[]{:S(2)}) collective-permute-start(bf16[80,2048]{1,0:T(8,128)(2,1)S(1)} %get-tuple-element.56), channel_id=1, source_target_pairs={{0,24},{8,16},{16,8},{24,0},{1,25},{9,17},{17,9},{25,1},{2,26},{10... | collective-permute-start | bytes 983048 | tf_op jit(solution)/shard_map/ppermute | solution.py:218
  189.7 23.2 %collective-permute-start.45 = (bf16[128,2048]{1,0:T(8,128)(2,1)S(1)}, bf16[128,2048]{1,0:T(8,128)(2,1)S(1)}, u32[]{:S(2)}, u32[]{:S(2)}) collective-permute-start(bf16[128,2048]{1,0:T(8,128)(2,1)S(1)} %get-tuple-element.88), channel_id=1, source_target_pairs={{0,1},{1,0},{2,3},{3,2},{4,5},{5,4},{6,7},{7,6},{8,9},{9,8},{10,11... | collective-permute-start | bytes 1572872 | tf_op jit(solution)/shard_map/ppermute | solution.py:210
  192.4 18.1 %collective-permute-start.25 = (bf16[80,2048]{1,0:T(8,128)(2,1)S(1)}, bf16[80,2048]{1,0:T(8,128)(2,1)S(1)}, u32[]{:S(2)}, u32[]{:S(2)}) collective-permute-start(bf16[80,2048]{1,0:T(8,128)(2,1)S(1)} %get-tuple-element.66), channel_id=1, source_target_pairs={{0,24},{8,16},{16,8},{24,0},{1,25},{9,17},{17,9},{25,1},{2,26},{10... | collective-permute-start | bytes 983048 | tf_op jit(solution)/shard_map/ppermute | solution.py:218
  210.5 14.8 %collective-permute-start.35 = (bf16[128,2048]{1,0:T(8,128)(2,1)S(1)}, bf16[128,2048]{1,0:T(8,128)(2,1)S(1)}, u32[]{:S(2)}, u32[]{:S(2)}) collective-permute-start(bf16[128,2048]{1,0:T(8,128)(2,1)S(1)} %add_convert_fusion.3), channel_id=1, source_target_pairs={{0,2},{1,3},{2,0},{3,1},{4,6},{5,7},{6,4},{7,5},{8,10},{9,11},{10,... | collective-permute-start | bytes 1572872 | tf_op jit(solution)/shard_map/ppermute | solution.py:213
  210.7 35.0 %copy-start.12 = (bf16[128,2048]{1,0:T(8,128)(2,1)S(1)}, bf16[128,2048]{1,0:T(8,128)(2,1)}, u32[]{:S(2)}) copy-start(bf16[128,2048]{1,0:T(8,128)(2,1)} %copy-done.11) | copy-start | bytes 1572868
  211.5 13.8 %collective-permute-start.26 = (bf16[128,2048]{1,0:T(8,128)(2,1)S(1)}, bf16[128,2048]{1,0:T(8,128)(2,1)S(1)}, u32[]{:S(2)}, u32[]{:S(2)}) collective-permute-start(bf16[128,2048]{1,0:T(8,128)(2,1)S(1)} %get-tuple-element.68), channel_id=1, source_target_pairs={{0,1},{1,0},{2,3},{3,2},{4,5},{5,4},{6,7},{7,6},{8,9},{9,8},{10,11... | collective-permute-start | bytes 1572872 | tf_op jit(solution)/shard_map/ppermute | solution.py:210
  212.7 13.5 %collective-permute-start.16 = (bf16[128,2048]{1,0:T(8,128)(2,1)S(1)}, bf16[128,2048]{1,0:T(8,128)(2,1)S(1)}, u32[]{:S(2)}, u32[]{:S(2)}) collective-permute-start(bf16[128,2048]{1,0:T(8,128)(2,1)S(1)} %get-tuple-element.58), channel_id=1, source_target_pairs={{0,1},{1,0},{2,3},{3,2},{4,5},{5,4},{6,7},{7,6},{8,9},{9,8},{10,11... | collective-permute-start | bytes 1572872 | tf_op jit(solution)/shard_map/ppermute | solution.py:210
  213.0 32.7 %collective-permute-start.46 = (bf16[128,2048]{1,0:T(8,128)(2,1)S(1)}, bf16[128,2048]{1,0:T(8,128)(2,1)S(1)}, u32[]{:S(2)}, u32[]{:S(2)}) collective-permute-start(bf16[128,2048]{1,0:T(8,128)(2,1)S(1)} %add_convert_fusion.1), channel_id=1, source_target_pairs={{0,2},{1,3},{2,0},{3,1},{4,6},{5,7},{6,4},{7,5},{8,10},{9,11},{10,... | collective-permute-start | bytes 1572872 | tf_op jit(solution)/shard_map/ppermute | solution.py:213
  225.5 20.2 %collective-permute-start.36 = (bf16[128,2048]{1,0:T(8,128)(2,1)S(1)}, bf16[128,2048]{1,0:T(8,128)(2,1)S(1)}, u32[]{:S(2)}, u32[]{:S(2)}) collective-permute-start(bf16[128,2048]{1,0:T(8,128)(2,1)S(1)} %add_convert_fusion.2), channel_id=1, source_target_pairs={{0,6},{1,7},{2,4},{3,5},{4,2},{5,3},{6,0},{7,1},{8,14},{9,15},{10,... | collective-permute-start | bytes 1572872 | tf_op jit(solution)/shard_map/ppermute | solution.py:213

commit v2 on v1

--- a/solution.py
+++ b/solution.py
@@ -19,12 +19,14 @@
     return lax.dot_general(a, b, (((ca,), (cb,)), ((), ())), preferred_element_type=F32)
 
 
-def call(body, outs, scratch=(), limit=24):
+def call(body, outs, scratch=(), limit=24, away=()):
     def run(*args):
         specs = []
         placed = []
-        for x in args:
+        for i, x in enumerate(args):
             space = pltpu.SMEM if x.size == 1 else pltpu.VMEM
+            if i in away:
+                space = pltpu.HBM
             specs.append(pl.BlockSpec(memory_space=space))
             placed.append(pltpu.with_memory_space_constraint(x, space))
         return pl.pallas_call(
@@ -39,24 +41,67 @@
     return run
 
 
-def state_kernel(k_ref, v_ref, s_ref):
+def column_copies(pairs, sems):
+    parts = sems.shape[1]
+    copies = []
+    for i in range(parts):
+        for n, (src, dst) in enumerate(pairs):
+            width = dst.shape[1] // parts
+            cols = pl.ds(i * width, width)
+            copy = pltpu.make_async_copy(src.at[:, cols], dst.at[:, cols], sems.at[n, i])
+            copy.start()
+            copies.append(copy)
+
+    def wait(i):
+        for copy in copies[i * len(pairs) : (i + 1) * len(pairs)]:
+            copy.wait()
+
+    return wait
+
+
+def state_kernel(k_hbm, v_hbm, s_ref, k_ref, v_ref, sems):
     heads = k_ref.shape[1] // HEAD
-    for h in range(heads):
-        cols = slice(h * HEAD, (h + 1) * HEAD)
-        s_ref[cols, :] = dot(k_ref[:, cols], v_ref[:, cols], 0, 0).astype(BF)
-
-
-def inside_kernel(q_ref, k_ref, v_ref, o_ref):
+    parts = sems.shape[1]
+    wait = column_copies([(k_hbm, k_ref), (v_hbm, v_ref)], sems)
+    for i in range(parts):
+        wait(i)
+        for h in range(i * heads // parts, (i + 1) * heads // parts):
+            cols = slice(h * HEAD, (h + 1) * HEAD)
+            s_ref[cols, :] = dot(k_ref[:, cols], v_ref[:, cols], 0, 0).astype(BF)
+
+
+def inside_kernel(
+    q_hbm, k_hbm, v_hbm, w_hbm, core_ref, group_ref, place_ref,
+    o_ref, w_ref, q_ref, k_ref, v_ref, sems, w_sem,
+):
     tokens = q_ref.shape[0]
     heads = q_ref.shape[1] // HEAD
+    parts = sems.shape[1]
+    wait = column_copies([(q_hbm, q_ref), (k_hbm, k_ref), (v_hbm, v_ref)], sems)
+    bring = pltpu.make_async_copy(w_hbm, w_ref, w_sem)
+    bring.start()
     rows = lax.broadcasted_iota(jnp.int32, (tokens, tokens), 0)
     cols = lax.broadcasted_iota(jnp.int32, (tokens, tokens), 1)
     causal = rows >= cols
     for h in range(heads):
+        if h % (heads // parts) == 0:
+            wait(h // (heads // parts))
         part = slice(h * HEAD, (h + 1) * HEAD)
         scores = dot(q_ref[:, part], k_ref[:, part], 1, 1)
         scores = jnp.where(causal, scores, 0.0).astype(BF)
         o_ref[:, part] = dot(scores, v_ref[:, part])
+    bring.wait()
+
+
+def add_kernel(*refs):
+    total = refs[0][...].astype(F32)
+    for more in refs[1:-1]:
+        total = total + more[...].astype(F32)
+    refs[-1][...] = total.astype(BF)
+
+
+def added(*parts):
+    return call(add_kernel, [(parts[0].shape, BF)])(*parts)[0]
 
 
 def project_kernel(
@@ -91,7 +136,25 @@
     moe_ref[...] = (res_ref[...].astype(F32) * scale * mgain_ref[...]).astype(BF)
 
 
-def rank_kernel(route_ref, rank_ref):
+def pack_kernel(own_ref, par_ref, out_ref):
+    count = own_ref.shape[0]
+    out_ref[:count, :] = own_ref[...]
+    out_ref[count:, :] = par_ref[...]
+
+
+def rank_kernel(groups, length, group_ref, place_ref, *refs):
+    packs = refs[:-2]
+    route_ref, rank_ref = refs[-2:]
+    count = groups * length
+    place = place_ref[0]
+    group = group_ref[0]
+    row = 0
+    for pack in packs:
+        for block in range(2):
+            for k in range(groups):
+                at = block * count + (group ^ k) * length + place
+                route_ref[row : row + 1, :] = pack[pl.ds(at, 1), :]
+                row += 1
     tokens = route_ref.shape[1]
     rows = lax.broadcasted_iota(jnp.int32, (tokens, tokens), 0)
     cols = lax.broadcasted_iota(jnp.int32, (tokens, tokens), 1)
@@ -206,6 +269,8 @@
     capacity = tokens * TOP * 5 // (4 * expert_count)
     slots = -(-capacity // 8) * 8
 
+    scalars = [x.reshape(1) for x in (core, group, place)]
+
     def swap(x):
         return lax.ppermute(x, "seq", [(s, s ^ 1) for s in range(length)])
 
@@ -217,8 +282,9 @@
             return x
         return lax.ppermute(x, "grp", [(g, g ^ m) for g in range(groups)])
 
-    def later(x, m):
-        return lax.ppermute(x, "seq", [(s, s + 2 * m) for s in range(length - 2 * m)])
+    def later(x, m, froms):
+        pairs = [(2 * z + c, 2 * (z + m) + c) for z in froms for c in range(2)]
+        return lax.ppermute(x, "seq", pairs)
 
     queries = lin_query.reshape(tokens, -1)
     keys = lin_key.reshape(tokens, -1)
@@ -226,40 +292,49 @@
     inner = queries.shape[1]
     half = inner // 2
 
-    states = call(state_kernel, [((inner, HEAD), BF)])(keys, values)[0]
+    states = call(
+        state_kernel,
+        [((inner, HEAD), BF)],
+        [pltpu.VMEM(keys.shape, BF)] * 2 + [pltpu.SemaphoreType.DMA((2, 4))],
+        away=(0, 1),
+    )(keys, values)[0]
     pair = swap(states)
     summed = (states.astype(F32) + pair.astype(F32)).astype(BF)
     summed = lax.dynamic_slice_in_dim(summed, core * half, half, axis=0)
-    arrived = [later(summed, m) for m in range(1, stages)]
+    if stages == 4:
+        arrived = [later(summed, 1, range(3)), later(summed, 2, [0])]
+        upto = added(summed, arrived[0])
+        arrived.append(later(upto, 2, [1]))
+    else:
+        arrived = [later(summed, m, range(stages - m)) for m in range(1, stages)]
 
     chosen = expert_ids.reshape(tokens, TOP).T
     scores = route_scores.reshape(tokens, TOP)
     shares = (scores / jnp.sum(scores, axis=1, keepdims=True)).T
     hit = chosen[None] == jnp.arange(expert_count, dtype=jnp.int32)[:, None, None]
     dense = jnp.sum(jnp.where(hit, shares[None], 0.0), axis=1)
-    both = jnp.stack([dense, swap(dense)])
-    routes = jnp.stack([both] + [along(both, m) for m in range(1, stages)])
-    routes = routes.reshape(stages, 2, groups, length, tokens)
-    routes = lax.dynamic_index_in_dim(routes, place, axis=3, keepdims=False)
-    routes = jnp.stack(
-        [
-            lax.dynamic_index_in_dim(routes, group ^ k, axis=2, keepdims=False)
-            for k in range(groups)
-        ],
-        axis=2,
-    ).reshape(stages * 2 * groups, tokens)
-
-    inside = call(inside_kernel, [((tokens, inner), F32)])(queries, keys, values)[0]
-    ranks = call(rank_kernel, [(routes.shape, F32)])(routes)[0]
-    total = arrived[0].astype(F32)
-    for more in arrived[1:]:
-        total = total + more.astype(F32)
-    mine = total.astype(BF)
+    shape = (2 * expert_count, tokens)
+    both = call(pack_kernel, [(shape, F32)])(dense, swap(dense))[0]
+    packs = [both] + [along(both, m) for m in range(1, stages)]
+
+    inside, out_proj = call(
+        inside_kernel,
+        [((tokens, inner), F32), (out_proj.shape, BF)],
+        [pltpu.VMEM(keys.shape, BF)] * 3
+        + [pltpu.SemaphoreType.DMA((3, 4)), pltpu.SemaphoreType.DMA],
+        away=(0, 1, 2, 3),
+    )(queries, keys, values, out_proj, *scalars)
+    shape = (stages * 2 * groups, tokens)
+    body = functools.partial(rank_kernel, groups, length)
+    routes, ranks = call(body, [(shape, F32)] * 2)(
+        *scalars[1:], *packs
+    )
+    mine = added(*arrived)
     other = swap(mine)
     residual, moe_in = call(
         project_kernel, [((tokens, features), BF)] * 2, [pltpu.VMEM((tokens, inner), BF)]
     )(
-        core.reshape(1),
+        scalars[0],
         inside,
         queries,
         mine,

time: 247 us -> 233 us (0.943)
  waiting for transfers between devices: 149 us -> 126 us
  starting transfers between devices: 56.9 us -> 68.7 us
  local copies, waits for them, and re-layouts: 10.1 us -> 4.64 us
    ppermute x9, waiting for transfers between devices: 71.6 us -> 57.9 us  [along(): return lax.ppermute(x, 'seq', [(s, s ^ 2 * m) for s in range(length)])]
    ppermute x9, starting transfers between devices: 13.6 us -> 22.6 us  [along(): return lax.ppermute(x, 'seq', [(s, s ^ 2 * m) for s in range(length)])]
    ppermute x3, waiting for transfers between devices: 13.4 us -> 6.24 us  [later(): return lax.ppermute(x, 'seq', pairs)]
    unnamed x34 -> x24, local copies, waits for them, and re-layouts: 10.1 us -> 4.64 us
    ppermute x24, waiting for transfers between devices: 62.7 us -> 58.8 us  [across(): return lax.ppermute(x, 'grp', [(g, g ^ m) for g in range(groups)])]
    ppermute x24, starting transfers between devices: 31.2 us -> 34.2 us  [across(): return lax.ppermute(x, 'grp', [(g, g ^ m) for g in range(groups)])]
    pallas_call x16 -> x19, Pallas kernels: 28.4 us -> 30.7 us  [run(): pl.pallas_call(body, in_specs=specs, out_specs=[pl.BlockSpec(memory_space...]
  transfers between devices with their start and end apart: 47 -> 47, of which waited for: 24 -> 23; matrix products, arithmetic and copies ran while one was open for 0% -> 0% of each run, Pallas kernels for 10% -> 11%
where the time goes in v2:
time: 233 us; the launch traced here: 232 us
  waiting for transfers between devices  126 us (54%)
  starting transfers between devices  68.7 us (29%)
  Pallas kernels  30.7 us (13%)
  local copies, waits for them, and re-layouts  4.64 us (2%)
    ppermute x24, waiting for transfers between devices, across(): return lax.ppermute(x, 'grp', [(g, g ^ m) for g in range(groups)])  58.8 us
    ppermute x9, waiting for transfers between devices, along(): return lax.ppermute(x, 'seq', [(s, s ^ 2 * m) for s in range(length)])  57.9 us
    ppermute x24, starting transfers between devices, across(): return lax.ppermute(x, 'grp', [(g, g ^ m) for g in range(groups)])  34.2 us
    pallas_call x19, Pallas kernels, run(): pl.pallas_call(body, in_specs=specs, out_specs=[pl.BlockSpec(memory_space...  30.7 us
    ppermute x9, starting transfers between devices, along(): return lax.ppermute(x, 'seq', [(s, s ^ 2 * m) for s in range(length)])  22.6 us
    ppermute x3, starting transfers between devices, later(): return lax.ppermute(x, 'seq', pairs)  10 us
    ppermute x3, waiting for transfers between devices, later(): return lax.ppermute(x, 'seq', pairs)  6.24 us
  transfers between devices with their start and end apart: 47, of which 23 were waited for; matrix products, arithmetic and copies ran while one was open for 0% of the time, Pallas kernels for 11%

profile of v2, /device:TPU:0, one launch (start us, length us, event | category | flops | bytes accessed | tf_op | source)
XLA Modules:
  0.0 232.3 jit_solution(11908362384467311978)
XLA Ops:
  0.0 1.9 shard_map.119
  2.5 1.5 collective-permute-done.pair_ref
  4.1 4.9 %collective-permute-start.1 = (bf16[1024,128]{1,0:T(8,128)(2,1)S(1)}, bf16[1024,128]{1,0:T(8,128)(2,1)S(1)}, u32[]{:S(2)}, u32[]{:S(2)}) collective-permute-start(bf16[1024,128]{1,0:T(8,128)(2,1)S(1)} %add_convert_fusion.4.refs_0_), channel_id=1, source_target_pairs={{0,2},{1,3},{2,4},{3,5},{4,6},{5,7},{8,10},{9,11},{10,12},{11,13},... | collective-permute-start | bytes 786440 | tf_op jit(solution)/shard_map/ppermute | solution.py:287
  8.9 4.5 %collective-permute-start.2 = (bf16[1024,128]{1,0:T(8,128)(2,1)S(1)}, bf16[1024,128]{1,0:T(8,128)(2,1)S(1)}, u32[]{:S(2)}, u32[]{:S(2)}) collective-permute-start(bf16[1024,128]{1,0:T(8,128)(2,1)S(1)} %add_convert_fusion.4.refs_0_), channel_id=1, source_target_pairs={{0,4},{1,5},{8,12},{9,13},{16,20},{17,21},{24,28},{25,29}} | collective-permute-start | bytes 786440 | tf_op jit(solution)/shard_map/ppermute | solution.py:287
  13.5 2.2 collective-permute-done.1.refs_1_.refs_0_
  16.4 4.1 %collective-permute-done.2.refs_1_ = bf16[1024,128]{1,0:T(8,128)(2,1)S(1)} collective-permute-done((bf16[1024,128]{1,0:T(8,128)(2,1)S(1)}, bf16[1024,128]{1,0:T(8,128)(2,1)S(1)}, u32[]{:S(2)}, u32[]{:S(2)}) %collective-permute-start.2) | collective-permute-done | bytes 262176 | tf_op jit(solution)/shard_map/ppermute | solution.py:287
  20.7 4.2 %shard_map.118 = (f32[128,2048]{1,0:T(8,128)S(1)}, bf16[2048,2048]{1,0:T(8,128)(2,1)S(1)}) custom-call(bf16[128,2048]{1,0:T(8,128)(2,1)} %bitcast.20, bf16[128,2048]{1,0:T(8,128)(2,1)} %bitcast.26, bf16[128,2048]{1,0:T(8,128)(2,1)} %bitcast.28, bf16[2048,2048]{1,0:T(8,128)(2,1)} %w_hbm.1, s32[1]{0:T(128)} %bitcast.core_ref, s32[1]{0:T(128)} %bitcast.4.group_ref, ...), custom_call_target="tpu_custom_call" | custom-call | tf_op jit(solution)/shard_map/pallas_call | solution.py:32
  25.0 2.9 %shard_map.122 = (bf16[128,2048]{1,0:T(8,128)(2,1)S(1)}, bf16[128,2048]{1,0:T(8,128)(2,1)}) custom-call(s32[1]{0:T(128)} %bitcast.core_ref, f32[128,2048]{1,0:T(8,128)S(1)} %get-tuple-element.51.in_ref, bf16[128,2048]{1,0:T(8,128)(2,1)S(1)} %bitcast.21, bf16[1024,128]{1,0:T(8,128)(2,1)S(1)} %shard_map.121.mine_ref, ...), custom_call_target="tpu_custom_call" | custom-call | tf_op jit(solution)/shard_map/pallas_call | solution.py:32
  27.8 0.8 copy-done.6
  28.6 4.2 %collective-permute-start.17 = (bf16[128,2048]{1,0:T(8,128)(2,1)}, bf16[128,2048]{1,0:T(8,128)(2,1)}, u32[]{:S(2)}, u32[]{:S(2)}) collective-permute-start(bf16[128,2048]{1,0:T(8,128)(2,1)} %get-tuple-element.54.own_ref), channel_id=1, source_target_pairs={{0,4},{1,5},{2,6},{3,7},{4,0},{5,1},{6,2},{7,3},{8,12},{9,13},{10,... | collective-permute-start | bytes 1572872 | tf_op jit(solution)/shard_map/ppermute | solution.py:278
  32.9 6.3 %collective-permute-start.37 = (bf16[128,2048]{1,0:T(8,128)(2,1)}, bf16[128,2048]{1,0:T(8,128)(2,1)}, u32[]{:S(2)}, u32[]{:S(2)}) collective-permute-start(bf16[128,2048]{1,0:T(8,128)(2,1)} %get-tuple-element.54.own_ref), channel_id=1, source_target_pairs={{0,2},{1,3},{2,0},{3,1},{4,6},{5,7},{6,4},{7,5},{8,10},{9,11},{10,... | collective-permute-start | bytes 1572872 | tf_op jit(solution)/shard_map/ppermute | solution.py:278
  39.2 17.9 %collective-permute-done.17.own_ref = bf16[128,2048]{1,0:T(8,128)(2,1)} collective-permute-done((bf16[128,2048]{1,0:T(8,128)(2,1)}, bf16[128,2048]{1,0:T(8,128)(2,1)}, u32[]{:S(2)}, u32[]{:S(2)}) %collective-permute-start.17) | collective-permute-done | bytes 524320 | tf_op jit(solution)/shard_map/ppermute | solution.py:278
  57.1 0.8 collective-permute-start.18
  58.5 1.5 collective-permute-done.6.par_ref
  60.0 1.3 collective-permute-start.7
  61.3 11.1 %collective-permute-done.7.refs_1_ = f32[64,128]{1,0:T(8,128)S(1)} collective-permute-done((f32[64,128]{1,0:T(8,128)S(1)}, f32[64,128]{1,0:T(8,128)S(1)}, u32[]{:S(2)}, u32[]{:S(2)}) %collective-permute-start.7) | collective-permute-done | bytes 32800 | tf_op jit(solution)/shard_map/ppermute | solution.py:278
  72.4 2.7 %collective-permute-start.8 = (f32[64,128]{1,0:T(8,128)S(1)}, f32[64,128]{1,0:T(8,128)S(1)}, u32[]{:S(2)}, u32[]{:S(2)}) collective-permute-start(f32[64,128]{1,0:T(8,128)S(1)} %shard_map.123.refs_0_), channel_id=1, source_target_pairs={{0,4},{1,5},{2,6},{3,7},{4,0},{5,1},{6,2},{7,3},{8,12},{9,13},{10,... | collective-permute-start | bytes 98312 | tf_op jit(solution)/shard_map/ppermute | solution.py:278
  75.1 2.4 %collective-permute-done.8.refs_2_ = f32[64,128]{1,0:T(8,128)S(1)} collective-permute-done((f32[64,128]{1,0:T(8,128)S(1)}, f32[64,128]{1,0:T(8,128)S(1)}, u32[]{:S(2)}, u32[]{:S(2)}) %collective-permute-start.8) | collective-permute-done | bytes 32800 | tf_op jit(solution)/shard_map/ppermute | solution.py:278
  77.6 3.6 %collective-permute-start.9 = (f32[64,128]{1,0:T(8,128)S(1)}, f32[64,128]{1,0:T(8,128)S(1)}, u32[]{:S(2)}, u32[]{:S(2)}) collective-permute-start(f32[64,128]{1,0:T(8,128)S(1)} %shard_map.123.refs_0_), channel_id=1, source_target_pairs={{0,6},{1,7},{2,4},{3,5},{4,2},{5,3},{6,0},{7,1},{8,14},{9,15},{10,... | collective-permute-start | bytes 98312 | tf_op jit(solution)/shard_map/ppermute | solution.py:278
  81.2 2.1 collective-permute-done.9.refs_3_
  83.4 1.7 shard_map.125
  85.1 1.6 collective-permute-start.10
  86.7 1.7 shard_map.131
  89.0 1.5 collective-permute-start.29
  90.5 1.5 collective-permute-start.30
  92.0 1.5 shard_map.134
  93.5 2.2 collective-permute-done.10.refs_1_
  95.8 1.5 collective-permute-start.11
  97.3 5.5 %collective-permute-done.28.refs_1_ = bf16[80,2048]{1,0:T(8,128)(2,1)S(1)} collective-permute-done((bf16[80,2048]{1,0:T(8,128)(2,1)S(1)}, bf16[80,2048]{1,0:T(8,128)(2,1)S(1)}, u32[]{:S(2)}, u32[]{:S(2)}) %collective-permute-start.28) | collective-permute-done | bytes 327712 | tf_op jit(solution)/shard_map/ppermute | solution.py:283
  102.8 1.5 collective-permute-start.39
  104.3 1.5 collective-permute-start.40
  105.8 5.0 %collective-permute-done.30.refs_3_ = bf16[80,2048]{1,0:T(8,128)(2,1)S(1)} collective-permute-done((bf16[80,2048]{1,0:T(8,128)(2,1)S(1)}, bf16[80,2048]{1,0:T(8,128)(2,1)S(1)}, u32[]{:S(2)}, u32[]{:S(2)}) %collective-permute-start.30) | collective-permute-done | bytes 327712 | tf_op jit(solution)/shard_map/ppermute | solution.py:283
  110.8 1.4 collective-permute-start.41
  112.2 1.9 copy-done.1
  114.1 1.9 copy-done.3
  116.0 3.2 %shard_map.132 = (bf16[80,2048]{1,0:T(8,128)(2,1)S(1)}, bf16[80,2048]{1,0:T(8,128)(2,1)S(1)}, bf16[80,2048]{1,0:T(8,128)(2,1)S(1)}, bf16[80,2048]{1,0:T(8,128)(2,1)S(1)}) custom-call(bf16[80,2048]{1,0:T(8,128)(2,1)S(1)} %get-tuple-element.77.refs_0_, bf16[80,2048]{1,0:T(8,128)(2,1)S(1)} %collective-permute-done.28.refs_1_, ...), custom_call_target="tpu_custom_call" | custom-call | tf_op jit(solution)/shard_map/pallas_call | solution.py:32
  120.3 1.6 collective-permute-start.32
  121.9 1.4 collective-permute-start.33
  123.4 4.1 %collective-permute-done.40.refs_2_ = bf16[80,2048]{1,0:T(8,128)(2,1)S(1)} collective-permute-done((bf16[80,2048]{1,0:T(8,128)(2,1)S(1)}, bf16[80,2048]{1,0:T(8,128)(2,1)S(1)}, u32[]{:S(2)}, u32[]{:S(2)}) %collective-permute-start.40) | collective-permute-done | bytes 327712 | tf_op jit(solution)/shard_map/ppermute | solution.py:283
  127.4 1.5 collective-permute-start.20
  128.9 1.5 collective-permute-start.21
  130.9 2.4 %collective-permute-start.22 = (bf16[80,2048]{1,0:T(8,128)(2,1)S(1)}, bf16[80,2048]{1,0:T(8,128)(2,1)S(1)}, u32[]{:S(2)}, u32[]{:S(2)}) collective-permute-start(bf16[80,2048]{1,0:T(8,128)(2,1)S(1)} %get-tuple-element.70), channel_id=1, source_target_pairs={{0,24},{8,16},{16,8},{24,0},{1,25},{9,17},{17,9},{25,1},{2,26},{10... | collective-permute-start | bytes 983048 | tf_op jit(solution)/shard_map/ppermute | solution.py:283
  133.3 3.2 %shard_map.135 = (bf16[80,2048]{1,0:T(8,128)(2,1)S(1)}, bf16[80,2048]{1,0:T(8,128)(2,1)S(1)}, bf16[80,2048]{1,0:T(8,128)(2,1)S(1)}, bf16[80,2048]{1,0:T(8,128)(2,1)S(1)}) custom-call(bf16[80,2048]{1,0:T(8,128)(2,1)S(1)} %get-tuple-element.87.refs_0_, bf16[80,2048]{1,0:T(8,128)(2,1)S(1)} %collective-permute-done.39.refs_1_, ...), custom_call_target="tpu_custom_call" | custom-call | tf_op jit(solution)/shard_map/pallas_call | solution.py:32
  136.6 4.9 %collective-permute-done.32.refs_2_ = bf16[80,2048]{1,0:T(8,128)(2,1)S(1)} collective-permute-done((bf16[80,2048]{1,0:T(8,128)(2,1)S(1)}, bf16[80,2048]{1,0:T(8,128)(2,1)S(1)}, u32[]{:S(2)}, u32[]{:S(2)}) %collective-permute-start.32) | collective-permute-done | bytes 327712 | tf_op jit(solution)/shard_map/ppermute | solution.py:283
  141.5 2.4 %collective-permute-start.12 = (bf16[80,2048]{1,0:T(8,128)(2,1)S(1)}, bf16[80,2048]{1,0:T(8,128)(2,1)S(1)}, u32[]{:S(2)}, u32[]{:S(2)}) collective-permute-start(bf16[80,2048]{1,0:T(8,128)(2,1)S(1)} %get-tuple-element.59), channel_id=1, source_target_pairs={{0,24},{8,16},{16,8},{24,0},{1,25},{9,17},{17,9},{25,1},{2,26},{10... | collective-permute-start | bytes 983048 | tf_op jit(solution)/shard_map/ppermute | solution.py:283
  144.9 1.5 collective-permute-start.43
  147.2 14.3 %collective-permute-done.21.refs_2_ = bf16[80,2048]{1,0:T(8,128)(2,1)S(1)} collective-permute-done((bf16[80,2048]{1,0:T(8,128)(2,1)S(1)}, bf16[80,2048]{1,0:T(8,128)(2,1)S(1)}, u32[]{:S(2)}, u32[]{:S(2)}) %collective-permute-start.21) | collective-permute-done | bytes 327712 | tf_op jit(solution)/shard_map/ppermute | solution.py:283
  161.5 1.9 collective-permute-start.44
  163.4 3.4 %shard_map.129 = (bf16[80,2048]{1,0:T(8,128)(2,1)S(1)}, bf16[80,2048]{1,0:T(8,128)(2,1)S(1)}, bf16[80,2048]{1,0:T(8,128)(2,1)S(1)}, bf16[80,2048]{1,0:T(8,128)(2,1)S(1)}) custom-call(bf16[80,2048]{1,0:T(8,128)(2,1)S(1)} %get-tuple-element.67.refs_0_, bf16[80,2048]{1,0:T(8,128)(2,1)S(1)} %collective-permute-done.20.refs_1_, ...), custom_call_target="tpu_custom_call" | custom-call | tf_op jit(solution)/shard_map/pallas_call | solution.py:32
  167.4 1.0 collective-permute-start.24
  168.4 6.2 %collective-permute-done.43.refs_2_ = bf16[80,2048]{1,0:T(8,128)(2,1)S(1)} collective-permute-done((bf16[80,2048]{1,0:T(8,128)(2,1)S(1)}, bf16[80,2048]{1,0:T(8,128)(2,1)S(1)}, u32[]{:S(2)}, u32[]{:S(2)}) %collective-permute-start.43) | collective-permute-done | bytes 327712 | tf_op jit(solution)/shard_map/ppermute | solution.py:283
  174.7 2.3 collective-permute-start.25
  176.9 3.2 %shard_map.126 = (bf16[80,2048]{1,0:T(8,128)(2,1)S(1)}, bf16[80,2048]{1,0:T(8,128)(2,1)S(1)}, bf16[80,2048]{1,0:T(8,128)(2,1)S(1)}, bf16[80,2048]{1,0:T(8,128)(2,1)S(1)}) custom-call(bf16[80,2048]{1,0:T(8,128)(2,1)S(1)} %get-tuple-element.56.refs_0_, bf16[80,2048]{1,0:T(8,128)(2,1)S(1)} %collective-permute-done.10.refs_1_, ...), custom_call_target="tpu_custom_call" | custom-call | tf_op jit(solution)/shard_map/pallas_call | solution.py:32
  180.2 1.0 collective-permute-start.13
  182.3 6.4 %collective-permute-done.24.refs_2_ = bf16[80,2048]{1,0:T(8,128)(2,1)S(1)} collective-permute-done((bf16[80,2048]{1,0:T(8,128)(2,1)S(1)}, bf16[80,2048]{1,0:T(8,128)(2,1)S(1)}, u32[]{:S(2)}, u32[]{:S(2)}) %collective-permute-start.24) | collective-permute-done | bytes 327712 | tf_op jit(solution)/shard_map/ppermute | solution.py:283
  188.7 2.3 collective-permute-start.15
  192.4 1.2 collective-permute-done.13.refs_1_
  193.6 8.1 %collective-permute-done.14.refs_2_ = bf16[80,2048]{1,0:T(8,128)(2,1)S(1)} collective-permute-done((bf16[80,2048]{1,0:T(8,128)(2,1)S(1)}, bf16[80,2048]{1,0:T(8,128)(2,1)S(1)}, u32[]{:S(2)}, u32[]{:S(2)}) %collective-permute-start.14) | collective-permute-done | bytes 327712 | tf_op jit(solution)/shard_map/ppermute | solution.py:283
  201.7 0.7 shard_map.127
  202.8 4.7 %collective-permute-done.35 = bf16[128,2048]{1,0:T(8,128)(2,1)S(1)} collective-permute-done((bf16[128,2048]{1,0:T(8,128)(2,1)S(1)}, bf16[128,2048]{1,0:T(8,128)(2,1)S(1)}, u32[]{:S(2)}, u32[]{:S(2)}) %collective-permute-start.35) | collective-permute-done | bytes 524320 | tf_op jit(solution)/shard_map/ppermute | solution.py:278
  207.7 3.6 %collective-permute-start.36 = (bf16[128,2048]{1,0:T(8,128)(2,1)S(1)}, bf16[128,2048]{1,0:T(8,128)(2,1)S(1)}, u32[]{:S(2)}, u32[]{:S(2)}) collective-permute-start(bf16[128,2048]{1,0:T(8,128)(2,1)S(1)} %add_convert_fusion.2), channel_id=1, source_target_pairs={{0,6},{1,7},{2,4},{3,5},{4,2},{5,3},{6,0},{7,1},{8,14},{9,15},{10,... | collective-permute-start | bytes 1572872 | tf_op jit(solution)/shard_map/ppermute | solution.py:278
  211.3 6.6 %collective-permute-done.46 = bf16[128,2048]{1,0:T(8,128)(2,1)S(1)} collective-permute-done((bf16[128,2048]{1,0:T(8,128)(2,1)S(1)}, bf16[128,2048]{1,0:T(8,128)(2,1)S(1)}, u32[]{:S(2)}, u32[]{:S(2)}) %collective-permute-start.46) | collective-permute-done | bytes 524320 | tf_op jit(solution)/shard_map/ppermute | solution.py:278
  217.9 13.2 %collective-permute-done.36 = bf16[128,2048]{1,0:T(8,128)(2,1)S(1)} collective-permute-done((bf16[128,2048]{1,0:T(8,128)(2,1)S(1)}, bf16[128,2048]{1,0:T(8,128)(2,1)S(1)}, u32[]{:S(2)}, u32[]{:S(2)}) %collective-permute-start.36) | collective-permute-done | bytes 524320 | tf_op jit(solution)/shard_map/ppermute | solution.py:278
  231.1 1.2 fusion
  (81 shorter events, 9.9 us)
Async XLA Ops:
  1.9 2.1 collective-permute-start
  4.1 11.5 %collective-permute-start.1 = (bf16[1024,128]{1,0:T(8,128)(2,1)S(1)}, bf16[1024,128]{1,0:T(8,128)(2,1)S(1)}, u32[]{:S(2)}, u32[]{:S(2)}) collective-permute-start(bf16[1024,128]{1,0:T(8,128)(2,1)S(1)} %add_convert_fusion.4.refs_0_), channel_id=1, source_target_pairs={{0,2},{1,3},{2,4},{3,5},{4,6},{5,7},{8,10},{9,11},{10,12},{11,13},... | collective-permute-start | bytes 786440 | tf_op jit(solution)/shard_map/ppermute | solution.py:287
  8.9 11.5 %collective-permute-start.2 = (bf16[1024,128]{1,0:T(8,128)(2,1)S(1)}, bf16[1024,128]{1,0:T(8,128)(2,1)S(1)}, u32[]{:S(2)}, u32[]{:S(2)}) collective-permute-start(bf16[1024,128]{1,0:T(8,128)(2,1)S(1)} %add_convert_fusion.4.refs_0_), channel_id=1, source_target_pairs={{0,4},{1,5},{8,12},{9,13},{16,20},{17,21},{24,28},{25,29}} | collective-permute-start | bytes 786440 | tf_op jit(solution)/shard_map/ppermute | solution.py:287
  15.7 4.8 %collective-permute-start.3 = (bf16[1024,128]{1,0:T(8,128)(2,1)S(1)}, bf16[1024,128]{1,0:T(8,128)(2,1)S(1)}, u32[]{:S(2)}, u32[]{:S(2)}) collective-permute-start(bf16[1024,128]{1,0:T(8,128)(2,1)S(1)} %shard_map.120), channel_id=1, source_target_pairs={{2,6},{3,7},{10,14},{11,15},{18,22},{19,23},{26,30},{27,31}} | collective-permute-start | bytes 786440 | tf_op jit(solution)/shard_map/ppermute | solution.py:287
  20.5 4.3 %collective-permute-start.4 = (bf16[1024,128]{1,0:T(8,128)(2,1)S(1)}, bf16[1024,128]{1,0:T(8,128)(2,1)S(1)}, u32[]{:S(2)}, u32[]{:S(2)}) collective-permute-start(bf16[1024,128]{1,0:T(8,128)(2,1)S(1)} %shard_map.121.mine_ref), channel_id=1, source_target_pairs={{0,1},{1,0},{2,3},{3,2},{4,5},{5,4},{6,7},{7,6},{8,9},{9,8},{10,11... | collective-permute-start | bytes 786440 | tf_op jit(solution)/shard_map/ppermute | solution.py:275
  20.6 4.3 %copy-start.4 = (bf16[1,128,2048]{2,1,0:T(8,128)(2,1)S(1)}, bf16[1,128,2048]{2,1,0:T(8,128)(2,1)}, u32[]{:S(2)}) copy-start(bf16[1,128,2048]{2,1,0:T(8,128)(2,1)} %param.13) | copy-start | bytes 1572868
  20.6 4.3 %copy-start.5 = (bf16[1,128,2048]{2,1,0:T(8,128)(2,1)S(1)}, bf16[1,128,2048]{2,1,0:T(8,128)(2,1)}, u32[]{:S(2)}) copy-start(bf16[1,128,2048]{2,1,0:T(8,128)(2,1)} %param.12) | copy-start | bytes 1572868
  20.7 4.3 %copy-start.8 = (f32[2048]{0:T(1024)S(1)}, f32[2048]{0:T(1024)}, u32[]{:S(2)}) copy-start(f32[2048]{0:T(1024)} %param.16) | copy-start | bytes 24580
  20.7 4.3 %copy-start.9 = (f32[2048]{0:T(1024)S(1)}, f32[2048]{0:T(1024)}, u32[]{:S(2)}) copy-start(f32[2048]{0:T(1024)} %param.18) | copy-start | bytes 24580
  24.9 32.1 %copy-start.10 = (f32[1,128,8]{1,2,0:T(8,128)S(1)}, f32[1,128,8]{1,2,0:T(8,128)}, u32[]{:S(2)}) copy-start(f32[1,128,8]{1,2,0:T(8,128)} %param.20) | copy-start | bytes 12292
  25.0 33.1 %copy-start.11 = (s32[1,128,8]{1,2,0:T(8,128)S(1)}, s32[1,128,8]{1,2,0:T(8,128)}, u32[]{:S(2)}) copy-start(s32[1,128,8]{1,2,0:T(8,128)} %param.19) | copy-start | bytes 12292
  27.8 0.8 copy-start.6
  28.6 83.6 %copy-start = (bf16[1,2048,768]{2,1,0:T(8,128)(2,1)S(1)}, bf16[1,2048,768]{2,1,0:T(8,128)(2,1)}, u32[]{:S(2)}) copy-start(bf16[1,2048,768]{2,1,0:T(8,128)(2,1)} %refs_4_.7) | copy-start | bytes 9437188
  28.6 28.4 %collective-permute-start.17 = (bf16[128,2048]{1,0:T(8,128)(2,1)}, bf16[128,2048]{1,0:T(8,128)(2,1)}, u32[]{:S(2)}, u32[]{:S(2)}) collective-permute-start(bf16[128,2048]{1,0:T(8,128)(2,1)} %get-tuple-element.54.own_ref), channel_id=1, source_target_pairs={{0,4},{1,5},{2,6},{3,7},{4,0},{5,1},{6,2},{7,3},{8,12},{9,13},{10,... | collective-permute-start | bytes 1572872 | tf_op jit(solution)/shard_map/ppermute | solution.py:278
  32.9 25.0 %collective-permute-start.37 = (bf16[128,2048]{1,0:T(8,128)(2,1)}, bf16[128,2048]{1,0:T(8,128)(2,1)}, u32[]{:S(2)}, u32[]{:S(2)}) collective-permute-start(bf16[128,2048]{1,0:T(8,128)(2,1)} %get-tuple-element.54.own_ref), channel_id=1, source_target_pairs={{0,2},{1,3},{2,0},{3,1},{4,6},{5,7},{6,4},{7,5},{8,10},{9,11},{10,... | collective-permute-start | bytes 1572872 | tf_op jit(solution)/shard_map/ppermute | solution.py:278
  39.2 44.3 %collective-permute-start.5 = (bf16[128,2048]{1,0:T(8,128)(2,1)}, bf16[128,2048]{1,0:T(8,128)(2,1)}, u32[]{:S(2)}, u32[]{:S(2)}) collective-permute-start(bf16[128,2048]{1,0:T(8,128)(2,1)} %get-tuple-element.54.own_ref), channel_id=1, source_target_pairs={{0,1},{1,0},{2,3},{3,2},{4,5},{5,4},{6,7},{7,6},{8,9},{9,8},{10,11... | collective-permute-start | bytes 1572872 | tf_op jit(solution)/shard_map/ppermute | solution.py:275
  57.1 29.6 %collective-permute-start.27 = (bf16[128,2048]{1,0:T(8,128)(2,1)}, bf16[128,2048]{1,0:T(8,128)(2,1)}, u32[]{:S(2)}, u32[]{:S(2)}) collective-permute-start(bf16[128,2048]{1,0:T(8,128)(2,1)} %collective-permute-done.17.own_ref), channel_id=1, source_target_pairs={{0,1},{1,0},{2,3},{3,2},{4,5},{5,4},{6,7},{7,6},{8,9},{9,8},{10,11... | collective-permute-start | bytes 1572872 | tf_op jit(solution)/shard_map/ppermute | solution.py:275
  57.1 33.4 %collective-permute-start.18 = (bf16[128,2048]{1,0:T(8,128)(2,1)}, bf16[128,2048]{1,0:T(8,128)(2,1)S(1)}, u32[]{:S(2)}, u32[]{:S(2)}) collective-permute-start(bf16[128,2048]{1,0:T(8,128)(2,1)} %collective-permute-done.17.own_ref), channel_id=1, source_target_pairs={{0,2},{1,3},{2,0},{3,1},{4,6},{5,7},{6,4},{7,5},{8,10},{9,11},{10,... | collective-permute-start | bytes 1572872 | tf_op jit(solution)/shard_map/ppermute | solution.py:278
  57.9 32.6 %collective-permute-start.38 = (bf16[128,2048]{1,0:T(8,128)(2,1)}, bf16[128,2048]{1,0:T(8,128)(2,1)S(1)}, u32[]{:S(2)}, u32[]{:S(2)}) collective-permute-start(bf16[128,2048]{1,0:T(8,128)(2,1)} %collective-permute-done.37.own_ref), channel_id=1, source_target_pairs={{0,1},{1,0},{2,3},{3,2},{4,5},{5,4},{6,7},{7,6},{8,9},{9,8},{10,11... | collective-permute-start | bytes 1572872 | tf_op jit(solution)/shard_map/ppermute | solution.py:275
  58.1 1.9 collective-permute-start.6
  60.0 12.4 %collective-permute-start.7 = (f32[64,128]{1,0:T(8,128)S(1)}, f32[64,128]{1,0:T(8,128)S(1)}, u32[]{:S(2)}, u32[]{:S(2)}) collective-permute-start(f32[64,128]{1,0:T(8,128)S(1)} %shard_map.123.refs_0_), channel_id=1, source_target_pairs={{0,2},{1,3},{2,0},{3,1},{4,6},{5,7},{6,4},{7,5},{8,10},{9,11},{10,... | collective-permute-start | bytes 98312 | tf_op jit(solution)/shard_map/ppermute | solution.py:278
  72.4 5.2 %collective-permute-start.8 = (f32[64,128]{1,0:T(8,128)S(1)}, f32[64,128]{1,0:T(8,128)S(1)}, u32[]{:S(2)}, u32[]{:S(2)}) collective-permute-start(f32[64,128]{1,0:T(8,128)S(1)} %shard_map.123.refs_0_), channel_id=1, source_target_pairs={{0,4},{1,5},{2,6},{3,7},{4,0},{5,1},{6,2},{7,3},{8,12},{9,13},{10,... | collective-permute-start | bytes 98312 | tf_op jit(solution)/shard_map/ppermute | solution.py:278
  77.6 5.7 %collective-permute-start.9 = (f32[64,128]{1,0:T(8,128)S(1)}, f32[64,128]{1,0:T(8,128)S(1)}, u32[]{:S(2)}, u32[]{:S(2)}) collective-permute-start(f32[64,128]{1,0:T(8,128)S(1)} %shard_map.123.refs_0_), channel_id=1, source_target_pairs={{0,6},{1,7},{2,4},{3,5},{4,2},{5,3},{6,0},{7,1},{8,14},{9,15},{10,... | collective-permute-start | bytes 98312 | tf_op jit(solution)/shard_map/ppermute | solution.py:278
  85.1 10.6 %collective-permute-start.10 = (bf16[80,2048]{1,0:T(8,128)(2,1)S(1)}, bf16[80,2048]{1,0:T(8,128)(2,1)S(1)}, u32[]{:S(2)}, u32[]{:S(2)}) collective-permute-start(bf16[80,2048]{1,0:T(8,128)(2,1)S(1)} %get-tuple-element.57), channel_id=1, source_target_pairs={{0,8},{8,0},{16,24},{24,16},{1,9},{9,1},{17,25},{25,17},{2,10},{10... | collective-permute-start | bytes 983048 | tf_op jit(solution)/shard_map/ppermute | solution.py:283
  88.4 14.4 %collective-permute-start.28 = (bf16[80,2048]{1,0:T(8,128)(2,1)S(1)}, bf16[80,2048]{1,0:T(8,128)(2,1)S(1)}, u32[]{:S(2)}, u32[]{:S(2)}) collective-permute-start(bf16[80,2048]{1,0:T(8,128)(2,1)S(1)} %get-tuple-element.78), channel_id=1, source_target_pairs={{0,8},{8,0},{16,24},{24,16},{1,9},{9,1},{17,25},{25,17},{2,10},{10... | collective-permute-start | bytes 983048 | tf_op jit(solution)/shard_map/ppermute | solution.py:283
  89.0 15.3 %collective-permute-start.29 = (bf16[80,2048]{1,0:T(8,128)(2,1)S(1)}, bf16[80,2048]{1,0:T(8,128)(2,1)S(1)}, u32[]{:S(2)}, u32[]{:S(2)}) collective-permute-start(bf16[80,2048]{1,0:T(8,128)(2,1)S(1)} %get-tuple-element.79), channel_id=1, source_target_pairs={{0,16},{8,24},{16,0},{24,8},{1,17},{9,25},{17,1},{25,9},{2,18},{10... | collective-permute-start | bytes 983048 | tf_op jit(solution)/shard_map/ppermute | solution.py:283
  90.5 28.7 %collective-permute-start.19 = (bf16[128,2048]{1,0:T(8,128)(2,1)S(1)}, bf16[128,2048]{1,0:T(8,128)(2,1)S(1)}, u32[]{:S(2)}, u32[]{:S(2)}) collective-permute-start(bf16[128,2048]{1,0:T(8,128)(2,1)S(1)} %collective-permute-done.18.own_ref), channel_id=1, source_target_pairs={{0,1},{1,0},{2,3},{3,2},{4,5},{5,4},{6,7},{7,6},{8,9},{9,8},{10,11... | collective-permute-start | bytes 1572872 | tf_op jit(solution)/shard_map/ppermute | solution.py:275
  90.5 20.3 %collective-permute-start.30 = (bf16[80,2048]{1,0:T(8,128)(2,1)S(1)}, bf16[80,2048]{1,0:T(8,128)(2,1)S(1)}, u32[]{:S(2)}, u32[]{:S(2)}) collective-permute-start(bf16[80,2048]{1,0:T(8,128)(2,1)S(1)} %get-tuple-element.80), channel_id=1, source_target_pairs={{0,24},{8,16},{16,8},{24,0},{1,25},{9,17},{17,9},{25,1},{2,26},{10... | collective-permute-start | bytes 983048 | tf_op jit(solution)/shard_map/ppermute | solution.py:283
  95.8 24.6 %collective-permute-start.11 = (bf16[80,2048]{1,0:T(8,128)(2,1)S(1)}, bf16[80,2048]{1,0:T(8,128)(2,1)S(1)}, u32[]{:S(2)}, u32[]{:S(2)}) collective-permute-start(bf16[80,2048]{1,0:T(8,128)(2,1)S(1)} %get-tuple-element.58), channel_id=1, source_target_pairs={{0,16},{8,24},{16,0},{24,8},{1,17},{9,25},{17,1},{25,9},{2,18},{10... | collective-permute-start | bytes 983048 | tf_op jit(solution)/shard_map/ppermute | solution.py:283
  102.8 19.1 %collective-permute-start.39 = (bf16[80,2048]{1,0:T(8,128)(2,1)S(1)}, bf16[80,2048]{1,0:T(8,128)(2,1)S(1)}, u32[]{:S(2)}, u32[]{:S(2)}) collective-permute-start(bf16[80,2048]{1,0:T(8,128)(2,1)S(1)} %get-tuple-element.88), channel_id=1, source_target_pairs={{0,8},{8,0},{16,24},{24,16},{1,9},{9,1},{17,25},{25,17},{2,10},{10... | collective-permute-start | bytes 983048 | tf_op jit(solution)/shard_map/ppermute | solution.py:283
  104.3 23.1 %collective-permute-start.40 = (bf16[80,2048]{1,0:T(8,128)(2,1)S(1)}, bf16[80,2048]{1,0:T(8,128)(2,1)S(1)}, u32[]{:S(2)}, u32[]{:S(2)}) collective-permute-start(bf16[80,2048]{1,0:T(8,128)(2,1)S(1)} %get-tuple-element.89), channel_id=1, source_target_pairs={{0,16},{8,24},{16,0},{24,8},{1,17},{9,25},{17,1},{25,9},{2,18},{10... | collective-permute-start | bytes 983048 | tf_op jit(solution)/shard_map/ppermute | solution.py:283
  110.8 18.1 %collective-permute-start.41 = (bf16[80,2048]{1,0:T(8,128)(2,1)S(1)}, bf16[80,2048]{1,0:T(8,128)(2,1)S(1)}, u32[]{:S(2)}, u32[]{:S(2)}) collective-permute-start(bf16[80,2048]{1,0:T(8,128)(2,1)S(1)} %get-tuple-element.90), channel_id=1, source_target_pairs={{0,24},{8,16},{16,8},{24,0},{1,25},{9,17},{17,9},{25,1},{2,26},{10... | collective-permute-start | bytes 983048 | tf_op jit(solution)/shard_map/ppermute | solution.py:283
  112.2 1.9 copy-start.1
  114.1 1.9 copy-start.3
  116.0 17.3 %copy-start.2 = (bf16[1,2048,768]{2,1,0:T(8,128)(2,1)S(1)}, bf16[1,2048,768]{2,1,0:T(8,128)(2,1)}, u32[]{:S(2)}) copy-start(bf16[1,2048,768]{2,1,0:T(8,128)(2,1)} %refs_5_.7) | copy-start | bytes 9437188
  119.2 11.6 %collective-permute-start.31 = (bf16[80,2048]{1,0:T(8,128)(2,1)S(1)}, bf16[80,2048]{1,0:T(8,128)(2,1)S(1)}, u32[]{:S(2)}, u32[]{:S(2)}) collective-permute-start(bf16[80,2048]{1,0:T(8,128)(2,1)S(1)} %get-tuple-element.82), channel_id=1, source_target_pairs={{0,8},{8,0},{16,24},{24,16},{1,9},{9,1},{17,25},{25,17},{2,10},{10... | collective-permute-start | bytes 983048 | tf_op jit(solution)/shard_map/ppermute | solution.py:283
  120.3 21.1 %collective-permute-start.32 = (bf16[80,2048]{1,0:T(8,128)(2,1)S(1)}, bf16[80,2048]{1,0:T(8,128)(2,1)S(1)}, u32[]{:S(2)}, u32[]{:S(2)}) collective-permute-start(bf16[80,2048]{1,0:T(8,128)(2,1)S(1)} %get-tuple-element.83), channel_id=1, source_target_pairs={{0,16},{8,24},{16,0},{24,8},{1,17},{9,25},{17,1},{25,9},{2,18},{10... | collective-permute-start | bytes 983048 | tf_op jit(solution)/shard_map/ppermute | solution.py:283
  121.9 22.0 %collective-permute-start.33 = (bf16[80,2048]{1,0:T(8,128)(2,1)S(1)}, bf16[80,2048]{1,0:T(8,128)(2,1)S(1)}, u32[]{:S(2)}, u32[]{:S(2)}) collective-permute-start(bf16[80,2048]{1,0:T(8,128)(2,1)S(1)} %get-tuple-element.84), channel_id=1, source_target_pairs={{0,24},{8,16},{16,8},{24,0},{1,25},{9,17},{17,9},{25,1},{2,26},{10... | collective-permute-start | bytes 983048 | tf_op jit(solution)/shard_map/ppermute | solution.py:283
  127.4 17.5 %collective-permute-start.20 = (bf16[80,2048]{1,0:T(8,128)(2,1)S(1)}, bf16[80,2048]{1,0:T(8,128)(2,1)S(1)}, u32[]{:S(2)}, u32[]{:S(2)}) collective-permute-start(bf16[80,2048]{1,0:T(8,128)(2,1)S(1)} %get-tuple-element.68), channel_id=1, source_target_pairs={{0,8},{8,0},{16,24},{24,16},{1,9},{9,1},{17,25},{25,17},{2,10},{10... | collective-permute-start | bytes 983048 | tf_op jit(solution)/shard_map/ppermute | solution.py:283
  128.9 32.5 %collective-permute-start.21 = (bf16[80,2048]{1,0:T(8,128)(2,1)S(1)}, bf16[80,2048]{1,0:T(8,128)(2,1)S(1)}, u32[]{:S(2)}, u32[]{:S(2)}) collective-permute-start(bf16[80,2048]{1,0:T(8,128)(2,1)S(1)} %get-tuple-element.69), channel_id=1, source_target_pairs={{0,16},{8,24},{16,0},{24,8},{1,17},{9,25},{17,1},{25,9},{2,18},{10... | collective-permute-start | bytes 983048 | tf_op jit(solution)/shard_map/ppermute | solution.py:283
  130.9 30.6 %collective-permute-start.22 = (bf16[80,2048]{1,0:T(8,128)(2,1)S(1)}, bf16[80,2048]{1,0:T(8,128)(2,1)S(1)}, u32[]{:S(2)}, u32[]{:S(2)}) collective-permute-start(bf16[80,2048]{1,0:T(8,128)(2,1)S(1)} %get-tuple-element.70), channel_id=1, source_target_pairs={{0,24},{8,16},{16,8},{24,0},{1,25},{9,17},{17,9},{25,1},{2,26},{10... | collective-permute-start | bytes 983048 | tf_op jit(solution)/shard_map/ppermute | solution.py:283
  141.5 25.4 %collective-permute-start.12 = (bf16[80,2048]{1,0:T(8,128)(2,1)S(1)}, bf16[80,2048]{1,0:T(8,128)(2,1)S(1)}, u32[]{:S(2)}, u32[]{:S(2)}) collective-permute-start(bf16[80,2048]{1,0:T(8,128)(2,1)S(1)} %get-tuple-element.59), channel_id=1, source_target_pairs={{0,24},{8,16},{16,8},{24,0},{1,25},{9,17},{17,9},{25,1},{2,26},{10... | collective-permute-start | bytes 983048 | tf_op jit(solution)/shard_map/ppermute | solution.py:283
  143.9 23.5 %collective-permute-start.42 = (bf16[80,2048]{1,0:T(8,128)(2,1)S(1)}, bf16[80,2048]{1,0:T(8,128)(2,1)S(1)}, u32[]{:S(2)}, u32[]{:S(2)}) collective-permute-start(bf16[80,2048]{1,0:T(8,128)(2,1)S(1)} %get-tuple-element.92), channel_id=1, source_target_pairs={{0,8},{8,0},{16,24},{24,16},{1,9},{9,1},{17,25},{25,17},{2,10},{10... | collective-permute-start | bytes 983048 | tf_op jit(solution)/shard_map/ppermute | solution.py:283
  144.9 29.7 %collective-permute-start.43 = (bf16[80,2048]{1,0:T(8,128)(2,1)S(1)}, bf16[80,2048]{1,0:T(8,128)(2,1)S(1)}, u32[]{:S(2)}, u32[]{:S(2)}) collective-permute-start(bf16[80,2048]{1,0:T(8,128)(2,1)S(1)} %get-tuple-element.93), channel_id=1, source_target_pairs={{0,16},{8,24},{16,0},{24,8},{1,17},{9,25},{17,1},{25,9},{2,18},{10... | collective-permute-start | bytes 983048 | tf_op jit(solution)/shard_map/ppermute | solution.py:283
  161.4 30.2 %collective-permute-start.34 = (bf16[128,2048]{1,0:T(8,128)(2,1)S(1)}, bf16[128,2048]{1,0:T(8,128)(2,1)S(1)}, u32[]{:S(2)}, u32[]{:S(2)}) collective-permute-start(bf16[128,2048]{1,0:T(8,128)(2,1)S(1)} %get-tuple-element.86), channel_id=1, source_target_pairs={{0,1},{1,0},{2,3},{3,2},{4,5},{5,4},{6,7},{7,6},{8,9},{9,8},{10,11... | collective-permute-start | bytes 1572872 | tf_op jit(solution)/shard_map/ppermute | solution.py:275
  161.5 18.7 %collective-permute-start.44 = (bf16[80,2048]{1,0:T(8,128)(2,1)S(1)}, bf16[80,2048]{1,0:T(8,128)(2,1)S(1)}, u32[]{:S(2)}, u32[]{:S(2)}) collective-permute-start(bf16[80,2048]{1,0:T(8,128)(2,1)S(1)} %get-tuple-element.94), channel_id=1, source_target_pairs={{0,24},{8,16},{16,8},{24,0},{1,25},{9,17},{17,9},{25,1},{2,26},{10... | collective-permute-start | bytes 983048 | tf_op jit(solution)/shard_map/ppermute | solution.py:283
  166.8 15.1 %collective-permute-start.23 = (bf16[80,2048]{1,0:T(8,128)(2,1)S(1)}, bf16[80,2048]{1,0:T(8,128)(2,1)S(1)}, u32[]{:S(2)}, u32[]{:S(2)}) collective-permute-start(bf16[80,2048]{1,0:T(8,128)(2,1)S(1)} %get-tuple-element.72), channel_id=1, source_target_pairs={{0,8},{8,0},{16,24},{24,16},{1,9},{9,1},{17,25},{25,17},{2,10},{10... | collective-permute-start | bytes 983048 | tf_op jit(solution)/shard_map/ppermute | solution.py:283
  167.4 21.2 %collective-permute-start.24 = (bf16[80,2048]{1,0:T(8,128)(2,1)S(1)}, bf16[80,2048]{1,0:T(8,128)(2,1)S(1)}, u32[]{:S(2)}, u32[]{:S(2)}) collective-permute-start(bf16[80,2048]{1,0:T(8,128)(2,1)S(1)} %get-tuple-element.73), channel_id=1, source_target_pairs={{0,16},{8,24},{16,0},{24,8},{1,17},{9,25},{17,1},{25,9},{2,18},{10... | collective-permute-start | bytes 983048 | tf_op jit(solution)/shard_map/ppermute | solution.py:283
  174.7 16.3 %collective-permute-start.25 = (bf16[80,2048]{1,0:T(8,128)(2,1)S(1)}, bf16[80,2048]{1,0:T(8,128)(2,1)S(1)}, u32[]{:S(2)}, u32[]{:S(2)}) collective-permute-start(bf16[80,2048]{1,0:T(8,128)(2,1)S(1)} %get-tuple-element.74), channel_id=1, source_target_pairs={{0,24},{8,16},{16,8},{24,0},{1,25},{9,17},{17,9},{25,1},{2,26},{10... | collective-permute-start | bytes 983048 | tf_op jit(solution)/shard_map/ppermute | solution.py:283
  180.2 13.5 %collective-permute-start.13 = (bf16[80,2048]{1,0:T(8,128)(2,1)S(1)}, bf16[80,2048]{1,0:T(8,128)(2,1)S(1)}, u32[]{:S(2)}, u32[]{:S(2)}) collective-permute-start(bf16[80,2048]{1,0:T(8,128)(2,1)S(1)} %get-tuple-element.61), channel_id=1, source_target_pairs={{0,8},{8,0},{16,24},{24,16},{1,9},{9,1},{17,25},{25,17},{2,10},{10... | collective-permute-start | bytes 983048 | tf_op jit(solution)/shard_map/ppermute | solution.py:283
  182.0 19.7 %collective-permute-start.14 = (bf16[80,2048]{1,0:T(8,128)(2,1)S(1)}, bf16[80,2048]{1,0:T(8,128)(2,1)S(1)}, u32[]{:S(2)}, u32[]{:S(2)}) collective-permute-start(bf16[80,2048]{1,0:T(8,128)(2,1)S(1)} %get-tuple-element.62), channel_id=1, source_target_pairs={{0,16},{8,24},{16,0},{24,8},{1,17},{9,25},{17,1},{25,9},{2,18},{10... | collective-permute-start | bytes 983048 | tf_op jit(solution)/shard_map/ppermute | solution.py:283
  188.7 13.1 %collective-permute-start.15 = (bf16[80,2048]{1,0:T(8,128)(2,1)S(1)}, bf16[80,2048]{1,0:T(8,128)(2,1)S(1)}, u32[]{:S(2)}, u32[]{:S(2)}) collective-permute-start(bf16[80,2048]{1,0:T(8,128)(2,1)S(1)} %get-tuple-element.63), channel_id=1, source_target_pairs={{0,24},{8,16},{16,8},{24,0},{1,25},{9,17},{17,9},{25,1},{2,26},{10... | collective-permute-start | bytes 983048 | tf_op jit(solution)/shard_map/ppermute | solution.py:283
  190.9 11.6 %collective-permute-start.45 = (bf16[128,2048]{1,0:T(8,128)(2,1)S(1)}, bf16[128,2048]{1,0:T(8,128)(2,1)S(1)}, u32[]{:S(2)}, u32[]{:S(2)}) collective-permute-start(bf16[128,2048]{1,0:T(8,128)(2,1)S(1)} %get-tuple-element.96), channel_id=1, source_target_pairs={{0,1},{1,0},{2,3},{3,2},{4,5},{5,4},{6,7},{7,6},{8,9},{9,8},{10,11... | collective-permute-start | bytes 1572872 | tf_op jit(solution)/shard_map/ppermute | solution.py:275
  191.7 11.1 %collective-permute-start.26 = (bf16[128,2048]{1,0:T(8,128)(2,1)S(1)}, bf16[128,2048]{1,0:T(8,128)(2,1)S(1)}, u32[]{:S(2)}, u32[]{:S(2)}) collective-permute-start(bf16[128,2048]{1,0:T(8,128)(2,1)S(1)} %get-tuple-element.76), channel_id=1, source_target_pairs={{0,1},{1,0},{2,3},{3,2},{4,5},{5,4},{6,7},{7,6},{8,9},{9,8},{10,11... | collective-permute-start | bytes 1572872 | tf_op jit(solution)/shard_map/ppermute | solution.py:275
  192.3 38.8 %copy-start.7 = (bf16[128,2048]{1,0:T(8,128)(2,1)S(1)}, bf16[128,2048]{1,0:T(8,128)(2,1)}, u32[]{:S(2)}) copy-start(bf16[128,2048]{1,0:T(8,128)(2,1)} %copy-done.6) | copy-start | bytes 1572868
  193.6 13.8 %collective-permute-start.35 = (bf16[128,2048]{1,0:T(8,128)(2,1)S(1)}, bf16[128,2048]{1,0:T(8,128)(2,1)S(1)}, u32[]{:S(2)}, u32[]{:S(2)}) collective-permute-start(bf16[128,2048]{1,0:T(8,128)(2,1)S(1)} %add_convert_fusion.3), channel_id=1, source_target_pairs={{0,2},{1,3},{2,0},{3,1},{4,6},{5,7},{6,4},{7,5},{8,10},{9,11},{10,... | collective-permute-start | bytes 1572872 | tf_op jit(solution)/shard_map/ppermute | solution.py:278
  202.5 8.8 %collective-permute-start.16 = (bf16[128,2048]{1,0:T(8,128)(2,1)S(1)}, bf16[128,2048]{1,0:T(8,128)(2,1)S(1)}, u32[]{:S(2)}, u32[]{:S(2)}) collective-permute-start(bf16[128,2048]{1,0:T(8,128)(2,1)S(1)} %get-tuple-element.66), channel_id=1, source_target_pairs={{0,1},{1,0},{2,3},{3,2},{4,5},{5,4},{6,7},{7,6},{8,9},{9,8},{10,11... | collective-permute-start | bytes 1572872 | tf_op jit(solution)/shard_map/ppermute | solution.py:275
  202.7 15.2 %collective-permute-start.46 = (bf16[128,2048]{1,0:T(8,128)(2,1)S(1)}, bf16[128,2048]{1,0:T(8,128)(2,1)S(1)}, u32[]{:S(2)}, u32[]{:S(2)}) collective-permute-start(bf16[128,2048]{1,0:T(8,128)(2,1)S(1)} %add_convert_fusion.1), channel_id=1, source_target_pairs={{0,2},{1,3},{2,0},{3,1},{4,6},{5,7},{6,4},{7,5},{8,10},{9,11},{10,... | collective-permute-start | bytes 1572872 | tf_op jit(solution)/shard_map/ppermute | solution.py:278
  207.7 23.3 %collective-permute-start.36 = (bf16[128,2048]{1,0:T(8,128)(2,1)S(1)}, bf16[128,2048]{1,0:T(8,128)(2,1)S(1)}, u32[]{:S(2)}, u32[]{:S(2)}) collective-permute-start(bf16[128,2048]{1,0:T(8,128)(2,1)S(1)} %add_convert_fusion.2), channel_id=1, source_target_pairs={{0,6},{1,7},{2,4},{3,5},{4,2},{5,3},{6,0},{7,1},{8,14},{9,15},{10,... | collective-permute-start | bytes 1572872 | tf_op jit(solution)/shard_map/ppermute | solution.py:278

commit v3 on v2

--- a/solution.py
+++ b/solution.py
@@ -97,6 +97,15 @@
     total = refs[0][...].astype(F32)
     for more in refs[1:-1]:
         total = total + more[...].astype(F32)
+    refs[-1][...] = total.astype(BF)
+
+
+def prefix_kernel(takes, place_ref, *refs):
+    chip = lax.shift_right_logical(place_ref[0], 1)
+    total = jnp.zeros(refs[-1].shape, F32)
+    for chips, ref in zip(takes, refs):
+        takes_it = functools.reduce(jnp.logical_or, [chip == z for z in chips])
+        total = total + jnp.where(takes_it, ref[...].astype(F32), 0.0)
     refs[-1][...] = total.astype(BF)
 
 
@@ -282,6 +291,17 @@
             return x
         return lax.ppermute(x, "grp", [(g, g ^ m) for g in range(groups)])
 
+    def between(x, chips):
+        both = list(chips) + [(b, a) for a, b in chips]
+        return lax.ppermute(
+            x, "seq", sorted((2 * a + c, 2 * b + c) for a, b in both for c in range(2))
+        )
+
+    def onward(x, chips):
+        return lax.ppermute(
+            x, "seq", sorted((2 * a + c, 2 * b + c) for a, b in chips for c in range(2))
+        )
+
     def later(x, m, froms):
         pairs = [(2 * z + c, 2 * (z + m) + c) for z in froms for c in range(2)]
         return lax.ppermute(x, "seq", pairs)
@@ -302,9 +322,10 @@
     summed = (states.astype(F32) + pair.astype(F32)).astype(BF)
     summed = lax.dynamic_slice_in_dim(summed, core * half, half, axis=0)
     if stages == 4:
-        arrived = [later(summed, 1, range(3)), later(summed, 2, [0])]
-        upto = added(summed, arrived[0])
-        arrived.append(later(upto, 2, [1]))
+        arrived = [
+            between(summed, [(0, 1), (2, 3)]), between(summed, [(1, 2)]), between(summed, [(0, 2)])
+        ]
+        arrived.append(between(added(summed, arrived[0]), [(1, 3)]))
     else:
         arrived = [later(summed, m, range(stages - m)) for m in range(1, stages)]
 
@@ -329,7 +350,12 @@
     routes, ranks = call(body, [(shape, F32)] * 2)(
         *scalars[1:], *packs
     )
-    mine = added(*arrived)
+    if stages == 4:
+        takes = [(1, 3), (2,), (2,), (3,)]
+        body = functools.partial(prefix_kernel, takes)
+        mine = call(body, [(summed.shape, BF)])(scalars[2], *arrived)[0]
+    else:
+        mine = added(*arrived)
     other = swap(mine)
     residual, moe_in = call(
         project_kernel, [((tokens, features), BF)] * 2, [pltpu.VMEM((tokens, inner), BF)]
@@ -346,14 +372,21 @@
         moe_gain.reshape(1, features),
     )
 
-    routing = sending(stages)
     returning = homing(stages)
     blocks = {0: moe_in}
     outs = {}
     partners = {0: swap(moe_in)}
-    for m in range(1, stages):
-        source, shift = routing[m]
-        blocks[m] = along(blocks[source], shift)
+    if stages == 4:
+        blocks[1] = between(moe_in, [(0, 1), (2, 3)])
+        across_middle = between(moe_in, [(1, 2)])
+        outward = [(1, 0), (2, 3)]
+        near = onward(across_middle, outward)
+        far = between(blocks[1], [(1, 2)])
+        blocks[2] = added(near, far)
+        blocks[3] = added(across_middle, onward(far, outward))
+    else:
+        for m in range(1, stages):
+            blocks[m] = along(moe_in, m)
     for m in range(stages):
         base = m * 2 * groups
         partner = swap(blocks[m]) if m else partners[0]
@@ -375,12 +408,6 @@
     return combined.astype(BF).reshape(1, tokens, features)
 
 
-def sending(stages):
-    if stages == 4:
-        return {1: (0, 1), 2: (0, 2), 3: (2, 1)}
-    return {m: (0, m) for m in range(1, stages)}
-
-
 def homing(stages):
     if stages == 4:
         return {2: (3, 1), 3: (0, 3), 1: (0, 1)}

time: 233 us -> 244 us (1.047)
  waiting for transfers between devices: 126 us -> 152 us
  starting transfers between devices: 68.7 us -> 53.7 us
  local copies, waits for them, and re-layouts: 4.64 us -> 7.48 us
    ppermute x3 -> x9, waiting for transfers between devices: 6.24 us -> 42.4 us  [the longest x7 28.3 us: between(): lax.ppermute(x, 'seq', sorted(((2 * a + c, 2 * b + c) for a, b in both fo...]
    ppermute x9 -> x6, starting transfers between devices: 22.6 us -> 7.26 us  [along(): return lax.ppermute(x, 'seq', [(s, s ^ 2 * m) for s in range(length)])]
    ppermute x9 -> x6, waiting for transfers between devices: 57.9 us -> 42.8 us  [along(): return lax.ppermute(x, 'seq', [(s, s ^ 2 * m) for s in range(length)])]
    ppermute x24, starting transfers between devices: 34.2 us -> 29.5 us  [across(): return lax.ppermute(x, 'grp', [(g, g ^ m) for g in range(groups)])]
    ppermute x24, waiting for transfers between devices: 58.8 us -> 63.4 us  [across(): return lax.ppermute(x, 'grp', [(g, g ^ m) for g in range(groups)])]
    ppermute x3 -> x9, starting transfers between devices: 10 us -> 14.5 us  [the longest x7 11.6 us: between(): lax.ppermute(x, 'seq', sorted(((2 * a + c, 2 * b + c) for a, b in both fo...]
    unnamed x24 -> x38, local copies, waits for them, and re-layouts: 4.64 us -> 7.48 us
    pallas_call x19 -> x21, Pallas kernels: 30.7 us -> 28.7 us  [run(): pl.pallas_call(body, in_specs=specs, out_specs=[pl.BlockSpec(memory_space...]
  transfers between devices with their start and end apart: 47 -> 50, of which waited for: 23 -> 29; matrix products, arithmetic and copies ran while one was open for 0% -> 0% of each run, Pallas kernels for 11% -> 10%
where the time goes in v3:
time: 244 us
  waiting for transfers between devices  152 us (62%)
  starting transfers between devices  53.7 us (22%)
  Pallas kernels  28.7 us (12%)
  local copies, waits for them, and re-layouts  7.48 us (3%)
    ppermute x24, waiting for transfers between devices, across(): return lax.ppermute(x, 'grp', [(g, g ^ m) for g in range(groups)])  63.4 us
    ppermute x6, waiting for transfers between devices, along(): return lax.ppermute(x, 'seq', [(s, s ^ 2 * m) for s in range(length)])  42.8 us
    ppermute x24, starting transfers between devices, across(): return lax.ppermute(x, 'grp', [(g, g ^ m) for g in range(groups)])  29.5 us
    pallas_call x21, Pallas kernels, run(): pl.pallas_call(body, in_specs=specs, out_specs=[pl.BlockSpec(memory_space...  28.7 us
    ppermute x7, waiting for transfers between devices, between(): lax.ppermute(x, 'seq', sorted(((2 * a + c, 2 * b + c) for a, b in both fo...  28.3 us
    ppermute x2, waiting for transfers between devices, onward(): lax.ppermute(x, 'seq', sorted(((2 * a + c, 2 * b + c) for a, b in chips f...  14.1 us
    ppermute x7, starting transfers between devices, between(): lax.ppermute(x, 'seq', sorted(((2 * a + c, 2 * b + c) for a, b in both fo...  11.6 us
    unnamed x38, local copies, waits for them, and re-layouts  7.48 us
  transfers between devices with their start and end apart: 50, of which 29 were waited for; matrix products, arithmetic and copies ran while one was open for 0% of the time, Pallas kernels for 10%

profile of v3, /device:TPU:0, one launch (start us, length us, event | category | flops | bytes accessed | tf_op | source)
XLA Modules:
  0.0 243.9 jit_solution(17582441794385186309)
XLA Ops:
  0.0 1.9 shard_map.119
  2.5 1.5 collective-permute-done.pair_ref
  4.1 3.0 %collective-permute-start.1 = (bf16[1024,128]{1,0:T(8,128)(2,1)S(1)}, bf16[1024,128]{1,0:T(8,128)(2,1)S(1)}, u32[]{:S(2)}, u32[]{:S(2)}) collective-permute-start(bf16[1024,128]{1,0:T(8,128)(2,1)S(1)} %add_convert_fusion.4.refs_0_), channel_id=1, source_target_pairs={{0,2},{1,3},{2,0},{3,1},{4,6},{5,7},{6,4},{7,5},{8,10},{9,11},{10,... | collective-permute-start | bytes 786440 | tf_op jit(solution)/shard_map/ppermute | solution.py:296
  7.8 5.7 %collective-permute-start.3 = (bf16[1024,128]{1,0:T(8,128)(2,1)S(1)}, bf16[1024,128]{1,0:T(8,128)(2,1)S(1)}, u32[]{:S(2)}, u32[]{:S(2)}) collective-permute-start(bf16[1024,128]{1,0:T(8,128)(2,1)S(1)} %add_convert_fusion.4.refs_0_), channel_id=1, source_target_pairs={{0,4},{1,5},{4,0},{5,1},{8,12},{9,13},{12,8},{13,9},{16,20},{17,21... | collective-permute-start | bytes 786440 | tf_op jit(solution)/shard_map/ppermute | solution.py:296
  14.5 14.7 %collective-permute-done.3.refs_2_ = bf16[1024,128]{1,0:T(8,128)(2,1)S(1)} collective-permute-done((bf16[1024,128]{1,0:T(8,128)(2,1)S(1)}, bf16[1024,128]{1,0:T(8,128)(2,1)S(1)}, u32[]{:S(2)}, u32[]{:S(2)}) %collective-permute-start.3) | collective-permute-done | bytes 262176 | tf_op jit(solution)/shard_map/ppermute | solution.py:296
  29.5 4.2 %shard_map.118 = (f32[128,2048]{1,0:T(8,128)S(1)}, bf16[2048,2048]{1,0:T(8,128)(2,1)S(1)}) custom-call(bf16[128,2048]{1,0:T(8,128)(2,1)} %bitcast.20, bf16[128,2048]{1,0:T(8,128)(2,1)} %bitcast.26, bf16[128,2048]{1,0:T(8,128)(2,1)} %bitcast.28, bf16[2048,2048]{1,0:T(8,128)(2,1)} %w_hbm.1, s32[1]{0:T(128)} %bitcast.core_ref, s32[1]{0:T(128)} %bitcast.4.group_ref, ...), custom_call_target="tpu_custom_call" | custom-call | tf_op jit(solution)/shard_map/pallas_call | solution.py:32
  33.7 1.9 shard_map.122
  35.7 0.8 copy-done.13
  37.3 13.5 %collective-permute-done.19.own_ref = bf16[128,2048]{1,0:T(8,128)(2,1)S(1)} collective-permute-done((bf16[128,2048]{1,0:T(8,128)(2,1)S(1)}, bf16[128,2048]{1,0:T(8,128)(2,1)S(1)}, u32[]{:S(2)}, u32[]{:S(2)}) %collective-permute-start.19) | collective-permute-done | bytes 524320 | tf_op jit(solution)/shard_map/ppermute | solution.py:296
  51.5 1.3 collective-permute-start.30
  53.6 14.1 %collective-permute-done.30.refs_0_ = bf16[128,2048]{1,0:T(8,128)(2,1)S(1)} collective-permute-done((bf16[128,2048]{1,0:T(8,128)(2,1)S(1)}, bf16[128,2048]{1,0:T(8,128)(2,1)S(1)}, u32[]{:S(2)}, u32[]{:S(2)}) %collective-permute-start.30) | collective-permute-done | bytes 524320 | tf_op jit(solution)/shard_map/ppermute | solution.py:301
  67.7 0.9 shard_map.132.own_ref
  70.0 1.6 collective-permute-start.21
  72.3 1.5 collective-permute-done.7.par_ref
  73.9 2.0 collective-permute-start.10
  75.9 3.7 %collective-permute-done.10.refs_3_ = f32[64,128]{1,0:T(8,128)S(1)} collective-permute-done((f32[64,128]{1,0:T(8,128)S(1)}, f32[64,128]{1,0:T(8,128)S(1)}, u32[]{:S(2)}, u32[]{:S(2)}) %collective-permute-start.10) | collective-permute-done | bytes 32800 | tf_op jit(solution)/shard_map/ppermute | solution.py:287
  79.6 0.9 collective-permute-start.8
  80.5 7.2 %collective-permute-done.8.refs_1_ = f32[64,128]{1,0:T(8,128)S(1)} collective-permute-done((f32[64,128]{1,0:T(8,128)S(1)}, f32[64,128]{1,0:T(8,128)S(1)}, u32[]{:S(2)}, u32[]{:S(2)}) %collective-permute-start.8) | collective-permute-done | bytes 32800 | tf_op jit(solution)/shard_map/ppermute | solution.py:287
  87.8 4.7 %collective-permute-done.9.refs_2_ = f32[64,128]{1,0:T(8,128)S(1)} collective-permute-done((f32[64,128]{1,0:T(8,128)S(1)}, f32[64,128]{1,0:T(8,128)S(1)}, u32[]{:S(2)}, u32[]{:S(2)}) %collective-permute-start.9) | collective-permute-done | bytes 32800 | tf_op jit(solution)/shard_map/ppermute | solution.py:287
  92.6 1.7 shard_map.133
  94.3 1.6 collective-permute-start.32
  95.9 1.5 collective-permute-start.33
  97.9 1.0 copy-done.7
  99.1 1.0 copy-done.12
  100.7 1.6 collective-permute-start.11
  102.2 2.7 %collective-permute-done.32.refs_1_ = bf16[80,2048]{1,0:T(8,128)(2,1)S(1)} collective-permute-done((bf16[80,2048]{1,0:T(8,128)(2,1)S(1)}, bf16[80,2048]{1,0:T(8,128)(2,1)S(1)}, u32[]{:S(2)}, u32[]{:S(2)}) %collective-permute-start.32) | collective-permute-done | bytes 327712 | tf_op jit(solution)/shard_map/ppermute | solution.py:292
  105.0 1.5 collective-permute-start.12
  106.5 1.0 copy-done.10
  108.0 1.6 collective-permute-done.33.refs_2_
  109.6 3.4 %collective-permute-done.34.refs_3_ = bf16[80,2048]{1,0:T(8,128)(2,1)S(1)} collective-permute-done((bf16[80,2048]{1,0:T(8,128)(2,1)S(1)}, bf16[80,2048]{1,0:T(8,128)(2,1)S(1)}, u32[]{:S(2)}, u32[]{:S(2)}) %collective-permute-start.34) | collective-permute-done | bytes 327712 | tf_op jit(solution)/shard_map/ppermute | solution.py:292
  113.5 1.9 copy-done.2
  115.4 3.2 %shard_map.134 = (bf16[80,2048]{1,0:T(8,128)(2,1)S(1)}, bf16[80,2048]{1,0:T(8,128)(2,1)S(1)}, bf16[80,2048]{1,0:T(8,128)(2,1)S(1)}, bf16[80,2048]{1,0:T(8,128)(2,1)S(1)}) custom-call(bf16[80,2048]{1,0:T(8,128)(2,1)S(1)} %get-tuple-element.77.refs_0_, bf16[80,2048]{1,0:T(8,128)(2,1)S(1)} %collective-permute-done.32.refs_1_, ...), custom_call_target="tpu_custom_call" | custom-call | tf_op jit(solution)/shard_map/pallas_call | solution.py:32
  119.1 2.4 collective-permute-start.44
  122.0 4.0 %collective-permute-done.42.refs_1_ = bf16[80,2048]{1,0:T(8,128)(2,1)S(1)} collective-permute-done((bf16[80,2048]{1,0:T(8,128)(2,1)S(1)}, bf16[80,2048]{1,0:T(8,128)(2,1)S(1)}, u32[]{:S(2)}, u32[]{:S(2)}) %collective-permute-start.42) | collective-permute-done | bytes 327712 | tf_op jit(solution)/shard_map/ppermute | solution.py:292
  126.1 1.5 collective-permute-start.36
  127.6 1.4 collective-permute-start.37
  129.5 1.1 collective-permute-done.43.refs_2_
  130.8 3.3 %collective-permute-done.44.refs_3_ = bf16[80,2048]{1,0:T(8,128)(2,1)S(1)} collective-permute-done((bf16[80,2048]{1,0:T(8,128)(2,1)S(1)}, bf16[80,2048]{1,0:T(8,128)(2,1)S(1)}, u32[]{:S(2)}, u32[]{:S(2)}) %collective-permute-start.44) | collective-permute-done | bytes 327712 | tf_op jit(solution)/shard_map/ppermute | solution.py:292
  134.6 5.6 %collective-permute-done.35.refs_1_ = bf16[80,2048]{1,0:T(8,128)(2,1)S(1)} collective-permute-done((bf16[80,2048]{1,0:T(8,128)(2,1)S(1)}, bf16[80,2048]{1,0:T(8,128)(2,1)S(1)}, u32[]{:S(2)}, u32[]{:S(2)}) %collective-permute-start.35) | collective-permute-done | bytes 327712 | tf_op jit(solution)/shard_map/ppermute | solution.py:292
  140.2 2.4 collective-permute-start.25
  142.6 3.2 %shard_map.137 = (bf16[80,2048]{1,0:T(8,128)(2,1)S(1)}, bf16[80,2048]{1,0:T(8,128)(2,1)S(1)}, bf16[80,2048]{1,0:T(8,128)(2,1)S(1)}, bf16[80,2048]{1,0:T(8,128)(2,1)S(1)}) custom-call(bf16[80,2048]{1,0:T(8,128)(2,1)S(1)} %get-tuple-element.87.refs_0_, bf16[80,2048]{1,0:T(8,128)(2,1)S(1)} %collective-permute-done.42.refs_1_, ...), custom_call_target="tpu_custom_call" | custom-call | tf_op jit(solution)/shard_map/pallas_call | solution.py:32
  146.4 1.8 collective-permute-done.37.refs_3_
  148.2 1.5 collective-permute-start.45
  150.4 3.8 %collective-permute-done.23.refs_1_ = bf16[80,2048]{1,0:T(8,128)(2,1)S(1)} collective-permute-done((bf16[80,2048]{1,0:T(8,128)(2,1)S(1)}, bf16[80,2048]{1,0:T(8,128)(2,1)S(1)}, u32[]{:S(2)}, u32[]{:S(2)}) %collective-permute-start.23) | collective-permute-done | bytes 327712 | tf_op jit(solution)/shard_map/ppermute | solution.py:292
  154.3 11.2 %collective-permute-done.24.refs_2_ = bf16[80,2048]{1,0:T(8,128)(2,1)S(1)} collective-permute-done((bf16[80,2048]{1,0:T(8,128)(2,1)S(1)}, bf16[80,2048]{1,0:T(8,128)(2,1)S(1)}, u32[]{:S(2)}, u32[]{:S(2)}) %collective-permute-start.24) | collective-permute-done | bytes 327712 | tf_op jit(solution)/shard_map/ppermute | solution.py:292
  165.4 3.0 %collective-permute-start.46 = (bf16[80,2048]{1,0:T(8,128)(2,1)S(1)}, bf16[80,2048]{1,0:T(8,128)(2,1)S(1)}, u32[]{:S(2)}, u32[]{:S(2)}) collective-permute-start(bf16[80,2048]{1,0:T(8,128)(2,1)S(1)} %get-tuple-element.93), channel_id=1, source_target_pairs={{0,16},{8,24},{16,0},{24,8},{1,17},{9,25},{17,1},{25,9},{2,18},{10... | collective-permute-start | bytes 983048 | tf_op jit(solution)/shard_map/ppermute | solution.py:292
  168.4 3.2 %shard_map.130 = (bf16[80,2048]{1,0:T(8,128)(2,1)S(1)}, bf16[80,2048]{1,0:T(8,128)(2,1)S(1)}, bf16[80,2048]{1,0:T(8,128)(2,1)S(1)}, bf16[80,2048]{1,0:T(8,128)(2,1)S(1)}) custom-call(bf16[80,2048]{1,0:T(8,128)(2,1)S(1)} %get-tuple-element.67.refs_0_, bf16[80,2048]{1,0:T(8,128)(2,1)S(1)} %collective-permute-done.23.refs_1_, ...), custom_call_target="tpu_custom_call" | custom-call | tf_op jit(solution)/shard_map/pallas_call | solution.py:32
  171.6 1.5 collective-permute-start.26
  173.2 2.2 collective-permute-done.45.refs_1_
  175.4 1.5 collective-permute-start.27
  176.9 3.5 %shard_map.126 = (bf16[80,2048]{1,0:T(8,128)(2,1)S(1)}, bf16[80,2048]{1,0:T(8,128)(2,1)S(1)}, bf16[80,2048]{1,0:T(8,128)(2,1)S(1)}, bf16[80,2048]{1,0:T(8,128)(2,1)S(1)}) custom-call(bf16[80,2048]{1,0:T(8,128)(2,1)S(1)} %get-tuple-element.56.refs_0_, bf16[80,2048]{1,0:T(8,128)(2,1)S(1)} %collective-permute-done.11.refs_1_, ...), custom_call_target="tpu_custom_call" | custom-call | tf_op jit(solution)/shard_map/pallas_call | solution.py:32
  180.3 1.7 collective-permute-done.46.refs_2_
  182.0 1.4 collective-permute-done.47.refs_3_
  183.4 1.3 collective-permute-start.15
  185.4 1.8 collective-permute-start.16
  187.1 2.3 collective-permute-done.26.refs_1_
  189.6 2.3 collective-permute-start.28
  192.0 16.7 %collective-permute-done.28.refs_3_ = bf16[80,2048]{1,0:T(8,128)(2,1)S(1)} collective-permute-done((bf16[80,2048]{1,0:T(8,128)(2,1)S(1)}, bf16[80,2048]{1,0:T(8,128)(2,1)S(1)}, u32[]{:S(2)}, u32[]{:S(2)}) %collective-permute-start.28) | collective-permute-done | bytes 327712 | tf_op jit(solution)/shard_map/ppermute | solution.py:292
  211.0 2.1 collective-permute-start.49
  213.1 10.4 %collective-permute-done.39 = bf16[128,2048]{1,0:T(8,128)(2,1)S(1)} collective-permute-done((bf16[128,2048]{1,0:T(8,128)(2,1)S(1)}, bf16[128,2048]{1,0:T(8,128)(2,1)S(1)}, u32[]{:S(2)}, u32[]{:S(2)}) %collective-permute-start.39) | collective-permute-done | bytes 524320 | tf_op jit(solution)/shard_map/ppermute | solution.py:287
  223.7 2.1 collective-permute-start.40
  225.8 8.3 %collective-permute-done.49 = bf16[128,2048]{1,0:T(8,128)(2,1)S(1)} collective-permute-done((bf16[128,2048]{1,0:T(8,128)(2,1)S(1)}, bf16[128,2048]{1,0:T(8,128)(2,1)S(1)}, u32[]{:S(2)}, u32[]{:S(2)}) %collective-permute-start.49) | collective-permute-done | bytes 524320 | tf_op jit(solution)/shard_map/ppermute | solution.py:287
  234.1 8.5 %collective-permute-done.40 = bf16[128,2048]{1,0:T(8,128)(2,1)S(1)} collective-permute-done((bf16[128,2048]{1,0:T(8,128)(2,1)S(1)}, bf16[128,2048]{1,0:T(8,128)(2,1)S(1)}, u32[]{:S(2)}, u32[]{:S(2)}) %collective-permute-start.40) | collective-permute-done | bytes 524320 | tf_op jit(solution)/shard_map/ppermute | solution.py:287
  242.6 1.2 fusion
  (103 shorter events, 16.3 us)
Async XLA Ops:
  1.9 2.1 collective-permute-start
  4.1 9.6 %collective-permute-start.1 = (bf16[1024,128]{1,0:T(8,128)(2,1)S(1)}, bf16[1024,128]{1,0:T(8,128)(2,1)S(1)}, u32[]{:S(2)}, u32[]{:S(2)}) collective-permute-start(bf16[1024,128]{1,0:T(8,128)(2,1)S(1)} %add_convert_fusion.4.refs_0_), channel_id=1, source_target_pairs={{0,2},{1,3},{2,0},{3,1},{4,6},{5,7},{6,4},{7,5},{8,10},{9,11},{10,... | collective-permute-start | bytes 786440 | tf_op jit(solution)/shard_map/ppermute | solution.py:296
  7.1 7.4 %collective-permute-start.2 = (bf16[1024,128]{1,0:T(8,128)(2,1)S(1)}, bf16[1024,128]{1,0:T(8,128)(2,1)S(1)}, u32[]{:S(2)}, u32[]{:S(2)}) collective-permute-start(bf16[1024,128]{1,0:T(8,128)(2,1)S(1)} %add_convert_fusion.4.refs_0_), channel_id=1, source_target_pairs={{2,4},{3,5},{4,2},{5,3},{10,12},{11,13},{12,10},{13,11},{18,20},{1... | collective-permute-start | bytes 786440 | tf_op jit(solution)/shard_map/ppermute | solution.py:296
  7.8 21.4 %collective-permute-start.3 = (bf16[1024,128]{1,0:T(8,128)(2,1)S(1)}, bf16[1024,128]{1,0:T(8,128)(2,1)S(1)}, u32[]{:S(2)}, u32[]{:S(2)}) collective-permute-start(bf16[1024,128]{1,0:T(8,128)(2,1)S(1)} %add_convert_fusion.4.refs_0_), channel_id=1, source_target_pairs={{0,4},{1,5},{4,0},{5,1},{8,12},{9,13},{12,8},{13,9},{16,20},{17,21... | collective-permute-start | bytes 786440 | tf_op jit(solution)/shard_map/ppermute | solution.py:296
  13.8 15.4 %collective-permute-start.4 = (bf16[1024,128]{1,0:T(8,128)(2,1)S(1)}, bf16[1024,128]{1,0:T(8,128)(2,1)S(1)}, u32[]{:S(2)}, u32[]{:S(2)}) collective-permute-start(bf16[1024,128]{1,0:T(8,128)(2,1)S(1)} %shard_map.120), channel_id=1, source_target_pairs={{2,6},{3,7},{6,2},{7,3},{10,14},{11,15},{14,10},{15,11},{18,22},{1... | collective-permute-start | bytes 786440 | tf_op jit(solution)/shard_map/ppermute | solution.py:296
  29.3 4.3 %collective-permute-start.5 = (bf16[1024,128]{1,0:T(8,128)(2,1)S(1)}, bf16[1024,128]{1,0:T(8,128)(2,1)S(1)}, u32[]{:S(2)}, u32[]{:S(2)}) collective-permute-start(bf16[1024,128]{1,0:T(8,128)(2,1)S(1)} %shard_map.121.mine_ref), channel_id=1, source_target_pairs={{0,1},{1,0},{2,3},{3,2},{4,5},{5,4},{6,7},{7,6},{8,9},{9,8},{10,11... | collective-permute-start | bytes 786440 | tf_op jit(solution)/shard_map/ppermute | solution.py:284
  29.4 4.3 %copy-start.4 = (bf16[1,128,2048]{2,1,0:T(8,128)(2,1)S(1)}, bf16[1,128,2048]{2,1,0:T(8,128)(2,1)}, u32[]{:S(2)}) copy-start(bf16[1,128,2048]{2,1,0:T(8,128)(2,1)} %param.13) | copy-start | bytes 1572868
  29.4 4.3 %copy-start.5 = (bf16[1,128,2048]{2,1,0:T(8,128)(2,1)S(1)}, bf16[1,128,2048]{2,1,0:T(8,128)(2,1)}, u32[]{:S(2)}) copy-start(bf16[1,128,2048]{2,1,0:T(8,128)(2,1)} %param.12) | copy-start | bytes 1572868
  29.4 4.3 %copy-start.15 = (f32[2048]{0:T(1024)S(1)}, f32[2048]{0:T(1024)}, u32[]{:S(2)}) copy-start(f32[2048]{0:T(1024)} %param.16) | copy-start | bytes 24580
  29.5 4.3 %copy-start.16 = (f32[2048]{0:T(1024)S(1)}, f32[2048]{0:T(1024)}, u32[]{:S(2)}) copy-start(f32[2048]{0:T(1024)} %param.18) | copy-start | bytes 24580
  33.7 35.7 %copy-start.17 = (f32[1,128,8]{1,2,0:T(8,128)S(1)}, f32[1,128,8]{1,2,0:T(8,128)}, u32[]{:S(2)}) copy-start(f32[1,128,8]{1,2,0:T(8,128)} %param.20) | copy-start | bytes 12292
  33.7 38.1 %copy-start.18 = (s32[1,128,8]{1,2,0:T(8,128)S(1)}, s32[1,128,8]{1,2,0:T(8,128)}, u32[]{:S(2)}) copy-start(s32[1,128,8]{1,2,0:T(8,128)} %param.19) | copy-start | bytes 12292
  36.5 32.1 %copy-start.11 = (bf16[128,2048]{1,0:T(8,128)(2,1)}, bf16[128,2048]{1,0:T(8,128)(2,1)S(1)}, u32[]{:S(2)}) copy-start(bf16[128,2048]{1,0:T(8,128)(2,1)S(1)} %get-tuple-element.54.own_ref) | copy-start | bytes 1572868
  36.5 77.0 %copy-start = (bf16[1,2048,768]{2,1,0:T(8,128)(2,1)S(1)}, bf16[1,2048,768]{2,1,0:T(8,128)(2,1)}, u32[]{:S(2)}) copy-start(bf16[1,2048,768]{2,1,0:T(8,128)(2,1)} %refs_4_.7) | copy-start | bytes 9437188
  36.5 14.3 %collective-permute-start.19 = (bf16[128,2048]{1,0:T(8,128)(2,1)S(1)}, bf16[128,2048]{1,0:T(8,128)(2,1)S(1)}, u32[]{:S(2)}, u32[]{:S(2)}) collective-permute-start(bf16[128,2048]{1,0:T(8,128)(2,1)S(1)} %get-tuple-element.54.own_ref), channel_id=1, source_target_pairs={{0,2},{1,3},{2,0},{3,1},{4,6},{5,7},{6,4},{7,5},{8,10},{9,11},{10,... | collective-permute-start | bytes 1572872 | tf_op jit(solution)/shard_map/ppermute | solution.py:296
  36.5 15.0 %collective-permute-start.18 = (bf16[128,2048]{1,0:T(8,128)(2,1)S(1)}, bf16[128,2048]{1,0:T(8,128)(2,1)S(1)}, u32[]{:S(2)}, u32[]{:S(2)}) collective-permute-start(bf16[128,2048]{1,0:T(8,128)(2,1)S(1)} %get-tuple-element.54.own_ref), channel_id=1, source_target_pairs={{2,4},{3,5},{4,2},{5,3},{10,12},{11,13},{12,10},{13,11},{18,20},{1... | collective-permute-start | bytes 1572872 | tf_op jit(solution)/shard_map/ppermute | solution.py:296
  50.8 2.8 %copy-start.9 = (bf16[128,2048]{1,0:T(8,128)(2,1)}, bf16[128,2048]{1,0:T(8,128)(2,1)S(1)}, u32[]{:S(2)}) copy-start(bf16[128,2048]{1,0:T(8,128)(2,1)S(1)} %collective-permute-done.19.own_ref) | copy-start | bytes 1572868
  50.8 2.8 %collective-permute-start.20 = (bf16[128,2048]{1,0:T(8,128)(2,1)S(1)}, bf16[128,2048]{1,0:T(8,128)(2,1)S(1)}, u32[]{:S(2)}, u32[]{:S(2)}) collective-permute-start(bf16[128,2048]{1,0:T(8,128)(2,1)S(1)} %collective-permute-done.19.own_ref), channel_id=1, source_target_pairs={{2,4},{3,5},{4,2},{5,3},{10,12},{11,13},{12,10},{13,11},{18,20},{1... | collective-permute-start | bytes 1572872 | tf_op jit(solution)/shard_map/ppermute | solution.py:296
  51.5 16.2 %collective-permute-start.30 = (bf16[128,2048]{1,0:T(8,128)(2,1)S(1)}, bf16[128,2048]{1,0:T(8,128)(2,1)S(1)}, u32[]{:S(2)}, u32[]{:S(2)}) collective-permute-start(bf16[128,2048]{1,0:T(8,128)(2,1)S(1)} %collective-permute-done.18.refs_0_), channel_id=1, source_target_pairs={{2,0},{3,1},{4,6},{5,7},{10,8},{11,9},{12,14},{13,15},{18,16},{19,... | collective-permute-start | bytes 1572872 | tf_op jit(solution)/shard_map/ppermute | solution.py:301
  69.4 23.2 %collective-permute-start.31 = (bf16[128,2048]{1,0:T(8,128)(2,1)}, bf16[128,2048]{1,0:T(8,128)(2,1)}, u32[]{:S(2)}, u32[]{:S(2)}) collective-permute-start(bf16[128,2048]{1,0:T(8,128)(2,1)} %shard_map.132.own_ref), channel_id=1, source_target_pairs={{0,1},{1,0},{2,3},{3,2},{4,5},{5,4},{6,7},{7,6},{8,9},{9,8},{10,11... | collective-permute-start | bytes 1572872 | tf_op jit(solution)/shard_map/ppermute | solution.py:284
  69.5 44.0 %copy-start.1 = (bf16[1,2048,768]{2,1,0:T(8,128)(2,1)S(1)}, bf16[1,2048,768]{2,1,0:T(8,128)(2,1)}, u32[]{:S(2)}) copy-start(bf16[1,2048,768]{2,1,0:T(8,128)(2,1)} %refs_5_.7) | copy-start | bytes 9437188
  69.5 29.6 %collective-permute-start.6 = (bf16[128,2048]{1,0:T(8,128)(2,1)}, bf16[128,2048]{1,0:T(8,128)(2,1)S(1)}, u32[]{:S(2)}, u32[]{:S(2)}) collective-permute-start(bf16[128,2048]{1,0:T(8,128)(2,1)} %copy-done.11), channel_id=1, source_target_pairs={{0,1},{1,0},{2,3},{3,2},{4,5},{5,4},{6,7},{7,6},{8,9},{9,8},{10,11... | collective-permute-start | bytes 1572872 | tf_op jit(solution)/shard_map/ppermute | solution.py:284
  70.0 27.3 %collective-permute-start.21 = (bf16[128,2048]{1,0:T(8,128)(2,1)}, bf16[128,2048]{1,0:T(8,128)(2,1)S(1)}, u32[]{:S(2)}, u32[]{:S(2)}) collective-permute-start(bf16[128,2048]{1,0:T(8,128)(2,1)} %copy-done.8), channel_id=1, source_target_pairs={{2,0},{3,1},{4,6},{5,7},{10,8},{11,9},{12,14},{13,15},{18,16},{19,... | collective-permute-start | bytes 1572872 | tf_op jit(solution)/shard_map/ppermute | solution.py:301
  71.7 29.0 %collective-permute-start.41 = (bf16[128,2048]{1,0:T(8,128)(2,1)}, bf16[128,2048]{1,0:T(8,128)(2,1)S(1)}, u32[]{:S(2)}, u32[]{:S(2)}) collective-permute-start(bf16[128,2048]{1,0:T(8,128)(2,1)} %copy-done.9), channel_id=1, source_target_pairs={{0,1},{1,0},{2,3},{3,2},{4,5},{5,4},{6,7},{7,6},{8,9},{9,8},{10,11... | collective-permute-start | bytes 1572872 | tf_op jit(solution)/shard_map/ppermute | solution.py:284
  71.9 1.9 collective-permute-start.7
  73.9 5.7 %collective-permute-start.10 = (f32[64,128]{1,0:T(8,128)S(1)}, f32[64,128]{1,0:T(8,128)S(1)}, u32[]{:S(2)}, u32[]{:S(2)}) collective-permute-start(f32[64,128]{1,0:T(8,128)S(1)} %shard_map.123.refs_0_), channel_id=1, source_target_pairs={{0,6},{1,7},{2,4},{3,5},{4,2},{5,3},{6,0},{7,1},{8,14},{9,15},{10,... | collective-permute-start | bytes 98312 | tf_op jit(solution)/shard_map/ppermute | solution.py:287
  79.6 8.1 %collective-permute-start.8 = (f32[64,128]{1,0:T(8,128)S(1)}, f32[64,128]{1,0:T(8,128)S(1)}, u32[]{:S(2)}, u32[]{:S(2)}) collective-permute-start(f32[64,128]{1,0:T(8,128)S(1)} %shard_map.123.refs_0_), channel_id=1, source_target_pairs={{0,2},{1,3},{2,0},{3,1},{4,6},{5,7},{6,4},{7,5},{8,10},{9,11},{10,... | collective-permute-start | bytes 98312 | tf_op jit(solution)/shard_map/ppermute | solution.py:287
  87.7 4.8 %collective-permute-start.9 = (f32[64,128]{1,0:T(8,128)S(1)}, f32[64,128]{1,0:T(8,128)S(1)}, u32[]{:S(2)}, u32[]{:S(2)}) collective-permute-start(f32[64,128]{1,0:T(8,128)S(1)} %shard_map.123.refs_0_), channel_id=1, source_target_pairs={{0,4},{1,5},{2,6},{3,7},{4,0},{5,1},{6,2},{7,3},{8,12},{9,13},{10,... | collective-permute-start | bytes 98312 | tf_op jit(solution)/shard_map/ppermute | solution.py:287
  94.3 10.6 %collective-permute-start.32 = (bf16[80,2048]{1,0:T(8,128)(2,1)S(1)}, bf16[80,2048]{1,0:T(8,128)(2,1)S(1)}, u32[]{:S(2)}, u32[]{:S(2)}) collective-permute-start(bf16[80,2048]{1,0:T(8,128)(2,1)S(1)} %get-tuple-element.78), channel_id=1, source_target_pairs={{0,8},{8,0},{16,24},{24,16},{1,9},{9,1},{17,25},{25,17},{2,10},{10... | collective-permute-start | bytes 983048 | tf_op jit(solution)/shard_map/ppermute | solution.py:292
  95.9 13.8 %collective-permute-start.33 = (bf16[80,2048]{1,0:T(8,128)(2,1)S(1)}, bf16[80,2048]{1,0:T(8,128)(2,1)S(1)}, u32[]{:S(2)}, u32[]{:S(2)}) collective-permute-start(bf16[80,2048]{1,0:T(8,128)(2,1)S(1)} %get-tuple-element.79), channel_id=1, source_target_pairs={{0,16},{8,24},{16,0},{24,8},{1,17},{9,25},{17,1},{25,9},{2,18},{10... | collective-permute-start | bytes 983048 | tf_op jit(solution)/shard_map/ppermute | solution.py:292
  97.4 15.6 %collective-permute-start.34 = (bf16[80,2048]{1,0:T(8,128)(2,1)S(1)}, bf16[80,2048]{1,0:T(8,128)(2,1)S(1)}, u32[]{:S(2)}, u32[]{:S(2)}) collective-permute-start(bf16[80,2048]{1,0:T(8,128)(2,1)S(1)} %get-tuple-element.80), channel_id=1, source_target_pairs={{0,24},{8,16},{16,8},{24,0},{1,25},{9,17},{17,9},{25,1},{2,26},{10... | collective-permute-start | bytes 983048 | tf_op jit(solution)/shard_map/ppermute | solution.py:292
  99.0 28.5 %collective-permute-start.22 = (bf16[128,2048]{1,0:T(8,128)(2,1)S(1)}, bf16[128,2048]{1,0:T(8,128)(2,1)S(1)}, u32[]{:S(2)}, u32[]{:S(2)}) collective-permute-start(bf16[128,2048]{1,0:T(8,128)(2,1)S(1)} %shard_map.128.own_ref), channel_id=1, source_target_pairs={{0,1},{1,0},{2,3},{3,2},{4,5},{5,4},{6,7},{7,6},{8,9},{9,8},{10,11... | collective-permute-start | bytes 1572872 | tf_op jit(solution)/shard_map/ppermute | solution.py:284
  99.1 1.0 copy-start.12
  100.7 18.4 %collective-permute-start.11 = (bf16[80,2048]{1,0:T(8,128)(2,1)S(1)}, bf16[80,2048]{1,0:T(8,128)(2,1)S(1)}, u32[]{:S(2)}, u32[]{:S(2)}) collective-permute-start(bf16[80,2048]{1,0:T(8,128)(2,1)S(1)} %get-tuple-element.57), channel_id=1, source_target_pairs={{0,8},{8,0},{16,24},{24,16},{1,9},{9,1},{17,25},{25,17},{2,10},{10... | collective-permute-start | bytes 983048 | tf_op jit(solution)/shard_map/ppermute | solution.py:292
  105.0 16.5 %collective-permute-start.12 = (bf16[80,2048]{1,0:T(8,128)(2,1)S(1)}, bf16[80,2048]{1,0:T(8,128)(2,1)S(1)}, u32[]{:S(2)}, u32[]{:S(2)}) collective-permute-start(bf16[80,2048]{1,0:T(8,128)(2,1)S(1)} %get-tuple-element.58), channel_id=1, source_target_pairs={{0,16},{8,24},{16,0},{24,8},{1,17},{9,25},{17,1},{25,9},{2,18},{10... | collective-permute-start | bytes 983048 | tf_op jit(solution)/shard_map/ppermute | solution.py:292
  109.6 16.4 %collective-permute-start.42 = (bf16[80,2048]{1,0:T(8,128)(2,1)S(1)}, bf16[80,2048]{1,0:T(8,128)(2,1)S(1)}, u32[]{:S(2)}, u32[]{:S(2)}) collective-permute-start(bf16[80,2048]{1,0:T(8,128)(2,1)S(1)} %get-tuple-element.88), channel_id=1, source_target_pairs={{0,8},{8,0},{16,24},{24,16},{1,9},{9,1},{17,25},{25,17},{2,10},{10... | collective-permute-start | bytes 983048 | tf_op jit(solution)/shard_map/ppermute | solution.py:292
  113.0 17.7 %collective-permute-start.43 = (bf16[80,2048]{1,0:T(8,128)(2,1)S(1)}, bf16[80,2048]{1,0:T(8,128)(2,1)S(1)}, u32[]{:S(2)}, u32[]{:S(2)}) collective-permute-start(bf16[80,2048]{1,0:T(8,128)(2,1)S(1)} %get-tuple-element.89), channel_id=1, source_target_pairs={{0,16},{8,24},{16,0},{24,8},{1,17},{9,25},{17,1},{25,9},{2,18},{10... | collective-permute-start | bytes 983048 | tf_op jit(solution)/shard_map/ppermute | solution.py:292
  113.5 1.9 copy-start.2
  115.4 27.2 %copy-start.3 = (bf16[1,768,2048]{2,1,0:T(8,128)(2,1)S(1)}, bf16[1,768,2048]{2,1,0:T(8,128)(2,1)}, u32[]{:S(2)}) copy-start(bf16[1,768,2048]{2,1,0:T(8,128)(2,1)} %refs_6_.7) | copy-start | bytes 9437188
  119.1 15.0 %collective-permute-start.44 = (bf16[80,2048]{1,0:T(8,128)(2,1)S(1)}, bf16[80,2048]{1,0:T(8,128)(2,1)S(1)}, u32[]{:S(2)}, u32[]{:S(2)}) collective-permute-start(bf16[80,2048]{1,0:T(8,128)(2,1)S(1)} %get-tuple-element.90), channel_id=1, source_target_pairs={{0,24},{8,16},{16,8},{24,0},{1,25},{9,17},{17,9},{25,1},{2,26},{10... | collective-permute-start | bytes 983048 | tf_op jit(solution)/shard_map/ppermute | solution.py:292
  121.5 18.7 %collective-permute-start.35 = (bf16[80,2048]{1,0:T(8,128)(2,1)S(1)}, bf16[80,2048]{1,0:T(8,128)(2,1)S(1)}, u32[]{:S(2)}, u32[]{:S(2)}) collective-permute-start(bf16[80,2048]{1,0:T(8,128)(2,1)S(1)} %get-tuple-element.82), channel_id=1, source_target_pairs={{0,8},{8,0},{16,24},{24,16},{1,9},{9,1},{17,25},{25,17},{2,10},{10... | collective-permute-start | bytes 983048 | tf_op jit(solution)/shard_map/ppermute | solution.py:292
  126.1 19.8 %collective-permute-start.36 = (bf16[80,2048]{1,0:T(8,128)(2,1)S(1)}, bf16[80,2048]{1,0:T(8,128)(2,1)S(1)}, u32[]{:S(2)}, u32[]{:S(2)}) collective-permute-start(bf16[80,2048]{1,0:T(8,128)(2,1)S(1)} %get-tuple-element.83), channel_id=1, source_target_pairs={{0,16},{8,24},{16,0},{24,8},{1,17},{9,25},{17,1},{25,9},{2,18},{10... | collective-permute-start | bytes 983048 | tf_op jit(solution)/shard_map/ppermute | solution.py:292
  127.6 20.6 %collective-permute-start.37 = (bf16[80,2048]{1,0:T(8,128)(2,1)S(1)}, bf16[80,2048]{1,0:T(8,128)(2,1)S(1)}, u32[]{:S(2)}, u32[]{:S(2)}) collective-permute-start(bf16[80,2048]{1,0:T(8,128)(2,1)S(1)} %get-tuple-element.84), channel_id=1, source_target_pairs={{0,24},{8,16},{16,8},{24,0},{1,25},{9,17},{17,9},{25,1},{2,26},{10... | collective-permute-start | bytes 983048 | tf_op jit(solution)/shard_map/ppermute | solution.py:292
  130.6 23.6 %collective-permute-start.23 = (bf16[80,2048]{1,0:T(8,128)(2,1)S(1)}, bf16[80,2048]{1,0:T(8,128)(2,1)S(1)}, u32[]{:S(2)}, u32[]{:S(2)}) collective-permute-start(bf16[80,2048]{1,0:T(8,128)(2,1)S(1)} %get-tuple-element.68), channel_id=1, source_target_pairs={{0,8},{8,0},{16,24},{24,16},{1,9},{9,1},{17,25},{25,17},{2,10},{10... | collective-permute-start | bytes 983048 | tf_op jit(solution)/shard_map/ppermute | solution.py:292
  134.1 31.3 %collective-permute-start.24 = (bf16[80,2048]{1,0:T(8,128)(2,1)S(1)}, bf16[80,2048]{1,0:T(8,128)(2,1)S(1)}, u32[]{:S(2)}, u32[]{:S(2)}) collective-permute-start(bf16[80,2048]{1,0:T(8,128)(2,1)S(1)} %get-tuple-element.69), channel_id=1, source_target_pairs={{0,16},{8,24},{16,0},{24,8},{1,17},{9,25},{17,1},{25,9},{2,18},{10... | collective-permute-start | bytes 983048 | tf_op jit(solution)/shard_map/ppermute | solution.py:292
  140.2 28.2 %collective-permute-start.25 = (bf16[80,2048]{1,0:T(8,128)(2,1)S(1)}, bf16[80,2048]{1,0:T(8,128)(2,1)S(1)}, u32[]{:S(2)}, u32[]{:S(2)}) collective-permute-start(bf16[80,2048]{1,0:T(8,128)(2,1)S(1)} %get-tuple-element.70), channel_id=1, source_target_pairs={{0,24},{8,16},{16,8},{24,0},{1,25},{9,17},{17,9},{25,1},{2,26},{10... | collective-permute-start | bytes 983048 | tf_op jit(solution)/shard_map/ppermute | solution.py:292
  145.8 25.8 %collective-permute-start.13 = (bf16[80,2048]{1,0:T(8,128)(2,1)S(1)}, bf16[80,2048]{1,0:T(8,128)(2,1)S(1)}, u32[]{:S(2)}, u32[]{:S(2)}) collective-permute-start(bf16[80,2048]{1,0:T(8,128)(2,1)S(1)} %get-tuple-element.59), channel_id=1, source_target_pairs={{0,24},{8,16},{16,8},{24,0},{1,25},{9,17},{17,9},{25,1},{2,26},{10... | collective-permute-start | bytes 983048 | tf_op jit(solution)/shard_map/ppermute | solution.py:292
  148.2 27.2 %collective-permute-start.45 = (bf16[80,2048]{1,0:T(8,128)(2,1)S(1)}, bf16[80,2048]{1,0:T(8,128)(2,1)S(1)}, u32[]{:S(2)}, u32[]{:S(2)}) collective-permute-start(bf16[80,2048]{1,0:T(8,128)(2,1)S(1)} %get-tuple-element.92), channel_id=1, source_target_pairs={{0,8},{8,0},{16,24},{24,16},{1,9},{9,1},{17,25},{25,17},{2,10},{10... | collective-permute-start | bytes 983048 | tf_op jit(solution)/shard_map/ppermute | solution.py:292
  154.3 31.1 %collective-permute-start.38 = (bf16[128,2048]{1,0:T(8,128)(2,1)S(1)}, bf16[128,2048]{1,0:T(8,128)(2,1)S(1)}, u32[]{:S(2)}, u32[]{:S(2)}) collective-permute-start(bf16[128,2048]{1,0:T(8,128)(2,1)S(1)} %get-tuple-element.86), channel_id=1, source_target_pairs={{0,1},{1,0},{2,3},{3,2},{4,5},{5,4},{6,7},{7,6},{8,9},{9,8},{10,11... | collective-permute-start | bytes 1572872 | tf_op jit(solution)/shard_map/ppermute | solution.py:284
  165.4 16.6 %collective-permute-start.46 = (bf16[80,2048]{1,0:T(8,128)(2,1)S(1)}, bf16[80,2048]{1,0:T(8,128)(2,1)S(1)}, u32[]{:S(2)}, u32[]{:S(2)}) collective-permute-start(bf16[80,2048]{1,0:T(8,128)(2,1)S(1)} %get-tuple-element.93), channel_id=1, source_target_pairs={{0,16},{8,24},{16,0},{24,8},{1,17},{9,25},{17,1},{25,9},{2,18},{10... | collective-permute-start | bytes 983048 | tf_op jit(solution)/shard_map/ppermute | solution.py:292
  168.4 15.0 %collective-permute-start.47 = (bf16[80,2048]{1,0:T(8,128)(2,1)S(1)}, bf16[80,2048]{1,0:T(8,128)(2,1)S(1)}, u32[]{:S(2)}, u32[]{:S(2)}) collective-permute-start(bf16[80,2048]{1,0:T(8,128)(2,1)S(1)} %get-tuple-element.94), channel_id=1, source_target_pairs={{0,24},{8,16},{16,8},{24,0},{1,25},{9,17},{17,9},{25,1},{2,26},{10... | collective-permute-start | bytes 983048 | tf_op jit(solution)/shard_map/ppermute | solution.py:292
  171.6 17.8 %collective-permute-start.26 = (bf16[80,2048]{1,0:T(8,128)(2,1)S(1)}, bf16[80,2048]{1,0:T(8,128)(2,1)S(1)}, u32[]{:S(2)}, u32[]{:S(2)}) collective-permute-start(bf16[80,2048]{1,0:T(8,128)(2,1)S(1)} %get-tuple-element.72), channel_id=1, source_target_pairs={{0,8},{8,0},{16,24},{24,16},{1,9},{9,1},{17,25},{25,17},{2,10},{10... | collective-permute-start | bytes 983048 | tf_op jit(solution)/shard_map/ppermute | solution.py:292
  175.4 14.3 %collective-permute-start.27 = (bf16[80,2048]{1,0:T(8,128)(2,1)S(1)}, bf16[80,2048]{1,0:T(8,128)(2,1)S(1)}, u32[]{:S(2)}, u32[]{:S(2)}) collective-permute-start(bf16[80,2048]{1,0:T(8,128)(2,1)S(1)} %get-tuple-element.73), channel_id=1, source_target_pairs={{0,16},{8,24},{16,0},{24,8},{1,17},{9,25},{17,1},{25,9},{2,18},{10... | collective-permute-start | bytes 983048 | tf_op jit(solution)/shard_map/ppermute | solution.py:292
  182.0 27.4 %collective-permute-start.14 = (bf16[80,2048]{1,0:T(8,128)(2,1)S(1)}, bf16[80,2048]{1,0:T(8,128)(2,1)S(1)}, u32[]{:S(2)}, u32[]{:S(2)}) collective-permute-start(bf16[80,2048]{1,0:T(8,128)(2,1)S(1)} %get-tuple-element.61), channel_id=1, source_target_pairs={{0,8},{8,0},{16,24},{24,16},{1,9},{9,1},{17,25},{25,17},{2,10},{10... | collective-permute-start | bytes 983048 | tf_op jit(solution)/shard_map/ppermute | solution.py:292
  183.4 26.2 %collective-permute-start.15 = (bf16[80,2048]{1,0:T(8,128)(2,1)S(1)}, bf16[80,2048]{1,0:T(8,128)(2,1)S(1)}, u32[]{:S(2)}, u32[]{:S(2)}) collective-permute-start(bf16[80,2048]{1,0:T(8,128)(2,1)S(1)} %get-tuple-element.62), channel_id=1, source_target_pairs={{0,16},{8,24},{16,0},{24,8},{1,17},{9,25},{17,1},{25,9},{2,18},{10... | collective-permute-start | bytes 983048 | tf_op jit(solution)/shard_map/ppermute | solution.py:292
  185.4 24.2 %collective-permute-start.16 = (bf16[80,2048]{1,0:T(8,128)(2,1)S(1)}, bf16[80,2048]{1,0:T(8,128)(2,1)S(1)}, u32[]{:S(2)}, u32[]{:S(2)}) collective-permute-start(bf16[80,2048]{1,0:T(8,128)(2,1)S(1)} %get-tuple-element.63), channel_id=1, source_target_pairs={{0,24},{8,16},{16,8},{24,0},{1,25},{9,17},{17,9},{25,1},{2,26},{10... | collective-permute-start | bytes 983048 | tf_op jit(solution)/shard_map/ppermute | solution.py:292
  189.5 21.4 %collective-permute-start.48 = (bf16[128,2048]{1,0:T(8,128)(2,1)S(1)}, bf16[128,2048]{1,0:T(8,128)(2,1)S(1)}, u32[]{:S(2)}, u32[]{:S(2)}) collective-permute-start(bf16[128,2048]{1,0:T(8,128)(2,1)S(1)} %get-tuple-element.96), channel_id=1, source_target_pairs={{0,1},{1,0},{2,3},{3,2},{4,5},{5,4},{6,7},{7,6},{8,9},{9,8},{10,11... | collective-permute-start | bytes 1572872 | tf_op jit(solution)/shard_map/ppermute | solution.py:284
  189.6 19.0 %collective-permute-start.28 = (bf16[80,2048]{1,0:T(8,128)(2,1)S(1)}, bf16[80,2048]{1,0:T(8,128)(2,1)S(1)}, u32[]{:S(2)}, u32[]{:S(2)}) collective-permute-start(bf16[80,2048]{1,0:T(8,128)(2,1)S(1)} %get-tuple-element.74), channel_id=1, source_target_pairs={{0,24},{8,16},{16,8},{24,0},{1,25},{9,17},{17,9},{25,1},{2,26},{10... | collective-permute-start | bytes 983048 | tf_op jit(solution)/shard_map/ppermute | solution.py:292
  208.7 14.8 %collective-permute-start.39 = (bf16[128,2048]{1,0:T(8,128)(2,1)S(1)}, bf16[128,2048]{1,0:T(8,128)(2,1)S(1)}, u32[]{:S(2)}, u32[]{:S(2)}) collective-permute-start(bf16[128,2048]{1,0:T(8,128)(2,1)S(1)} %add_convert_fusion.3), channel_id=1, source_target_pairs={{0,2},{1,3},{2,0},{3,1},{4,6},{5,7},{6,4},{7,5},{8,10},{9,11},{10,... | collective-permute-start | bytes 1572872 | tf_op jit(solution)/shard_map/ppermute | solution.py:287
  208.7 33.9 %copy-start.14 = (bf16[128,2048]{1,0:T(8,128)(2,1)S(1)}, bf16[128,2048]{1,0:T(8,128)(2,1)}, u32[]{:S(2)}) copy-start(bf16[128,2048]{1,0:T(8,128)(2,1)} %copy-done.13) | copy-start | bytes 1572868
  209.5 14.0 %collective-permute-start.29 = (bf16[128,2048]{1,0:T(8,128)(2,1)S(1)}, bf16[128,2048]{1,0:T(8,128)(2,1)S(1)}, u32[]{:S(2)}, u32[]{:S(2)}) collective-permute-start(bf16[128,2048]{1,0:T(8,128)(2,1)S(1)} %get-tuple-element.76), channel_id=1, source_target_pairs={{0,1},{1,0},{2,3},{3,2},{4,5},{5,4},{6,7},{7,6},{8,9},{9,8},{10,11... | collective-permute-start | bytes 1572872 | tf_op jit(solution)/shard_map/ppermute | solution.py:284
  210.3 15.5 %collective-permute-start.17 = (bf16[128,2048]{1,0:T(8,128)(2,1)S(1)}, bf16[128,2048]{1,0:T(8,128)(2,1)S(1)}, u32[]{:S(2)}, u32[]{:S(2)}) collective-permute-start(bf16[128,2048]{1,0:T(8,128)(2,1)S(1)} %get-tuple-element.66), channel_id=1, source_target_pairs={{0,1},{1,0},{2,3},{3,2},{4,5},{5,4},{6,7},{7,6},{8,9},{9,8},{10,11... | collective-permute-start | bytes 1572872 | tf_op jit(solution)/shard_map/ppermute | solution.py:284
  211.0 23.2 %collective-permute-start.49 = (bf16[128,2048]{1,0:T(8,128)(2,1)S(1)}, bf16[128,2048]{1,0:T(8,128)(2,1)S(1)}, u32[]{:S(2)}, u32[]{:S(2)}) collective-permute-start(bf16[128,2048]{1,0:T(8,128)(2,1)S(1)} %add_convert_fusion.1), channel_id=1, source_target_pairs={{0,2},{1,3},{2,0},{3,1},{4,6},{5,7},{6,4},{7,5},{8,10},{9,11},{10,... | collective-permute-start | bytes 1572872 | tf_op jit(solution)/shard_map/ppermute | solution.py:287
  223.7 18.9 %collective-permute-start.40 = (bf16[128,2048]{1,0:T(8,128)(2,1)S(1)}, bf16[128,2048]{1,0:T(8,128)(2,1)S(1)}, u32[]{:S(2)}, u32[]{:S(2)}) collective-permute-start(bf16[128,2048]{1,0:T(8,128)(2,1)S(1)} %add_convert_fusion.2), channel_id=1, source_target_pairs={{0,6},{1,7},{2,4},{3,5},{4,2},{5,3},{6,0},{7,1},{8,14},{9,15},{10,... | collective-permute-start | bytes 1572872 | tf_op jit(solution)/shard_map/ppermute | solution.py:287
  (5 other events, 4.5 us)

commit v4 on v2

--- a/solution.py
+++ b/solution.py
@@ -19,7 +19,7 @@
     return lax.dot_general(a, b, (((ca,), (cb,)), ((), ())), preferred_element_type=F32)
 
 
-def call(body, outs, scratch=(), limit=24, away=()):
+def call(body, outs, scratch=(), limit=24, away=(), leave=False):
     def run(*args):
         specs = []
         placed = []
@@ -33,7 +33,10 @@
             body,
             in_specs=specs,
             out_specs=[pl.BlockSpec(memory_space=pltpu.VMEM)] * len(outs),
-            out_shape=[pltpu.VMEM(shape, dtype) for shape, dtype in outs],
+            out_shape=[
+                jax.ShapeDtypeStruct(shape, dtype) if leave else pltpu.VMEM(shape, dtype)
+                for shape, dtype in outs
+            ],
             scratch_shapes=list(scratch),
             compiler_params=pltpu.CompilerParams(vmem_limit_bytes=limit << 20),
         )(*placed)
@@ -149,12 +152,14 @@
     place = place_ref[0]
     group = group_ref[0]
     row = 0
-    for pack in packs:
-        for block in range(2):
-            for k in range(groups):
-                at = block * count + (group ^ k) * length + place
-                route_ref[row : row + 1, :] = pack[pl.ds(at, 1), :]
-                row += 1
+    for straight in range(2):
+        for pack in packs:
+            for side in range(2):
+                for k in range(groups):
+                    at = (group ^ k) * length
+                    at = at + ((place ^ side) if straight else side * count + place)
+                    route_ref[row : row + 1, :] = pack[pl.ds(at, 1), :]
+                    row += 1
     tokens = route_ref.shape[1]
     rows = lax.broadcasted_iota(jnp.int32, (tokens, tokens), 0)
     cols = lax.broadcasted_iota(jnp.int32, (tokens, tokens), 1)
@@ -212,14 +217,54 @@
     return call(body, [shape] * 2)(*backs, rank, weight)
 
 
-def expert_kernel(groups, *refs):
-    xs = refs[:groups]
-    gate_ref, up_ref, down_ref = refs[groups : groups + 3]
-    outs = refs[groups + 3 : 2 * groups + 3]
-    hidden_ref = refs[2 * groups + 3]
-    rows, features = xs[0].shape
+def straight_select_kernel(slots, base, own_ref, rank_ref, *outs):
+    rows = [slots_of(rank_ref, 1.0, base + i, slots) for i in range(len(outs))]
+    picked = dot(jnp.concatenate(rows, axis=0).astype(BF), own_ref[...]).astype(BF)
+    for i, out in enumerate(outs):
+        out[...] = picked[i * slots : (i + 1) * slots]
+
+
+def straight_select(slots, count, base, own, rank):
+    body = functools.partial(straight_select_kernel, slots, base)
+    shape = ((slots, own.shape[1]), BF)
+    return call(body, [shape] * count)(own, rank)
+
+
+def straight_combine_kernel(slots, count, base, *refs):
+    backs = refs[:count]
+    rank_ref, weight_ref = refs[count : count + 2]
+    more = refs[count + 2 : -1]
+    rows = stacked(backs)
+    parts = []
+    for i in range(count):
+        row = base + i
+        parts.append(slots_of(rank_ref, weight_ref[row : row + 1, :], row, slots))
+    total = dot(jnp.concatenate(parts, axis=0).astype(BF), rows, 0, 0)
+    for ref in more:
+        total = total + ref[...].astype(F32)
+    refs[-1][...] = total.astype(BF)
+
+
+def straight_combine(slots, base, backs, rank, weight, more, leave):
+    body = functools.partial(straight_combine_kernel, slots, len(backs), base)
+    shape = ((rank.shape[1], backs[0].shape[1]), BF)
+    return call(body, [shape], leave=leave)(*backs, rank, weight, *more)[0]
+
+
+def stacked(refs):
+    if refs[0].shape[0] % 16 == 0:
+        return jnp.concatenate([r[...] for r in refs], axis=0)
+    return jnp.concatenate([r[...].astype(F32) for r in refs], axis=0).astype(BF)
+
+
+def expert_kernel(count, starts, *refs):
+    xs = refs[:count]
+    gate_ref, up_ref, down_ref = refs[count : count + 3]
+    outs = refs[count + 3 : -1]
+    hidden_ref = refs[-1]
+    features = xs[0].shape[1]
     units = gate_ref.shape[2]
-    x = jnp.concatenate([r[...] for r in xs], axis=0)
+    x = stacked(xs)
     width = 256
     for j in range(units // width):
         at = slice(j * width, (j + 1) * width)
@@ -230,17 +275,28 @@
     width = 512
     for j in range(features // width):
         at = slice(j * width, (j + 1) * width)
-        out = dot(hidden, down_ref[0, :, at]).astype(BF)
-        for k in range(groups):
-            outs[k][:, at] = out[k * rows : (k + 1) * rows]
-
-
-def experts(xs, gate, up, down):
-    groups = len(xs)
-    body = functools.partial(expert_kernel, groups)
-    scratch = [pltpu.VMEM((groups * xs[0].shape[0], gate.shape[2]), BF)]
-    outs = [(xs[0].shape, BF)] * groups
-    return call(body, outs, scratch)(*xs, gate, up, down)
+        out = dot(hidden, down_ref[0, :, at])
+        for ref, start in zip(outs, starts):
+            ref[:, at] = out[start : start + ref.shape[0]].astype(BF)
+
+
+def experts(xs, straight_in, straight_out, groups, gate, up, down):
+    total = sum(x.shape[0] for x in xs)
+    features = xs[0].shape[1]
+    slots = total // (2 * groups)
+    if straight_out:
+        count, rows = 2 * groups, slots
+        starts = [
+            (side * groups + k if straight_in else 2 * k + side) * slots
+            for side in range(2)
+            for k in range(groups)
+        ]
+    else:
+        count, rows = groups, 2 * slots
+        starts = [k * rows for k in range(groups)]
+    body = functools.partial(expert_kernel, len(xs), starts)
+    scratch = [pltpu.VMEM((total, gate.shape[2]), BF)]
+    return call(body, [((rows, features), BF)] * count, scratch)(*xs, gate, up, down)
 
 
 def on_device(
@@ -282,6 +338,20 @@
             return x
         return lax.ppermute(x, "grp", [(g, g ^ m) for g in range(groups)])
 
+    def straight(parts):
+        moved = []
+        for i, x in enumerate(parts):
+            side, k = divmod(i, groups)
+            if i:
+                pairs = [
+                    (g * length + s, (g ^ k) * length + (s ^ side))
+                    for g in range(groups)
+                    for s in range(length)
+                ]
+                x = lax.ppermute(x, ("grp", "seq"), pairs)
+            moved.append(x)
+        return moved
+
     def later(x, m, froms):
         pairs = [(2 * z + c, 2 * (z + m) + c) for z in froms for c in range(2)]
         return lax.ppermute(x, "seq", pairs)
@@ -324,7 +394,7 @@
         + [pltpu.SemaphoreType.DMA((3, 4)), pltpu.SemaphoreType.DMA],
         away=(0, 1, 2, 3),
     )(queries, keys, values, out_proj, *scalars)
-    shape = (stages * 2 * groups, tokens)
+    shape = (2 * stages * 2 * groups, tokens)
     body = functools.partial(rank_kernel, groups, length)
     routes, ranks = call(body, [(shape, F32)] * 2)(
         *scalars[1:], *packs
@@ -350,29 +420,48 @@
     returning = homing(stages)
     blocks = {0: moe_in}
     outs = {}
-    partners = {0: swap(moe_in)}
     for m in range(1, stages):
         source, shift = routing[m]
         blocks[m] = along(blocks[source], shift)
     for m in range(stages):
         base = m * 2 * groups
-        partner = swap(blocks[m]) if m else partners[0]
-        picked = select(slots, groups, base, blocks[m], partner, ranks)
-        taken = [across(picked[k], k) for k in range(groups)]
-        outs[m] = experts(taken, gate_weight, up_weight, down_weight)
+        near = m in STRAIGHT_OUT
+        partner = None if near else swap(blocks[m])
+        if near:
+            base += stages * 2 * groups
+            picked = straight_select(slots, 2 * groups, base, blocks[m], ranks)
+        else:
+            picked = select(slots, groups, base, blocks[m], partner, ranks)
+        if near:
+            taken = straight(picked)
+        else:
+            taken = [across(picked[k], k) for k in range(groups)]
+        outs[m] = experts(
+            taken, near, m in STRAIGHT_BACK, groups, gate_weight, up_weight, down_weight
+        )
     sums = {m: [] for m in range(stages)}
+    sums[0].append(residual)
     for m in back_order(stages):
         base = m * 2 * groups
-        backs = [across(outs[m][k], k) for k in range(groups)]
-        own, par = combine(slots, base, backs, ranks, routes)
-        part = own.astype(F32) + swap(par).astype(F32)
-        for more in sums[m]:
-            part = part + more.astype(F32)
+        if m in STRAIGHT_BACK:
+            base += stages * 2 * groups
+            backs = straight(outs[m])
+            part = straight_combine(slots, base, backs, ranks, routes, sums[m], m == 0)
+        else:
+            backs = [across(outs[m][k], k) for k in range(groups)]
+            own, par = combine(slots, base, backs, ranks, routes)
+            part = own.astype(F32) + swap(par).astype(F32)
+            for more in sums[m]:
+                part = part + more.astype(F32)
+            part = part.astype(BF)
         if m:
             into, shift = returning[m]
-            sums[into].append(along(part.astype(BF), shift))
-    combined = residual.astype(F32) + part
-    return combined.astype(BF).reshape(1, tokens, features)
+            sums[into].append(along(part, shift))
+    return part.reshape(1, tokens, features)
+
+
+STRAIGHT_OUT = (0, 1)
+STRAIGHT_BACK = (0, 1)
 
 
 def sending(stages):

time: 233 us -> 238 us (1.021)
  waiting for transfers between devices: 126 us -> 133 us
  local copies, waits for them, and re-layouts: 4.64 us -> 8.13 us
  starting transfers between devices: 68.7 us -> 66.3 us
    ppermute x0 -> x28, waiting for transfers between devices: none -> 40.4 us  [straight(): x = lax.ppermute(x, ('grp', 'seq'), pairs)]
    ppermute x0 -> x28, starting transfers between devices: none -> 26.1 us  [straight(): x = lax.ppermute(x, ('grp', 'seq'), pairs)]
    ppermute x9, waiting for transfers between devices: 57.9 us -> 35.4 us  [along(): return lax.ppermute(x, 'seq', [(s, s ^ 2 * m) for s in range(length)])]
    ppermute x24 -> x12, starting transfers between devices: 34.2 us -> 14.3 us  [across(): return lax.ppermute(x, 'grp', [(g, g ^ m) for g in range(groups)])]
    ppermute x24 -> x12, waiting for transfers between devices: 58.8 us -> 48.4 us  [across(): return lax.ppermute(x, 'grp', [(g, g ^ m) for g in range(groups)])]
    ppermute x9, starting transfers between devices: 22.6 us -> 14 us  [along(): return lax.ppermute(x, 'seq', [(s, s ^ 2 * m) for s in range(length)])]
    unnamed x24 -> x36, local copies, waits for them, and re-layouts: 4.64 us -> 8.13 us
  transfers between devices with their start and end apart: 47 -> 59, of which waited for: 23 -> 31; matrix products, arithmetic and copies ran while one was open for 0% -> 0% of each run, Pallas kernels for 11% -> 10%
where the time goes in v4:
time: 238 us; the launch traced here: 237 us
  waiting for transfers between devices  133 us (56%)
  starting transfers between devices  66.3 us (28%)
  Pallas kernels  28.8 us (12%)
  local copies, waits for them, and re-layouts  8.13 us (3%)
    ppermute x12, waiting for transfers between devices, across(): return lax.ppermute(x, 'grp', [(g, g ^ m) for g in range(groups)])  48.4 us
    ppermute x28, waiting for transfers between devices, straight(): x = lax.ppermute(x, ('grp', 'seq'), pairs)  40.4 us
    ppermute x9, waiting for transfers between devices, along(): return lax.ppermute(x, 'seq', [(s, s ^ 2 * m) for s in range(length)])  35.4 us
    pallas_call x19, Pallas kernels, run(): pl.pallas_call(body, in_specs=specs, out_specs=[pl.BlockSpec(memory_space...  28.8 us
    ppermute x28, starting transfers between devices, straight(): x = lax.ppermute(x, ('grp', 'seq'), pairs)  26.1 us
    ppermute x12, starting transfers between devices, across(): return lax.ppermute(x, 'grp', [(g, g ^ m) for g in range(groups)])  14.3 us
    ppermute x9, starting transfers between devices, along(): return lax.ppermute(x, 'seq', [(s, s ^ 2 * m) for s in range(length)])  14 us
    ppermute x3, starting transfers between devices, later(): return lax.ppermute(x, 'seq', pairs)  10 us
  transfers between devices with their start and end apart: 59, of which 31 were waited for; matrix products, arithmetic and copies ran while one was open for 0% of the time, Pallas kernels for 10%

profile of v4, /device:TPU:0, one launch (start us, length us, event | category | flops | bytes accessed | tf_op | source)
XLA Modules:
  0.0 237.3 jit_solution(8159238694437016986)
XLA Ops:
  0.0 1.9 shard_map.119
  2.5 1.5 collective-permute-done.pair_ref
  4.1 4.9 %collective-permute-start.1 = (bf16[1024,128]{1,0:T(8,128)(2,1)S(1)}, bf16[1024,128]{1,0:T(8,128)(2,1)S(1)}, u32[]{:S(2)}, u32[]{:S(2)}) collective-permute-start(bf16[1024,128]{1,0:T(8,128)(2,1)S(1)} %add_convert_fusion.2.refs_0_), channel_id=1, source_target_pairs={{0,2},{1,3},{2,4},{3,5},{4,6},{5,7},{8,10},{9,11},{10,12},{11,13},... | collective-permute-start | bytes 786440 | tf_op jit(solution)/shard_map/ppermute | solution.py:357
  9.0 4.5 %collective-permute-start.2 = (bf16[1024,128]{1,0:T(8,128)(2,1)S(1)}, bf16[1024,128]{1,0:T(8,128)(2,1)S(1)}, u32[]{:S(2)}, u32[]{:S(2)}) collective-permute-start(bf16[1024,128]{1,0:T(8,128)(2,1)S(1)} %add_convert_fusion.2.refs_0_), channel_id=1, source_target_pairs={{0,4},{1,5},{8,12},{9,13},{16,20},{17,21},{24,28},{25,29}} | collective-permute-start | bytes 786440 | tf_op jit(solution)/shard_map/ppermute | solution.py:357
  13.5 2.2 collective-permute-done.1.refs_1_.refs_0_
  16.4 4.1 %collective-permute-done.2.refs_1_ = bf16[1024,128]{1,0:T(8,128)(2,1)S(1)} collective-permute-done((bf16[1024,128]{1,0:T(8,128)(2,1)S(1)}, bf16[1024,128]{1,0:T(8,128)(2,1)S(1)}, u32[]{:S(2)}, u32[]{:S(2)}) %collective-permute-start.2) | collective-permute-done | bytes 262176 | tf_op jit(solution)/shard_map/ppermute | solution.py:357
  20.7 4.2 %shard_map.118 = (f32[128,2048]{1,0:T(8,128)S(1)}, bf16[2048,2048]{1,0:T(8,128)(2,1)S(1)}) custom-call(bf16[128,2048]{1,0:T(8,128)(2,1)} %bitcast.19, bf16[128,2048]{1,0:T(8,128)(2,1)} %bitcast.25, bf16[128,2048]{1,0:T(8,128)(2,1)} %bitcast.27, bf16[2048,2048]{1,0:T(8,128)(2,1)} %w_hbm.1, s32[1]{0:T(128)} %bitcast.core_ref, s32[1]{0:T(128)} %bitcast.4.group_ref, ...), custom_call_target="tpu_custom_call" | custom-call | tf_op jit(solution)/shard_map/pallas_call | solution.py:32
  27.6 2.0 shard_map.122
  31.3 4.2 %collective-permute-start.23 = (bf16[128,2048]{1,0:T(8,128)(2,1)S(1)}, bf16[128,2048]{1,0:T(8,128)(2,1)}, u32[]{:S(2)}, u32[]{:S(2)}) collective-permute-start(bf16[128,2048]{1,0:T(8,128)(2,1)S(1)} %get-tuple-element.65.own_ref), channel_id=1, source_target_pairs={{0,4},{1,5},{2,6},{3,7},{4,0},{5,1},{6,2},{7,3},{8,12},{9,13},{10,... | collective-permute-start | bytes 1572872 | tf_op jit(solution)/shard_map/ppermute | solution.py:334
  35.5 23.9 %collective-permute-done.23.own_ref = bf16[128,2048]{1,0:T(8,128)(2,1)} collective-permute-done((bf16[128,2048]{1,0:T(8,128)(2,1)S(1)}, bf16[128,2048]{1,0:T(8,128)(2,1)}, u32[]{:S(2)}, u32[]{:S(2)}) %collective-permute-start.23) | collective-permute-done | bytes 524320 | tf_op jit(solution)/shard_map/ppermute | solution.py:334
  60.5 1.2 collective-permute-done.5.par_ref
  61.7 1.1 collective-permute-start.6
  62.8 3.0 %collective-permute-start.7 = (f32[64,128]{1,0:T(8,128)S(1)}, f32[64,128]{1,0:T(8,128)S(1)}, u32[]{:S(2)}, u32[]{:S(2)}) collective-permute-start(f32[64,128]{1,0:T(8,128)S(1)} %shard_map.123.refs_0_), channel_id=1, source_target_pairs={{0,4},{1,5},{2,6},{3,7},{4,0},{5,1},{6,2},{7,3},{8,12},{9,13},{10,... | collective-permute-start | bytes 98312 | tf_op jit(solution)/shard_map/ppermute | solution.py:334
  66.4 9.0 %collective-permute-done.6.refs_1_ = f32[64,128]{1,0:T(8,128)S(1)} collective-permute-done((f32[64,128]{1,0:T(8,128)S(1)}, f32[64,128]{1,0:T(8,128)S(1)}, u32[]{:S(2)}, u32[]{:S(2)}) %collective-permute-start.6) | collective-permute-done | bytes 32800 | tf_op jit(solution)/shard_map/ppermute | solution.py:334
  75.4 2.5 %collective-permute-done.8.refs_3_ = f32[64,128]{1,0:T(8,128)S(1)} collective-permute-done((f32[64,128]{1,0:T(8,128)S(1)}, f32[64,128]{1,0:T(8,128)S(1)}, u32[]{:S(2)}, u32[]{:S(2)}) %collective-permute-start.8) | collective-permute-done | bytes 32800 | tf_op jit(solution)/shard_map/ppermute | solution.py:334
  78.0 1.7 shard_map.130
  79.7 1.6 collective-permute-start.34
  81.3 1.5 collective-permute-start.35
  83.3 7.1 %collective-permute-done.34.refs_1_ = bf16[80,2048]{1,0:T(8,128)(2,1)S(1)} collective-permute-done((bf16[80,2048]{1,0:T(8,128)(2,1)S(1)}, bf16[80,2048]{1,0:T(8,128)(2,1)S(1)}, u32[]{:S(2)}, u32[]{:S(2)}) %collective-permute-start.34) | collective-permute-done | bytes 327712 | tf_op jit(solution)/shard_map/ppermute | solution.py:339
  90.4 7.1 %collective-permute-done.35.refs_2_ = bf16[80,2048]{1,0:T(8,128)(2,1)S(1)} collective-permute-done((bf16[80,2048]{1,0:T(8,128)(2,1)S(1)}, bf16[80,2048]{1,0:T(8,128)(2,1)S(1)}, u32[]{:S(2)}, u32[]{:S(2)}) %collective-permute-start.35) | collective-permute-done | bytes 327712 | tf_op jit(solution)/shard_map/ppermute | solution.py:339
  97.5 1.9 copy-done.1
  99.4 1.9 copy-done.3
  101.3 3.2 %shard_map.131 = (bf16[80,2048]{1,0:T(8,128)(2,1)S(1)}, bf16[80,2048]{1,0:T(8,128)(2,1)S(1)}, bf16[80,2048]{1,0:T(8,128)(2,1)S(1)}, bf16[80,2048]{1,0:T(8,128)(2,1)S(1)}) custom-call(bf16[80,2048]{1,0:T(8,128)(2,1)S(1)} %get-tuple-element.95.refs_0_, bf16[80,2048]{1,0:T(8,128)(2,1)S(1)} %collective-permute-done.34.refs_1_, ...), custom_call_target="tpu_custom_call" | custom-call | tf_op jit(solution)/shard_map/pallas_call | solution.py:32
  104.5 1.3 collective-permute-start.37
  106.7 1.4 collective-permute-start.39
  108.1 1.5 shard_map.127
  109.6 1.3 collective-permute-start.26
  111.8 3.4 %collective-permute-done.37.refs_1_ = bf16[80,2048]{1,0:T(8,128)(2,1)S(1)} collective-permute-done((bf16[80,2048]{1,0:T(8,128)(2,1)S(1)}, bf16[80,2048]{1,0:T(8,128)(2,1)S(1)}, u32[]{:S(2)}, u32[]{:S(2)}) %collective-permute-start.37) | collective-permute-done | bytes 327712 | tf_op jit(solution)/shard_map/ppermute | solution.py:339
  115.2 1.5 collective-permute-start.28
  116.7 6.8 %collective-permute-done.38.refs_2_ = bf16[80,2048]{1,0:T(8,128)(2,1)S(1)} collective-permute-done((bf16[80,2048]{1,0:T(8,128)(2,1)S(1)}, bf16[80,2048]{1,0:T(8,128)(2,1)S(1)}, u32[]{:S(2)}, u32[]{:S(2)}) %collective-permute-start.38) | collective-permute-done | bytes 327712 | tf_op jit(solution)/shard_map/ppermute | solution.py:339
  124.3 5.0 %collective-permute-done.26.refs_1_ = bf16[80,2048]{1,0:T(8,128)(2,1)S(1)} collective-permute-done((bf16[80,2048]{1,0:T(8,128)(2,1)S(1)}, bf16[80,2048]{1,0:T(8,128)(2,1)S(1)}, u32[]{:S(2)}, u32[]{:S(2)}) %collective-permute-start.26) | collective-permute-done | bytes 327712 | tf_op jit(solution)/shard_map/ppermute | solution.py:339
  129.3 6.0 %collective-permute-done.27.refs_2_ = bf16[80,2048]{1,0:T(8,128)(2,1)S(1)} collective-permute-done((bf16[80,2048]{1,0:T(8,128)(2,1)S(1)}, bf16[80,2048]{1,0:T(8,128)(2,1)S(1)}, u32[]{:S(2)}, u32[]{:S(2)}) %collective-permute-start.27) | collective-permute-done | bytes 327712 | tf_op jit(solution)/shard_map/ppermute | solution.py:339
  135.3 3.2 %shard_map.128 = (bf16[80,2048]{1,0:T(8,128)(2,1)S(1)}, bf16[80,2048]{1,0:T(8,128)(2,1)S(1)}, bf16[80,2048]{1,0:T(8,128)(2,1)S(1)}, bf16[80,2048]{1,0:T(8,128)(2,1)S(1)}) custom-call(bf16[80,2048]{1,0:T(8,128)(2,1)S(1)} %get-tuple-element.85.refs_0_, bf16[80,2048]{1,0:T(8,128)(2,1)S(1)} %collective-permute-done.26.refs_1_, ...), custom_call_target="tpu_custom_call" | custom-call | tf_op jit(solution)/shard_map/pallas_call | solution.py:32
  139.1 1.2 collective-permute-start.30
  140.3 1.7 collective-permute-start.31
  143.2 6.0 %collective-permute-done.29.refs_1_ = bf16[80,2048]{1,0:T(8,128)(2,1)S(1)} collective-permute-done((bf16[80,2048]{1,0:T(8,128)(2,1)S(1)}, bf16[80,2048]{1,0:T(8,128)(2,1)S(1)}, u32[]{:S(2)}, u32[]{:S(2)}) %collective-permute-start.29) | collective-permute-done | bytes 327712 | tf_op jit(solution)/shard_map/ppermute | solution.py:339
  149.7 7.0 %collective-permute-done.30.refs_2_ = bf16[80,2048]{1,0:T(8,128)(2,1)S(1)} collective-permute-done((bf16[80,2048]{1,0:T(8,128)(2,1)S(1)}, bf16[80,2048]{1,0:T(8,128)(2,1)S(1)}, u32[]{:S(2)}, u32[]{:S(2)}) %collective-permute-start.30) | collective-permute-done | bytes 327712 | tf_op jit(solution)/shard_map/ppermute | solution.py:339
  156.7 1.5 collective-permute-start.46
  159.0 1.8 collective-permute-start.48
  160.8 2.8 %collective-permute-done.46.refs_3_ = bf16[40,2048]{1,0:T(8,128)(2,1)S(1)} collective-permute-done((bf16[40,2048]{1,0:T(8,128)(2,1)S(1)}, bf16[40,2048]{1,0:T(8,128)(2,1)S(1)}, u32[]{:S(2)}, u32[]{:S(2)}) %collective-permute-start.46) | collective-permute-done | bytes 163872 | tf_op jit(solution)/shard_map/ppermute | solution.py:351
  165.5 5.0 %collective-permute-done.49.refs_6_ = bf16[40,2048]{1,0:T(8,128)(2,1)S(1)} collective-permute-done((bf16[40,2048]{1,0:T(8,128)(2,1)S(1)}, bf16[40,2048]{1,0:T(8,128)(2,1)S(1)}, u32[]{:S(2)}, u32[]{:S(2)}) %collective-permute-start.49) | collective-permute-done | bytes 163872 | tf_op jit(solution)/shard_map/ppermute | solution.py:351
  170.6 3.2 %shard_map.134 = (bf16[40,2048]{1,0:T(8,128)(2,1)S(1)}, bf16[40,2048]{1,0:T(8,128)(2,1)S(1)}, bf16[40,2048]{1,0:T(8,128)(2,1)S(1)}, bf16[40,2048]{1,0:T(8,128)(2...) custom-call(bf16[40,2048]{1,0:T(8,128)(2,1)S(1)} %get-tuple-element., ...), custom_call_target="tpu_custom_call" | custom-call | tf_op jit(solution)/shard_map/pallas_call | solution.py:32
  174.1 1.3 collective-permute-start.52
  175.4 1.9 collective-permute-start.53
  177.4 3.6 %collective-permute-done.51.refs_1_ = bf16[40,2048]{1,0:T(8,128)(2,1)S(1)} collective-permute-done((bf16[40,2048]{1,0:T(8,128)(2,1)S(1)}, bf16[40,2048]{1,0:T(8,128)(2,1)S(1)}, u32[]{:S(2)}, u32[]{:S(2)}) %collective-permute-start.51) | collective-permute-done | bytes 163872 | tf_op jit(solution)/shard_map/ppermute | solution.py:351
  181.6 2.8 %collective-permute-done.53.refs_3_ = bf16[40,2048]{1,0:T(8,128)(2,1)S(1)} collective-permute-done((bf16[40,2048]{1,0:T(8,128)(2,1)S(1)}, bf16[40,2048]{1,0:T(8,128)(2,1)S(1)}, u32[]{:S(2)}, u32[]{:S(2)}) %collective-permute-start.53) | collective-permute-done | bytes 163872 | tf_op jit(solution)/shard_map/ppermute | solution.py:351
  184.4 2.0 collective-permute-start.56
  187.2 1.2 collective-permute-start.10
  188.5 5.6 %collective-permute-done.56.refs_6_ = bf16[40,2048]{1,0:T(8,128)(2,1)S(1)} collective-permute-done((bf16[40,2048]{1,0:T(8,128)(2,1)S(1)}, bf16[40,2048]{1,0:T(8,128)(2,1)S(1)}, u32[]{:S(2)}, u32[]{:S(2)}) %collective-permute-start.56) | collective-permute-done | bytes 163872 | tf_op jit(solution)/shard_map/ppermute | solution.py:351
  194.1 2.0 collective-permute-start.11
  196.6 1.6 collective-permute-done.10.refs_2_
  198.2 3.3 %collective-permute-done.11.refs_3_ = bf16[40,2048]{1,0:T(8,128)(2,1)S(1)} collective-permute-done((bf16[40,2048]{1,0:T(8,128)(2,1)S(1)}, bf16[40,2048]{1,0:T(8,128)(2,1)S(1)}, u32[]{:S(2)}, u32[]{:S(2)}) %collective-permute-start.11) | collective-permute-done | bytes 163872 | tf_op jit(solution)/shard_map/ppermute | solution.py:351
  201.5 1.6 collective-permute-start.14
  205.4 4.0 %collective-permute-start.42 = (bf16[128,2048]{1,0:T(8,128)(2,1)S(1)}, bf16[128,2048]{1,0:T(8,128)(2,1)S(1)}, u32[]{:S(2)}, u32[]{:S(2)}) collective-permute-start(bf16[128,2048]{1,0:T(8,128)(2,1)S(1)} %add_convert_fusion), channel_id=1, source_target_pairs={{0,6},{1,7},{2,4},{3,5},{4,2},{5,3},{6,0},{7,1},{8,14},{9,15},{10,... | collective-permute-start | bytes 1572872 | tf_op jit(solution)/shard_map/ppermute | solution.py:334
  209.5 1.4 collective-permute-done.14.refs_6_
  210.9 2.0 collective-permute-done.9.refs_1_
  212.9 3.2 %shard_map.126 = (bf16[40,2048]{1,0:T(8,128)(2,1)S(1)}, bf16[40,2048]{1,0:T(8,128)(2,1)S(1)}, bf16[40,2048]{1,0:T(8,128)(2,1)S(1)}, bf16[40,2048]{1,0:T(8,128)(2...) custom-call(bf16[40,2048]{1,0:T(8,128)(2,1)S(1)} %get-tuple-element., ...), custom_call_target="tpu_custom_call" | custom-call | tf_op jit(solution)/shard_map/pallas_call | solution.py:32
  218.0 1.7 collective-permute-start.18
  219.7 3.6 %collective-permute-done.16.refs_1_ = bf16[40,2048]{1,0:T(8,128)(2,1)S(1)} collective-permute-done((bf16[40,2048]{1,0:T(8,128)(2,1)S(1)}, bf16[40,2048]{1,0:T(8,128)(2,1)S(1)}, u32[]{:S(2)}, u32[]{:S(2)}) %collective-permute-start.16) | collective-permute-done | bytes 163872 | tf_op jit(solution)/shard_map/ppermute | solution.py:351
  224.2 2.8 %collective-permute-start.20 = (bf16[40,2048]{1,0:T(8,128)(2,1)S(1)}, bf16[40,2048]{1,0:T(8,128)(2,1)S(1)}, u32[]{:S(2)}, u32[]{:S(2)}) collective-permute-start(bf16[40,2048]{1,0:T(8,128)(2,1)S(1)} %get-tuple-element.80), channel_id=1, source_target_pairs={{0,9},{1,8},{2,11},{3,10},{4,13},{5,12},{6,15},{7,14},{8,1},{9,0},... | collective-permute-start | bytes 491528 | tf_op jit(solution)/shard_map/ppermute | solution.py:351
  227.0 1.5 collective-permute-start.21
  229.2 1.9 collective-permute-done.20.refs_5_
  231.1 4.5 %collective-permute-done.21.refs_6_ = bf16[40,2048]{1,0:T(8,128)(2,1)S(1)} collective-permute-done((bf16[40,2048]{1,0:T(8,128)(2,1)S(1)}, bf16[40,2048]{1,0:T(8,128)(2,1)S(1)}, u32[]{:S(2)}, u32[]{:S(2)}) %collective-permute-start.21) | collective-permute-done | bytes 163872 | tf_op jit(solution)/shard_map/ppermute | solution.py:351
  235.9 1.3 shard_map.136
  (115 shorter events, 24.0 us)
Async XLA Ops:
  1.9 2.1 collective-permute-start
  4.1 11.5 %collective-permute-start.1 = (bf16[1024,128]{1,0:T(8,128)(2,1)S(1)}, bf16[1024,128]{1,0:T(8,128)(2,1)S(1)}, u32[]{:S(2)}, u32[]{:S(2)}) collective-permute-start(bf16[1024,128]{1,0:T(8,128)(2,1)S(1)} %add_convert_fusion.2.refs_0_), channel_id=1, source_target_pairs={{0,2},{1,3},{2,4},{3,5},{4,6},{5,7},{8,10},{9,11},{10,12},{11,13},... | collective-permute-start | bytes 786440 | tf_op jit(solution)/shard_map/ppermute | solution.py:357
  9.0 11.5 %collective-permute-start.2 = (bf16[1024,128]{1,0:T(8,128)(2,1)S(1)}, bf16[1024,128]{1,0:T(8,128)(2,1)S(1)}, u32[]{:S(2)}, u32[]{:S(2)}) collective-permute-start(bf16[1024,128]{1,0:T(8,128)(2,1)S(1)} %add_convert_fusion.2.refs_0_), channel_id=1, source_target_pairs={{0,4},{1,5},{8,12},{9,13},{16,20},{17,21},{24,28},{25,29}} | collective-permute-start | bytes 786440 | tf_op jit(solution)/shard_map/ppermute | solution.py:357
  15.7 4.8 %collective-permute-start.3 = (bf16[1024,128]{1,0:T(8,128)(2,1)S(1)}, bf16[1024,128]{1,0:T(8,128)(2,1)S(1)}, u32[]{:S(2)}, u32[]{:S(2)}) collective-permute-start(bf16[1024,128]{1,0:T(8,128)(2,1)S(1)} %shard_map.120), channel_id=1, source_target_pairs={{2,6},{3,7},{10,14},{11,15},{18,22},{19,23},{26,30},{27,31}} | collective-permute-start | bytes 786440 | tf_op jit(solution)/shard_map/ppermute | solution.py:357
  20.6 4.4 %collective-permute-start.4 = (bf16[1024,128]{1,0:T(8,128)(2,1)S(1)}, bf16[1024,128]{1,0:T(8,128)(2,1)S(1)}, u32[]{:S(2)}, u32[]{:S(2)}) collective-permute-start(bf16[1024,128]{1,0:T(8,128)(2,1)S(1)} %shard_map.121.mine_ref), channel_id=1, source_target_pairs={{0,1},{1,0},{2,3},{3,2},{4,5},{5,4},{6,7},{7,6},{8,9},{9,8},{10,11... | collective-permute-start | bytes 786440 | tf_op jit(solution)/shard_map/ppermute | solution.py:331
  27.6 32.5 %copy-start.16 = (f32[1,128,8]{1,2,0:T(8,128)S(1)}, f32[1,128,8]{1,2,0:T(8,128)}, u32[]{:S(2)}) copy-start(f32[1,128,8]{1,2,0:T(8,128)} %param.20) | copy-start | bytes 12292
  27.6 32.5 %copy-start.17 = (s32[1,128,8]{1,2,0:T(8,128)S(1)}, s32[1,128,8]{1,2,0:T(8,128)}, u32[]{:S(2)}) copy-start(s32[1,128,8]{1,2,0:T(8,128)} %param.19) | copy-start | bytes 12292
  27.6 69.9 %copy-start = (bf16[1,2048,768]{2,1,0:T(8,128)(2,1)S(1)}, bf16[1,2048,768]{2,1,0:T(8,128)(2,1)}, u32[]{:S(2)}) copy-start(bf16[1,2048,768]{2,1,0:T(8,128)(2,1)} %refs_8_.3) | copy-start | bytes 9437188
  31.3 28.1 %collective-permute-start.23 = (bf16[128,2048]{1,0:T(8,128)(2,1)S(1)}, bf16[128,2048]{1,0:T(8,128)(2,1)}, u32[]{:S(2)}, u32[]{:S(2)}) collective-permute-start(bf16[128,2048]{1,0:T(8,128)(2,1)S(1)} %get-tuple-element.65.own_ref), channel_id=1, source_target_pairs={{0,4},{1,5},{2,6},{3,7},{4,0},{5,1},{6,2},{7,3},{8,12},{9,13},{10,... | collective-permute-start | bytes 1572872 | tf_op jit(solution)/shard_map/ppermute | solution.py:334
  59.4 18.6 %collective-permute-start.33 = (bf16[128,2048]{1,0:T(8,128)(2,1)}, bf16[128,2048]{1,0:T(8,128)(2,1)}, u32[]{:S(2)}, u32[]{:S(2)}) collective-permute-start(bf16[128,2048]{1,0:T(8,128)(2,1)} %collective-permute-done.23.own_ref), channel_id=1, source_target_pairs={{0,1},{1,0},{2,3},{3,2},{4,5},{5,4},{6,7},{7,6},{8,9},{9,8},{10,11... | collective-permute-start | bytes 1572872 | tf_op jit(solution)/shard_map/ppermute | solution.py:331
  59.4 23.9 %collective-permute-start.24 = (bf16[128,2048]{1,0:T(8,128)(2,1)}, bf16[128,2048]{1,0:T(8,128)(2,1)}, u32[]{:S(2)}, u32[]{:S(2)}) collective-permute-start(bf16[128,2048]{1,0:T(8,128)(2,1)} %collective-permute-done.23.own_ref), channel_id=1, source_target_pairs={{0,2},{1,3},{2,0},{3,1},{4,6},{5,7},{6,4},{7,5},{8,10},{9,11},{10,... | collective-permute-start | bytes 1572872 | tf_op jit(solution)/shard_map/ppermute | solution.py:334
  60.2 1.5 collective-permute-start.5
  61.7 13.7 %collective-permute-start.6 = (f32[64,128]{1,0:T(8,128)S(1)}, f32[64,128]{1,0:T(8,128)S(1)}, u32[]{:S(2)}, u32[]{:S(2)}) collective-permute-start(f32[64,128]{1,0:T(8,128)S(1)} %shard_map.123.refs_0_), channel_id=1, source_target_pairs={{0,2},{1,3},{2,0},{3,1},{4,6},{5,7},{6,4},{7,5},{8,10},{9,11},{10,... | collective-permute-start | bytes 98312 | tf_op jit(solution)/shard_map/ppermute | solution.py:334
  62.8 12.6 %collective-permute-start.7 = (f32[64,128]{1,0:T(8,128)S(1)}, f32[64,128]{1,0:T(8,128)S(1)}, u32[]{:S(2)}, u32[]{:S(2)}) collective-permute-start(f32[64,128]{1,0:T(8,128)S(1)} %shard_map.123.refs_0_), channel_id=1, source_target_pairs={{0,4},{1,5},{2,6},{3,7},{4,0},{5,1},{6,2},{7,3},{8,12},{9,13},{10,... | collective-permute-start | bytes 98312 | tf_op jit(solution)/shard_map/ppermute | solution.py:334
  65.8 12.1 %collective-permute-start.8 = (f32[64,128]{1,0:T(8,128)S(1)}, f32[64,128]{1,0:T(8,128)S(1)}, u32[]{:S(2)}, u32[]{:S(2)}) collective-permute-start(f32[64,128]{1,0:T(8,128)S(1)} %shard_map.123.refs_0_), channel_id=1, source_target_pairs={{0,6},{1,7},{2,4},{3,5},{4,2},{5,3},{6,0},{7,1},{8,14},{9,15},{10,... | collective-permute-start | bytes 98312 | tf_op jit(solution)/shard_map/ppermute | solution.py:334
  79.7 10.6 %collective-permute-start.34 = (bf16[80,2048]{1,0:T(8,128)(2,1)S(1)}, bf16[80,2048]{1,0:T(8,128)(2,1)S(1)}, u32[]{:S(2)}, u32[]{:S(2)}) collective-permute-start(bf16[80,2048]{1,0:T(8,128)(2,1)S(1)} %get-tuple-element.96), channel_id=1, source_target_pairs={{0,8},{8,0},{16,24},{24,16},{1,9},{9,1},{17,25},{25,17},{2,10},{10... | collective-permute-start | bytes 983048 | tf_op jit(solution)/shard_map/ppermute | solution.py:339
  81.3 16.2 %collective-permute-start.35 = (bf16[80,2048]{1,0:T(8,128)(2,1)S(1)}, bf16[80,2048]{1,0:T(8,128)(2,1)S(1)}, u32[]{:S(2)}, u32[]{:S(2)}) collective-permute-start(bf16[80,2048]{1,0:T(8,128)(2,1)S(1)} %get-tuple-element.97), channel_id=1, source_target_pairs={{0,16},{8,24},{16,0},{24,8},{1,17},{9,25},{17,1},{25,9},{2,18},{10... | collective-permute-start | bytes 983048 | tf_op jit(solution)/shard_map/ppermute | solution.py:339
  82.8 14.7 %collective-permute-start.36 = (bf16[80,2048]{1,0:T(8,128)(2,1)S(1)}, bf16[80,2048]{1,0:T(8,128)(2,1)S(1)}, u32[]{:S(2)}, u32[]{:S(2)}) collective-permute-start(bf16[80,2048]{1,0:T(8,128)(2,1)S(1)} %get-tuple-element.98), channel_id=1, source_target_pairs={{0,24},{8,16},{16,8},{24,0},{1,25},{9,17},{17,9},{25,1},{2,26},{10... | collective-permute-start | bytes 983048 | tf_op jit(solution)/shard_map/ppermute | solution.py:339
  83.3 24.8 %collective-permute-start.25 = (bf16[128,2048]{1,0:T(8,128)(2,1)}, bf16[128,2048]{1,0:T(8,128)(2,1)S(1)}, u32[]{:S(2)}, u32[]{:S(2)}) collective-permute-start(bf16[128,2048]{1,0:T(8,128)(2,1)} %collective-permute-done.24.own_ref), channel_id=1, source_target_pairs={{0,1},{1,0},{2,3},{3,2},{4,5},{5,4},{6,7},{7,6},{8,9},{9,8},{10,11... | collective-permute-start | bytes 1572872 | tf_op jit(solution)/shard_map/ppermute | solution.py:331
  101.3 33.9 %copy-start.2 = (bf16[1,2048,768]{2,1,0:T(8,128)(2,1)S(1)}, bf16[1,2048,768]{2,1,0:T(8,128)(2,1)}, u32[]{:S(2)}) copy-start(bf16[1,2048,768]{2,1,0:T(8,128)(2,1)} %refs_9_.3) | copy-start | bytes 9437188
  104.5 10.6 %collective-permute-start.37 = (bf16[80,2048]{1,0:T(8,128)(2,1)S(1)}, bf16[80,2048]{1,0:T(8,128)(2,1)S(1)}, u32[]{:S(2)}, u32[]{:S(2)}) collective-permute-start(bf16[80,2048]{1,0:T(8,128)(2,1)S(1)} %get-tuple-element.100), channel_id=1, source_target_pairs={{0,8},{8,0},{16,24},{24,16},{1,9},{9,1},{17,25},{25,17},{2,10},{10... | collective-permute-start | bytes 983048 | tf_op jit(solution)/shard_map/ppermute | solution.py:339
  105.8 17.6 %collective-permute-start.38 = (bf16[80,2048]{1,0:T(8,128)(2,1)S(1)}, bf16[80,2048]{1,0:T(8,128)(2,1)S(1)}, u32[]{:S(2)}, u32[]{:S(2)}) collective-permute-start(bf16[80,2048]{1,0:T(8,128)(2,1)S(1)} %get-tuple-element.101), channel_id=1, source_target_pairs={{0,16},{8,24},{16,0},{24,8},{1,17},{9,25},{17,1},{25,9},{2,18},{10... | collective-permute-start | bytes 983048 | tf_op jit(solution)/shard_map/ppermute | solution.py:339
  106.7 16.8 %collective-permute-start.39 = (bf16[80,2048]{1,0:T(8,128)(2,1)S(1)}, bf16[80,2048]{1,0:T(8,128)(2,1)S(1)}, u32[]{:S(2)}, u32[]{:S(2)}) collective-permute-start(bf16[80,2048]{1,0:T(8,128)(2,1)S(1)} %get-tuple-element.102), channel_id=1, source_target_pairs={{0,24},{8,16},{16,8},{24,0},{1,25},{9,17},{17,9},{25,1},{2,26},{10... | collective-permute-start | bytes 983048 | tf_op jit(solution)/shard_map/ppermute | solution.py:339
  109.6 19.6 %collective-permute-start.26 = (bf16[80,2048]{1,0:T(8,128)(2,1)S(1)}, bf16[80,2048]{1,0:T(8,128)(2,1)S(1)}, u32[]{:S(2)}, u32[]{:S(2)}) collective-permute-start(bf16[80,2048]{1,0:T(8,128)(2,1)S(1)} %get-tuple-element.86), channel_id=1, source_target_pairs={{0,8},{8,0},{16,24},{24,16},{1,9},{9,1},{17,25},{25,17},{2,10},{10... | collective-permute-start | bytes 983048 | tf_op jit(solution)/shard_map/ppermute | solution.py:339
  110.9 24.3 %collective-permute-start.27 = (bf16[80,2048]{1,0:T(8,128)(2,1)S(1)}, bf16[80,2048]{1,0:T(8,128)(2,1)S(1)}, u32[]{:S(2)}, u32[]{:S(2)}) collective-permute-start(bf16[80,2048]{1,0:T(8,128)(2,1)S(1)} %get-tuple-element.87), channel_id=1, source_target_pairs={{0,16},{8,24},{16,0},{24,8},{1,17},{9,25},{17,1},{25,9},{2,18},{10... | collective-permute-start | bytes 983048 | tf_op jit(solution)/shard_map/ppermute | solution.py:339
  115.2 20.1 %collective-permute-start.28 = (bf16[80,2048]{1,0:T(8,128)(2,1)S(1)}, bf16[80,2048]{1,0:T(8,128)(2,1)S(1)}, u32[]{:S(2)}, u32[]{:S(2)}) collective-permute-start(bf16[80,2048]{1,0:T(8,128)(2,1)S(1)} %get-tuple-element.88), channel_id=1, source_target_pairs={{0,24},{8,16},{16,8},{24,0},{1,25},{9,17},{17,9},{25,1},{2,26},{10... | collective-permute-start | bytes 983048 | tf_op jit(solution)/shard_map/ppermute | solution.py:339
  123.5 18.6 %collective-permute-start.43 = (bf16[128,2048]{1,0:T(8,128)(2,1)S(1)}, bf16[128,2048]{1,0:T(8,128)(2,1)S(1)}, u32[]{:S(2)}, u32[]{:S(2)}) collective-permute-start(bf16[128,2048]{1,0:T(8,128)(2,1)S(1)} %copy-done.9), channel_id=1, source_target_pairs={{0,2},{1,3},{2,0},{3,1},{4,6},{5,7},{6,4},{7,5},{8,10},{9,11},{10,... | collective-permute-start | bytes 1572872 | tf_op jit(solution)/shard_map/ppermute | solution.py:334
  124.2 39.4 %collective-permute-start.40 = (bf16[128,2048]{1,0:T(8,128)(2,1)S(1)}, bf16[128,2048]{1,0:T(8,128)(2,1)S(1)}, u32[]{:S(2)}, u32[]{:S(2)}) collective-permute-start(bf16[128,2048]{1,0:T(8,128)(2,1)S(1)} %get-tuple-element.104), channel_id=1, source_target_pairs={{0,1},{1,0},{2,3},{3,2},{4,5},{5,4},{6,7},{7,6},{8,9},{9,8},{10,11... | collective-permute-start | bytes 1572872 | tf_op jit(solution)/shard_map/ppermute | solution.py:331
  138.5 10.7 %collective-permute-start.29 = (bf16[80,2048]{1,0:T(8,128)(2,1)S(1)}, bf16[80,2048]{1,0:T(8,128)(2,1)S(1)}, u32[]{:S(2)}, u32[]{:S(2)}) collective-permute-start(bf16[80,2048]{1,0:T(8,128)(2,1)S(1)} %get-tuple-element.90), channel_id=1, source_target_pairs={{0,8},{8,0},{16,24},{24,16},{1,9},{9,1},{17,25},{25,17},{2,10},{10... | collective-permute-start | bytes 983048 | tf_op jit(solution)/shard_map/ppermute | solution.py:339
  139.1 17.6 %collective-permute-start.30 = (bf16[80,2048]{1,0:T(8,128)(2,1)S(1)}, bf16[80,2048]{1,0:T(8,128)(2,1)S(1)}, u32[]{:S(2)}, u32[]{:S(2)}) collective-permute-start(bf16[80,2048]{1,0:T(8,128)(2,1)S(1)} %get-tuple-element.91), channel_id=1, source_target_pairs={{0,16},{8,24},{16,0},{24,8},{1,17},{9,25},{17,1},{25,9},{2,18},{10... | collective-permute-start | bytes 983048 | tf_op jit(solution)/shard_map/ppermute | solution.py:339
  140.3 17.9 %collective-permute-start.31 = (bf16[80,2048]{1,0:T(8,128)(2,1)S(1)}, bf16[80,2048]{1,0:T(8,128)(2,1)S(1)}, u32[]{:S(2)}, u32[]{:S(2)}) collective-permute-start(bf16[80,2048]{1,0:T(8,128)(2,1)S(1)} %get-tuple-element.92), channel_id=1, source_target_pairs={{0,24},{8,16},{16,8},{24,0},{1,25},{9,17},{17,9},{25,1},{2,26},{10... | collective-permute-start | bytes 983048 | tf_op jit(solution)/shard_map/ppermute | solution.py:339
  142.5 16.4 %collective-permute-start.44 = (bf16[40,2048]{1,0:T(8,128)(2,1)S(1)}, bf16[40,2048]{1,0:T(8,128)(2,1)S(1)}, u32[]{:S(2)}, u32[]{:S(2)}) collective-permute-start(bf16[40,2048]{1,0:T(8,128)(2,1)S(1)} %get-tuple-element.106), channel_id=1, source_target_pairs={{0,8},{1,9},{2,10},{3,11},{4,12},{5,13},{6,14},{7,15},{8,0},{9,1},... | collective-permute-start | bytes 491528 | tf_op jit(solution)/shard_map/ppermute | solution.py:351
  149.2 11.6 %collective-permute-start.45 = (bf16[40,2048]{1,0:T(8,128)(2,1)S(1)}, bf16[40,2048]{1,0:T(8,128)(2,1)S(1)}, u32[]{:S(2)}, u32[]{:S(2)}) collective-permute-start(bf16[40,2048]{1,0:T(8,128)(2,1)S(1)} %get-tuple-element.107), channel_id=1, source_target_pairs={{0,16},{1,17},{2,18},{3,19},{4,20},{5,21},{6,22},{7,23},{8,24},{9,... | collective-permute-start | bytes 491528 | tf_op jit(solution)/shard_map/ppermute | solution.py:351
  156.7 6.9 %collective-permute-start.46 = (bf16[40,2048]{1,0:T(8,128)(2,1)S(1)}, bf16[40,2048]{1,0:T(8,128)(2,1)S(1)}, u32[]{:S(2)}, u32[]{:S(2)}) collective-permute-start(bf16[40,2048]{1,0:T(8,128)(2,1)S(1)} %get-tuple-element.108), channel_id=1, source_target_pairs={{0,24},{1,25},{2,26},{3,27},{4,28},{5,29},{6,30},{7,31},{8,16},{9,... | collective-permute-start | bytes 491528 | tf_op jit(solution)/shard_map/ppermute | solution.py:351
  158.2 6.5 %collective-permute-start.47 = (bf16[40,2048]{1,0:T(8,128)(2,1)S(1)}, bf16[40,2048]{1,0:T(8,128)(2,1)S(1)}, u32[]{:S(2)}, u32[]{:S(2)}) collective-permute-start(bf16[40,2048]{1,0:T(8,128)(2,1)S(1)} %get-tuple-element.109), channel_id=1, source_target_pairs={{0,1},{1,0},{2,3},{3,2},{4,5},{5,4},{6,7},{7,6},{8,9},{9,8},{10,11... | collective-permute-start | bytes 491528 | tf_op jit(solution)/shard_map/ppermute | solution.py:351
  159.0 6.6 %collective-permute-start.48 = (bf16[40,2048]{1,0:T(8,128)(2,1)S(1)}, bf16[40,2048]{1,0:T(8,128)(2,1)S(1)}, u32[]{:S(2)}, u32[]{:S(2)}) collective-permute-start(bf16[40,2048]{1,0:T(8,128)(2,1)S(1)} %get-tuple-element.110), channel_id=1, source_target_pairs={{0,9},{1,8},{2,11},{3,10},{4,13},{5,12},{6,15},{7,14},{8,1},{9,0},... | collective-permute-start | bytes 491528 | tf_op jit(solution)/shard_map/ppermute | solution.py:351
  160.8 9.8 %collective-permute-start.49 = (bf16[40,2048]{1,0:T(8,128)(2,1)S(1)}, bf16[40,2048]{1,0:T(8,128)(2,1)S(1)}, u32[]{:S(2)}, u32[]{:S(2)}) collective-permute-start(bf16[40,2048]{1,0:T(8,128)(2,1)S(1)} %get-tuple-element.111), channel_id=1, source_target_pairs={{0,17},{1,16},{2,19},{3,18},{4,21},{5,20},{6,23},{7,22},{8,25},{9,... | collective-permute-start | bytes 491528 | tf_op jit(solution)/shard_map/ppermute | solution.py:351
  163.6 7.0 %collective-permute-start.50 = (bf16[40,2048]{1,0:T(8,128)(2,1)S(1)}, bf16[40,2048]{1,0:T(8,128)(2,1)S(1)}, u32[]{:S(2)}, u32[]{:S(2)}) collective-permute-start(bf16[40,2048]{1,0:T(8,128)(2,1)S(1)} %get-tuple-element.112), channel_id=1, source_target_pairs={{0,25},{1,24},{2,27},{3,26},{4,29},{5,28},{6,31},{7,30},{8,17},{9,... | collective-permute-start | bytes 491528 | tf_op jit(solution)/shard_map/ppermute | solution.py:351
  163.6 39.5 %collective-permute-start.32 = (bf16[128,2048]{1,0:T(8,128)(2,1)S(1)}, bf16[128,2048]{1,0:T(8,128)(2,1)S(1)}, u32[]{:S(2)}, u32[]{:S(2)}) collective-permute-start(bf16[128,2048]{1,0:T(8,128)(2,1)S(1)} %get-tuple-element.94), channel_id=1, source_target_pairs={{0,1},{1,0},{2,3},{3,2},{4,5},{5,4},{6,7},{7,6},{8,9},{9,8},{10,11... | collective-permute-start | bytes 1572872 | tf_op jit(solution)/shard_map/ppermute | solution.py:331
  164.7 39.1 %collective-permute-start.41 = (bf16[128,2048]{1,0:T(8,128)(2,1)S(1)}, bf16[128,2048]{1,0:T(8,128)(2,1)S(1)}, u32[]{:S(2)}, u32[]{:S(2)}) collective-permute-start(bf16[128,2048]{1,0:T(8,128)(2,1)S(1)} %add_convert_fusion.1), channel_id=1, source_target_pairs={{0,2},{1,3},{2,0},{3,1},{4,6},{5,7},{6,4},{7,5},{8,10},{9,11},{10,... | collective-permute-start | bytes 1572872 | tf_op jit(solution)/shard_map/ppermute | solution.py:334
  173.8 7.1 %collective-permute-start.51 = (bf16[40,2048]{1,0:T(8,128)(2,1)S(1)}, bf16[40,2048]{1,0:T(8,128)(2,1)S(1)}, u32[]{:S(2)}, u32[]{:S(2)}) collective-permute-start(bf16[40,2048]{1,0:T(8,128)(2,1)S(1)} %get-tuple-element.114), channel_id=1, source_target_pairs={{0,8},{1,9},{2,10},{3,11},{4,12},{5,13},{6,14},{7,15},{8,0},{9,1},... | collective-permute-start | bytes 491528 | tf_op jit(solution)/shard_map/ppermute | solution.py:351
  174.1 6.9 %collective-permute-start.52 = (bf16[40,2048]{1,0:T(8,128)(2,1)S(1)}, bf16[40,2048]{1,0:T(8,128)(2,1)S(1)}, u32[]{:S(2)}, u32[]{:S(2)}) collective-permute-start(bf16[40,2048]{1,0:T(8,128)(2,1)S(1)} %get-tuple-element.115), channel_id=1, source_target_pairs={{0,16},{1,17},{2,18},{3,19},{4,20},{5,21},{6,22},{7,23},{8,24},{9,... | collective-permute-start | bytes 491528 | tf_op jit(solution)/shard_map/ppermute | solution.py:351
  175.4 8.9 %collective-permute-start.53 = (bf16[40,2048]{1,0:T(8,128)(2,1)S(1)}, bf16[40,2048]{1,0:T(8,128)(2,1)S(1)}, u32[]{:S(2)}, u32[]{:S(2)}) collective-permute-start(bf16[40,2048]{1,0:T(8,128)(2,1)S(1)} %get-tuple-element.116), channel_id=1, source_target_pairs={{0,24},{1,25},{2,26},{3,27},{4,28},{5,29},{6,30},{7,31},{8,16},{9,... | collective-permute-start | bytes 491528 | tf_op jit(solution)/shard_map/ppermute | solution.py:351
  180.9 5.5 %collective-permute-start.54 = (bf16[40,2048]{1,0:T(8,128)(2,1)S(1)}, bf16[40,2048]{1,0:T(8,128)(2,1)S(1)}, u32[]{:S(2)}, u32[]{:S(2)}) collective-permute-start(bf16[40,2048]{1,0:T(8,128)(2,1)S(1)} %get-tuple-element.117), channel_id=1, source_target_pairs={{0,1},{1,0},{2,3},{3,2},{4,5},{5,4},{6,7},{7,6},{8,9},{9,8},{10,11... | collective-permute-start | bytes 491528 | tf_op jit(solution)/shard_map/ppermute | solution.py:351
  181.0 6.3 %collective-permute-start.55 = (bf16[40,2048]{1,0:T(8,128)(2,1)S(1)}, bf16[40,2048]{1,0:T(8,128)(2,1)S(1)}, u32[]{:S(2)}, u32[]{:S(2)}) collective-permute-start(bf16[40,2048]{1,0:T(8,128)(2,1)S(1)} %get-tuple-element.118), channel_id=1, source_target_pairs={{0,9},{1,8},{2,11},{3,10},{4,13},{5,12},{6,15},{7,14},{8,1},{9,0},... | collective-permute-start | bytes 491528 | tf_op jit(solution)/shard_map/ppermute | solution.py:351
  184.4 9.7 %collective-permute-start.56 = (bf16[40,2048]{1,0:T(8,128)(2,1)S(1)}, bf16[40,2048]{1,0:T(8,128)(2,1)S(1)}, u32[]{:S(2)}, u32[]{:S(2)}) collective-permute-start(bf16[40,2048]{1,0:T(8,128)(2,1)S(1)} %get-tuple-element.119), channel_id=1, source_target_pairs={{0,17},{1,16},{2,19},{3,18},{4,21},{5,20},{6,23},{7,22},{8,25},{9,... | collective-permute-start | bytes 491528 | tf_op jit(solution)/shard_map/ppermute | solution.py:351
  186.4 9.7 %collective-permute-start.57 = (bf16[40,2048]{1,0:T(8,128)(2,1)S(1)}, bf16[40,2048]{1,0:T(8,128)(2,1)S(1)}, u32[]{:S(2)}, u32[]{:S(2)}) collective-permute-start(bf16[40,2048]{1,0:T(8,128)(2,1)S(1)} %get-tuple-element.120), channel_id=1, source_target_pairs={{0,25},{1,24},{2,27},{3,26},{4,29},{5,28},{6,31},{7,30},{8,17},{9,... | collective-permute-start | bytes 491528 | tf_op jit(solution)/shard_map/ppermute | solution.py:351
  187.2 10.9 %collective-permute-start.10 = (bf16[40,2048]{1,0:T(8,128)(2,1)S(1)}, bf16[40,2048]{1,0:T(8,128)(2,1)S(1)}, u32[]{:S(2)}, u32[]{:S(2)}) collective-permute-start(bf16[40,2048]{1,0:T(8,128)(2,1)S(1)} %get-tuple-element.69), channel_id=1, source_target_pairs={{0,16},{1,17},{2,18},{3,19},{4,20},{5,21},{6,22},{7,23},{8,24},{9,... | collective-permute-start | bytes 491528 | tf_op jit(solution)/shard_map/ppermute | solution.py:351
  194.1 7.4 %collective-permute-start.11 = (bf16[40,2048]{1,0:T(8,128)(2,1)S(1)}, bf16[40,2048]{1,0:T(8,128)(2,1)S(1)}, u32[]{:S(2)}, u32[]{:S(2)}) collective-permute-start(bf16[40,2048]{1,0:T(8,128)(2,1)S(1)} %get-tuple-element.70), channel_id=1, source_target_pairs={{0,24},{1,25},{2,26},{3,27},{4,28},{5,29},{6,30},{7,31},{8,16},{9,... | collective-permute-start | bytes 491528 | tf_op jit(solution)/shard_map/ppermute | solution.py:351
  196.1 8.8 %collective-permute-start.12 = (bf16[40,2048]{1,0:T(8,128)(2,1)S(1)}, bf16[40,2048]{1,0:T(8,128)(2,1)S(1)}, u32[]{:S(2)}, u32[]{:S(2)}) collective-permute-start(bf16[40,2048]{1,0:T(8,128)(2,1)S(1)} %get-tuple-element.71), channel_id=1, source_target_pairs={{0,1},{1,0},{2,3},{3,2},{4,5},{5,4},{6,7},{7,6},{8,9},{9,8},{10,11... | collective-permute-start | bytes 491528 | tf_op jit(solution)/shard_map/ppermute | solution.py:351
  198.2 7.2 %collective-permute-start.13 = (bf16[40,2048]{1,0:T(8,128)(2,1)S(1)}, bf16[40,2048]{1,0:T(8,128)(2,1)S(1)}, u32[]{:S(2)}, u32[]{:S(2)}) collective-permute-start(bf16[40,2048]{1,0:T(8,128)(2,1)S(1)} %get-tuple-element.72), channel_id=1, source_target_pairs={{0,9},{1,8},{2,11},{3,10},{4,13},{5,12},{6,15},{7,14},{8,1},{9,0},... | collective-permute-start | bytes 491528 | tf_op jit(solution)/shard_map/ppermute | solution.py:351
  201.5 9.4 %collective-permute-start.14 = (bf16[40,2048]{1,0:T(8,128)(2,1)S(1)}, bf16[40,2048]{1,0:T(8,128)(2,1)S(1)}, u32[]{:S(2)}, u32[]{:S(2)}) collective-permute-start(bf16[40,2048]{1,0:T(8,128)(2,1)S(1)} %get-tuple-element.73), channel_id=1, source_target_pairs={{0,17},{1,16},{2,19},{3,18},{4,21},{5,20},{6,23},{7,22},{8,25},{9,... | collective-permute-start | bytes 491528 | tf_op jit(solution)/shard_map/ppermute | solution.py:351
  203.1 7.8 %collective-permute-start.15 = (bf16[40,2048]{1,0:T(8,128)(2,1)S(1)}, bf16[40,2048]{1,0:T(8,128)(2,1)S(1)}, u32[]{:S(2)}, u32[]{:S(2)}) collective-permute-start(bf16[40,2048]{1,0:T(8,128)(2,1)S(1)} %get-tuple-element.74), channel_id=1, source_target_pairs={{0,25},{1,24},{2,27},{3,26},{4,29},{5,28},{6,31},{7,30},{8,17},{9,... | collective-permute-start | bytes 491528 | tf_op jit(solution)/shard_map/ppermute | solution.py:351
  203.8 9.1 %collective-permute-start.9 = (bf16[40,2048]{1,0:T(8,128)(2,1)S(1)}, bf16[40,2048]{1,0:T(8,128)(2,1)S(1)}, u32[]{:S(2)}, u32[]{:S(2)}) collective-permute-start(bf16[40,2048]{1,0:T(8,128)(2,1)S(1)} %get-tuple-element.68), channel_id=1, source_target_pairs={{0,8},{1,9},{2,10},{3,11},{4,12},{5,13},{6,14},{7,15},{8,0},{9,1},... | collective-permute-start | bytes 491528 | tf_op jit(solution)/shard_map/ppermute | solution.py:351
  204.9 31.0 %collective-permute-start.58 = (bf16[128,2048]{1,0:T(8,128)(2,1)S(1)}, bf16[128,2048]{1,0:T(8,128)(2,1)S(1)}, u32[]{:S(2)}, u32[]{:S(2)}) collective-permute-start(bf16[128,2048]{1,0:T(8,128)(2,1)S(1)} %shard_map.135), channel_id=1, source_target_pairs={{0,2},{1,3},{2,0},{3,1},{4,6},{5,7},{6,4},{7,5},{8,10},{9,11},{10,... | collective-permute-start | bytes 1572872 | tf_op jit(solution)/shard_map/ppermute | solution.py:334
  205.4 30.5 %collective-permute-start.42 = (bf16[128,2048]{1,0:T(8,128)(2,1)S(1)}, bf16[128,2048]{1,0:T(8,128)(2,1)S(1)}, u32[]{:S(2)}, u32[]{:S(2)}) collective-permute-start(bf16[128,2048]{1,0:T(8,128)(2,1)S(1)} %add_convert_fusion), channel_id=1, source_target_pairs={{0,6},{1,7},{2,4},{3,5},{4,2},{5,3},{6,0},{7,1},{8,14},{9,15},{10,... | collective-permute-start | bytes 1572872 | tf_op jit(solution)/shard_map/ppermute | solution.py:334
  212.9 23.0 %copy-start.11 = (bf16[128,2048]{1,0:T(8,128)(2,1)S(1)}, bf16[128,2048]{1,0:T(8,128)(2,1)}, u32[]{:S(2)}) copy-start(bf16[128,2048]{1,0:T(8,128)(2,1)} %copy-done.10) | copy-start | bytes 1572868
  216.2 7.1 %collective-permute-start.16 = (bf16[40,2048]{1,0:T(8,128)(2,1)S(1)}, bf16[40,2048]{1,0:T(8,128)(2,1)S(1)}, u32[]{:S(2)}, u32[]{:S(2)}) collective-permute-start(bf16[40,2048]{1,0:T(8,128)(2,1)S(1)} %get-tuple-element.76), channel_id=1, source_target_pairs={{0,8},{1,9},{2,10},{3,11},{4,12},{5,13},{6,14},{7,15},{8,0},{9,1},... | collective-permute-start | bytes 491528 | tf_op jit(solution)/shard_map/ppermute | solution.py:351
  217.0 7.3 %collective-permute-start.17 = (bf16[40,2048]{1,0:T(8,128)(2,1)S(1)}, bf16[40,2048]{1,0:T(8,128)(2,1)S(1)}, u32[]{:S(2)}, u32[]{:S(2)}) collective-permute-start(bf16[40,2048]{1,0:T(8,128)(2,1)S(1)} %get-tuple-element.77), channel_id=1, source_target_pairs={{0,16},{1,17},{2,18},{3,19},{4,20},{5,21},{6,22},{7,23},{8,24},{9,... | collective-permute-start | bytes 491528 | tf_op jit(solution)/shard_map/ppermute | solution.py:351
  218.0 9.0 %collective-permute-start.18 = (bf16[40,2048]{1,0:T(8,128)(2,1)S(1)}, bf16[40,2048]{1,0:T(8,128)(2,1)S(1)}, u32[]{:S(2)}, u32[]{:S(2)}) collective-permute-start(bf16[40,2048]{1,0:T(8,128)(2,1)S(1)} %get-tuple-element.78), channel_id=1, source_target_pairs={{0,24},{1,25},{2,26},{3,27},{4,28},{5,29},{6,30},{7,31},{8,16},{9,... | collective-permute-start | bytes 491528 | tf_op jit(solution)/shard_map/ppermute | solution.py:351
  223.3 5.2 %collective-permute-start.19 = (bf16[40,2048]{1,0:T(8,128)(2,1)S(1)}, bf16[40,2048]{1,0:T(8,128)(2,1)S(1)}, u32[]{:S(2)}, u32[]{:S(2)}) collective-permute-start(bf16[40,2048]{1,0:T(8,128)(2,1)S(1)} %get-tuple-element.79), channel_id=1, source_target_pairs={{0,1},{1,0},{2,3},{3,2},{4,5},{5,4},{6,7},{7,6},{8,9},{9,8},{10,11... | collective-permute-start | bytes 491528 | tf_op jit(solution)/shard_map/ppermute | solution.py:351
  224.2 6.9 %collective-permute-start.20 = (bf16[40,2048]{1,0:T(8,128)(2,1)S(1)}, bf16[40,2048]{1,0:T(8,128)(2,1)S(1)}, u32[]{:S(2)}, u32[]{:S(2)}) collective-permute-start(bf16[40,2048]{1,0:T(8,128)(2,1)S(1)} %get-tuple-element.80), channel_id=1, source_target_pairs={{0,9},{1,8},{2,11},{3,10},{4,13},{5,12},{6,15},{7,14},{8,1},{9,0},... | collective-permute-start | bytes 491528 | tf_op jit(solution)/shard_map/ppermute | solution.py:351
  227.0 8.6 %collective-permute-start.21 = (bf16[40,2048]{1,0:T(8,128)(2,1)S(1)}, bf16[40,2048]{1,0:T(8,128)(2,1)S(1)}, u32[]{:S(2)}, u32[]{:S(2)}) collective-permute-start(bf16[40,2048]{1,0:T(8,128)(2,1)S(1)} %get-tuple-element.81), channel_id=1, source_target_pairs={{0,17},{1,16},{2,19},{3,18},{4,21},{5,20},{6,23},{7,22},{8,25},{9,... | collective-permute-start | bytes 491528 | tf_op jit(solution)/shard_map/ppermute | solution.py:351
  228.5 7.4 %collective-permute-start.22 = (bf16[40,2048]{1,0:T(8,128)(2,1)S(1)}, bf16[40,2048]{1,0:T(8,128)(2,1)S(1)}, u32[]{:S(2)}, u32[]{:S(2)}) collective-permute-start(bf16[40,2048]{1,0:T(8,128)(2,1)S(1)} %get-tuple-element.82), channel_id=1, source_target_pairs={{0,25},{1,24},{2,27},{3,26},{4,29},{5,28},{6,31},{7,30},{8,17},{9,... | collective-permute-start | bytes 491528 | tf_op jit(solution)/shard_map/ppermute | solution.py:351
  (13 other events, 71.1 us)

commit v5 on v4

--- a/solution.py
+++ b/solution.py
@@ -139,27 +139,18 @@
     moe_ref[...] = (res_ref[...].astype(F32) * scale * mgain_ref[...]).astype(BF)
 
 
-def pack_kernel(own_ref, par_ref, out_ref):
-    count = own_ref.shape[0]
-    out_ref[:count, :] = own_ref[...]
-    out_ref[count:, :] = par_ref[...]
-
-
 def rank_kernel(groups, length, group_ref, place_ref, *refs):
-    packs = refs[:-2]
+    tables = refs[:-2]
     route_ref, rank_ref = refs[-2:]
-    count = groups * length
     place = place_ref[0]
     group = group_ref[0]
     row = 0
-    for straight in range(2):
-        for pack in packs:
-            for side in range(2):
-                for k in range(groups):
-                    at = (group ^ k) * length
-                    at = at + ((place ^ side) if straight else side * count + place)
-                    route_ref[row : row + 1, :] = pack[pl.ds(at, 1), :]
-                    row += 1
+    for table in tables:
+        for side in range(2):
+            for k in range(groups):
+                at = (group ^ k) * length + (place ^ side)
+                route_ref[row : row + 1, :] = table[pl.ds(at, 1), :]
+                row += 1
     tokens = route_ref.shape[1]
     rows = lax.broadcasted_iota(jnp.int32, (tokens, tokens), 0)
     cols = lax.broadcasted_iota(jnp.int32, (tokens, tokens), 1)
@@ -175,62 +166,20 @@
     return jnp.where(number == rank, value, 0.0)
 
 
-def select_kernel(slots, base, own_ref, par_ref, rank_ref, *outs):
-    groups = len(outs)
-    picks = []
-    for block in range(2):
-        rows = [slots_of(rank_ref, 1.0, base + block * groups + k, slots) for k in range(groups)]
-        picks.append(jnp.concatenate(rows, axis=0).astype(BF))
-    first = dot(picks[0], own_ref[...])
-    second = dot(picks[1], par_ref[...])
-    for k in range(groups):
-        at = slice(k * slots, (k + 1) * slots)
-        outs[k][...] = jnp.concatenate([first[at], second[at]], axis=0).astype(BF)
-
-
-def select(slots, groups, base, own, par, rank):
-    shape = ((2 * slots, own.shape[1]), BF)
-    body = functools.partial(select_kernel, slots, base)
-    return call(body, [shape] * groups)(own, par, rank)
-
-
-def combine_kernel(slots, groups, base, *refs):
-    backs = refs[:groups]
-    rank_ref, weight_ref, own_ref, par_ref = refs[groups:]
-    rows = jnp.concatenate([r[...] for r in backs], axis=0)
-    zero = jnp.zeros((slots, rank_ref.shape[1]), F32)
-    sides = []
-    for block in range(2):
-        parts = []
-        for k in range(groups):
-            row = base + block * groups + k
-            mine = slots_of(rank_ref, weight_ref[row : row + 1, :], row, slots)
-            parts += [mine, zero] if block == 0 else [zero, mine]
-        sides.append(jnp.concatenate(parts, axis=0).astype(BF))
-    own_ref[...] = dot(sides[0], rows, 0, 0).astype(BF)
-    par_ref[...] = dot(sides[1], rows, 0, 0).astype(BF)
-
-
-def combine(slots, base, backs, rank, weight):
-    shape = ((rank.shape[1], backs[0].shape[1]), BF)
-    body = functools.partial(combine_kernel, slots, len(backs), base)
-    return call(body, [shape] * 2)(*backs, rank, weight)
-
-
-def straight_select_kernel(slots, base, own_ref, rank_ref, *outs):
+def select_kernel(slots, base, own_ref, rank_ref, *outs):
     rows = [slots_of(rank_ref, 1.0, base + i, slots) for i in range(len(outs))]
     picked = dot(jnp.concatenate(rows, axis=0).astype(BF), own_ref[...]).astype(BF)
     for i, out in enumerate(outs):
         out[...] = picked[i * slots : (i + 1) * slots]
 
 
-def straight_select(slots, count, base, own, rank):
-    body = functools.partial(straight_select_kernel, slots, base)
+def select(slots, count, base, own, rank):
+    body = functools.partial(select_kernel, slots, base)
     shape = ((slots, own.shape[1]), BF)
     return call(body, [shape] * count)(own, rank)
 
 
-def straight_combine_kernel(slots, count, base, *refs):
+def combine_kernel(slots, count, base, *refs):
     backs = refs[:count]
     rank_ref, weight_ref = refs[count : count + 2]
     more = refs[count + 2 : -1]
@@ -245,8 +194,8 @@
     refs[-1][...] = total.astype(BF)
 
 
-def straight_combine(slots, base, backs, rank, weight, more, leave):
-    body = functools.partial(straight_combine_kernel, slots, len(backs), base)
+def combine(slots, base, backs, rank, weight, more, leave):
+    body = functools.partial(combine_kernel, slots, len(backs), base)
     shape = ((rank.shape[1], backs[0].shape[1]), BF)
     return call(body, [shape], leave=leave)(*backs, rank, weight, *more)[0]
 
@@ -257,12 +206,12 @@
     return jnp.concatenate([r[...].astype(F32) for r in refs], axis=0).astype(BF)
 
 
-def expert_kernel(count, starts, *refs):
+def expert_kernel(count, *refs):
     xs = refs[:count]
     gate_ref, up_ref, down_ref = refs[count : count + 3]
     outs = refs[count + 3 : -1]
     hidden_ref = refs[-1]
-    features = xs[0].shape[1]
+    slots, features = xs[0].shape
     units = gate_ref.shape[2]
     x = stacked(xs)
     width = 256
@@ -276,27 +225,15 @@
     for j in range(features // width):
         at = slice(j * width, (j + 1) * width)
         out = dot(hidden, down_ref[0, :, at])
-        for ref, start in zip(outs, starts):
-            ref[:, at] = out[start : start + ref.shape[0]].astype(BF)
-
-
-def experts(xs, straight_in, straight_out, groups, gate, up, down):
-    total = sum(x.shape[0] for x in xs)
-    features = xs[0].shape[1]
-    slots = total // (2 * groups)
-    if straight_out:
-        count, rows = 2 * groups, slots
-        starts = [
-            (side * groups + k if straight_in else 2 * k + side) * slots
-            for side in range(2)
-            for k in range(groups)
-        ]
-    else:
-        count, rows = groups, 2 * slots
-        starts = [k * rows for k in range(groups)]
-    body = functools.partial(expert_kernel, len(xs), starts)
-    scratch = [pltpu.VMEM((total, gate.shape[2]), BF)]
-    return call(body, [((rows, features), BF)] * count, scratch)(*xs, gate, up, down)
+        for i, ref in enumerate(outs):
+            ref[:, at] = out[i * slots : (i + 1) * slots].astype(BF)
+
+
+def experts(xs, gate, up, down):
+    body = functools.partial(expert_kernel, len(xs))
+    scratch = [pltpu.VMEM((sum(x.shape[0] for x in xs), gate.shape[2]), BF)]
+    outs = [(xs[0].shape, BF)] * len(xs)
+    return call(body, outs, scratch)(*xs, gate, up, down)
 
 
 def on_device(
@@ -333,11 +270,6 @@
     def along(x, m):
         return lax.ppermute(x, "seq", [(s, s ^ (2 * m)) for s in range(length)])
 
-    def across(x, m):
-        if m == 0:
-            return x
-        return lax.ppermute(x, "grp", [(g, g ^ m) for g in range(groups)])
-
     def straight(parts):
         moved = []
         for i, x in enumerate(parts):
@@ -383,9 +315,7 @@
     shares = (scores / jnp.sum(scores, axis=1, keepdims=True)).T
     hit = chosen[None] == jnp.arange(expert_count, dtype=jnp.int32)[:, None, None]
     dense = jnp.sum(jnp.where(hit, shares[None], 0.0), axis=1)
-    shape = (2 * expert_count, tokens)
-    both = call(pack_kernel, [(shape, F32)])(dense, swap(dense))[0]
-    packs = [both] + [along(both, m) for m in range(1, stages)]
+    tables = [dense] + [along(dense, m) for m in range(1, stages)]
 
     inside, out_proj = call(
         inside_kernel,
@@ -394,10 +324,10 @@
         + [pltpu.SemaphoreType.DMA((3, 4)), pltpu.SemaphoreType.DMA],
         away=(0, 1, 2, 3),
     )(queries, keys, values, out_proj, *scalars)
-    shape = (2 * stages * 2 * groups, tokens)
+    shape = (stages * 2 * groups, tokens)
     body = functools.partial(rank_kernel, groups, length)
     routes, ranks = call(body, [(shape, F32)] * 2)(
-        *scalars[1:], *packs
+        *scalars[1:], *tables
     )
     mine = added(*arrived)
     other = swap(mine)
@@ -425,45 +355,21 @@
         blocks[m] = along(blocks[source], shift)
     for m in range(stages):
         base = m * 2 * groups
-        near = m in STRAIGHT_OUT
-        partner = None if near else swap(blocks[m])
-        if near:
-            base += stages * 2 * groups
-            picked = straight_select(slots, 2 * groups, base, blocks[m], ranks)
-        else:
-            picked = select(slots, groups, base, blocks[m], partner, ranks)
-        if near:
-            taken = straight(picked)
-        else:
-            taken = [across(picked[k], k) for k in range(groups)]
-        outs[m] = experts(
-            taken, near, m in STRAIGHT_BACK, groups, gate_weight, up_weight, down_weight
-        )
+        picked = select(slots, 2 * groups, base, blocks[m], ranks)
+        taken = straight(picked)
+        outs[m] = experts(taken, gate_weight, up_weight, down_weight)
     sums = {m: [] for m in range(stages)}
     sums[0].append(residual)
     for m in back_order(stages):
         base = m * 2 * groups
-        if m in STRAIGHT_BACK:
-            base += stages * 2 * groups
-            backs = straight(outs[m])
-            part = straight_combine(slots, base, backs, ranks, routes, sums[m], m == 0)
-        else:
-            backs = [across(outs[m][k], k) for k in range(groups)]
-            own, par = combine(slots, base, backs, ranks, routes)
-            part = own.astype(F32) + swap(par).astype(F32)
-            for more in sums[m]:
-                part = part + more.astype(F32)
-            part = part.astype(BF)
+        backs = straight(outs[m])
+        part = combine(slots, base, backs, ranks, routes, sums[m], m == 0)
         if m:
             into, shift = returning[m]
             sums[into].append(along(part, shift))
     return part.reshape(1, tokens, features)
 
 
-STRAIGHT_OUT = (0, 1)
-STRAIGHT_BACK = (0, 1)
-
-
 def sending(stages):
     if stages == 4:
         return {1: (0, 1), 2: (0, 2), 3: (2, 1)}

time: 238 us -> 211 us (0.89)
  waiting for transfers between devices: 133 us -> 74.9 us
  starting transfers between devices: 66.3 us -> 97.4 us
    ppermute x12 -> x0, waiting for transfers between devices: 48.4 us -> none  [across(): return lax.ppermute(x, 'grp', [(g, g ^ m) for g in range(groups)])]
    ppermute x28 -> x56, starting transfers between devices: 26.1 us -> 67.3 us  [straight(): x = lax.ppermute(x, ('grp', 'seq'), pairs)]
    ppermute x9, waiting for transfers between devices: 35.4 us -> 20.5 us  [along(): return lax.ppermute(x, 'seq', [(s, s ^ 2 * m) for s in range(length)])]
    ppermute x12 -> x0, starting transfers between devices: 14.3 us -> none  [across(): return lax.ppermute(x, 'grp', [(g, g ^ m) for g in range(groups)])]
    ppermute x28 -> x56, waiting for transfers between devices: 40.4 us -> 46.6 us  [straight(): x = lax.ppermute(x, ('grp', 'seq'), pairs)]
    ppermute x9, starting transfers between devices: 14 us -> 19.5 us  [along(): return lax.ppermute(x, 'seq', [(s, s ^ 2 * m) for s in range(length)])]
    pallas_call x19 -> x18, Pallas kernels: 28.8 us -> 29.9 us  [run(): pl.pallas_call(body, in_specs=specs, out_specs=[pl.BlockSpec(memory_space...]
    unnamed x36 -> x32, local copies, waits for them, and re-layouts: 8.13 us -> 7.3 us
  transfers between devices with their start and end apart: 59 -> 70, of which waited for: 31 -> 31; matrix products, arithmetic and copies ran while one was open for 0% -> 0% of each run, Pallas kernels for 10% -> 11%
where the time goes in v5:
time: 211 us; the launch traced here: 210 us
  starting transfers between devices  97.4 us (46%)
  waiting for transfers between devices  74.9 us (35%)
  Pallas kernels  29.9 us (14%)
  local copies, waits for them, and re-layouts  7.3 us (3%)
    ppermute x56, starting transfers between devices, straight(): x = lax.ppermute(x, ('grp', 'seq'), pairs)  67.3 us
    ppermute x56, waiting for transfers between devices, straight(): x = lax.ppermute(x, ('grp', 'seq'), pairs)  46.6 us
    pallas_call x18, Pallas kernels, run(): pl.pallas_call(body, in_specs=specs, out_specs=[pl.BlockSpec(memory_space...  29.9 us
    ppermute x9, waiting for transfers between devices, along(): return lax.ppermute(x, 'seq', [(s, s ^ 2 * m) for s in range(length)])  20.5 us
    ppermute x9, starting transfers between devices, along(): return lax.ppermute(x, 'seq', [(s, s ^ 2 * m) for s in range(length)])  19.5 us
    ppermute x3, starting transfers between devices, later(): return lax.ppermute(x, 'seq', pairs)  10 us
    unnamed x32, local copies, waits for them, and re-layouts  7.3 us
    ppermute x3, waiting for transfers between devices, later(): return lax.ppermute(x, 'seq', pairs)  6.24 us
  transfers between devices with their start and end apart: 70, of which 31 were waited for; matrix products, arithmetic and copies ran while one was open for 0% of the time, Pallas kernels for 11%

profile of v5, /device:TPU:0, one launch (start us, length us, event | category | flops | bytes accessed | tf_op | source)
XLA Modules:
  0.0 210.0 jit_solution(15610220194866364189)
XLA Ops:
  0.0 1.9 shard_map.119
  2.5 1.5 collective-permute-done.pair_ref
  4.1 4.9 %collective-permute-start.1 = (bf16[1024,128]{1,0:T(8,128)(2,1)S(1)}, bf16[1024,128]{1,0:T(8,128)(2,1)S(1)}, u32[]{:S(2)}, u32[]{:S(2)}) collective-permute-start(bf16[1024,128]{1,0:T(8,128)(2,1)S(1)} %add_convert_fusion.refs_0_), channel_id=1, source_target_pairs={{0,2},{1,3},{2,4},{3,5},{4,6},{5,7},{8,10},{9,11},{10,12},{11,13},... | collective-permute-start | bytes 786440 | tf_op jit(solution)/shard_map/ppermute | solution.py:289
  9.0 4.5 %collective-permute-start.2 = (bf16[1024,128]{1,0:T(8,128)(2,1)S(1)}, bf16[1024,128]{1,0:T(8,128)(2,1)S(1)}, u32[]{:S(2)}, u32[]{:S(2)}) collective-permute-start(bf16[1024,128]{1,0:T(8,128)(2,1)S(1)} %add_convert_fusion.refs_0_), channel_id=1, source_target_pairs={{0,4},{1,5},{8,12},{9,13},{16,20},{17,21},{24,28},{25,29}} | collective-permute-start | bytes 786440 | tf_op jit(solution)/shard_map/ppermute | solution.py:289
  13.5 2.2 %collective-permute-done.1.refs_1_.refs_0_ = bf16[1024,128]{1,0:T(8,128)(2,1)S(1)} collective-permute-done((bf16[1024,128]{1,0:T(8,128)(2,1)S(1)}, bf16[1024,128]{1,0:T(8,128)(2,1)S(1)}, u32[]{:S(2)}, u32[]{:S(2)}) %collective-permute-start.1) | collective-permute-done | bytes 262176 | tf_op jit(solution)/shard_map/ppermute | solution.py:289
  16.4 4.1 %collective-permute-done.2.refs_1_ = bf16[1024,128]{1,0:T(8,128)(2,1)S(1)} collective-permute-done((bf16[1024,128]{1,0:T(8,128)(2,1)S(1)}, bf16[1024,128]{1,0:T(8,128)(2,1)S(1)}, u32[]{:S(2)}, u32[]{:S(2)}) %collective-permute-start.2) | collective-permute-done | bytes 262176 | tf_op jit(solution)/shard_map/ppermute | solution.py:289
  20.7 4.2 %shard_map.118 = (f32[128,2048]{1,0:T(8,128)S(1)}, bf16[2048,2048]{1,0:T(8,128)(2,1)S(1)}) custom-call(bf16[128,2048]{1,0:T(8,128)(2,1)} %bitcast.19, bf16[128,2048]{1,0:T(8,128)(2,1)} %bitcast.25, bf16[128,2048]{1,0:T(8,128)(2,1)} %bitcast.27, bf16[2048,2048]{1,0:T(8,128)(2,1)} %w_hbm.1, s32[1]{0:T(128)} %bitcast.core_ref, s32[1]{0:T(128)} %bitcast.4.group_ref, ...), custom_call_target="tpu_custom_call" | custom-call | tf_op jit(solution)/shard_map/pallas_call | solution.py:32
  27.6 2.9 %shard_map.122 = (bf16[128,2048]{1,0:T(8,128)(2,1)S(1)}, bf16[128,2048]{1,0:T(8,128)(2,1)}) custom-call(s32[1]{0:T(128)} %bitcast.core_ref, f32[128,2048]{1,0:T(8,128)S(1)} %get-tuple-element.75.in_ref, bf16[128,2048]{1,0:T(8,128)(2,1)S(1)} %bitcast.20, bf16[1024,128]{1,0:T(8,128)(2,1)S(1)} %shard_map.121.mine_ref, bf16[1024,128]{1,0:T(8,128)(2,1)S(1)} %copy-done.11, ...), custom_call_target="tpu_custom_call" | custom-call | tf_op jit(solution)/shard_map/pallas_call | solution.py:32
  31.3 7.1 %collective-permute-start.54 = (bf16[128,2048]{1,0:T(8,128)(2,1)}, bf16[128,2048]{1,0:T(8,128)(2,1)}, u32[]{:S(2)}, u32[]{:S(2)}) collective-permute-start(bf16[128,2048]{1,0:T(8,128)(2,1)} %get-tuple-element.77.own_ref), channel_id=1, source_target_pairs={{0,2},{1,3},{2,0},{3,1},{4,6},{5,7},{6,4},{7,5},{8,10},{9,11},{10,... | collective-permute-start | bytes 1572872 | tf_op jit(solution)/shard_map/ppermute | solution.py:271
  38.4 3.4 %collective-permute-start.22 = (bf16[128,2048]{1,0:T(8,128)(2,1)}, bf16[128,2048]{1,0:T(8,128)(2,1)}, u32[]{:S(2)}, u32[]{:S(2)}) collective-permute-start(bf16[128,2048]{1,0:T(8,128)(2,1)} %get-tuple-element.77.own_ref), channel_id=1, source_target_pairs={{0,4},{1,5},{2,6},{3,7},{4,0},{5,1},{6,2},{7,3},{8,12},{9,13},{10,... | collective-permute-start | bytes 1572872 | tf_op jit(solution)/shard_map/ppermute | solution.py:271
  42.0 4.3 %collective-permute-start.7 = (f32[32,128]{1,0:T(8,128)S(1)}, f32[32,128]{1,0:T(8,128)S(1)}, u32[]{:S(2)}, u32[]{:S(2)}) collective-permute-start(f32[32,128]{1,0:T(8,128)S(1)} %select_reduce_fusion.refs_0_), channel_id=1, source_target_pairs={{0,6},{1,7},{2,4},{3,5},{4,2},{5,3},{6,0},{7,1},{8,14},{9,15},{10,... | collective-permute-start | bytes 49160 | tf_op jit(solution)/shard_map/ppermute | solution.py:271
  46.3 16.2 %collective-permute-done.5.refs_1_ = f32[32,128]{1,0:T(8,128)S(1)} collective-permute-done((f32[32,128]{1,0:T(8,128)S(1)}, f32[32,128]{1,0:T(8,128)S(1)}, u32[]{:S(2)}, u32[]{:S(2)}) %collective-permute-start.5) | collective-permute-done | bytes 16416 | tf_op jit(solution)/shard_map/ppermute | solution.py:271
  62.5 4.3 %collective-permute-done.6.refs_2_ = f32[32,128]{1,0:T(8,128)S(1)} collective-permute-done((f32[32,128]{1,0:T(8,128)S(1)}, f32[32,128]{1,0:T(8,128)S(1)}, u32[]{:S(2)}, u32[]{:S(2)}) %collective-permute-start.6) | collective-permute-done | bytes 16416 | tf_op jit(solution)/shard_map/ppermute | solution.py:271
  67.0 1.5 shard_map.124
  68.5 2.5 %collective-permute-start.10 = (bf16[40,2048]{1,0:T(8,128)(2,1)S(1)}, bf16[40,2048]{1,0:T(8,128)(2,1)S(1)}, u32[]{:S(2)}, u32[]{:S(2)}) collective-permute-start(bf16[40,2048]{1,0:T(8,128)(2,1)S(1)} %get-tuple-element.82), channel_id=1, source_target_pairs={{0,24},{1,25},{2,26},{3,27},{4,28},{5,29},{6,30},{7,31},{8,16},{9,... | collective-permute-start | bytes 491528 | tf_op jit(solution)/shard_map/ppermute | solution.py:283
  71.0 1.5 shard_map.132
  73.7 2.4 %collective-permute-start.57 = (bf16[40,2048]{1,0:T(8,128)(2,1)S(1)}, bf16[40,2048]{1,0:T(8,128)(2,1)S(1)}, u32[]{:S(2)}, u32[]{:S(2)}) collective-permute-start(bf16[40,2048]{1,0:T(8,128)(2,1)S(1)} %get-tuple-element.132), channel_id=1, source_target_pairs={{0,24},{1,25},{2,26},{3,27},{4,28},{5,29},{6,30},{7,31},{8,16},{9,... | collective-permute-start | bytes 491528 | tf_op jit(solution)/shard_map/ppermute | solution.py:283
  76.1 1.5 shard_map.128
  79.7 1.9 collective-permute-start.40
  83.1 2.2 %collective-permute-start.42 = (bf16[40,2048]{1,0:T(8,128)(2,1)S(1)}, bf16[40,2048]{1,0:T(8,128)(2,1)S(1)}, u32[]{:S(2)}, u32[]{:S(2)}) collective-permute-start(bf16[40,2048]{1,0:T(8,128)(2,1)S(1)} %get-tuple-element.118), channel_id=1, source_target_pairs={{0,9},{1,8},{2,11},{3,10},{4,13},{5,12},{6,15},{7,14},{8,1},{9,0},... | collective-permute-start | bytes 491528 | tf_op jit(solution)/shard_map/ppermute | solution.py:283
  85.4 1.3 collective-permute-done.38.refs_1_
  88.7 1.5 collective-permute-done.40.refs_3_
  90.3 2.9 %collective-permute-start.58 = (bf16[40,2048]{1,0:T(8,128)(2,1)S(1)}, bf16[40,2048]{1,0:T(8,128)(2,1)S(1)}, u32[]{:S(2)}, u32[]{:S(2)}) collective-permute-start(bf16[40,2048]{1,0:T(8,128)(2,1)S(1)} %get-tuple-element.133), channel_id=1, source_target_pairs={{0,1},{1,0},{2,3},{3,2},{4,5},{5,4},{6,7},{7,6},{8,9},{9,8},{10,11... | collective-permute-start | bytes 491528 | tf_op jit(solution)/shard_map/ppermute | solution.py:283
  94.2 2.9 %collective-permute-done.44.refs_7_ = bf16[40,2048]{1,0:T(8,128)(2,1)S(1)} collective-permute-done((bf16[40,2048]{1,0:T(8,128)(2,1)S(1)}, bf16[40,2048]{1,0:T(8,128)(2,1)S(1)}, u32[]{:S(2)}, u32[]{:S(2)}) %collective-permute-start.44) | collective-permute-done | bytes 163872 | tf_op jit(solution)/shard_map/ppermute | solution.py:283
  97.1 1.9 collective-permute-start.61
  99.0 1.9 copy-done.1
  100.9 1.9 copy-done.3
  102.8 3.2 %shard_map.129 = (bf16[40,2048]{1,0:T(8,128)(2,1)S(1)}, bf16[40,2048]{1,0:T(8,128)(2,1)S(1)}, bf16[40,2048]{1,0:T(8,128)(2,1)S(1)}, bf16[40,2048]{1,0:T(8,128)(2...) custom-call(bf16[40,2048]{1,0:T(8,128)(2,1)S(1)} %get-tuple-element., ...), custom_call_target="tpu_custom_call" | custom-call | tf_op jit(solution)/shard_map/pallas_call | solution.py:32
  106.7 1.5 collective-permute-start.46
  108.2 1.4 collective-permute-start.47
  109.6 3.6 %collective-permute-done.45.refs_1_ = bf16[40,2048]{1,0:T(8,128)(2,1)S(1)} collective-permute-done((bf16[40,2048]{1,0:T(8,128)(2,1)S(1)}, bf16[40,2048]{1,0:T(8,128)(2,1)S(1)}, u32[]{:S(2)}, u32[]{:S(2)}) %collective-permute-start.45) | collective-permute-done | bytes 163872 | tf_op jit(solution)/shard_map/ppermute | solution.py:283
  113.2 2.3 %collective-permute-done.46.refs_2_ = bf16[40,2048]{1,0:T(8,128)(2,1)S(1)} collective-permute-done((bf16[40,2048]{1,0:T(8,128)(2,1)S(1)}, bf16[40,2048]{1,0:T(8,128)(2,1)S(1)}, u32[]{:S(2)}, u32[]{:S(2)}) %collective-permute-start.46) | collective-permute-done | bytes 163872 | tf_op jit(solution)/shard_map/ppermute | solution.py:283
  115.5 1.8 collective-permute-done.47.refs_3_
  117.3 1.8 collective-permute-start.51
  119.2 3.2 %shard_map.133 = (bf16[40,2048]{1,0:T(8,128)(2,1)S(1)}, bf16[40,2048]{1,0:T(8,128)(2,1)S(1)}, bf16[40,2048]{1,0:T(8,128)(2,1)S(1)}, bf16[40,2048]{1,0:T(8,128)(2...) custom-call(bf16[40,2048]{1,0:T(8,128)(2,1)S(1)} %get-tuple-element., ...), custom_call_target="tpu_custom_call" | custom-call | tf_op jit(solution)/shard_map/pallas_call | solution.py:32
  123.1 1.4 collective-permute-start.63
  125.0 3.3 %collective-permute-start.64 = (bf16[40,2048]{1,0:T(8,128)(2,1)S(1)}, bf16[40,2048]{1,0:T(8,128)(2,1)S(1)}, u32[]{:S(2)}, u32[]{:S(2)}) collective-permute-start(bf16[40,2048]{1,0:T(8,128)(2,1)S(1)} %get-tuple-element.140), channel_id=1, source_target_pairs={{0,24},{1,25},{2,26},{3,27},{4,28},{5,29},{6,30},{7,31},{8,16},{9,... | collective-permute-start | bytes 491528 | tf_op jit(solution)/shard_map/ppermute | solution.py:283
  129.4 1.8 collective-permute-start.25
  131.2 4.1 %collective-permute-start.26 = (bf16[40,2048]{1,0:T(8,128)(2,1)S(1)}, bf16[40,2048]{1,0:T(8,128)(2,1)S(1)}, u32[]{:S(2)}, u32[]{:S(2)}) collective-permute-start(bf16[40,2048]{1,0:T(8,128)(2,1)S(1)} %get-tuple-element.100), channel_id=1, source_target_pairs={{0,24},{1,25},{2,26},{3,27},{4,28},{5,29},{6,30},{7,31},{8,16},{9,... | collective-permute-start | bytes 491528 | tf_op jit(solution)/shard_map/ppermute | solution.py:283
  136.4 1.2 collective-permute-done.25.refs_2_
  137.6 1.8 collective-permute-start.29
  139.4 1.4 collective-permute-done.26.refs_3_
  142.9 3.0 %collective-permute-start.67 = (bf16[40,2048]{1,0:T(8,128)(2,1)S(1)}, bf16[40,2048]{1,0:T(8,128)(2,1)S(1)}, u32[]{:S(2)}, u32[]{:S(2)}) collective-permute-start(bf16[40,2048]{1,0:T(8,128)(2,1)S(1)} %get-tuple-element.143), channel_id=1, source_target_pairs={{0,17},{1,16},{2,19},{3,18},{4,21},{5,20},{6,23},{7,22},{8,25},{9,... | collective-permute-start | bytes 491528 | tf_op jit(solution)/shard_map/ppermute | solution.py:283
  145.9 1.8 collective-permute-done.30.refs_7_
  147.7 4.0 %collective-permute-start.68 = (bf16[40,2048]{1,0:T(8,128)(2,1)S(1)}, bf16[40,2048]{1,0:T(8,128)(2,1)S(1)}, u32[]{:S(2)}, u32[]{:S(2)}) collective-permute-start(bf16[40,2048]{1,0:T(8,128)(2,1)S(1)} %get-tuple-element.144), channel_id=1, source_target_pairs={{0,25},{1,24},{2,27},{3,26},{4,29},{5,28},{6,31},{7,30},{8,17},{9,... | collective-permute-start | bytes 491528 | tf_op jit(solution)/shard_map/ppermute | solution.py:283
  151.6 3.2 %shard_map.127 = (bf16[40,2048]{1,0:T(8,128)(2,1)S(1)}, bf16[40,2048]{1,0:T(8,128)(2,1)S(1)}, bf16[40,2048]{1,0:T(8,128)(2,1)S(1)}, bf16[40,2048]{1,0:T(8,128)(2...) custom-call(bf16[40,2048]{1,0:T(8,128)(2,1)S(1)} %get-tuple-element., ...), custom_call_target="tpu_custom_call" | custom-call | tf_op jit(solution)/shard_map/pallas_call | solution.py:32
  155.5 1.8 collective-permute-start.32
  157.3 4.9 %collective-permute-start.33 = (bf16[40,2048]{1,0:T(8,128)(2,1)S(1)}, bf16[40,2048]{1,0:T(8,128)(2,1)S(1)}, u32[]{:S(2)}, u32[]{:S(2)}) collective-permute-start(bf16[40,2048]{1,0:T(8,128)(2,1)S(1)} %get-tuple-element.108), channel_id=1, source_target_pairs={{0,24},{1,25},{2,26},{3,27},{4,28},{5,29},{6,30},{7,31},{8,16},{9,... | collective-permute-start | bytes 491528 | tf_op jit(solution)/shard_map/ppermute | solution.py:283
  162.6 2.9 %collective-permute-start.37 = (bf16[40,2048]{1,0:T(8,128)(2,1)S(1)}, bf16[40,2048]{1,0:T(8,128)(2,1)S(1)}, u32[]{:S(2)}, u32[]{:S(2)}) collective-permute-start(bf16[40,2048]{1,0:T(8,128)(2,1)S(1)} %get-tuple-element.112), channel_id=1, source_target_pairs={{0,25},{1,24},{2,27},{3,26},{4,29},{5,28},{6,31},{7,30},{8,17},{9,... | collective-permute-start | bytes 491528 | tf_op jit(solution)/shard_map/ppermute | solution.py:283
  165.5 1.7 collective-permute-done.33.refs_3_
  167.6 2.9 %collective-permute-start.13 = (bf16[40,2048]{1,0:T(8,128)(2,1)S(1)}, bf16[40,2048]{1,0:T(8,128)(2,1)S(1)}, u32[]{:S(2)}, u32[]{:S(2)}) collective-permute-start(bf16[40,2048]{1,0:T(8,128)(2,1)S(1)} %get-tuple-element.85), channel_id=1, source_target_pairs={{0,17},{1,16},{2,19},{3,18},{4,21},{5,20},{6,23},{7,22},{8,25},{9,... | collective-permute-start | bytes 491528 | tf_op jit(solution)/shard_map/ppermute | solution.py:283
  172.5 1.4 collective-permute-done.37.refs_7_
  175.0 2.4 %collective-permute-done.12.refs_5_ = bf16[40,2048]{1,0:T(8,128)(2,1)S(1)} collective-permute-done((bf16[40,2048]{1,0:T(8,128)(2,1)S(1)}, bf16[40,2048]{1,0:T(8,128)(2,1)S(1)}, u32[]{:S(2)}, u32[]{:S(2)}) %collective-permute-start.12) | collective-permute-done | bytes 163872 | tf_op jit(solution)/shard_map/ppermute | solution.py:283
  178.1 2.3 %collective-permute-start.53 = (bf16[128,2048]{1,0:T(8,128)(2,1)S(1)}, bf16[128,2048]{1,0:T(8,128)(2,1)S(1)}, u32[]{:S(2)}, u32[]{:S(2)}) collective-permute-start(bf16[128,2048]{1,0:T(8,128)(2,1)S(1)} %shard_map.131), channel_id=1, source_target_pairs={{0,6},{1,7},{2,4},{3,5},{4,2},{5,3},{6,0},{7,1},{8,14},{9,15},{10,... | collective-permute-start | bytes 1572872 | tf_op jit(solution)/shard_map/ppermute | solution.py:271
  180.9 2.7 %collective-permute-done.8.refs_1_ = bf16[40,2048]{1,0:T(8,128)(2,1)S(1)} collective-permute-done((bf16[40,2048]{1,0:T(8,128)(2,1)S(1)}, bf16[40,2048]{1,0:T(8,128)(2,1)S(1)}, u32[]{:S(2)}, u32[]{:S(2)}) %collective-permute-start.8) | collective-permute-done | bytes 163872 | tf_op jit(solution)/shard_map/ppermute | solution.py:283
  184.2 3.2 %shard_map.125 = (bf16[40,2048]{1,0:T(8,128)(2,1)S(1)}, bf16[40,2048]{1,0:T(8,128)(2,1)S(1)}, bf16[40,2048]{1,0:T(8,128)(2,1)S(1)}, bf16[40,2048]{1,0:T(8,128)(2...) custom-call(bf16[40,2048]{1,0:T(8,128)(2,1)S(1)} %get-tuple-element., ...), custom_call_target="tpu_custom_call" | custom-call | tf_op jit(solution)/shard_map/pallas_call | solution.py:32
  187.4 1.9 collective-permute-start.15
  189.4 1.3 collective-permute-start.16
  191.0 3.6 %collective-permute-done.15.refs_1_ = bf16[40,2048]{1,0:T(8,128)(2,1)S(1)} collective-permute-done((bf16[40,2048]{1,0:T(8,128)(2,1)S(1)}, bf16[40,2048]{1,0:T(8,128)(2,1)S(1)}, u32[]{:S(2)}, u32[]{:S(2)}) %collective-permute-start.15) | collective-permute-done | bytes 163872 | tf_op jit(solution)/shard_map/ppermute | solution.py:283
  194.6 3.8 %collective-permute-done.16.refs_2_ = bf16[40,2048]{1,0:T(8,128)(2,1)S(1)} collective-permute-done((bf16[40,2048]{1,0:T(8,128)(2,1)S(1)}, bf16[40,2048]{1,0:T(8,128)(2,1)S(1)}, u32[]{:S(2)}, u32[]{:S(2)}) %collective-permute-start.16) | collective-permute-done | bytes 163872 | tf_op jit(solution)/shard_map/ppermute | solution.py:283
  198.4 1.8 collective-permute-start.20
  201.4 1.7 collective-permute-done.19.refs_5_
  203.1 4.5 %collective-permute-done.20.refs_6_ = bf16[40,2048]{1,0:T(8,128)(2,1)S(1)} collective-permute-done((bf16[40,2048]{1,0:T(8,128)(2,1)S(1)}, bf16[40,2048]{1,0:T(8,128)(2,1)S(1)}, u32[]{:S(2)}, u32[]{:S(2)}) %collective-permute-start.20) | collective-permute-done | bytes 163872 | tf_op jit(solution)/shard_map/ppermute | solution.py:283
  208.7 1.3 shard_map.135
  (130 shorter events, 28.4 us)
Async XLA Ops:
  4.1 11.5 %collective-permute-start.1 = (bf16[1024,128]{1,0:T(8,128)(2,1)S(1)}, bf16[1024,128]{1,0:T(8,128)(2,1)S(1)}, u32[]{:S(2)}, u32[]{:S(2)}) collective-permute-start(bf16[1024,128]{1,0:T(8,128)(2,1)S(1)} %add_convert_fusion.refs_0_), channel_id=1, source_target_pairs={{0,2},{1,3},{2,4},{3,5},{4,6},{5,7},{8,10},{9,11},{10,12},{11,13},... | collective-permute-start | bytes 786440 | tf_op jit(solution)/shard_map/ppermute | solution.py:289
  9.0 11.5 %collective-permute-start.2 = (bf16[1024,128]{1,0:T(8,128)(2,1)S(1)}, bf16[1024,128]{1,0:T(8,128)(2,1)S(1)}, u32[]{:S(2)}, u32[]{:S(2)}) collective-permute-start(bf16[1024,128]{1,0:T(8,128)(2,1)S(1)} %add_convert_fusion.refs_0_), channel_id=1, source_target_pairs={{0,4},{1,5},{8,12},{9,13},{16,20},{17,21},{24,28},{25,29}} | collective-permute-start | bytes 786440 | tf_op jit(solution)/shard_map/ppermute | solution.py:289
  31.3 39.7 %collective-permute-start.54 = (bf16[128,2048]{1,0:T(8,128)(2,1)}, bf16[128,2048]{1,0:T(8,128)(2,1)}, u32[]{:S(2)}, u32[]{:S(2)}) collective-permute-start(bf16[128,2048]{1,0:T(8,128)(2,1)} %get-tuple-element.77.own_ref), channel_id=1, source_target_pairs={{0,2},{1,3},{2,0},{3,1},{4,6},{5,7},{6,4},{7,5},{8,10},{9,11},{10,... | collective-permute-start | bytes 1572872 | tf_op jit(solution)/shard_map/ppermute | solution.py:271
  38.4 37.7 %collective-permute-start.22 = (bf16[128,2048]{1,0:T(8,128)(2,1)}, bf16[128,2048]{1,0:T(8,128)(2,1)}, u32[]{:S(2)}, u32[]{:S(2)}) collective-permute-start(bf16[128,2048]{1,0:T(8,128)(2,1)} %get-tuple-element.77.own_ref), channel_id=1, source_target_pairs={{0,4},{1,5},{2,6},{3,7},{4,0},{5,1},{6,2},{7,3},{8,12},{9,13},{10,... | collective-permute-start | bytes 1572872 | tf_op jit(solution)/shard_map/ppermute | solution.py:271
  41.9 20.6 %collective-permute-start.5 = (f32[32,128]{1,0:T(8,128)S(1)}, f32[32,128]{1,0:T(8,128)S(1)}, u32[]{:S(2)}, u32[]{:S(2)}) collective-permute-start(f32[32,128]{1,0:T(8,128)S(1)} %select_reduce_fusion.refs_0_), channel_id=1, source_target_pairs={{0,2},{1,3},{2,0},{3,1},{4,6},{5,7},{6,4},{7,5},{8,10},{9,11},{10,... | collective-permute-start | bytes 49160 | tf_op jit(solution)/shard_map/ppermute | solution.py:271
  42.0 24.9 %collective-permute-start.6 = (f32[32,128]{1,0:T(8,128)S(1)}, f32[32,128]{1,0:T(8,128)S(1)}, u32[]{:S(2)}, u32[]{:S(2)}) collective-permute-start(f32[32,128]{1,0:T(8,128)S(1)} %select_reduce_fusion.refs_0_), channel_id=1, source_target_pairs={{0,4},{1,5},{2,6},{3,7},{4,0},{5,1},{6,2},{7,3},{8,12},{9,13},{10,... | collective-permute-start | bytes 49160 | tf_op jit(solution)/shard_map/ppermute | solution.py:271
  42.0 24.8 %collective-permute-start.7 = (f32[32,128]{1,0:T(8,128)S(1)}, f32[32,128]{1,0:T(8,128)S(1)}, u32[]{:S(2)}, u32[]{:S(2)}) collective-permute-start(f32[32,128]{1,0:T(8,128)S(1)} %select_reduce_fusion.refs_0_), channel_id=1, source_target_pairs={{0,6},{1,7},{2,4},{3,5},{4,2},{5,3},{6,0},{7,1},{8,14},{9,15},{10,... | collective-permute-start | bytes 49160 | tf_op jit(solution)/shard_map/ppermute | solution.py:271
  68.5 9.7 %collective-permute-start.10 = (bf16[40,2048]{1,0:T(8,128)(2,1)S(1)}, bf16[40,2048]{1,0:T(8,128)(2,1)S(1)}, u32[]{:S(2)}, u32[]{:S(2)}) collective-permute-start(bf16[40,2048]{1,0:T(8,128)(2,1)S(1)} %get-tuple-element.82), channel_id=1, source_target_pairs={{0,24},{1,25},{2,26},{3,27},{4,28},{5,29},{6,30},{7,31},{8,16},{9,... | collective-permute-start | bytes 491528 | tf_op jit(solution)/shard_map/ppermute | solution.py:283
  72.5 7.1 %collective-permute-start.55 = (bf16[40,2048]{1,0:T(8,128)(2,1)S(1)}, bf16[40,2048]{1,0:T(8,128)(2,1)S(1)}, u32[]{:S(2)}, u32[]{:S(2)}) collective-permute-start(bf16[40,2048]{1,0:T(8,128)(2,1)S(1)} %get-tuple-element.130), channel_id=1, source_target_pairs={{0,8},{1,9},{2,10},{3,11},{4,12},{5,13},{6,14},{7,15},{8,0},{9,1},... | collective-permute-start | bytes 491528 | tf_op jit(solution)/shard_map/ppermute | solution.py:283
  73.1 9.1 %collective-permute-start.56 = (bf16[40,2048]{1,0:T(8,128)(2,1)S(1)}, bf16[40,2048]{1,0:T(8,128)(2,1)S(1)}, u32[]{:S(2)}, u32[]{:S(2)}) collective-permute-start(bf16[40,2048]{1,0:T(8,128)(2,1)S(1)} %get-tuple-element.131), channel_id=1, source_target_pairs={{0,16},{1,17},{2,18},{3,19},{4,20},{5,21},{6,22},{7,23},{8,24},{9,... | collective-permute-start | bytes 491528 | tf_op jit(solution)/shard_map/ppermute | solution.py:283
  73.7 9.5 %collective-permute-start.57 = (bf16[40,2048]{1,0:T(8,128)(2,1)S(1)}, bf16[40,2048]{1,0:T(8,128)(2,1)S(1)}, u32[]{:S(2)}, u32[]{:S(2)}) collective-permute-start(bf16[40,2048]{1,0:T(8,128)(2,1)S(1)} %get-tuple-element.132), channel_id=1, source_target_pairs={{0,24},{1,25},{2,26},{3,27},{4,28},{5,29},{6,30},{7,31},{8,16},{9,... | collective-permute-start | bytes 491528 | tf_op jit(solution)/shard_map/ppermute | solution.py:283
  77.6 9.1 %collective-permute-start.38 = (bf16[40,2048]{1,0:T(8,128)(2,1)S(1)}, bf16[40,2048]{1,0:T(8,128)(2,1)S(1)}, u32[]{:S(2)}, u32[]{:S(2)}) collective-permute-start(bf16[40,2048]{1,0:T(8,128)(2,1)S(1)} %get-tuple-element.114), channel_id=1, source_target_pairs={{0,8},{1,9},{2,10},{3,11},{4,12},{5,13},{6,14},{7,15},{8,0},{9,1},... | collective-permute-start | bytes 491528 | tf_op jit(solution)/shard_map/ppermute | solution.py:283
  78.2 9.6 %collective-permute-start.39 = (bf16[40,2048]{1,0:T(8,128)(2,1)S(1)}, bf16[40,2048]{1,0:T(8,128)(2,1)S(1)}, u32[]{:S(2)}, u32[]{:S(2)}) collective-permute-start(bf16[40,2048]{1,0:T(8,128)(2,1)S(1)} %get-tuple-element.115), channel_id=1, source_target_pairs={{0,16},{1,17},{2,18},{3,19},{4,20},{5,21},{6,22},{7,23},{8,24},{9,... | collective-permute-start | bytes 491528 | tf_op jit(solution)/shard_map/ppermute | solution.py:283
  79.7 10.5 %collective-permute-start.40 = (bf16[40,2048]{1,0:T(8,128)(2,1)S(1)}, bf16[40,2048]{1,0:T(8,128)(2,1)S(1)}, u32[]{:S(2)}, u32[]{:S(2)}) collective-permute-start(bf16[40,2048]{1,0:T(8,128)(2,1)S(1)} %get-tuple-element.116), channel_id=1, source_target_pairs={{0,24},{1,25},{2,26},{3,27},{4,28},{5,29},{6,30},{7,31},{8,16},{9,... | collective-permute-start | bytes 491528 | tf_op jit(solution)/shard_map/ppermute | solution.py:283
  82.2 8.0 %collective-permute-start.41 = (bf16[40,2048]{1,0:T(8,128)(2,1)S(1)}, bf16[40,2048]{1,0:T(8,128)(2,1)S(1)}, u32[]{:S(2)}, u32[]{:S(2)}) collective-permute-start(bf16[40,2048]{1,0:T(8,128)(2,1)S(1)} %get-tuple-element.117), channel_id=1, source_target_pairs={{0,1},{1,0},{2,3},{3,2},{4,5},{5,4},{6,7},{7,6},{8,9},{9,8},{10,11... | collective-permute-start | bytes 491528 | tf_op jit(solution)/shard_map/ppermute | solution.py:283
  83.1 10.0 %collective-permute-start.42 = (bf16[40,2048]{1,0:T(8,128)(2,1)S(1)}, bf16[40,2048]{1,0:T(8,128)(2,1)S(1)}, u32[]{:S(2)}, u32[]{:S(2)}) collective-permute-start(bf16[40,2048]{1,0:T(8,128)(2,1)S(1)} %get-tuple-element.118), channel_id=1, source_target_pairs={{0,9},{1,8},{2,11},{3,10},{4,13},{5,12},{6,15},{7,14},{8,1},{9,0},... | collective-permute-start | bytes 491528 | tf_op jit(solution)/shard_map/ppermute | solution.py:283
  86.7 6.9 %collective-permute-start.43 = (bf16[40,2048]{1,0:T(8,128)(2,1)S(1)}, bf16[40,2048]{1,0:T(8,128)(2,1)S(1)}, u32[]{:S(2)}, u32[]{:S(2)}) collective-permute-start(bf16[40,2048]{1,0:T(8,128)(2,1)S(1)} %get-tuple-element.119), channel_id=1, source_target_pairs={{0,17},{1,16},{2,19},{3,18},{4,21},{5,20},{6,23},{7,22},{8,25},{9,... | collective-permute-start | bytes 491528 | tf_op jit(solution)/shard_map/ppermute | solution.py:283
  87.8 35.3 %collective-permute-start.23 = (bf16[128,2048]{1,0:T(8,128)(2,1)}, bf16[128,2048]{1,0:T(8,128)(2,1)S(1)}, u32[]{:S(2)}, u32[]{:S(2)}) collective-permute-start(bf16[128,2048]{1,0:T(8,128)(2,1)} %collective-permute-done.22.own_ref), channel_id=1, source_target_pairs={{0,2},{1,3},{2,0},{3,1},{4,6},{5,7},{6,4},{7,5},{8,10},{9,11},{10,... | collective-permute-start | bytes 1572872 | tf_op jit(solution)/shard_map/ppermute | solution.py:271
  90.2 6.9 %collective-permute-start.44 = (bf16[40,2048]{1,0:T(8,128)(2,1)S(1)}, bf16[40,2048]{1,0:T(8,128)(2,1)S(1)}, u32[]{:S(2)}, u32[]{:S(2)}) collective-permute-start(bf16[40,2048]{1,0:T(8,128)(2,1)S(1)} %get-tuple-element.120), channel_id=1, source_target_pairs={{0,25},{1,24},{2,27},{3,26},{4,29},{5,28},{6,31},{7,30},{8,17},{9,... | collective-permute-start | bytes 491528 | tf_op jit(solution)/shard_map/ppermute | solution.py:283
  90.3 15.8 %collective-permute-start.58 = (bf16[40,2048]{1,0:T(8,128)(2,1)S(1)}, bf16[40,2048]{1,0:T(8,128)(2,1)S(1)}, u32[]{:S(2)}, u32[]{:S(2)}) collective-permute-start(bf16[40,2048]{1,0:T(8,128)(2,1)S(1)} %get-tuple-element.133), channel_id=1, source_target_pairs={{0,1},{1,0},{2,3},{3,2},{4,5},{5,4},{6,7},{7,6},{8,9},{9,8},{10,11... | collective-permute-start | bytes 491528 | tf_op jit(solution)/shard_map/ppermute | solution.py:283
  93.1 13.5 %collective-permute-start.59 = (bf16[40,2048]{1,0:T(8,128)(2,1)S(1)}, bf16[40,2048]{1,0:T(8,128)(2,1)S(1)}, u32[]{:S(2)}, u32[]{:S(2)}) collective-permute-start(bf16[40,2048]{1,0:T(8,128)(2,1)S(1)} %get-tuple-element.134), channel_id=1, source_target_pairs={{0,9},{1,8},{2,11},{3,10},{4,13},{5,12},{6,15},{7,14},{8,1},{9,0},... | collective-permute-start | bytes 491528 | tf_op jit(solution)/shard_map/ppermute | solution.py:283
  93.6 14.6 %collective-permute-start.60 = (bf16[40,2048]{1,0:T(8,128)(2,1)S(1)}, bf16[40,2048]{1,0:T(8,128)(2,1)S(1)}, u32[]{:S(2)}, u32[]{:S(2)}) collective-permute-start(bf16[40,2048]{1,0:T(8,128)(2,1)S(1)} %get-tuple-element.135), channel_id=1, source_target_pairs={{0,17},{1,16},{2,19},{3,18},{4,21},{5,20},{6,23},{7,22},{8,25},{9,... | collective-permute-start | bytes 491528 | tf_op jit(solution)/shard_map/ppermute | solution.py:283
  97.1 12.5 %collective-permute-start.61 = (bf16[40,2048]{1,0:T(8,128)(2,1)S(1)}, bf16[40,2048]{1,0:T(8,128)(2,1)S(1)}, u32[]{:S(2)}, u32[]{:S(2)}) collective-permute-start(bf16[40,2048]{1,0:T(8,128)(2,1)S(1)} %get-tuple-element.136), channel_id=1, source_target_pairs={{0,25},{1,24},{2,27},{3,26},{4,29},{5,28},{6,31},{7,30},{8,17},{9,... | collective-permute-start | bytes 491528 | tf_op jit(solution)/shard_map/ppermute | solution.py:283
  106.1 7.1 %collective-permute-start.45 = (bf16[40,2048]{1,0:T(8,128)(2,1)S(1)}, bf16[40,2048]{1,0:T(8,128)(2,1)S(1)}, u32[]{:S(2)}, u32[]{:S(2)}) collective-permute-start(bf16[40,2048]{1,0:T(8,128)(2,1)S(1)} %get-tuple-element.122), channel_id=1, source_target_pairs={{0,8},{1,9},{2,10},{3,11},{4,12},{5,13},{6,14},{7,15},{8,0},{9,1},... | collective-permute-start | bytes 491528 | tf_op jit(solution)/shard_map/ppermute | solution.py:283
  106.7 8.8 %collective-permute-start.46 = (bf16[40,2048]{1,0:T(8,128)(2,1)S(1)}, bf16[40,2048]{1,0:T(8,128)(2,1)S(1)}, u32[]{:S(2)}, u32[]{:S(2)}) collective-permute-start(bf16[40,2048]{1,0:T(8,128)(2,1)S(1)} %get-tuple-element.123), channel_id=1, source_target_pairs={{0,16},{1,17},{2,18},{3,19},{4,20},{5,21},{6,22},{7,23},{8,24},{9,... | collective-permute-start | bytes 491528 | tf_op jit(solution)/shard_map/ppermute | solution.py:283
  108.2 9.1 %collective-permute-start.47 = (bf16[40,2048]{1,0:T(8,128)(2,1)S(1)}, bf16[40,2048]{1,0:T(8,128)(2,1)S(1)}, u32[]{:S(2)}, u32[]{:S(2)}) collective-permute-start(bf16[40,2048]{1,0:T(8,128)(2,1)S(1)} %get-tuple-element.124), channel_id=1, source_target_pairs={{0,24},{1,25},{2,26},{3,27},{4,28},{5,29},{6,30},{7,31},{8,16},{9,... | collective-permute-start | bytes 491528 | tf_op jit(solution)/shard_map/ppermute | solution.py:283
  109.6 9.4 %collective-permute-start.48 = (bf16[40,2048]{1,0:T(8,128)(2,1)S(1)}, bf16[40,2048]{1,0:T(8,128)(2,1)S(1)}, u32[]{:S(2)}, u32[]{:S(2)}) collective-permute-start(bf16[40,2048]{1,0:T(8,128)(2,1)S(1)} %get-tuple-element.125), channel_id=1, source_target_pairs={{0,1},{1,0},{2,3},{3,2},{4,5},{5,4},{6,7},{7,6},{8,9},{9,8},{10,11... | collective-permute-start | bytes 491528 | tf_op jit(solution)/shard_map/ppermute | solution.py:283
  113.2 9.2 %collective-permute-start.49 = (bf16[40,2048]{1,0:T(8,128)(2,1)S(1)}, bf16[40,2048]{1,0:T(8,128)(2,1)S(1)}, u32[]{:S(2)}, u32[]{:S(2)}) collective-permute-start(bf16[40,2048]{1,0:T(8,128)(2,1)S(1)} %get-tuple-element.126), channel_id=1, source_target_pairs={{0,9},{1,8},{2,11},{3,10},{4,13},{5,12},{6,15},{7,14},{8,1},{9,0},... | collective-permute-start | bytes 491528 | tf_op jit(solution)/shard_map/ppermute | solution.py:283
  115.5 9.5 %collective-permute-start.50 = (bf16[40,2048]{1,0:T(8,128)(2,1)S(1)}, bf16[40,2048]{1,0:T(8,128)(2,1)S(1)}, u32[]{:S(2)}, u32[]{:S(2)}) collective-permute-start(bf16[40,2048]{1,0:T(8,128)(2,1)S(1)} %get-tuple-element.127), channel_id=1, source_target_pairs={{0,17},{1,16},{2,19},{3,18},{4,21},{5,20},{6,23},{7,22},{8,25},{9,... | collective-permute-start | bytes 491528 | tf_op jit(solution)/shard_map/ppermute | solution.py:283
  117.3 11.0 %collective-permute-start.51 = (bf16[40,2048]{1,0:T(8,128)(2,1)S(1)}, bf16[40,2048]{1,0:T(8,128)(2,1)S(1)}, u32[]{:S(2)}, u32[]{:S(2)}) collective-permute-start(bf16[40,2048]{1,0:T(8,128)(2,1)S(1)} %get-tuple-element.128), channel_id=1, source_target_pairs={{0,25},{1,24},{2,27},{3,26},{4,29},{5,28},{6,31},{7,30},{8,17},{9,... | collective-permute-start | bytes 491528 | tf_op jit(solution)/shard_map/ppermute | solution.py:283
  119.1 9.7 %collective-permute-start.11 = (bf16[40,2048]{1,0:T(8,128)(2,1)S(1)}, bf16[40,2048]{1,0:T(8,128)(2,1)S(1)}, u32[]{:S(2)}, u32[]{:S(2)}) collective-permute-start(bf16[40,2048]{1,0:T(8,128)(2,1)S(1)} %get-tuple-element.83), channel_id=1, source_target_pairs={{0,1},{1,0},{2,3},{3,2},{4,5},{5,4},{6,7},{7,6},{8,9},{9,8},{10,11... | collective-permute-start | bytes 491528 | tf_op jit(solution)/shard_map/ppermute | solution.py:283
  122.4 7.0 %collective-permute-start.62 = (bf16[40,2048]{1,0:T(8,128)(2,1)S(1)}, bf16[40,2048]{1,0:T(8,128)(2,1)S(1)}, u32[]{:S(2)}, u32[]{:S(2)}) collective-permute-start(bf16[40,2048]{1,0:T(8,128)(2,1)S(1)} %get-tuple-element.138), channel_id=1, source_target_pairs={{0,8},{1,9},{2,10},{3,11},{4,12},{5,13},{6,14},{7,15},{8,0},{9,1},... | collective-permute-start | bytes 491528 | tf_op jit(solution)/shard_map/ppermute | solution.py:283
  123.1 8.1 %collective-permute-start.63 = (bf16[40,2048]{1,0:T(8,128)(2,1)S(1)}, bf16[40,2048]{1,0:T(8,128)(2,1)S(1)}, u32[]{:S(2)}, u32[]{:S(2)}) collective-permute-start(bf16[40,2048]{1,0:T(8,128)(2,1)S(1)} %get-tuple-element.139), channel_id=1, source_target_pairs={{0,16},{1,17},{2,18},{3,19},{4,20},{5,21},{6,22},{7,23},{8,24},{9,... | collective-permute-start | bytes 491528 | tf_op jit(solution)/shard_map/ppermute | solution.py:283
  125.0 10.3 %collective-permute-start.64 = (bf16[40,2048]{1,0:T(8,128)(2,1)S(1)}, bf16[40,2048]{1,0:T(8,128)(2,1)S(1)}, u32[]{:S(2)}, u32[]{:S(2)}) collective-permute-start(bf16[40,2048]{1,0:T(8,128)(2,1)S(1)} %get-tuple-element.140), channel_id=1, source_target_pairs={{0,24},{1,25},{2,26},{3,27},{4,28},{5,29},{6,30},{7,31},{8,16},{9,... | collective-permute-start | bytes 491528 | tf_op jit(solution)/shard_map/ppermute | solution.py:283
  128.3 8.1 %collective-permute-start.24 = (bf16[40,2048]{1,0:T(8,128)(2,1)S(1)}, bf16[40,2048]{1,0:T(8,128)(2,1)S(1)}, u32[]{:S(2)}, u32[]{:S(2)}) collective-permute-start(bf16[40,2048]{1,0:T(8,128)(2,1)S(1)} %get-tuple-element.98), channel_id=1, source_target_pairs={{0,8},{1,9},{2,10},{3,11},{4,12},{5,13},{6,14},{7,15},{8,0},{9,1},... | collective-permute-start | bytes 491528 | tf_op jit(solution)/shard_map/ppermute | solution.py:283
  128.8 33.4 %collective-permute-start.52 = (bf16[128,2048]{1,0:T(8,128)(2,1)S(1)}, bf16[128,2048]{1,0:T(8,128)(2,1)S(1)}, u32[]{:S(2)}, u32[]{:S(2)}) collective-permute-start(bf16[128,2048]{1,0:T(8,128)(2,1)S(1)} %shard_map.130), channel_id=1, source_target_pairs={{0,2},{1,3},{2,0},{3,1},{4,6},{5,7},{6,4},{7,5},{8,10},{9,11},{10,... | collective-permute-start | bytes 1572872 | tf_op jit(solution)/shard_map/ppermute | solution.py:271
  129.4 8.2 %collective-permute-start.25 = (bf16[40,2048]{1,0:T(8,128)(2,1)S(1)}, bf16[40,2048]{1,0:T(8,128)(2,1)S(1)}, u32[]{:S(2)}, u32[]{:S(2)}) collective-permute-start(bf16[40,2048]{1,0:T(8,128)(2,1)S(1)} %get-tuple-element.99), channel_id=1, source_target_pairs={{0,16},{1,17},{2,18},{3,19},{4,20},{5,21},{6,22},{7,23},{8,24},{9,... | collective-permute-start | bytes 491528 | tf_op jit(solution)/shard_map/ppermute | solution.py:283
  131.2 9.6 %collective-permute-start.26 = (bf16[40,2048]{1,0:T(8,128)(2,1)S(1)}, bf16[40,2048]{1,0:T(8,128)(2,1)S(1)}, u32[]{:S(2)}, u32[]{:S(2)}) collective-permute-start(bf16[40,2048]{1,0:T(8,128)(2,1)S(1)} %get-tuple-element.100), channel_id=1, source_target_pairs={{0,24},{1,25},{2,26},{3,27},{4,28},{5,29},{6,30},{7,31},{8,16},{9,... | collective-permute-start | bytes 491528 | tf_op jit(solution)/shard_map/ppermute | solution.py:283
  135.3 6.5 %collective-permute-start.27 = (bf16[40,2048]{1,0:T(8,128)(2,1)S(1)}, bf16[40,2048]{1,0:T(8,128)(2,1)S(1)}, u32[]{:S(2)}, u32[]{:S(2)}) collective-permute-start(bf16[40,2048]{1,0:T(8,128)(2,1)S(1)} %get-tuple-element.101), channel_id=1, source_target_pairs={{0,1},{1,0},{2,3},{3,2},{4,5},{5,4},{6,7},{7,6},{8,9},{9,8},{10,11... | collective-permute-start | bytes 491528 | tf_op jit(solution)/shard_map/ppermute | solution.py:283
  136.4 6.3 %collective-permute-start.28 = (bf16[40,2048]{1,0:T(8,128)(2,1)S(1)}, bf16[40,2048]{1,0:T(8,128)(2,1)S(1)}, u32[]{:S(2)}, u32[]{:S(2)}) collective-permute-start(bf16[40,2048]{1,0:T(8,128)(2,1)S(1)} %get-tuple-element.102), channel_id=1, source_target_pairs={{0,9},{1,8},{2,11},{3,10},{4,13},{5,12},{6,15},{7,14},{8,1},{9,0},... | collective-permute-start | bytes 491528 | tf_op jit(solution)/shard_map/ppermute | solution.py:283
  140.8 6.9 %collective-permute-start.30 = (bf16[40,2048]{1,0:T(8,128)(2,1)S(1)}, bf16[40,2048]{1,0:T(8,128)(2,1)S(1)}, u32[]{:S(2)}, u32[]{:S(2)}) collective-permute-start(bf16[40,2048]{1,0:T(8,128)(2,1)S(1)} %get-tuple-element.104), channel_id=1, source_target_pairs={{0,25},{1,24},{2,27},{3,26},{4,29},{5,28},{6,31},{7,30},{8,17},{9,... | collective-permute-start | bytes 491528 | tf_op jit(solution)/shard_map/ppermute | solution.py:283
  141.7 13.1 %collective-permute-start.65 = (bf16[40,2048]{1,0:T(8,128)(2,1)S(1)}, bf16[40,2048]{1,0:T(8,128)(2,1)S(1)}, u32[]{:S(2)}, u32[]{:S(2)}) collective-permute-start(bf16[40,2048]{1,0:T(8,128)(2,1)S(1)} %get-tuple-element.141), channel_id=1, source_target_pairs={{0,1},{1,0},{2,3},{3,2},{4,5},{5,4},{6,7},{7,6},{8,9},{9,8},{10,11... | collective-permute-start | bytes 491528 | tf_op jit(solution)/shard_map/ppermute | solution.py:283
  142.6 12.9 %collective-permute-start.66 = (bf16[40,2048]{1,0:T(8,128)(2,1)S(1)}, bf16[40,2048]{1,0:T(8,128)(2,1)S(1)}, u32[]{:S(2)}, u32[]{:S(2)}) collective-permute-start(bf16[40,2048]{1,0:T(8,128)(2,1)S(1)} %get-tuple-element.142), channel_id=1, source_target_pairs={{0,9},{1,8},{2,11},{3,10},{4,13},{5,12},{6,15},{7,14},{8,1},{9,0},... | collective-permute-start | bytes 491528 | tf_op jit(solution)/shard_map/ppermute | solution.py:283
  142.9 14.4 %collective-permute-start.67 = (bf16[40,2048]{1,0:T(8,128)(2,1)S(1)}, bf16[40,2048]{1,0:T(8,128)(2,1)S(1)}, u32[]{:S(2)}, u32[]{:S(2)}) collective-permute-start(bf16[40,2048]{1,0:T(8,128)(2,1)S(1)} %get-tuple-element.143), channel_id=1, source_target_pairs={{0,17},{1,16},{2,19},{3,18},{4,21},{5,20},{6,23},{7,22},{8,25},{9,... | collective-permute-start | bytes 491528 | tf_op jit(solution)/shard_map/ppermute | solution.py:283
  147.7 14.5 %collective-permute-start.68 = (bf16[40,2048]{1,0:T(8,128)(2,1)S(1)}, bf16[40,2048]{1,0:T(8,128)(2,1)S(1)}, u32[]{:S(2)}, u32[]{:S(2)}) collective-permute-start(bf16[40,2048]{1,0:T(8,128)(2,1)S(1)} %get-tuple-element.144), channel_id=1, source_target_pairs={{0,25},{1,24},{2,27},{3,26},{4,29},{5,28},{6,31},{7,30},{8,17},{9,... | collective-permute-start | bytes 491528 | tf_op jit(solution)/shard_map/ppermute | solution.py:283
  154.9 7.4 %collective-permute-start.31 = (bf16[40,2048]{1,0:T(8,128)(2,1)S(1)}, bf16[40,2048]{1,0:T(8,128)(2,1)S(1)}, u32[]{:S(2)}, u32[]{:S(2)}) collective-permute-start(bf16[40,2048]{1,0:T(8,128)(2,1)S(1)} %get-tuple-element.106), channel_id=1, source_target_pairs={{0,8},{1,9},{2,10},{3,11},{4,12},{5,13},{6,14},{7,15},{8,0},{9,1},... | collective-permute-start | bytes 491528 | tf_op jit(solution)/shard_map/ppermute | solution.py:283
  155.5 7.1 %collective-permute-start.32 = (bf16[40,2048]{1,0:T(8,128)(2,1)S(1)}, bf16[40,2048]{1,0:T(8,128)(2,1)S(1)}, u32[]{:S(2)}, u32[]{:S(2)}) collective-permute-start(bf16[40,2048]{1,0:T(8,128)(2,1)S(1)} %get-tuple-element.107), channel_id=1, source_target_pairs={{0,16},{1,17},{2,18},{3,19},{4,20},{5,21},{6,22},{7,23},{8,24},{9,... | collective-permute-start | bytes 491528 | tf_op jit(solution)/shard_map/ppermute | solution.py:283
  157.3 9.9 %collective-permute-start.33 = (bf16[40,2048]{1,0:T(8,128)(2,1)S(1)}, bf16[40,2048]{1,0:T(8,128)(2,1)S(1)}, u32[]{:S(2)}, u32[]{:S(2)}) collective-permute-start(bf16[40,2048]{1,0:T(8,128)(2,1)S(1)} %get-tuple-element.108), channel_id=1, source_target_pairs={{0,24},{1,25},{2,26},{3,27},{4,28},{5,29},{6,30},{7,31},{8,16},{9,... | collective-permute-start | bytes 491528 | tf_op jit(solution)/shard_map/ppermute | solution.py:283
  162.2 8.3 %collective-permute-start.35 = (bf16[40,2048]{1,0:T(8,128)(2,1)S(1)}, bf16[40,2048]{1,0:T(8,128)(2,1)S(1)}, u32[]{:S(2)}, u32[]{:S(2)}) collective-permute-start(bf16[40,2048]{1,0:T(8,128)(2,1)S(1)} %get-tuple-element.110), channel_id=1, source_target_pairs={{0,9},{1,8},{2,11},{3,10},{4,13},{5,12},{6,15},{7,14},{8,1},{9,0},... | collective-permute-start | bytes 491528 | tf_op jit(solution)/shard_map/ppermute | solution.py:283
  162.3 9.2 %collective-permute-start.36 = (bf16[40,2048]{1,0:T(8,128)(2,1)S(1)}, bf16[40,2048]{1,0:T(8,128)(2,1)S(1)}, u32[]{:S(2)}, u32[]{:S(2)}) collective-permute-start(bf16[40,2048]{1,0:T(8,128)(2,1)S(1)} %get-tuple-element.111), channel_id=1, source_target_pairs={{0,17},{1,16},{2,19},{3,18},{4,21},{5,20},{6,23},{7,22},{8,25},{9,... | collective-permute-start | bytes 491528 | tf_op jit(solution)/shard_map/ppermute | solution.py:283
  162.6 11.3 %collective-permute-start.37 = (bf16[40,2048]{1,0:T(8,128)(2,1)S(1)}, bf16[40,2048]{1,0:T(8,128)(2,1)S(1)}, u32[]{:S(2)}, u32[]{:S(2)}) collective-permute-start(bf16[40,2048]{1,0:T(8,128)(2,1)S(1)} %get-tuple-element.112), channel_id=1, source_target_pairs={{0,25},{1,24},{2,27},{3,26},{4,29},{5,28},{6,31},{7,30},{8,17},{9,... | collective-permute-start | bytes 491528 | tf_op jit(solution)/shard_map/ppermute | solution.py:283
  167.2 10.2 %collective-permute-start.12 = (bf16[40,2048]{1,0:T(8,128)(2,1)S(1)}, bf16[40,2048]{1,0:T(8,128)(2,1)S(1)}, u32[]{:S(2)}, u32[]{:S(2)}) collective-permute-start(bf16[40,2048]{1,0:T(8,128)(2,1)S(1)} %get-tuple-element.84), channel_id=1, source_target_pairs={{0,9},{1,8},{2,11},{3,10},{4,13},{5,12},{6,15},{7,14},{8,1},{9,0},... | collective-permute-start | bytes 491528 | tf_op jit(solution)/shard_map/ppermute | solution.py:283
  167.6 10.6 %collective-permute-start.13 = (bf16[40,2048]{1,0:T(8,128)(2,1)S(1)}, bf16[40,2048]{1,0:T(8,128)(2,1)S(1)}, u32[]{:S(2)}, u32[]{:S(2)}) collective-permute-start(bf16[40,2048]{1,0:T(8,128)(2,1)S(1)} %get-tuple-element.85), channel_id=1, source_target_pairs={{0,17},{1,16},{2,19},{3,18},{4,21},{5,20},{6,23},{7,22},{8,25},{9,... | collective-permute-start | bytes 491528 | tf_op jit(solution)/shard_map/ppermute | solution.py:283
  170.5 10.5 %collective-permute-start.14 = (bf16[40,2048]{1,0:T(8,128)(2,1)S(1)}, bf16[40,2048]{1,0:T(8,128)(2,1)S(1)}, u32[]{:S(2)}, u32[]{:S(2)}) collective-permute-start(bf16[40,2048]{1,0:T(8,128)(2,1)S(1)} %get-tuple-element.86), channel_id=1, source_target_pairs={{0,25},{1,24},{2,27},{3,26},{4,29},{5,28},{6,31},{7,30},{8,17},{9,... | collective-permute-start | bytes 491528 | tf_op jit(solution)/shard_map/ppermute | solution.py:283
  171.5 12.1 %collective-permute-start.8 = (bf16[40,2048]{1,0:T(8,128)(2,1)S(1)}, bf16[40,2048]{1,0:T(8,128)(2,1)S(1)}, u32[]{:S(2)}, u32[]{:S(2)}) collective-permute-start(bf16[40,2048]{1,0:T(8,128)(2,1)S(1)} %get-tuple-element.80), channel_id=1, source_target_pairs={{0,8},{1,9},{2,10},{3,11},{4,12},{5,13},{6,14},{7,15},{8,0},{9,1},... | collective-permute-start | bytes 491528 | tf_op jit(solution)/shard_map/ppermute | solution.py:283
  173.9 10.3 %collective-permute-start.9 = (bf16[40,2048]{1,0:T(8,128)(2,1)S(1)}, bf16[40,2048]{1,0:T(8,128)(2,1)S(1)}, u32[]{:S(2)}, u32[]{:S(2)}) collective-permute-start(bf16[40,2048]{1,0:T(8,128)(2,1)S(1)} %get-tuple-element.81), channel_id=1, source_target_pairs={{0,16},{1,17},{2,18},{3,19},{4,20},{5,21},{6,22},{7,23},{8,24},{9,... | collective-permute-start | bytes 491528 | tf_op jit(solution)/shard_map/ppermute | solution.py:283
  177.4 31.3 %collective-permute-start.69 = (bf16[128,2048]{1,0:T(8,128)(2,1)S(1)}, bf16[128,2048]{1,0:T(8,128)(2,1)S(1)}, u32[]{:S(2)}, u32[]{:S(2)}) collective-permute-start(bf16[128,2048]{1,0:T(8,128)(2,1)S(1)} %shard_map.134), channel_id=1, source_target_pairs={{0,2},{1,3},{2,0},{3,1},{4,6},{5,7},{6,4},{7,5},{8,10},{9,11},{10,... | collective-permute-start | bytes 1572872 | tf_op jit(solution)/shard_map/ppermute | solution.py:271
  178.1 30.5 %collective-permute-start.53 = (bf16[128,2048]{1,0:T(8,128)(2,1)S(1)}, bf16[128,2048]{1,0:T(8,128)(2,1)S(1)}, u32[]{:S(2)}, u32[]{:S(2)}) collective-permute-start(bf16[128,2048]{1,0:T(8,128)(2,1)S(1)} %shard_map.131), channel_id=1, source_target_pairs={{0,6},{1,7},{2,4},{3,5},{4,2},{5,3},{6,0},{7,1},{8,14},{9,15},{10,... | collective-permute-start | bytes 1572872 | tf_op jit(solution)/shard_map/ppermute | solution.py:271
  187.4 7.1 %collective-permute-start.15 = (bf16[40,2048]{1,0:T(8,128)(2,1)S(1)}, bf16[40,2048]{1,0:T(8,128)(2,1)S(1)}, u32[]{:S(2)}, u32[]{:S(2)}) collective-permute-start(bf16[40,2048]{1,0:T(8,128)(2,1)S(1)} %get-tuple-element.88), channel_id=1, source_target_pairs={{0,8},{1,9},{2,10},{3,11},{4,12},{5,13},{6,14},{7,15},{8,0},{9,1},... | collective-permute-start | bytes 491528 | tf_op jit(solution)/shard_map/ppermute | solution.py:283
  189.4 9.0 %collective-permute-start.16 = (bf16[40,2048]{1,0:T(8,128)(2,1)S(1)}, bf16[40,2048]{1,0:T(8,128)(2,1)S(1)}, u32[]{:S(2)}, u32[]{:S(2)}) collective-permute-start(bf16[40,2048]{1,0:T(8,128)(2,1)S(1)} %get-tuple-element.89), channel_id=1, source_target_pairs={{0,16},{1,17},{2,18},{3,19},{4,20},{5,21},{6,22},{7,23},{8,24},{9,... | collective-permute-start | bytes 491528 | tf_op jit(solution)/shard_map/ppermute | solution.py:283
  190.7 7.7 %collective-permute-start.17 = (bf16[40,2048]{1,0:T(8,128)(2,1)S(1)}, bf16[40,2048]{1,0:T(8,128)(2,1)S(1)}, u32[]{:S(2)}, u32[]{:S(2)}) collective-permute-start(bf16[40,2048]{1,0:T(8,128)(2,1)S(1)} %get-tuple-element.90), channel_id=1, source_target_pairs={{0,24},{1,25},{2,26},{3,27},{4,28},{5,29},{6,30},{7,31},{8,16},{9,... | collective-permute-start | bytes 491528 | tf_op jit(solution)/shard_map/ppermute | solution.py:283
  194.6 5.6 %collective-permute-start.18 = (bf16[40,2048]{1,0:T(8,128)(2,1)S(1)}, bf16[40,2048]{1,0:T(8,128)(2,1)S(1)}, u32[]{:S(2)}, u32[]{:S(2)}) collective-permute-start(bf16[40,2048]{1,0:T(8,128)(2,1)S(1)} %get-tuple-element.91), channel_id=1, source_target_pairs={{0,1},{1,0},{2,3},{3,2},{4,5},{5,4},{6,7},{7,6},{8,9},{9,8},{10,11... | collective-permute-start | bytes 491528 | tf_op jit(solution)/shard_map/ppermute | solution.py:283
  198.4 9.3 %collective-permute-start.20 = (bf16[40,2048]{1,0:T(8,128)(2,1)S(1)}, bf16[40,2048]{1,0:T(8,128)(2,1)S(1)}, u32[]{:S(2)}, u32[]{:S(2)}) collective-permute-start(bf16[40,2048]{1,0:T(8,128)(2,1)S(1)} %get-tuple-element.93), channel_id=1, source_target_pairs={{0,17},{1,16},{2,19},{3,18},{4,21},{5,20},{6,23},{7,22},{8,25},{9,... | collective-permute-start | bytes 491528 | tf_op jit(solution)/shard_map/ppermute | solution.py:283
  200.2 8.5 %collective-permute-start.21 = (bf16[40,2048]{1,0:T(8,128)(2,1)S(1)}, bf16[40,2048]{1,0:T(8,128)(2,1)S(1)}, u32[]{:S(2)}, u32[]{:S(2)}) collective-permute-start(bf16[40,2048]{1,0:T(8,128)(2,1)S(1)} %get-tuple-element.94), channel_id=1, source_target_pairs={{0,25},{1,24},{2,27},{3,26},{4,29},{5,28},{6,31},{7,30},{8,17},{9,... | collective-permute-start | bytes 491528 | tf_op jit(solution)/shard_map/ppermute | solution.py:283
  (22 other events, 231.4 us)

commit v6 on v5

--- a/solution.py
+++ b/solution.py
@@ -324,11 +324,17 @@
         + [pltpu.SemaphoreType.DMA((3, 4)), pltpu.SemaphoreType.DMA],
         away=(0, 1, 2, 3),
     )(queries, keys, values, out_proj, *scalars)
-    shape = (stages * 2 * groups, tokens)
-    body = functools.partial(rank_kernel, groups, length)
-    routes, ranks = call(body, [(shape, F32)] * 2)(
-        *scalars[1:], *tables
-    )
+
+    def ranked(held):
+        shape = (len(held) * 2 * groups, tokens)
+        body = functools.partial(rank_kernel, groups, length)
+        return call(body, [(shape, F32)] * 2)(*scalars[1:], *held)
+
+    own_tables = ranked(tables[:1])
+    rest_tables = ranked(tables[1:])
+    lookup = {m: (rest_tables, (m - 1) * 2 * groups) for m in range(1, stages)}
+    lookup[0] = (own_tables, 0)
+
     mine = added(*arrived)
     other = swap(mine)
     residual, moe_in = call(
@@ -354,14 +360,14 @@
         source, shift = routing[m]
         blocks[m] = along(blocks[source], shift)
     for m in range(stages):
-        base = m * 2 * groups
+        (routes, ranks), base = lookup[m]
         picked = select(slots, 2 * groups, base, blocks[m], ranks)
         taken = straight(picked)
         outs[m] = experts(taken, gate_weight, up_weight, down_weight)
     sums = {m: [] for m in range(stages)}
     sums[0].append(residual)
     for m in back_order(stages):
-        base = m * 2 * groups
+        (routes, ranks), base = lookup[m]
         backs = straight(outs[m])
         part = combine(slots, base, backs, ranks, routes, sums[m], m == 0)
         if m:

time: 211 us -> 209 us (level)
  starting transfers between devices: 97.4 us -> 79.6 us
  waiting for transfers between devices: 74.9 us -> 91.2 us
    ppermute x56, starting transfers between devices: 67.3 us -> 49 us  [straight(): x = lax.ppermute(x, ('grp', 'seq'), pairs)]
    ppermute x56, waiting for transfers between devices: 46.6 us -> 63.4 us  [straight(): x = lax.ppermute(x, ('grp', 'seq'), pairs)]
    pallas_call x18 -> x19, Pallas kernels: 29.9 us -> 30.1 us  [run(): pl.pallas_call(body, in_specs=specs, out_specs=[pl.BlockSpec(memory_space...]
where the time goes in v6:
time: 209 us
  waiting for transfers between devices  91.2 us (44%)
  starting transfers between devices  79.6 us (38%)
  Pallas kernels  30.1 us (14%)
  local copies, waits for them, and re-layouts  7.3 us (3%)
    ppermute x56, waiting for transfers between devices, straight(): x = lax.ppermute(x, ('grp', 'seq'), pairs)  63.4 us
    ppermute x56, starting transfers between devices, straight(): x = lax.ppermute(x, ('grp', 'seq'), pairs)  49 us
    pallas_call x19, Pallas kernels, run(): pl.pallas_call(body, in_specs=specs, out_specs=[pl.BlockSpec(memory_space...  30.1 us
    ppermute x9, waiting for transfers between devices, along(): return lax.ppermute(x, 'seq', [(s, s ^ 2 * m) for s in range(length)])  20.1 us
    ppermute x9, starting transfers between devices, along(): return lax.ppermute(x, 'seq', [(s, s ^ 2 * m) for s in range(length)])  19.9 us
    ppermute x3, starting transfers between devices, later(): return lax.ppermute(x, 'seq', pairs)  10 us
    unnamed x32, local copies, waits for them, and re-layouts  7.3 us
    ppermute x3, waiting for transfers between devices, later(): return lax.ppermute(x, 'seq', pairs)  6.24 us
  transfers between devices with their start and end apart: 70, of which 31 were waited for; matrix products, arithmetic and copies ran while one was open for 0% of the time, Pallas kernels for 11%

profile of v6, /device:TPU:0, one launch (start us, length us, event | category | flops | bytes accessed | tf_op | source)
XLA Modules:
  0.0 208.7 jit_solution(12727939027481482304)
XLA Ops:
  0.0 1.9 shard_map.119
  2.5 1.5 collective-permute-done.pair_ref
  4.1 4.9 %collective-permute-start.1 = (bf16[1024,128]{1,0:T(8,128)(2,1)S(1)}, bf16[1024,128]{1,0:T(8,128)(2,1)S(1)}, u32[]{:S(2)}, u32[]{:S(2)}) collective-permute-start(bf16[1024,128]{1,0:T(8,128)(2,1)S(1)} %add_convert_fusion.refs_0_), channel_id=1, source_target_pairs={{0,2},{1,3},{2,4},{3,5},{4,6},{5,7},{8,10},{9,11},{10,12},{11,13},... | collective-permute-start | bytes 786440 | tf_op jit(solution)/shard_map/ppermute | solution.py:289
  9.0 4.5 %collective-permute-start.2 = (bf16[1024,128]{1,0:T(8,128)(2,1)S(1)}, bf16[1024,128]{1,0:T(8,128)(2,1)S(1)}, u32[]{:S(2)}, u32[]{:S(2)}) collective-permute-start(bf16[1024,128]{1,0:T(8,128)(2,1)S(1)} %add_convert_fusion.refs_0_), channel_id=1, source_target_pairs={{0,4},{1,5},{8,12},{9,13},{16,20},{17,21},{24,28},{25,29}} | collective-permute-start | bytes 786440 | tf_op jit(solution)/shard_map/ppermute | solution.py:289
  13.5 2.2 %collective-permute-done.1.refs_1_.refs_0_ = bf16[1024,128]{1,0:T(8,128)(2,1)S(1)} collective-permute-done((bf16[1024,128]{1,0:T(8,128)(2,1)S(1)}, bf16[1024,128]{1,0:T(8,128)(2,1)S(1)}, u32[]{:S(2)}, u32[]{:S(2)}) %collective-permute-start.1) | collective-permute-done | bytes 262176 | tf_op jit(solution)/shard_map/ppermute | solution.py:289
  16.4 4.1 %collective-permute-done.2.refs_1_ = bf16[1024,128]{1,0:T(8,128)(2,1)S(1)} collective-permute-done((bf16[1024,128]{1,0:T(8,128)(2,1)S(1)}, bf16[1024,128]{1,0:T(8,128)(2,1)S(1)}, u32[]{:S(2)}, u32[]{:S(2)}) %collective-permute-start.2) | collective-permute-done | bytes 262176 | tf_op jit(solution)/shard_map/ppermute | solution.py:289
  20.7 4.2 %shard_map.118 = (f32[128,2048]{1,0:T(8,128)S(1)}, bf16[2048,2048]{1,0:T(8,128)(2,1)S(1)}) custom-call(bf16[128,2048]{1,0:T(8,128)(2,1)} %bitcast.19, bf16[128,2048]{1,0:T(8,128)(2,1)} %bitcast.25, bf16[128,2048]{1,0:T(8,128)(2,1)} %bitcast.27, bf16[2048,2048]{1,0:T(8,128)(2,1)} %w_hbm.1, s32[1]{0:T(128)} %bitcast.core_ref, s32[1]{0:T(128)} %bitcast.4.group_ref, ...), custom_call_target="tpu_custom_call" | custom-call | tf_op jit(solution)/shard_map/pallas_call | solution.py:32
  27.6 2.9 %shard_map.122 = (bf16[128,2048]{1,0:T(8,128)(2,1)S(1)}, bf16[128,2048]{1,0:T(8,128)(2,1)}) custom-call(s32[1]{0:T(128)} %bitcast.core_ref, f32[128,2048]{1,0:T(8,128)S(1)} %get-tuple-element.77.in_ref, bf16[128,2048]{1,0:T(8,128)(2,1)S(1)} %bitcast.20, bf16[1024,128]{1,0:T(8,128)(2,1)S(1)} %shard_map.121.mine_ref, bf16[1024,128]{1,0:T(8,128)(2,1)S(1)} %copy-done.11, ...), custom_call_target="tpu_custom_call" | custom-call | tf_op jit(solution)/shard_map/pallas_call | solution.py:32
  31.3 7.1 %collective-permute-start.54 = (bf16[128,2048]{1,0:T(8,128)(2,1)}, bf16[128,2048]{1,0:T(8,128)(2,1)}, u32[]{:S(2)}, u32[]{:S(2)}) collective-permute-start(bf16[128,2048]{1,0:T(8,128)(2,1)} %get-tuple-element.79.own_ref), channel_id=1, source_target_pairs={{0,2},{1,3},{2,0},{3,1},{4,6},{5,7},{6,4},{7,5},{8,10},{9,11},{10,... | collective-permute-start | bytes 1572872 | tf_op jit(solution)/shard_map/ppermute | solution.py:271
  38.4 3.4 %collective-permute-start.19 = (bf16[128,2048]{1,0:T(8,128)(2,1)}, bf16[128,2048]{1,0:T(8,128)(2,1)}, u32[]{:S(2)}, u32[]{:S(2)}) collective-permute-start(bf16[128,2048]{1,0:T(8,128)(2,1)} %get-tuple-element.79.own_ref), channel_id=1, source_target_pairs={{0,4},{1,5},{2,6},{3,7},{4,0},{5,1},{6,2},{7,3},{8,12},{9,13},{10,... | collective-permute-start | bytes 1572872 | tf_op jit(solution)/shard_map/ppermute | solution.py:271
  42.1 1.5 shard_map.124
  45.0 17.5 %collective-permute-done.21.refs_0_ = f32[32,128]{1,0:T(8,128)S(1)} collective-permute-done((f32[32,128]{1,0:T(8,128)S(1)}, f32[32,128]{1,0:T(8,128)S(1)}, u32[]{:S(2)}, u32[]{:S(2)}) %collective-permute-start.21) | collective-permute-done | bytes 16416 | tf_op jit(solution)/shard_map/ppermute | solution.py:271
  62.5 3.0 %collective-permute-start.23 = (f32[32,128]{1,0:T(8,128)S(1)}, f32[32,128]{1,0:T(8,128)S(1)}, u32[]{:S(2)}, u32[]{:S(2)}) collective-permute-start(f32[32,128]{1,0:T(8,128)S(1)} %select_reduce_fusion.refs_0_), channel_id=1, source_target_pairs={{0,6},{1,7},{2,4},{3,5},{4,2},{5,3},{6,0},{7,1},{8,14},{9,15},{10,... | collective-permute-start | bytes 49160 | tf_op jit(solution)/shard_map/ppermute | solution.py:271
  66.3 1.8 collective-permute-done.23.refs_2_
  68.2 1.5 shard_map.133
  69.7 1.6 collective-permute-start.55
  71.3 1.5 collective-permute-start.56
  73.3 1.5 shard_map.129
  74.8 1.6 collective-permute-start.38
  76.4 1.5 collective-permute-start.39
  77.9 1.4 collective-permute-start.40
  81.0 2.5 %collective-permute-done.38.refs_1_ = bf16[40,2048]{1,0:T(8,128)(2,1)S(1)} collective-permute-done((bf16[40,2048]{1,0:T(8,128)(2,1)S(1)}, bf16[40,2048]{1,0:T(8,128)(2,1)S(1)}, u32[]{:S(2)}, u32[]{:S(2)}) %collective-permute-start.38) | collective-permute-done | bytes 163872 | tf_op jit(solution)/shard_map/ppermute | solution.py:283
  83.6 2.4 %collective-permute-done.39.refs_2_ = bf16[40,2048]{1,0:T(8,128)(2,1)S(1)} collective-permute-done((bf16[40,2048]{1,0:T(8,128)(2,1)S(1)}, bf16[40,2048]{1,0:T(8,128)(2,1)S(1)}, u32[]{:S(2)}, u32[]{:S(2)}) %collective-permute-start.39) | collective-permute-done | bytes 163872 | tf_op jit(solution)/shard_map/ppermute | solution.py:283
  86.1 2.0 collective-permute-done.40.refs_3_
  88.7 1.3 collective-permute-start.59
  90.0 4.2 %collective-permute-done.43.refs_6_ = bf16[40,2048]{1,0:T(8,128)(2,1)S(1)} collective-permute-done((bf16[40,2048]{1,0:T(8,128)(2,1)S(1)}, bf16[40,2048]{1,0:T(8,128)(2,1)S(1)}, u32[]{:S(2)}, u32[]{:S(2)}) %collective-permute-start.43) | collective-permute-done | bytes 163872 | tf_op jit(solution)/shard_map/ppermute | solution.py:283
  94.3 2.5 %collective-permute-start.61 = (bf16[40,2048]{1,0:T(8,128)(2,1)S(1)}, bf16[40,2048]{1,0:T(8,128)(2,1)S(1)}, u32[]{:S(2)}, u32[]{:S(2)}) collective-permute-start(bf16[40,2048]{1,0:T(8,128)(2,1)S(1)} %get-tuple-element.140), channel_id=1, source_target_pairs={{0,25},{1,24},{2,27},{3,26},{4,29},{5,28},{6,31},{7,30},{8,17},{9,... | collective-permute-start | bytes 491528 | tf_op jit(solution)/shard_map/ppermute | solution.py:283
  96.7 1.9 copy-done.1
  98.6 1.9 copy-done.3
  100.5 3.2 %shard_map.130 = (bf16[40,2048]{1,0:T(8,128)(2,1)S(1)}, bf16[40,2048]{1,0:T(8,128)(2,1)S(1)}, bf16[40,2048]{1,0:T(8,128)(2,1)S(1)}, bf16[40,2048]{1,0:T(8,128)(2...) custom-call(bf16[40,2048]{1,0:T(8,128)(2,1)S(1)} %get-tuple-element., ...), custom_call_target="tpu_custom_call" | custom-call | tf_op jit(solution)/shard_map/pallas_call | solution.py:32
  104.6 2.7 %collective-permute-start.47 = (bf16[40,2048]{1,0:T(8,128)(2,1)S(1)}, bf16[40,2048]{1,0:T(8,128)(2,1)S(1)}, u32[]{:S(2)}, u32[]{:S(2)}) collective-permute-start(bf16[40,2048]{1,0:T(8,128)(2,1)S(1)} %get-tuple-element.128), channel_id=1, source_target_pairs={{0,24},{1,25},{2,26},{3,27},{4,28},{5,29},{6,30},{7,31},{8,16},{9,... | collective-permute-start | bytes 491528 | tf_op jit(solution)/shard_map/ppermute | solution.py:283
  107.3 3.6 %collective-permute-done.45.refs_1_ = bf16[40,2048]{1,0:T(8,128)(2,1)S(1)} collective-permute-done((bf16[40,2048]{1,0:T(8,128)(2,1)S(1)}, bf16[40,2048]{1,0:T(8,128)(2,1)S(1)}, u32[]{:S(2)}, u32[]{:S(2)}) %collective-permute-start.45) | collective-permute-done | bytes 163872 | tf_op jit(solution)/shard_map/ppermute | solution.py:283
  110.9 3.2 %collective-permute-done.46.refs_2_ = bf16[40,2048]{1,0:T(8,128)(2,1)S(1)} collective-permute-done((bf16[40,2048]{1,0:T(8,128)(2,1)S(1)}, bf16[40,2048]{1,0:T(8,128)(2,1)S(1)}, u32[]{:S(2)}, u32[]{:S(2)}) %collective-permute-start.46) | collective-permute-done | bytes 163872 | tf_op jit(solution)/shard_map/ppermute | solution.py:283
  114.1 2.6 %collective-permute-start.51 = (bf16[40,2048]{1,0:T(8,128)(2,1)S(1)}, bf16[40,2048]{1,0:T(8,128)(2,1)S(1)}, u32[]{:S(2)}, u32[]{:S(2)}) collective-permute-start(bf16[40,2048]{1,0:T(8,128)(2,1)S(1)} %get-tuple-element.132), channel_id=1, source_target_pairs={{0,25},{1,24},{2,27},{3,26},{4,29},{5,28},{6,31},{7,30},{8,17},{9,... | collective-permute-start | bytes 491528 | tf_op jit(solution)/shard_map/ppermute | solution.py:283
  116.8 3.2 %shard_map.134 = (bf16[40,2048]{1,0:T(8,128)(2,1)S(1)}, bf16[40,2048]{1,0:T(8,128)(2,1)S(1)}, bf16[40,2048]{1,0:T(8,128)(2,1)S(1)}, bf16[40,2048]{1,0:T(8,128)(2...) custom-call(bf16[40,2048]{1,0:T(8,128)(2,1)S(1)} %get-tuple-element., ...), custom_call_target="tpu_custom_call" | custom-call | tf_op jit(solution)/shard_map/pallas_call | solution.py:32
  120.1 1.5 collective-permute-start.62
  122.8 3.8 %collective-permute-done.50.refs_6_ = bf16[40,2048]{1,0:T(8,128)(2,1)S(1)} collective-permute-done((bf16[40,2048]{1,0:T(8,128)(2,1)S(1)}, bf16[40,2048]{1,0:T(8,128)(2,1)S(1)}, u32[]{:S(2)}, u32[]{:S(2)}) %collective-permute-start.50) | collective-permute-done | bytes 163872 | tf_op jit(solution)/shard_map/ppermute | solution.py:283
  126.6 2.2 %collective-permute-start.64 = (bf16[40,2048]{1,0:T(8,128)(2,1)S(1)}, bf16[40,2048]{1,0:T(8,128)(2,1)S(1)}, u32[]{:S(2)}, u32[]{:S(2)}) collective-permute-start(bf16[40,2048]{1,0:T(8,128)(2,1)S(1)} %get-tuple-element.144), channel_id=1, source_target_pairs={{0,24},{1,25},{2,26},{3,27},{4,28},{5,29},{6,30},{7,31},{8,16},{9,... | collective-permute-start | bytes 491528 | tf_op jit(solution)/shard_map/ppermute | solution.py:283
  130.7 2.0 collective-permute-start.25
  133.0 1.6 collective-permute-done.64.refs_3_
  134.6 3.1 %collective-permute-done.24.refs_1_ = bf16[40,2048]{1,0:T(8,128)(2,1)S(1)} collective-permute-done((bf16[40,2048]{1,0:T(8,128)(2,1)S(1)}, bf16[40,2048]{1,0:T(8,128)(2,1)S(1)}, u32[]{:S(2)}, u32[]{:S(2)}) %collective-permute-start.24) | collective-permute-done | bytes 163872 | tf_op jit(solution)/shard_map/ppermute | solution.py:283
  138.0 2.9 %collective-permute-done.25.refs_2_ = bf16[40,2048]{1,0:T(8,128)(2,1)S(1)} collective-permute-done((bf16[40,2048]{1,0:T(8,128)(2,1)S(1)}, bf16[40,2048]{1,0:T(8,128)(2,1)S(1)}, u32[]{:S(2)}, u32[]{:S(2)}) %collective-permute-start.25) | collective-permute-done | bytes 163872 | tf_op jit(solution)/shard_map/ppermute | solution.py:283
  140.9 2.8 %collective-permute-start.30 = (bf16[40,2048]{1,0:T(8,128)(2,1)S(1)}, bf16[40,2048]{1,0:T(8,128)(2,1)S(1)}, u32[]{:S(2)}, u32[]{:S(2)}) collective-permute-start(bf16[40,2048]{1,0:T(8,128)(2,1)S(1)} %get-tuple-element.107), channel_id=1, source_target_pairs={{0,25},{1,24},{2,27},{3,26},{4,29},{5,28},{6,31},{7,30},{8,17},{9,... | collective-permute-start | bytes 491528 | tf_op jit(solution)/shard_map/ppermute | solution.py:283
  143.7 1.8 collective-permute-start.66
  145.5 4.3 %collective-permute-done.29.refs_6_ = bf16[40,2048]{1,0:T(8,128)(2,1)S(1)} collective-permute-done((bf16[40,2048]{1,0:T(8,128)(2,1)S(1)}, bf16[40,2048]{1,0:T(8,128)(2,1)S(1)}, u32[]{:S(2)}, u32[]{:S(2)}) %collective-permute-start.29) | collective-permute-done | bytes 163872 | tf_op jit(solution)/shard_map/ppermute | solution.py:283
  150.2 2.6 %collective-permute-start.68 = (bf16[40,2048]{1,0:T(8,128)(2,1)S(1)}, bf16[40,2048]{1,0:T(8,128)(2,1)S(1)}, u32[]{:S(2)}, u32[]{:S(2)}) collective-permute-start(bf16[40,2048]{1,0:T(8,128)(2,1)S(1)} %get-tuple-element.148), channel_id=1, source_target_pairs={{0,25},{1,24},{2,27},{3,26},{4,29},{5,28},{6,31},{7,30},{8,17},{9,... | collective-permute-start | bytes 491528 | tf_op jit(solution)/shard_map/ppermute | solution.py:283
  152.8 3.2 %shard_map.128 = (bf16[40,2048]{1,0:T(8,128)(2,1)S(1)}, bf16[40,2048]{1,0:T(8,128)(2,1)S(1)}, bf16[40,2048]{1,0:T(8,128)(2,1)S(1)}, bf16[40,2048]{1,0:T(8,128)(2...) custom-call(bf16[40,2048]{1,0:T(8,128)(2,1)S(1)} %get-tuple-element., ...), custom_call_target="tpu_custom_call" | custom-call | tf_op jit(solution)/shard_map/pallas_call | solution.py:32
  156.3 2.7 %collective-permute-done.67.refs_6_ = bf16[40,2048]{1,0:T(8,128)(2,1)S(1)} collective-permute-done((bf16[40,2048]{1,0:T(8,128)(2,1)S(1)}, bf16[40,2048]{1,0:T(8,128)(2,1)S(1)}, u32[]{:S(2)}, u32[]{:S(2)}) %collective-permute-start.67) | collective-permute-done | bytes 163872 | tf_op jit(solution)/shard_map/ppermute | solution.py:283
  160.0 1.8 collective-permute-done.31.refs_1_
  162.3 3.1 %collective-permute-done.32.refs_2_ = bf16[40,2048]{1,0:T(8,128)(2,1)S(1)} collective-permute-done((bf16[40,2048]{1,0:T(8,128)(2,1)S(1)}, bf16[40,2048]{1,0:T(8,128)(2,1)S(1)}, u32[]{:S(2)}, u32[]{:S(2)}) %collective-permute-start.32) | collective-permute-done | bytes 163872 | tf_op jit(solution)/shard_map/ppermute | solution.py:283
  165.3 2.6 %collective-permute-start.37 = (bf16[40,2048]{1,0:T(8,128)(2,1)S(1)}, bf16[40,2048]{1,0:T(8,128)(2,1)S(1)}, u32[]{:S(2)}, u32[]{:S(2)}) collective-permute-start(bf16[40,2048]{1,0:T(8,128)(2,1)S(1)} %get-tuple-element.115), channel_id=1, source_target_pairs={{0,25},{1,24},{2,27},{3,26},{4,29},{5,28},{6,31},{7,30},{8,17},{9,... | collective-permute-start | bytes 491528 | tf_op jit(solution)/shard_map/ppermute | solution.py:283
  168.8 2.7 %collective-permute-start.7 = (bf16[40,2048]{1,0:T(8,128)(2,1)S(1)}, bf16[40,2048]{1,0:T(8,128)(2,1)S(1)}, u32[]{:S(2)}, u32[]{:S(2)}) collective-permute-start(bf16[40,2048]{1,0:T(8,128)(2,1)S(1)} %get-tuple-element.84), channel_id=1, source_target_pairs={{0,24},{1,25},{2,26},{3,27},{4,28},{5,29},{6,30},{7,31},{8,16},{9,... | collective-permute-start | bytes 491528 | tf_op jit(solution)/shard_map/ppermute | solution.py:283
  173.8 3.0 %collective-permute-done.5.refs_1_ = bf16[40,2048]{1,0:T(8,128)(2,1)S(1)} collective-permute-done((bf16[40,2048]{1,0:T(8,128)(2,1)S(1)}, bf16[40,2048]{1,0:T(8,128)(2,1)S(1)}, u32[]{:S(2)}, u32[]{:S(2)}) %collective-permute-start.5) | collective-permute-done | bytes 163872 | tf_op jit(solution)/shard_map/ppermute | solution.py:283
  176.8 2.2 %collective-permute-start.69 = (bf16[128,2048]{1,0:T(8,128)(2,1)S(1)}, bf16[128,2048]{1,0:T(8,128)(2,1)S(1)}, u32[]{:S(2)}, u32[]{:S(2)}) collective-permute-start(bf16[128,2048]{1,0:T(8,128)(2,1)S(1)} %shard_map.135), channel_id=1, source_target_pairs={{0,2},{1,3},{2,0},{3,1},{4,6},{5,7},{6,4},{7,5},{8,10},{9,11},{10,... | collective-permute-start | bytes 1572872 | tf_op jit(solution)/shard_map/ppermute | solution.py:271
  179.7 2.7 %collective-permute-start.53 = (bf16[128,2048]{1,0:T(8,128)(2,1)S(1)}, bf16[128,2048]{1,0:T(8,128)(2,1)S(1)}, u32[]{:S(2)}, u32[]{:S(2)}) collective-permute-start(bf16[128,2048]{1,0:T(8,128)(2,1)S(1)} %shard_map.132), channel_id=1, source_target_pairs={{0,6},{1,7},{2,4},{3,5},{4,2},{5,3},{6,0},{7,1},{8,14},{9,15},{10,... | collective-permute-start | bytes 1572872 | tf_op jit(solution)/shard_map/ppermute | solution.py:271
  182.8 3.2 %shard_map.125 = (bf16[40,2048]{1,0:T(8,128)(2,1)S(1)}, bf16[40,2048]{1,0:T(8,128)(2,1)S(1)}, bf16[40,2048]{1,0:T(8,128)(2,1)S(1)}, bf16[40,2048]{1,0:T(8,128)(2...) custom-call(bf16[40,2048]{1,0:T(8,128)(2,1)S(1)} %get-tuple-element., ...), custom_call_target="tpu_custom_call" | custom-call | tf_op jit(solution)/shard_map/pallas_call | solution.py:32
  186.0 2.2 %collective-permute-start.12 = (bf16[40,2048]{1,0:T(8,128)(2,1)S(1)}, bf16[40,2048]{1,0:T(8,128)(2,1)S(1)}, u32[]{:S(2)}, u32[]{:S(2)}) collective-permute-start(bf16[40,2048]{1,0:T(8,128)(2,1)S(1)} %get-tuple-element.90), channel_id=1, source_target_pairs={{0,8},{1,9},{2,10},{3,11},{4,12},{5,13},{6,14},{7,15},{8,0},{9,1},... | collective-permute-start | bytes 491528 | tf_op jit(solution)/shard_map/ppermute | solution.py:283
  188.4 1.4 collective-permute-start.14
  189.8 3.5 %collective-permute-done.12.refs_1_ = bf16[40,2048]{1,0:T(8,128)(2,1)S(1)} collective-permute-done((bf16[40,2048]{1,0:T(8,128)(2,1)S(1)}, bf16[40,2048]{1,0:T(8,128)(2,1)S(1)}, u32[]{:S(2)}, u32[]{:S(2)}) %collective-permute-start.12) | collective-permute-done | bytes 163872 | tf_op jit(solution)/shard_map/ppermute | solution.py:283
  193.3 4.7 %collective-permute-done.13.refs_2_ = bf16[40,2048]{1,0:T(8,128)(2,1)S(1)} collective-permute-done((bf16[40,2048]{1,0:T(8,128)(2,1)S(1)}, bf16[40,2048]{1,0:T(8,128)(2,1)S(1)}, u32[]{:S(2)}, u32[]{:S(2)}) %collective-permute-start.13) | collective-permute-done | bytes 163872 | tf_op jit(solution)/shard_map/ppermute | solution.py:283
  198.0 2.1 %collective-permute-start.18 = (bf16[40,2048]{1,0:T(8,128)(2,1)S(1)}, bf16[40,2048]{1,0:T(8,128)(2,1)S(1)}, u32[]{:S(2)}, u32[]{:S(2)}) collective-permute-start(bf16[40,2048]{1,0:T(8,128)(2,1)S(1)} %get-tuple-element.96), channel_id=1, source_target_pairs={{0,25},{1,24},{2,27},{3,26},{4,29},{5,28},{6,31},{7,30},{8,17},{9,... | collective-permute-start | bytes 491528 | tf_op jit(solution)/shard_map/ppermute | solution.py:283
  200.1 4.4 %collective-permute-done.16.refs_5_ = bf16[40,2048]{1,0:T(8,128)(2,1)S(1)} collective-permute-done((bf16[40,2048]{1,0:T(8,128)(2,1)S(1)}, bf16[40,2048]{1,0:T(8,128)(2,1)S(1)}, u32[]{:S(2)}, u32[]{:S(2)}) %collective-permute-start.16) | collective-permute-done | bytes 163872 | tf_op jit(solution)/shard_map/ppermute | solution.py:283
  204.5 2.9 %collective-permute-done.17.refs_6_ = bf16[40,2048]{1,0:T(8,128)(2,1)S(1)} collective-permute-done((bf16[40,2048]{1,0:T(8,128)(2,1)S(1)}, bf16[40,2048]{1,0:T(8,128)(2,1)S(1)}, u32[]{:S(2)}, u32[]{:S(2)}) %collective-permute-start.17) | collective-permute-done | bytes 163872 | tf_op jit(solution)/shard_map/ppermute | solution.py:283
  207.4 1.3 shard_map.136
  (131 shorter events, 22.0 us)
Async XLA Ops:
  4.1 11.5 %collective-permute-start.1 = (bf16[1024,128]{1,0:T(8,128)(2,1)S(1)}, bf16[1024,128]{1,0:T(8,128)(2,1)S(1)}, u32[]{:S(2)}, u32[]{:S(2)}) collective-permute-start(bf16[1024,128]{1,0:T(8,128)(2,1)S(1)} %add_convert_fusion.refs_0_), channel_id=1, source_target_pairs={{0,2},{1,3},{2,4},{3,5},{4,6},{5,7},{8,10},{9,11},{10,12},{11,13},... | collective-permute-start | bytes 786440 | tf_op jit(solution)/shard_map/ppermute | solution.py:289
  9.0 11.5 %collective-permute-start.2 = (bf16[1024,128]{1,0:T(8,128)(2,1)S(1)}, bf16[1024,128]{1,0:T(8,128)(2,1)S(1)}, u32[]{:S(2)}, u32[]{:S(2)}) collective-permute-start(bf16[1024,128]{1,0:T(8,128)(2,1)S(1)} %add_convert_fusion.refs_0_), channel_id=1, source_target_pairs={{0,4},{1,5},{8,12},{9,13},{16,20},{17,21},{24,28},{25,29}} | collective-permute-start | bytes 786440 | tf_op jit(solution)/shard_map/ppermute | solution.py:289
  31.3 36.9 %collective-permute-start.54 = (bf16[128,2048]{1,0:T(8,128)(2,1)}, bf16[128,2048]{1,0:T(8,128)(2,1)}, u32[]{:S(2)}, u32[]{:S(2)}) collective-permute-start(bf16[128,2048]{1,0:T(8,128)(2,1)} %get-tuple-element.79.own_ref), channel_id=1, source_target_pairs={{0,2},{1,3},{2,0},{3,1},{4,6},{5,7},{6,4},{7,5},{8,10},{9,11},{10,... | collective-permute-start | bytes 1572872 | tf_op jit(solution)/shard_map/ppermute | solution.py:271
  38.4 34.9 %collective-permute-start.19 = (bf16[128,2048]{1,0:T(8,128)(2,1)}, bf16[128,2048]{1,0:T(8,128)(2,1)}, u32[]{:S(2)}, u32[]{:S(2)}) collective-permute-start(bf16[128,2048]{1,0:T(8,128)(2,1)} %get-tuple-element.79.own_ref), channel_id=1, source_target_pairs={{0,4},{1,5},{2,6},{3,7},{4,0},{5,1},{6,2},{7,3},{8,12},{9,13},{10,... | collective-permute-start | bytes 1572872 | tf_op jit(solution)/shard_map/ppermute | solution.py:271
  41.9 20.6 %collective-permute-start.21 = (f32[32,128]{1,0:T(8,128)S(1)}, f32[32,128]{1,0:T(8,128)S(1)}, u32[]{:S(2)}, u32[]{:S(2)}) collective-permute-start(f32[32,128]{1,0:T(8,128)S(1)} %select_reduce_fusion.refs_0_), channel_id=1, source_target_pairs={{0,2},{1,3},{2,0},{3,1},{4,6},{5,7},{6,4},{7,5},{8,10},{9,11},{10,... | collective-permute-start | bytes 49160 | tf_op jit(solution)/shard_map/ppermute | solution.py:271
  43.6 32.7 %collective-permute-start.10 = (bf16[40,2048]{1,0:T(8,128)(2,1)S(1)}, bf16[40,2048]{1,0:T(8,128)(2,1)S(1)}, u32[]{:S(2)}, u32[]{:S(2)}) collective-permute-start(bf16[40,2048]{1,0:T(8,128)(2,1)S(1)} %get-tuple-element.87), channel_id=1, source_target_pairs={{0,17},{1,16},{2,19},{3,18},{4,21},{5,20},{6,23},{7,22},{8,25},{9,... | collective-permute-start | bytes 491528 | tf_op jit(solution)/shard_map/ppermute | solution.py:283
  44.7 21.6 %collective-permute-start.22 = (f32[32,128]{1,0:T(8,128)S(1)}, f32[32,128]{1,0:T(8,128)S(1)}, u32[]{:S(2)}, u32[]{:S(2)}) collective-permute-start(f32[32,128]{1,0:T(8,128)S(1)} %select_reduce_fusion.refs_0_), channel_id=1, source_target_pairs={{0,4},{1,5},{2,6},{3,7},{4,0},{5,1},{6,2},{7,3},{8,12},{9,13},{10,... | collective-permute-start | bytes 49160 | tf_op jit(solution)/shard_map/ppermute | solution.py:271
  69.7 8.2 %collective-permute-start.55 = (bf16[40,2048]{1,0:T(8,128)(2,1)S(1)}, bf16[40,2048]{1,0:T(8,128)(2,1)S(1)}, u32[]{:S(2)}, u32[]{:S(2)}) collective-permute-start(bf16[40,2048]{1,0:T(8,128)(2,1)S(1)} %get-tuple-element.134), channel_id=1, source_target_pairs={{0,8},{1,9},{2,10},{3,11},{4,12},{5,13},{6,14},{7,15},{8,0},{9,1},... | collective-permute-start | bytes 491528 | tf_op jit(solution)/shard_map/ppermute | solution.py:283
  71.3 9.3 %collective-permute-start.56 = (bf16[40,2048]{1,0:T(8,128)(2,1)S(1)}, bf16[40,2048]{1,0:T(8,128)(2,1)S(1)}, u32[]{:S(2)}, u32[]{:S(2)}) collective-permute-start(bf16[40,2048]{1,0:T(8,128)(2,1)S(1)} %get-tuple-element.135), channel_id=1, source_target_pairs={{0,16},{1,17},{2,18},{3,19},{4,20},{5,21},{6,22},{7,23},{8,24},{9,... | collective-permute-start | bytes 491528 | tf_op jit(solution)/shard_map/ppermute | solution.py:283
  72.8 8.2 %collective-permute-start.57 = (bf16[40,2048]{1,0:T(8,128)(2,1)S(1)}, bf16[40,2048]{1,0:T(8,128)(2,1)S(1)}, u32[]{:S(2)}, u32[]{:S(2)}) collective-permute-start(bf16[40,2048]{1,0:T(8,128)(2,1)S(1)} %get-tuple-element.136), channel_id=1, source_target_pairs={{0,24},{1,25},{2,26},{3,27},{4,28},{5,29},{6,30},{7,31},{8,16},{9,... | collective-permute-start | bytes 491528 | tf_op jit(solution)/shard_map/ppermute | solution.py:283
  74.8 8.8 %collective-permute-start.38 = (bf16[40,2048]{1,0:T(8,128)(2,1)S(1)}, bf16[40,2048]{1,0:T(8,128)(2,1)S(1)}, u32[]{:S(2)}, u32[]{:S(2)}) collective-permute-start(bf16[40,2048]{1,0:T(8,128)(2,1)S(1)} %get-tuple-element.118), channel_id=1, source_target_pairs={{0,8},{1,9},{2,10},{3,11},{4,12},{5,13},{6,14},{7,15},{8,0},{9,1},... | collective-permute-start | bytes 491528 | tf_op jit(solution)/shard_map/ppermute | solution.py:283
  76.4 9.6 %collective-permute-start.39 = (bf16[40,2048]{1,0:T(8,128)(2,1)S(1)}, bf16[40,2048]{1,0:T(8,128)(2,1)S(1)}, u32[]{:S(2)}, u32[]{:S(2)}) collective-permute-start(bf16[40,2048]{1,0:T(8,128)(2,1)S(1)} %get-tuple-element.119), channel_id=1, source_target_pairs={{0,16},{1,17},{2,18},{3,19},{4,20},{5,21},{6,22},{7,23},{8,24},{9,... | collective-permute-start | bytes 491528 | tf_op jit(solution)/shard_map/ppermute | solution.py:283
  77.9 10.1 %collective-permute-start.40 = (bf16[40,2048]{1,0:T(8,128)(2,1)S(1)}, bf16[40,2048]{1,0:T(8,128)(2,1)S(1)}, u32[]{:S(2)}, u32[]{:S(2)}) collective-permute-start(bf16[40,2048]{1,0:T(8,128)(2,1)S(1)} %get-tuple-element.120), channel_id=1, source_target_pairs={{0,24},{1,25},{2,26},{3,27},{4,28},{5,29},{6,30},{7,31},{8,16},{9,... | collective-permute-start | bytes 491528 | tf_op jit(solution)/shard_map/ppermute | solution.py:283
  80.6 7.5 %collective-permute-start.41 = (bf16[40,2048]{1,0:T(8,128)(2,1)S(1)}, bf16[40,2048]{1,0:T(8,128)(2,1)S(1)}, u32[]{:S(2)}, u32[]{:S(2)}) collective-permute-start(bf16[40,2048]{1,0:T(8,128)(2,1)S(1)} %get-tuple-element.121), channel_id=1, source_target_pairs={{0,1},{1,0},{2,3},{3,2},{4,5},{5,4},{6,7},{7,6},{8,9},{9,8},{10,11... | collective-permute-start | bytes 491528 | tf_op jit(solution)/shard_map/ppermute | solution.py:283
  81.0 7.7 %collective-permute-start.42 = (bf16[40,2048]{1,0:T(8,128)(2,1)S(1)}, bf16[40,2048]{1,0:T(8,128)(2,1)S(1)}, u32[]{:S(2)}, u32[]{:S(2)}) collective-permute-start(bf16[40,2048]{1,0:T(8,128)(2,1)S(1)} %get-tuple-element.122), channel_id=1, source_target_pairs={{0,9},{1,8},{2,11},{3,10},{4,13},{5,12},{6,15},{7,14},{8,1},{9,0},... | collective-permute-start | bytes 491528 | tf_op jit(solution)/shard_map/ppermute | solution.py:283
  83.6 10.7 %collective-permute-start.43 = (bf16[40,2048]{1,0:T(8,128)(2,1)S(1)}, bf16[40,2048]{1,0:T(8,128)(2,1)S(1)}, u32[]{:S(2)}, u32[]{:S(2)}) collective-permute-start(bf16[40,2048]{1,0:T(8,128)(2,1)S(1)} %get-tuple-element.123), channel_id=1, source_target_pairs={{0,17},{1,16},{2,19},{3,18},{4,21},{5,20},{6,23},{7,22},{8,25},{9,... | collective-permute-start | bytes 491528 | tf_op jit(solution)/shard_map/ppermute | solution.py:283
  86.0 35.5 %collective-permute-start.20 = (bf16[128,2048]{1,0:T(8,128)(2,1)}, bf16[128,2048]{1,0:T(8,128)(2,1)S(1)}, u32[]{:S(2)}, u32[]{:S(2)}) collective-permute-start(bf16[128,2048]{1,0:T(8,128)(2,1)} %collective-permute-done.19.own_ref), channel_id=1, source_target_pairs={{0,2},{1,3},{2,0},{3,1},{4,6},{5,7},{6,4},{7,5},{8,10},{9,11},{10,... | collective-permute-start | bytes 1572872 | tf_op jit(solution)/shard_map/ppermute | solution.py:271
  88.0 6.2 %collective-permute-start.44 = (bf16[40,2048]{1,0:T(8,128)(2,1)S(1)}, bf16[40,2048]{1,0:T(8,128)(2,1)S(1)}, u32[]{:S(2)}, u32[]{:S(2)}) collective-permute-start(bf16[40,2048]{1,0:T(8,128)(2,1)S(1)} %get-tuple-element.124), channel_id=1, source_target_pairs={{0,25},{1,24},{2,27},{3,26},{4,29},{5,28},{6,31},{7,30},{8,17},{9,... | collective-permute-start | bytes 491528 | tf_op jit(solution)/shard_map/ppermute | solution.py:283
  88.0 15.7 %collective-permute-start.58 = (bf16[40,2048]{1,0:T(8,128)(2,1)S(1)}, bf16[40,2048]{1,0:T(8,128)(2,1)S(1)}, u32[]{:S(2)}, u32[]{:S(2)}) collective-permute-start(bf16[40,2048]{1,0:T(8,128)(2,1)S(1)} %get-tuple-element.137), channel_id=1, source_target_pairs={{0,1},{1,0},{2,3},{3,2},{4,5},{5,4},{6,7},{7,6},{8,9},{9,8},{10,11... | collective-permute-start | bytes 491528 | tf_op jit(solution)/shard_map/ppermute | solution.py:283
  88.7 15.9 %collective-permute-start.59 = (bf16[40,2048]{1,0:T(8,128)(2,1)S(1)}, bf16[40,2048]{1,0:T(8,128)(2,1)S(1)}, u32[]{:S(2)}, u32[]{:S(2)}) collective-permute-start(bf16[40,2048]{1,0:T(8,128)(2,1)S(1)} %get-tuple-element.138), channel_id=1, source_target_pairs={{0,9},{1,8},{2,11},{3,10},{4,13},{5,12},{6,15},{7,14},{8,1},{9,0},... | collective-permute-start | bytes 491528 | tf_op jit(solution)/shard_map/ppermute | solution.py:283
  94.3 10.4 %collective-permute-start.60 = (bf16[40,2048]{1,0:T(8,128)(2,1)S(1)}, bf16[40,2048]{1,0:T(8,128)(2,1)S(1)}, u32[]{:S(2)}, u32[]{:S(2)}) collective-permute-start(bf16[40,2048]{1,0:T(8,128)(2,1)S(1)} %get-tuple-element.139), channel_id=1, source_target_pairs={{0,17},{1,16},{2,19},{3,18},{4,21},{5,20},{6,23},{7,22},{8,25},{9,... | collective-permute-start | bytes 491528 | tf_op jit(solution)/shard_map/ppermute | solution.py:283
  94.3 13.1 %collective-permute-start.61 = (bf16[40,2048]{1,0:T(8,128)(2,1)S(1)}, bf16[40,2048]{1,0:T(8,128)(2,1)S(1)}, u32[]{:S(2)}, u32[]{:S(2)}) collective-permute-start(bf16[40,2048]{1,0:T(8,128)(2,1)S(1)} %get-tuple-element.140), channel_id=1, source_target_pairs={{0,25},{1,24},{2,27},{3,26},{4,29},{5,28},{6,31},{7,30},{8,17},{9,... | collective-permute-start | bytes 491528 | tf_op jit(solution)/shard_map/ppermute | solution.py:283
  103.8 7.1 %collective-permute-start.45 = (bf16[40,2048]{1,0:T(8,128)(2,1)S(1)}, bf16[40,2048]{1,0:T(8,128)(2,1)S(1)}, u32[]{:S(2)}, u32[]{:S(2)}) collective-permute-start(bf16[40,2048]{1,0:T(8,128)(2,1)S(1)} %get-tuple-element.126), channel_id=1, source_target_pairs={{0,8},{1,9},{2,10},{3,11},{4,12},{5,13},{6,14},{7,15},{8,0},{9,1},... | collective-permute-start | bytes 491528 | tf_op jit(solution)/shard_map/ppermute | solution.py:283
  104.6 9.5 %collective-permute-start.46 = (bf16[40,2048]{1,0:T(8,128)(2,1)S(1)}, bf16[40,2048]{1,0:T(8,128)(2,1)S(1)}, u32[]{:S(2)}, u32[]{:S(2)}) collective-permute-start(bf16[40,2048]{1,0:T(8,128)(2,1)S(1)} %get-tuple-element.127), channel_id=1, source_target_pairs={{0,16},{1,17},{2,18},{3,19},{4,20},{5,21},{6,22},{7,23},{8,24},{9,... | collective-permute-start | bytes 491528 | tf_op jit(solution)/shard_map/ppermute | solution.py:283
  104.6 9.4 %collective-permute-start.47 = (bf16[40,2048]{1,0:T(8,128)(2,1)S(1)}, bf16[40,2048]{1,0:T(8,128)(2,1)S(1)}, u32[]{:S(2)}, u32[]{:S(2)}) collective-permute-start(bf16[40,2048]{1,0:T(8,128)(2,1)S(1)} %get-tuple-element.128), channel_id=1, source_target_pairs={{0,24},{1,25},{2,26},{3,27},{4,28},{5,29},{6,30},{7,31},{8,16},{9,... | collective-permute-start | bytes 491528 | tf_op jit(solution)/shard_map/ppermute | solution.py:283
  107.3 9.4 %collective-permute-start.48 = (bf16[40,2048]{1,0:T(8,128)(2,1)S(1)}, bf16[40,2048]{1,0:T(8,128)(2,1)S(1)}, u32[]{:S(2)}, u32[]{:S(2)}) collective-permute-start(bf16[40,2048]{1,0:T(8,128)(2,1)S(1)} %get-tuple-element.129), channel_id=1, source_target_pairs={{0,1},{1,0},{2,3},{3,2},{4,5},{5,4},{6,7},{7,6},{8,9},{9,8},{10,11... | collective-permute-start | bytes 491528 | tf_op jit(solution)/shard_map/ppermute | solution.py:283
  110.9 9.1 %collective-permute-start.49 = (bf16[40,2048]{1,0:T(8,128)(2,1)S(1)}, bf16[40,2048]{1,0:T(8,128)(2,1)S(1)}, u32[]{:S(2)}, u32[]{:S(2)}) collective-permute-start(bf16[40,2048]{1,0:T(8,128)(2,1)S(1)} %get-tuple-element.130), channel_id=1, source_target_pairs={{0,9},{1,8},{2,11},{3,10},{4,13},{5,12},{6,15},{7,14},{8,1},{9,0},... | collective-permute-start | bytes 491528 | tf_op jit(solution)/shard_map/ppermute | solution.py:283
  114.1 12.5 %collective-permute-start.50 = (bf16[40,2048]{1,0:T(8,128)(2,1)S(1)}, bf16[40,2048]{1,0:T(8,128)(2,1)S(1)}, u32[]{:S(2)}, u32[]{:S(2)}) collective-permute-start(bf16[40,2048]{1,0:T(8,128)(2,1)S(1)} %get-tuple-element.131), channel_id=1, source_target_pairs={{0,17},{1,16},{2,19},{3,18},{4,21},{5,20},{6,23},{7,22},{8,25},{9,... | collective-permute-start | bytes 491528 | tf_op jit(solution)/shard_map/ppermute | solution.py:283
  114.1 14.8 %collective-permute-start.51 = (bf16[40,2048]{1,0:T(8,128)(2,1)S(1)}, bf16[40,2048]{1,0:T(8,128)(2,1)S(1)}, u32[]{:S(2)}, u32[]{:S(2)}) collective-permute-start(bf16[40,2048]{1,0:T(8,128)(2,1)S(1)} %get-tuple-element.132), channel_id=1, source_target_pairs={{0,25},{1,24},{2,27},{3,26},{4,29},{5,28},{6,31},{7,30},{8,17},{9,... | collective-permute-start | bytes 491528 | tf_op jit(solution)/shard_map/ppermute | solution.py:283
  116.7 12.8 %collective-permute-start.11 = (bf16[40,2048]{1,0:T(8,128)(2,1)S(1)}, bf16[40,2048]{1,0:T(8,128)(2,1)S(1)}, u32[]{:S(2)}, u32[]{:S(2)}) collective-permute-start(bf16[40,2048]{1,0:T(8,128)(2,1)S(1)} %get-tuple-element.88), channel_id=1, source_target_pairs={{0,25},{1,24},{2,27},{3,26},{4,29},{5,28},{6,31},{7,30},{8,17},{9,... | collective-permute-start | bytes 491528 | tf_op jit(solution)/shard_map/ppermute | solution.py:283
  120.1 10.6 %collective-permute-start.62 = (bf16[40,2048]{1,0:T(8,128)(2,1)S(1)}, bf16[40,2048]{1,0:T(8,128)(2,1)S(1)}, u32[]{:S(2)}, u32[]{:S(2)}) collective-permute-start(bf16[40,2048]{1,0:T(8,128)(2,1)S(1)} %get-tuple-element.142), channel_id=1, source_target_pairs={{0,8},{1,9},{2,10},{3,11},{4,12},{5,13},{6,14},{7,15},{8,0},{9,1},... | collective-permute-start | bytes 491528 | tf_op jit(solution)/shard_map/ppermute | solution.py:283
  121.5 11.2 %collective-permute-start.63 = (bf16[40,2048]{1,0:T(8,128)(2,1)S(1)}, bf16[40,2048]{1,0:T(8,128)(2,1)S(1)}, u32[]{:S(2)}, u32[]{:S(2)}) collective-permute-start(bf16[40,2048]{1,0:T(8,128)(2,1)S(1)} %get-tuple-element.143), channel_id=1, source_target_pairs={{0,16},{1,17},{2,18},{3,19},{4,20},{5,21},{6,22},{7,23},{8,24},{9,... | collective-permute-start | bytes 491528 | tf_op jit(solution)/shard_map/ppermute | solution.py:283
  126.6 8.0 %collective-permute-start.64 = (bf16[40,2048]{1,0:T(8,128)(2,1)S(1)}, bf16[40,2048]{1,0:T(8,128)(2,1)S(1)}, u32[]{:S(2)}, u32[]{:S(2)}) collective-permute-start(bf16[40,2048]{1,0:T(8,128)(2,1)S(1)} %get-tuple-element.144), channel_id=1, source_target_pairs={{0,24},{1,25},{2,26},{3,27},{4,28},{5,29},{6,30},{7,31},{8,16},{9,... | collective-permute-start | bytes 491528 | tf_op jit(solution)/shard_map/ppermute | solution.py:283
  128.8 8.8 %collective-permute-start.24 = (bf16[40,2048]{1,0:T(8,128)(2,1)S(1)}, bf16[40,2048]{1,0:T(8,128)(2,1)S(1)}, u32[]{:S(2)}, u32[]{:S(2)}) collective-permute-start(bf16[40,2048]{1,0:T(8,128)(2,1)S(1)} %get-tuple-element.101), channel_id=1, source_target_pairs={{0,8},{1,9},{2,10},{3,11},{4,12},{5,13},{6,14},{7,15},{8,0},{9,1},... | collective-permute-start | bytes 491528 | tf_op jit(solution)/shard_map/ppermute | solution.py:283
  129.6 30.1 %collective-permute-start.52 = (bf16[128,2048]{1,0:T(8,128)(2,1)S(1)}, bf16[128,2048]{1,0:T(8,128)(2,1)S(1)}, u32[]{:S(2)}, u32[]{:S(2)}) collective-permute-start(bf16[128,2048]{1,0:T(8,128)(2,1)S(1)} %shard_map.131), channel_id=1, source_target_pairs={{0,2},{1,3},{2,0},{3,1},{4,6},{5,7},{6,4},{7,5},{8,10},{9,11},{10,... | collective-permute-start | bytes 1572872 | tf_op jit(solution)/shard_map/ppermute | solution.py:271
  130.7 10.2 %collective-permute-start.25 = (bf16[40,2048]{1,0:T(8,128)(2,1)S(1)}, bf16[40,2048]{1,0:T(8,128)(2,1)S(1)}, u32[]{:S(2)}, u32[]{:S(2)}) collective-permute-start(bf16[40,2048]{1,0:T(8,128)(2,1)S(1)} %get-tuple-element.102), channel_id=1, source_target_pairs={{0,16},{1,17},{2,18},{3,19},{4,20},{5,21},{6,22},{7,23},{8,24},{9,... | collective-permute-start | bytes 491528 | tf_op jit(solution)/shard_map/ppermute | solution.py:283
  132.7 8.2 %collective-permute-start.26 = (bf16[40,2048]{1,0:T(8,128)(2,1)S(1)}, bf16[40,2048]{1,0:T(8,128)(2,1)S(1)}, u32[]{:S(2)}, u32[]{:S(2)}) collective-permute-start(bf16[40,2048]{1,0:T(8,128)(2,1)S(1)} %get-tuple-element.103), channel_id=1, source_target_pairs={{0,24},{1,25},{2,26},{3,27},{4,28},{5,29},{6,30},{7,31},{8,16},{9,... | collective-permute-start | bytes 491528 | tf_op jit(solution)/shard_map/ppermute | solution.py:283
  134.6 9.1 %collective-permute-start.27 = (bf16[40,2048]{1,0:T(8,128)(2,1)S(1)}, bf16[40,2048]{1,0:T(8,128)(2,1)S(1)}, u32[]{:S(2)}, u32[]{:S(2)}) collective-permute-start(bf16[40,2048]{1,0:T(8,128)(2,1)S(1)} %get-tuple-element.104), channel_id=1, source_target_pairs={{0,1},{1,0},{2,3},{3,2},{4,5},{5,4},{6,7},{7,6},{8,9},{9,8},{10,11... | collective-permute-start | bytes 491528 | tf_op jit(solution)/shard_map/ppermute | solution.py:283
  137.6 6.1 %collective-permute-start.28 = (bf16[40,2048]{1,0:T(8,128)(2,1)S(1)}, bf16[40,2048]{1,0:T(8,128)(2,1)S(1)}, u32[]{:S(2)}, u32[]{:S(2)}) collective-permute-start(bf16[40,2048]{1,0:T(8,128)(2,1)S(1)} %get-tuple-element.105), channel_id=1, source_target_pairs={{0,9},{1,8},{2,11},{3,10},{4,13},{5,12},{6,15},{7,14},{8,1},{9,0},... | collective-permute-start | bytes 491528 | tf_op jit(solution)/shard_map/ppermute | solution.py:283
  140.9 8.9 %collective-permute-start.29 = (bf16[40,2048]{1,0:T(8,128)(2,1)S(1)}, bf16[40,2048]{1,0:T(8,128)(2,1)S(1)}, u32[]{:S(2)}, u32[]{:S(2)}) collective-permute-start(bf16[40,2048]{1,0:T(8,128)(2,1)S(1)} %get-tuple-element.106), channel_id=1, source_target_pairs={{0,17},{1,16},{2,19},{3,18},{4,21},{5,20},{6,23},{7,22},{8,25},{9,... | collective-permute-start | bytes 491528 | tf_op jit(solution)/shard_map/ppermute | solution.py:283
  140.9 9.3 %collective-permute-start.30 = (bf16[40,2048]{1,0:T(8,128)(2,1)S(1)}, bf16[40,2048]{1,0:T(8,128)(2,1)S(1)}, u32[]{:S(2)}, u32[]{:S(2)}) collective-permute-start(bf16[40,2048]{1,0:T(8,128)(2,1)S(1)} %get-tuple-element.107), channel_id=1, source_target_pairs={{0,25},{1,24},{2,27},{3,26},{4,29},{5,28},{6,31},{7,30},{8,17},{9,... | collective-permute-start | bytes 491528 | tf_op jit(solution)/shard_map/ppermute | solution.py:283
  143.7 12.4 %collective-permute-start.65 = (bf16[40,2048]{1,0:T(8,128)(2,1)S(1)}, bf16[40,2048]{1,0:T(8,128)(2,1)S(1)}, u32[]{:S(2)}, u32[]{:S(2)}) collective-permute-start(bf16[40,2048]{1,0:T(8,128)(2,1)S(1)} %get-tuple-element.145), channel_id=1, source_target_pairs={{0,1},{1,0},{2,3},{3,2},{4,5},{5,4},{6,7},{7,6},{8,9},{9,8},{10,11... | collective-permute-start | bytes 491528 | tf_op jit(solution)/shard_map/ppermute | solution.py:283
  143.7 12.6 %collective-permute-start.66 = (bf16[40,2048]{1,0:T(8,128)(2,1)S(1)}, bf16[40,2048]{1,0:T(8,128)(2,1)S(1)}, u32[]{:S(2)}, u32[]{:S(2)}) collective-permute-start(bf16[40,2048]{1,0:T(8,128)(2,1)S(1)} %get-tuple-element.146), channel_id=1, source_target_pairs={{0,9},{1,8},{2,11},{3,10},{4,13},{5,12},{6,15},{7,14},{8,1},{9,0},... | collective-permute-start | bytes 491528 | tf_op jit(solution)/shard_map/ppermute | solution.py:283
  149.8 9.2 %collective-permute-start.67 = (bf16[40,2048]{1,0:T(8,128)(2,1)S(1)}, bf16[40,2048]{1,0:T(8,128)(2,1)S(1)}, u32[]{:S(2)}, u32[]{:S(2)}) collective-permute-start(bf16[40,2048]{1,0:T(8,128)(2,1)S(1)} %get-tuple-element.147), channel_id=1, source_target_pairs={{0,17},{1,16},{2,19},{3,18},{4,21},{5,20},{6,23},{7,22},{8,25},{9,... | collective-permute-start | bytes 491528 | tf_op jit(solution)/shard_map/ppermute | solution.py:283
  150.2 9.5 %collective-permute-start.68 = (bf16[40,2048]{1,0:T(8,128)(2,1)S(1)}, bf16[40,2048]{1,0:T(8,128)(2,1)S(1)}, u32[]{:S(2)}, u32[]{:S(2)}) collective-permute-start(bf16[40,2048]{1,0:T(8,128)(2,1)S(1)} %get-tuple-element.148), channel_id=1, source_target_pairs={{0,25},{1,24},{2,27},{3,26},{4,29},{5,28},{6,31},{7,30},{8,17},{9,... | collective-permute-start | bytes 491528 | tf_op jit(solution)/shard_map/ppermute | solution.py:283
  156.3 9.0 %collective-permute-start.32 = (bf16[40,2048]{1,0:T(8,128)(2,1)S(1)}, bf16[40,2048]{1,0:T(8,128)(2,1)S(1)}, u32[]{:S(2)}, u32[]{:S(2)}) collective-permute-start(bf16[40,2048]{1,0:T(8,128)(2,1)S(1)} %get-tuple-element.110), channel_id=1, source_target_pairs={{0,16},{1,17},{2,18},{3,19},{4,20},{5,21},{6,22},{7,23},{8,24},{9,... | collective-permute-start | bytes 491528 | tf_op jit(solution)/shard_map/ppermute | solution.py:283
  159.0 9.0 %collective-permute-start.33 = (bf16[40,2048]{1,0:T(8,128)(2,1)S(1)}, bf16[40,2048]{1,0:T(8,128)(2,1)S(1)}, u32[]{:S(2)}, u32[]{:S(2)}) collective-permute-start(bf16[40,2048]{1,0:T(8,128)(2,1)S(1)} %get-tuple-element.111), channel_id=1, source_target_pairs={{0,24},{1,25},{2,26},{3,27},{4,28},{5,29},{6,30},{7,31},{8,16},{9,... | collective-permute-start | bytes 491528 | tf_op jit(solution)/shard_map/ppermute | solution.py:283
  159.6 8.7 %collective-permute-start.34 = (bf16[40,2048]{1,0:T(8,128)(2,1)S(1)}, bf16[40,2048]{1,0:T(8,128)(2,1)S(1)}, u32[]{:S(2)}, u32[]{:S(2)}) collective-permute-start(bf16[40,2048]{1,0:T(8,128)(2,1)S(1)} %get-tuple-element.112), channel_id=1, source_target_pairs={{0,1},{1,0},{2,3},{3,2},{4,5},{5,4},{6,7},{7,6},{8,9},{9,8},{10,11... | collective-permute-start | bytes 491528 | tf_op jit(solution)/shard_map/ppermute | solution.py:283
  159.6 9.1 %collective-permute-start.35 = (bf16[40,2048]{1,0:T(8,128)(2,1)S(1)}, bf16[40,2048]{1,0:T(8,128)(2,1)S(1)}, u32[]{:S(2)}, u32[]{:S(2)}) collective-permute-start(bf16[40,2048]{1,0:T(8,128)(2,1)S(1)} %get-tuple-element.113), channel_id=1, source_target_pairs={{0,9},{1,8},{2,11},{3,10},{4,13},{5,12},{6,15},{7,14},{8,1},{9,0},... | collective-permute-start | bytes 491528 | tf_op jit(solution)/shard_map/ppermute | solution.py:283
  161.8 10.7 %collective-permute-start.36 = (bf16[40,2048]{1,0:T(8,128)(2,1)S(1)}, bf16[40,2048]{1,0:T(8,128)(2,1)S(1)}, u32[]{:S(2)}, u32[]{:S(2)}) collective-permute-start(bf16[40,2048]{1,0:T(8,128)(2,1)S(1)} %get-tuple-element.114), channel_id=1, source_target_pairs={{0,17},{1,16},{2,19},{3,18},{4,21},{5,20},{6,23},{7,22},{8,25},{9,... | collective-permute-start | bytes 491528 | tf_op jit(solution)/shard_map/ppermute | solution.py:283
  165.3 7.5 %collective-permute-start.37 = (bf16[40,2048]{1,0:T(8,128)(2,1)S(1)}, bf16[40,2048]{1,0:T(8,128)(2,1)S(1)}, u32[]{:S(2)}, u32[]{:S(2)}) collective-permute-start(bf16[40,2048]{1,0:T(8,128)(2,1)S(1)} %get-tuple-element.115), channel_id=1, source_target_pairs={{0,25},{1,24},{2,27},{3,26},{4,29},{5,28},{6,31},{7,30},{8,17},{9,... | collective-permute-start | bytes 491528 | tf_op jit(solution)/shard_map/ppermute | solution.py:283
  167.9 8.9 %collective-permute-start.5 = (bf16[40,2048]{1,0:T(8,128)(2,1)S(1)}, bf16[40,2048]{1,0:T(8,128)(2,1)S(1)}, u32[]{:S(2)}, u32[]{:S(2)}) collective-permute-start(bf16[40,2048]{1,0:T(8,128)(2,1)S(1)} %get-tuple-element.82), channel_id=1, source_target_pairs={{0,8},{1,9},{2,10},{3,11},{4,12},{5,13},{6,14},{7,15},{8,0},{9,1},... | collective-permute-start | bytes 491528 | tf_op jit(solution)/shard_map/ppermute | solution.py:283
  168.3 11.4 %collective-permute-start.6 = (bf16[40,2048]{1,0:T(8,128)(2,1)S(1)}, bf16[40,2048]{1,0:T(8,128)(2,1)S(1)}, u32[]{:S(2)}, u32[]{:S(2)}) collective-permute-start(bf16[40,2048]{1,0:T(8,128)(2,1)S(1)} %get-tuple-element.83), channel_id=1, source_target_pairs={{0,16},{1,17},{2,18},{3,19},{4,20},{5,21},{6,22},{7,23},{8,24},{9,... | collective-permute-start | bytes 491528 | tf_op jit(solution)/shard_map/ppermute | solution.py:283
  168.8 13.7 %collective-permute-start.7 = (bf16[40,2048]{1,0:T(8,128)(2,1)S(1)}, bf16[40,2048]{1,0:T(8,128)(2,1)S(1)}, u32[]{:S(2)}, u32[]{:S(2)}) collective-permute-start(bf16[40,2048]{1,0:T(8,128)(2,1)S(1)} %get-tuple-element.84), channel_id=1, source_target_pairs={{0,24},{1,25},{2,26},{3,27},{4,28},{5,29},{6,30},{7,31},{8,16},{9,... | collective-permute-start | bytes 491528 | tf_op jit(solution)/shard_map/ppermute | solution.py:283
  172.5 10.0 %collective-permute-start.8 = (bf16[40,2048]{1,0:T(8,128)(2,1)S(1)}, bf16[40,2048]{1,0:T(8,128)(2,1)S(1)}, u32[]{:S(2)}, u32[]{:S(2)}) collective-permute-start(bf16[40,2048]{1,0:T(8,128)(2,1)S(1)} %get-tuple-element.85), channel_id=1, source_target_pairs={{0,1},{1,0},{2,3},{3,2},{4,5},{5,4},{6,7},{7,6},{8,9},{9,8},{10,11... | collective-permute-start | bytes 491528 | tf_op jit(solution)/shard_map/ppermute | solution.py:283
  172.9 9.9 %collective-permute-start.9 = (bf16[40,2048]{1,0:T(8,128)(2,1)S(1)}, bf16[40,2048]{1,0:T(8,128)(2,1)S(1)}, u32[]{:S(2)}, u32[]{:S(2)}) collective-permute-start(bf16[40,2048]{1,0:T(8,128)(2,1)S(1)} %get-tuple-element.86), channel_id=1, source_target_pairs={{0,9},{1,8},{2,11},{3,10},{4,13},{5,12},{6,15},{7,14},{8,1},{9,0},... | collective-permute-start | bytes 491528 | tf_op jit(solution)/shard_map/ppermute | solution.py:283
  176.8 30.5 %collective-permute-start.69 = (bf16[128,2048]{1,0:T(8,128)(2,1)S(1)}, bf16[128,2048]{1,0:T(8,128)(2,1)S(1)}, u32[]{:S(2)}, u32[]{:S(2)}) collective-permute-start(bf16[128,2048]{1,0:T(8,128)(2,1)S(1)} %shard_map.135), channel_id=1, source_target_pairs={{0,2},{1,3},{2,0},{3,1},{4,6},{5,7},{6,4},{7,5},{8,10},{9,11},{10,... | collective-permute-start | bytes 1572872 | tf_op jit(solution)/shard_map/ppermute | solution.py:271
  179.7 27.6 %collective-permute-start.53 = (bf16[128,2048]{1,0:T(8,128)(2,1)S(1)}, bf16[128,2048]{1,0:T(8,128)(2,1)S(1)}, u32[]{:S(2)}, u32[]{:S(2)}) collective-permute-start(bf16[128,2048]{1,0:T(8,128)(2,1)S(1)} %shard_map.132), channel_id=1, source_target_pairs={{0,6},{1,7},{2,4},{3,5},{4,2},{5,3},{6,0},{7,1},{8,14},{9,15},{10,... | collective-permute-start | bytes 1572872 | tf_op jit(solution)/shard_map/ppermute | solution.py:271
  186.0 7.3 %collective-permute-start.12 = (bf16[40,2048]{1,0:T(8,128)(2,1)S(1)}, bf16[40,2048]{1,0:T(8,128)(2,1)S(1)}, u32[]{:S(2)}, u32[]{:S(2)}) collective-permute-start(bf16[40,2048]{1,0:T(8,128)(2,1)S(1)} %get-tuple-element.90), channel_id=1, source_target_pairs={{0,8},{1,9},{2,10},{3,11},{4,12},{5,13},{6,14},{7,15},{8,0},{9,1},... | collective-permute-start | bytes 491528 | tf_op jit(solution)/shard_map/ppermute | solution.py:283
  188.2 9.8 %collective-permute-start.13 = (bf16[40,2048]{1,0:T(8,128)(2,1)S(1)}, bf16[40,2048]{1,0:T(8,128)(2,1)S(1)}, u32[]{:S(2)}, u32[]{:S(2)}) collective-permute-start(bf16[40,2048]{1,0:T(8,128)(2,1)S(1)} %get-tuple-element.91), channel_id=1, source_target_pairs={{0,16},{1,17},{2,18},{3,19},{4,20},{5,21},{6,22},{7,23},{8,24},{9,... | collective-permute-start | bytes 491528 | tf_op jit(solution)/shard_map/ppermute | solution.py:283
  188.4 9.6 %collective-permute-start.14 = (bf16[40,2048]{1,0:T(8,128)(2,1)S(1)}, bf16[40,2048]{1,0:T(8,128)(2,1)S(1)}, u32[]{:S(2)}, u32[]{:S(2)}) collective-permute-start(bf16[40,2048]{1,0:T(8,128)(2,1)S(1)} %get-tuple-element.92), channel_id=1, source_target_pairs={{0,24},{1,25},{2,26},{3,27},{4,28},{5,29},{6,30},{7,31},{8,16},{9,... | collective-permute-start | bytes 491528 | tf_op jit(solution)/shard_map/ppermute | solution.py:283
  198.0 6.5 %collective-permute-start.16 = (bf16[40,2048]{1,0:T(8,128)(2,1)S(1)}, bf16[40,2048]{1,0:T(8,128)(2,1)S(1)}, u32[]{:S(2)}, u32[]{:S(2)}) collective-permute-start(bf16[40,2048]{1,0:T(8,128)(2,1)S(1)} %get-tuple-element.94), channel_id=1, source_target_pairs={{0,9},{1,8},{2,11},{3,10},{4,13},{5,12},{6,15},{7,14},{8,1},{9,0},... | collective-permute-start | bytes 491528 | tf_op jit(solution)/shard_map/ppermute | solution.py:283
  198.0 9.4 %collective-permute-start.17 = (bf16[40,2048]{1,0:T(8,128)(2,1)S(1)}, bf16[40,2048]{1,0:T(8,128)(2,1)S(1)}, u32[]{:S(2)}, u32[]{:S(2)}) collective-permute-start(bf16[40,2048]{1,0:T(8,128)(2,1)S(1)} %get-tuple-element.95), channel_id=1, source_target_pairs={{0,17},{1,16},{2,19},{3,18},{4,21},{5,20},{6,23},{7,22},{8,25},{9,... | collective-permute-start | bytes 491528 | tf_op jit(solution)/shard_map/ppermute | solution.py:283
  198.0 9.3 %collective-permute-start.18 = (bf16[40,2048]{1,0:T(8,128)(2,1)S(1)}, bf16[40,2048]{1,0:T(8,128)(2,1)S(1)}, u32[]{:S(2)}, u32[]{:S(2)}) collective-permute-start(bf16[40,2048]{1,0:T(8,128)(2,1)S(1)} %get-tuple-element.96), channel_id=1, source_target_pairs={{0,25},{1,24},{2,27},{3,26},{4,29},{5,28},{6,31},{7,30},{8,17},{9,... | collective-permute-start | bytes 491528 | tf_op jit(solution)/shard_map/ppermute | solution.py:283
  (22 other events, 233.4 us)

commit v7 on v6

--- a/solution.py
+++ b/solution.py
@@ -32,7 +32,7 @@
         return pl.pallas_call(
             body,
             in_specs=specs,
-            out_specs=[pl.BlockSpec(memory_space=pltpu.VMEM)] * len(outs),
+            out_specs=[pl.BlockSpec(memory_space=pltpu.HBM if leave else pltpu.VMEM)] * len(outs),
             out_shape=[
                 jax.ShapeDtypeStruct(shape, dtype) if leave else pltpu.VMEM(shape, dtype)
                 for shape, dtype in outs
@@ -108,9 +108,11 @@
 
 
 def project_kernel(
-    core_ref, in_ref, q_ref, mine_ref, other_ref, pair_ref, gain_ref, resid_ref, w_ref, mgain_ref,
-    res_ref, moe_ref, normed_ref,
+    slots, core_ref, in_ref, q_ref, mine_ref, other_ref, pair_ref, gain_ref, resid_ref, w_ref,
+    mgain_ref, rank_ref, res_ref, moe_ref, *rest,
 ):
+    outs, normed_ref = rest[:-1], rest[-1]
+    pick = picks(slots, rank_ref, 0, len(outs))
     core = core_ref[0]
     heads = q_ref.shape[1] // HEAD
     half = heads // 2
@@ -136,7 +138,13 @@
         wide = rounded.astype(F32)
         square = square + jnp.sum(wide * wide, axis=1, keepdims=True)
     scale = lax.rsqrt(square / features + epsilon)
-    moe_ref[...] = (res_ref[...].astype(F32) * scale * mgain_ref[...]).astype(BF)
+    for i in range(4):
+        at = slice(i * width, (i + 1) * width)
+        moe_in = (res_ref[:, at].astype(F32) * scale * mgain_ref[:, at]).astype(BF)
+        moe_ref[:, at] = moe_in
+        picked = dot(pick, moe_in)
+        for k, out in enumerate(outs):
+            out[:, at] = picked[k * slots : (k + 1) * slots].astype(BF)
 
 
 def rank_kernel(groups, length, group_ref, place_ref, *refs):
@@ -166,9 +174,13 @@
     return jnp.where(number == rank, value, 0.0)
 
 
+def picks(slots, rank_ref, base, count):
+    rows = [slots_of(rank_ref, 1.0, base + i, slots) for i in range(count)]
+    return jnp.concatenate(rows, axis=0).astype(BF)
+
+
 def select_kernel(slots, base, own_ref, rank_ref, *outs):
-    rows = [slots_of(rank_ref, 1.0, base + i, slots) for i in range(len(outs))]
-    picked = dot(jnp.concatenate(rows, axis=0).astype(BF), own_ref[...]).astype(BF)
+    picked = dot(picks(slots, rank_ref, base, len(outs)), own_ref[...]).astype(BF)
     for i, out in enumerate(outs):
         out[...] = picked[i * slots : (i + 1) * slots]
 
@@ -184,20 +196,48 @@
     rank_ref, weight_ref = refs[count : count + 2]
     more = refs[count + 2 : -1]
     rows = stacked(backs)
-    parts = []
-    for i in range(count):
-        row = base + i
-        parts.append(slots_of(rank_ref, weight_ref[row : row + 1, :], row, slots))
-    total = dot(jnp.concatenate(parts, axis=0).astype(BF), rows, 0, 0)
+    total = dot(shares_of(slots, count, base, rank_ref, weight_ref), rows, 0, 0)
     for ref in more:
         total = total + ref[...].astype(F32)
     refs[-1][...] = total.astype(BF)
 
 
-def combine(slots, base, backs, rank, weight, more, leave):
-    body = functools.partial(combine_kernel, slots, len(backs), base)
+def finish_kernel(slots, count, base, *refs):
+    backs = refs[:count]
+    rank_ref, weight_ref = refs[count : count + 2]
+    more = refs[count + 2 : -3]
+    out_hbm, out_ref, sems = refs[-3:]
+    shares = shares_of(slots, count, base, rank_ref, weight_ref)
+    parts = sems.shape[0]
+    width = out_ref.shape[1] // parts
+    copies = []
+    for i in range(parts):
+        at = pl.ds(i * width, width)
+        total = dot(shares, stacked([r.at[:, at] for r in backs]), 0, 0)
+        for ref in more:
+            total = total + ref[:, at].astype(F32)
+        out_ref[:, at] = total.astype(BF)
+        copies.append(pltpu.make_async_copy(out_ref.at[:, at], out_hbm.at[:, at], sems.at[i]))
+        copies[-1].start()
+    for copy in copies:
+        copy.wait()
+
+
+def shares_of(slots, count, base, rank_ref, weight_ref):
+    parts = []
+    for row in range(base, base + count):
+        parts.append(slots_of(rank_ref, weight_ref[row : row + 1, :], row, slots))
+    return jnp.concatenate(parts, axis=0).astype(BF)
+
+
+def combine(slots, base, backs, rank, weight, more, last):
     shape = ((rank.shape[1], backs[0].shape[1]), BF)
-    return call(body, [shape], leave=leave)(*backs, rank, weight, *more)[0]
+    kernel, scratch = combine_kernel, []
+    if last:
+        kernel = finish_kernel
+        scratch = [pltpu.VMEM(*shape), pltpu.SemaphoreType.DMA((4,))]
+    body = functools.partial(kernel, slots, len(backs), base)
+    return call(body, [shape], scratch, leave=last)(*backs, rank, weight, *more)[0]
 
 
 def stacked(refs):
@@ -297,7 +337,7 @@
     states = call(
         state_kernel,
         [((inner, HEAD), BF)],
-        [pltpu.VMEM(keys.shape, BF)] * 2 + [pltpu.SemaphoreType.DMA((2, 4))],
+        [pltpu.VMEM(keys.shape, BF)] * 2 + [pltpu.SemaphoreType.DMA((2, 1))],
         away=(0, 1),
     )(keys, values)[0]
     pair = swap(states)
@@ -337,8 +377,10 @@
 
     mine = added(*arrived)
     other = swap(mine)
-    residual, moe_in = call(
-        project_kernel, [((tokens, features), BF)] * 2, [pltpu.VMEM((tokens, inner), BF)]
+    residual, moe_in, *near = call(
+        functools.partial(project_kernel, slots),
+        [((tokens, features), BF)] * 2 + [((slots, features), BF)] * (2 * groups),
+        [pltpu.VMEM((tokens, inner), BF)],
     )(
         scalars[0],
         inside,
@@ -350,6 +392,7 @@
         resid_in.reshape(tokens, features),
         out_proj,
         moe_gain.reshape(1, features),
+        own_tables[1],
     )
 
     routing = sending(stages)
@@ -361,7 +404,9 @@
         blocks[m] = along(blocks[source], shift)
     for m in range(stages):
         (routes, ranks), base = lookup[m]
-        picked = select(slots, 2 * groups, base, blocks[m], ranks)
+        picked = near
+        if m:
+            picked = select(slots, 2 * groups, base, blocks[m], ranks)
         taken = straight(picked)
         outs[m] = experts(taken, gate_weight, up_weight, down_weight)
     sums = {m: [] for m in range(stages)}

time: 209 us -> 198 us (0.947)
  local copies, waits for them, and re-layouts: 7.3 us -> 0.04 us
  waiting for transfers between devices: 91.2 us -> 85.2 us
  starting transfers between devices: 79.6 us -> 84.8 us
  Pallas kernels: 30.1 us -> 25.9 us
    ppermute x56, waiting for transfers between devices: 63.4 us -> 55.7 us  [straight(): x = lax.ppermute(x, ('grp', 'seq'), pairs)]
    unnamed x32 -> x18, local copies, waits for them, and re-layouts: 7.3 us -> 0.04 us
    pallas_call x19 -> x18, Pallas kernels: 30.1 us -> 25.9 us  [run(): pl.pallas_call(body, in_specs=specs, out_specs=[pl.BlockSpec(memory_space...]
    ppermute x56, starting transfers between devices: 49 us -> 51.8 us  [straight(): x = lax.ppermute(x, ('grp', 'seq'), pairs)]
    ppermute x9, starting transfers between devices: 19.9 us -> 22.3 us  [along(): return lax.ppermute(x, 'seq', [(s, s ^ 2 * m) for s in range(length)])]
  transfers between devices with their start and end apart: 70 -> 70, of which waited for: 31 -> 34; matrix products, arithmetic and copies ran while one was open for 0% -> 0% of each run, Pallas kernels for 11% -> 10%
where the time goes in v7:
time: 198 us; the launch traced here: 197 us
  waiting for transfers between devices  85.2 us (43%)
  starting transfers between devices  84.8 us (43%)
  Pallas kernels  25.9 us (13%)
    ppermute x56, waiting for transfers between devices, straight(): x = lax.ppermute(x, ('grp', 'seq'), pairs)  55.7 us
    ppermute x56, starting transfers between devices, straight(): x = lax.ppermute(x, ('grp', 'seq'), pairs)  51.8 us
    pallas_call x18, Pallas kernels, run(): pl.pallas_call(body, in_specs=specs, out_specs=[pl.BlockSpec(memory_space...  25.9 us
    ppermute x9, starting transfers between devices, along(): return lax.ppermute(x, 'seq', [(s, s ^ 2 * m) for s in range(length)])  22.3 us
    ppermute x9, waiting for transfers between devices, along(): return lax.ppermute(x, 'seq', [(s, s ^ 2 * m) for s in range(length)])  21.8 us
    ppermute x3, starting transfers between devices, later(): return lax.ppermute(x, 'seq', pairs)  10 us
    ppermute x3, waiting for transfers between devices, later(): return lax.ppermute(x, 'seq', pairs)  6.21 us
  transfers between devices with their start and end apart: 70, of which 34 were waited for; matrix products, arithmetic and copies ran while one was open for 0% of the time, Pallas kernels for 10%

profile of v7, /device:TPU:0, one launch (start us, length us, event | category | flops | bytes accessed | tf_op | source)
XLA Modules:
  0.0 196.6 jit_solution(6247188256147044607)
XLA Ops:
  0.0 1.6 shard_map.119
  2.2 1.5 collective-permute-done.pair_ref
  3.8 4.9 %collective-permute-start.1 = (bf16[1024,128]{1,0:T(8,128)(2,1)S(1)}, bf16[1024,128]{1,0:T(8,128)(2,1)S(1)}, u32[]{:S(2)}, u32[]{:S(2)}) collective-permute-start(bf16[1024,128]{1,0:T(8,128)(2,1)S(1)} %add_convert_fusion.refs_0_), channel_id=1, source_target_pairs={{0,2},{1,3},{2,4},{3,5},{4,6},{5,7},{8,10},{9,11},{10,12},{11,13},... | collective-permute-start | bytes 786440 | tf_op jit(solution)/shard_map/ppermute | solution.py:329
  8.6 4.5 %collective-permute-start.2 = (bf16[1024,128]{1,0:T(8,128)(2,1)S(1)}, bf16[1024,128]{1,0:T(8,128)(2,1)S(1)}, u32[]{:S(2)}, u32[]{:S(2)}) collective-permute-start(bf16[1024,128]{1,0:T(8,128)(2,1)S(1)} %add_convert_fusion.refs_0_), channel_id=1, source_target_pairs={{0,4},{1,5},{8,12},{9,13},{16,20},{17,21},{24,28},{25,29}} | collective-permute-start | bytes 786440 | tf_op jit(solution)/shard_map/ppermute | solution.py:329
  13.1 2.2 %collective-permute-done.1.refs_1_.refs_0_ = bf16[1024,128]{1,0:T(8,128)(2,1)S(1)} collective-permute-done((bf16[1024,128]{1,0:T(8,128)(2,1)S(1)}, bf16[1024,128]{1,0:T(8,128)(2,1)S(1)}, u32[]{:S(2)}, u32[]{:S(2)}) %collective-permute-start.1) | collective-permute-done | bytes 262176 | tf_op jit(solution)/shard_map/ppermute | solution.py:329
  16.1 4.1 %collective-permute-done.2.refs_1_ = bf16[1024,128]{1,0:T(8,128)(2,1)S(1)} collective-permute-done((bf16[1024,128]{1,0:T(8,128)(2,1)S(1)}, bf16[1024,128]{1,0:T(8,128)(2,1)S(1)}, u32[]{:S(2)}, u32[]{:S(2)}) %collective-permute-start.2) | collective-permute-done | bytes 262176 | tf_op jit(solution)/shard_map/ppermute | solution.py:329
  20.5 4.2 %shard_map.118 = (f32[128,2048]{1,0:T(8,128)S(1)}, bf16[2048,2048]{1,0:T(8,128)(2,1)S(1)}) custom-call(bf16[128,2048]{1,0:T(8,128)(2,1)} %bitcast.19, bf16[128,2048]{1,0:T(8,128)(2,1)} %bitcast.25, bf16[128,2048]{1,0:T(8,128)(2,1)} %bitcast.27, bf16[2048,2048]{1,0:T(8,128)(2,1)} %w_hbm.1, s32[1]{0:T(128)} %bitcast.core_ref, s32[1]{0:T(128)} %bitcast.4.group_ref, ...), custom_call_target="tpu_custom_call" | custom-call | tf_op jit(solution)/shard_map/pallas_call | solution.py:32
  24.8 2.5 %shard_map.123 = (bf16[128,2048]{1,0:T(8,128)(2,1)S(1)}, bf16[128,2048]{1,0:T(8,128)(2,1)S(1)}, bf16[40,2048]{1,0:T(8,128)(2,1)S(1)}, bf16[40,2048]{1,0:T(8,128)...) custom-call(s32[1]{0:T(128)} %bitcast.core_ref, ...), custom_call_target="tpu_custom_call" | custom-call | tf_op jit(solution)/shard_map/pallas_call | solution.py:32
  27.3 7.2 %collective-permute-start.54 = (bf16[128,2048]{1,0:T(8,128)(2,1)S(1)}, bf16[128,2048]{1,0:T(8,128)(2,1)S(1)}, u32[]{:S(2)}, u32[]{:S(2)}) collective-permute-start(bf16[128,2048]{1,0:T(8,128)(2,1)S(1)} %get-tuple-element.98), channel_id=1, source_target_pairs={{0,2},{1,3},{2,0},{3,1},{4,6},{5,7},{6,4},{7,5},{8,10},{9,11},{10,... | collective-permute-start | bytes 1572872 | tf_op jit(solution)/shard_map/ppermute | solution.py:311
  34.5 3.4 %collective-permute-start.19 = (bf16[128,2048]{1,0:T(8,128)(2,1)S(1)}, bf16[128,2048]{1,0:T(8,128)(2,1)S(1)}, u32[]{:S(2)}, u32[]{:S(2)}) collective-permute-start(bf16[128,2048]{1,0:T(8,128)(2,1)S(1)} %get-tuple-element.98), channel_id=1, source_target_pairs={{0,4},{1,5},{2,6},{3,7},{4,0},{5,1},{6,2},{7,3},{8,12},{9,13},{10,... | collective-permute-start | bytes 1572872 | tf_op jit(solution)/shard_map/ppermute | solution.py:311
  38.0 1.0 collective-permute-start.10
  39.4 19.1 %collective-permute-done.21.refs_0_ = f32[32,128]{1,0:T(8,128)S(1)} collective-permute-done((f32[32,128]{1,0:T(8,128)S(1)}, f32[32,128]{1,0:T(8,128)S(1)}, u32[]{:S(2)}, u32[]{:S(2)}) %collective-permute-start.21) | collective-permute-done | bytes 16416 | tf_op jit(solution)/shard_map/ppermute | solution.py:311
  58.4 2.8 %collective-permute-start.23 = (f32[32,128]{1,0:T(8,128)S(1)}, f32[32,128]{1,0:T(8,128)S(1)}, u32[]{:S(2)}, u32[]{:S(2)}) collective-permute-start(f32[32,128]{1,0:T(8,128)S(1)} %select_reduce_fusion.refs_0_), channel_id=1, source_target_pairs={{0,6},{1,7},{2,4},{3,5},{4,2},{5,3},{6,0},{7,1},{8,14},{9,15},{10,... | collective-permute-start | bytes 49160 | tf_op jit(solution)/shard_map/ppermute | solution.py:311
  62.2 1.8 collective-permute-done.23.refs_2_
  64.6 1.6 collective-permute-start.55
  66.2 1.5 collective-permute-start.56
  68.7 1.6 collective-permute-start.38
  70.2 1.5 collective-permute-start.39
  71.8 2.5 %collective-permute-start.40 = (bf16[40,2048]{1,0:T(8,128)(2,1)S(1)}, bf16[40,2048]{1,0:T(8,128)(2,1)S(1)}, u32[]{:S(2)}, u32[]{:S(2)}) collective-permute-start(bf16[40,2048]{1,0:T(8,128)(2,1)S(1)} %get-tuple-element.120), channel_id=1, source_target_pairs={{0,24},{1,25},{2,26},{3,27},{4,28},{5,29},{6,30},{7,31},{8,16},{9,... | collective-permute-start | bytes 491528 | tf_op jit(solution)/shard_map/ppermute | solution.py:323
  74.2 2.0 %collective-permute-done.56.refs_2_ = bf16[40,2048]{1,0:T(8,128)(2,1)S(1)} collective-permute-done((bf16[40,2048]{1,0:T(8,128)(2,1)S(1)}, bf16[40,2048]{1,0:T(8,128)(2,1)S(1)}, u32[]{:S(2)}, u32[]{:S(2)}) %collective-permute-start.56) | collective-permute-done | bytes 163872 | tf_op jit(solution)/shard_map/ppermute | solution.py:323
  76.5 2.0 %collective-permute-done.38.refs_1_ = bf16[40,2048]{1,0:T(8,128)(2,1)S(1)} collective-permute-done((bf16[40,2048]{1,0:T(8,128)(2,1)S(1)}, bf16[40,2048]{1,0:T(8,128)(2,1)S(1)}, u32[]{:S(2)}, u32[]{:S(2)}) %collective-permute-start.38) | collective-permute-done | bytes 163872 | tf_op jit(solution)/shard_map/ppermute | solution.py:323
  78.5 2.3 %collective-permute-done.39.refs_2_ = bf16[40,2048]{1,0:T(8,128)(2,1)S(1)} collective-permute-done((bf16[40,2048]{1,0:T(8,128)(2,1)S(1)}, bf16[40,2048]{1,0:T(8,128)(2,1)S(1)}, u32[]{:S(2)}, u32[]{:S(2)}) %collective-permute-start.39) | collective-permute-done | bytes 163872 | tf_op jit(solution)/shard_map/ppermute | solution.py:323
  81.6 1.4 collective-permute-done.40.refs_3_
  83.5 1.4 collective-permute-start.59
  84.9 4.3 %collective-permute-done.43.refs_6_ = bf16[40,2048]{1,0:T(8,128)(2,1)S(1)} collective-permute-done((bf16[40,2048]{1,0:T(8,128)(2,1)S(1)}, bf16[40,2048]{1,0:T(8,128)(2,1)S(1)}, u32[]{:S(2)}, u32[]{:S(2)}) %collective-permute-start.43) | collective-permute-done | bytes 163872 | tf_op jit(solution)/shard_map/ppermute | solution.py:323
  89.2 2.4 %collective-permute-start.61 = (bf16[40,2048]{1,0:T(8,128)(2,1)S(1)}, bf16[40,2048]{1,0:T(8,128)(2,1)S(1)}, u32[]{:S(2)}, u32[]{:S(2)}) collective-permute-start(bf16[40,2048]{1,0:T(8,128)(2,1)S(1)} %get-tuple-element.140), channel_id=1, source_target_pairs={{0,25},{1,24},{2,27},{3,26},{4,29},{5,28},{6,31},{7,30},{8,17},{9,... | collective-permute-start | bytes 491528 | tf_op jit(solution)/shard_map/ppermute | solution.py:323
  91.6 3.3 %shard_map.129 = (bf16[40,2048]{1,0:T(8,128)(2,1)S(1)}, bf16[40,2048]{1,0:T(8,128)(2,1)S(1)}, bf16[40,2048]{1,0:T(8,128)(2,1)S(1)}, bf16[40,2048]{1,0:T(8,128)(2...) custom-call(bf16[40,2048]{1,0:T(8,128)(2,1)S(1)} %get-tuple-element., ...), custom_call_target="tpu_custom_call" | custom-call | tf_op jit(solution)/shard_map/pallas_call | solution.py:32
  95.9 3.0 %collective-permute-done.60.refs_6_ = bf16[40,2048]{1,0:T(8,128)(2,1)S(1)} collective-permute-done((bf16[40,2048]{1,0:T(8,128)(2,1)S(1)}, bf16[40,2048]{1,0:T(8,128)(2,1)S(1)}, u32[]{:S(2)}, u32[]{:S(2)}) %collective-permute-start.60) | collective-permute-done | bytes 163872 | tf_op jit(solution)/shard_map/ppermute | solution.py:323
  100.3 1.1 collective-permute-done.45.refs_1_
  101.4 1.4 collective-permute-done.46.refs_2_
  102.8 4.1 %collective-permute-done.47.refs_3_ = bf16[40,2048]{1,0:T(8,128)(2,1)S(1)} collective-permute-done((bf16[40,2048]{1,0:T(8,128)(2,1)S(1)}, bf16[40,2048]{1,0:T(8,128)(2,1)S(1)}, u32[]{:S(2)}, u32[]{:S(2)}) %collective-permute-start.47) | collective-permute-done | bytes 163872 | tf_op jit(solution)/shard_map/ppermute | solution.py:323
  107.0 2.6 %collective-permute-start.11 = (bf16[40,2048]{1,0:T(8,128)(2,1)S(1)}, bf16[40,2048]{1,0:T(8,128)(2,1)S(1)}, u32[]{:S(2)}, u32[]{:S(2)}) collective-permute-start(bf16[40,2048]{1,0:T(8,128)(2,1)S(1)} %get-tuple-element.87), channel_id=1, source_target_pairs={{0,25},{1,24},{2,27},{3,26},{4,29},{5,28},{6,31},{7,30},{8,17},{9,... | collective-permute-start | bytes 491528 | tf_op jit(solution)/shard_map/ppermute | solution.py:323
  109.5 3.3 %shard_map.133 = (bf16[40,2048]{1,0:T(8,128)(2,1)S(1)}, bf16[40,2048]{1,0:T(8,128)(2,1)S(1)}, bf16[40,2048]{1,0:T(8,128)(2,1)S(1)}, bf16[40,2048]{1,0:T(8,128)(2...) custom-call(bf16[40,2048]{1,0:T(8,128)(2,1)S(1)} %get-tuple-element., ...), custom_call_target="tpu_custom_call" | custom-call | tf_op jit(solution)/shard_map/pallas_call | solution.py:32
  112.8 1.1 collective-permute-start.62
  114.9 2.0 %collective-permute-start.64 = (bf16[40,2048]{1,0:T(8,128)(2,1)S(1)}, bf16[40,2048]{1,0:T(8,128)(2,1)S(1)}, u32[]{:S(2)}, u32[]{:S(2)}) collective-permute-start(bf16[40,2048]{1,0:T(8,128)(2,1)S(1)} %get-tuple-element.144), channel_id=1, source_target_pairs={{0,24},{1,25},{2,26},{3,27},{4,28},{5,29},{6,30},{7,31},{8,16},{9,... | collective-permute-start | bytes 491528 | tf_op jit(solution)/shard_map/ppermute | solution.py:323
  117.0 1.0 collective-permute-start.24
  120.0 1.7 collective-permute-start.25
  122.5 2.2 %collective-permute-done.64.refs_3_ = bf16[40,2048]{1,0:T(8,128)(2,1)S(1)} collective-permute-done((bf16[40,2048]{1,0:T(8,128)(2,1)S(1)}, bf16[40,2048]{1,0:T(8,128)(2,1)S(1)}, u32[]{:S(2)}, u32[]{:S(2)}) %collective-permute-start.64) | collective-permute-done | bytes 163872 | tf_op jit(solution)/shard_map/ppermute | solution.py:323
  124.8 2.2 %collective-permute-done.24.refs_1_ = bf16[40,2048]{1,0:T(8,128)(2,1)S(1)} collective-permute-done((bf16[40,2048]{1,0:T(8,128)(2,1)S(1)}, bf16[40,2048]{1,0:T(8,128)(2,1)S(1)}, u32[]{:S(2)}, u32[]{:S(2)}) %collective-permute-start.24) | collective-permute-done | bytes 163872 | tf_op jit(solution)/shard_map/ppermute | solution.py:323
  128.3 1.6 collective-permute-start.29
  129.9 1.9 collective-permute-done.26.refs_3_
  132.5 1.5 collective-permute-done.28.refs_5_
  135.3 1.2 collective-permute-start.67
  136.5 2.5 %collective-permute-done.30.refs_7_ = bf16[40,2048]{1,0:T(8,128)(2,1)S(1)} collective-permute-done((bf16[40,2048]{1,0:T(8,128)(2,1)S(1)}, bf16[40,2048]{1,0:T(8,128)(2,1)S(1)}, u32[]{:S(2)}, u32[]{:S(2)}) %collective-permute-start.30) | collective-permute-done | bytes 163872 | tf_op jit(solution)/shard_map/ppermute | solution.py:323
  139.9 3.3 %shard_map.127 = (bf16[40,2048]{1,0:T(8,128)(2,1)S(1)}, bf16[40,2048]{1,0:T(8,128)(2,1)S(1)}, bf16[40,2048]{1,0:T(8,128)(2,1)S(1)}, bf16[40,2048]{1,0:T(8,128)(2...) custom-call(bf16[40,2048]{1,0:T(8,128)(2,1)S(1)} %get-tuple-element., ...), custom_call_target="tpu_custom_call" | custom-call | tf_op jit(solution)/shard_map/pallas_call | solution.py:32
  144.0 1.7 collective-permute-start.32
  145.7 1.1 collective-permute-start.33
  146.8 1.8 collective-permute-start.34
  148.6 1.3 collective-permute-done.31.refs_1_
  150.9 2.1 %collective-permute-done.32.refs_2_ = bf16[40,2048]{1,0:T(8,128)(2,1)S(1)} collective-permute-done((bf16[40,2048]{1,0:T(8,128)(2,1)S(1)}, bf16[40,2048]{1,0:T(8,128)(2,1)S(1)}, u32[]{:S(2)}, u32[]{:S(2)}) %collective-permute-start.32) | collective-permute-done | bytes 163872 | tf_op jit(solution)/shard_map/ppermute | solution.py:323
  153.0 2.0 %collective-permute-start.37 = (bf16[40,2048]{1,0:T(8,128)(2,1)S(1)}, bf16[40,2048]{1,0:T(8,128)(2,1)S(1)}, u32[]{:S(2)}, u32[]{:S(2)}) collective-permute-start(bf16[40,2048]{1,0:T(8,128)(2,1)S(1)} %get-tuple-element.115), channel_id=1, source_target_pairs={{0,25},{1,24},{2,27},{3,26},{4,29},{5,28},{6,31},{7,30},{8,17},{9,... | collective-permute-start | bytes 491528 | tf_op jit(solution)/shard_map/ppermute | solution.py:323
  155.7 1.7 collective-permute-start.6
  159.7 1.5 collective-permute-done.37.refs_7_
  162.6 6.8 %collective-permute-start.69 = (bf16[128,2048]{1,0:T(8,128)(2,1)S(1)}, bf16[128,2048]{1,0:T(8,128)(2,1)S(1)}, u32[]{:S(2)}, u32[]{:S(2)}) collective-permute-start(bf16[128,2048]{1,0:T(8,128)(2,1)S(1)} %shard_map.134), channel_id=1, source_target_pairs={{0,2},{1,3},{2,0},{3,1},{4,6},{5,7},{6,4},{7,5},{8,10},{9,11},{10,... | collective-permute-start | bytes 1572872 | tf_op jit(solution)/shard_map/ppermute | solution.py:311
  170.6 3.3 %shard_map.124 = (bf16[40,2048]{1,0:T(8,128)(2,1)S(1)}, bf16[40,2048]{1,0:T(8,128)(2,1)S(1)}, bf16[40,2048]{1,0:T(8,128)(2,1)S(1)}, bf16[40,2048]{1,0:T(8,128)(2...) custom-call(bf16[40,2048]{1,0:T(8,128)(2,1)S(1)} %get-tuple-element., ...), custom_call_target="tpu_custom_call" | custom-call | tf_op jit(solution)/shard_map/pallas_call | solution.py:32
  173.9 2.1 %collective-permute-start.12 = (bf16[40,2048]{1,0:T(8,128)(2,1)S(1)}, bf16[40,2048]{1,0:T(8,128)(2,1)S(1)}, u32[]{:S(2)}, u32[]{:S(2)}) collective-permute-start(bf16[40,2048]{1,0:T(8,128)(2,1)S(1)} %get-tuple-element.89), channel_id=1, source_target_pairs={{0,8},{1,9},{2,10},{3,11},{4,12},{5,13},{6,14},{7,15},{8,0},{9,1},... | collective-permute-start | bytes 491528 | tf_op jit(solution)/shard_map/ppermute | solution.py:323
  177.5 3.5 %collective-permute-done.12.refs_1_ = bf16[40,2048]{1,0:T(8,128)(2,1)S(1)} collective-permute-done((bf16[40,2048]{1,0:T(8,128)(2,1)S(1)}, bf16[40,2048]{1,0:T(8,128)(2,1)S(1)}, u32[]{:S(2)}, u32[]{:S(2)}) %collective-permute-start.12) | collective-permute-done | bytes 163872 | tf_op jit(solution)/shard_map/ppermute | solution.py:323
  181.1 2.3 %collective-permute-done.13.refs_2_ = bf16[40,2048]{1,0:T(8,128)(2,1)S(1)} collective-permute-done((bf16[40,2048]{1,0:T(8,128)(2,1)S(1)}, bf16[40,2048]{1,0:T(8,128)(2,1)S(1)}, u32[]{:S(2)}, u32[]{:S(2)}) %collective-permute-start.13) | collective-permute-done | bytes 163872 | tf_op jit(solution)/shard_map/ppermute | solution.py:323
  183.9 1.3 collective-permute-done.14.refs_3_
  185.2 2.0 %collective-permute-start.17 = (bf16[40,2048]{1,0:T(8,128)(2,1)S(1)}, bf16[40,2048]{1,0:T(8,128)(2,1)S(1)}, u32[]{:S(2)}, u32[]{:S(2)}) collective-permute-start(bf16[40,2048]{1,0:T(8,128)(2,1)S(1)} %get-tuple-element.94), channel_id=1, source_target_pairs={{0,17},{1,16},{2,19},{3,18},{4,21},{5,20},{6,23},{7,22},{8,25},{9,... | collective-permute-start | bytes 491528 | tf_op jit(solution)/shard_map/ppermute | solution.py:323
  187.2 1.7 collective-permute-done.16.refs_5_
  188.9 5.1 %collective-permute-done.17.refs_6_ = bf16[40,2048]{1,0:T(8,128)(2,1)S(1)} collective-permute-done((bf16[40,2048]{1,0:T(8,128)(2,1)S(1)}, bf16[40,2048]{1,0:T(8,128)(2,1)S(1)}, u32[]{:S(2)}, u32[]{:S(2)}) %collective-permute-start.17) | collective-permute-done | bytes 163872 | tf_op jit(solution)/shard_map/ppermute | solution.py:323
  194.0 1.2 collective-permute-done.18.refs_7_
  195.2 1.2 shard_map.135
  (116 shorter events, 26.3 us)
Async XLA Ops:
  3.8 11.5 %collective-permute-start.1 = (bf16[1024,128]{1,0:T(8,128)(2,1)S(1)}, bf16[1024,128]{1,0:T(8,128)(2,1)S(1)}, u32[]{:S(2)}, u32[]{:S(2)}) collective-permute-start(bf16[1024,128]{1,0:T(8,128)(2,1)S(1)} %add_convert_fusion.refs_0_), channel_id=1, source_target_pairs={{0,2},{1,3},{2,4},{3,5},{4,6},{5,7},{8,10},{9,11},{10,12},{11,13},... | collective-permute-start | bytes 786440 | tf_op jit(solution)/shard_map/ppermute | solution.py:329
  8.6 11.5 %collective-permute-start.2 = (bf16[1024,128]{1,0:T(8,128)(2,1)S(1)}, bf16[1024,128]{1,0:T(8,128)(2,1)S(1)}, u32[]{:S(2)}, u32[]{:S(2)}) collective-permute-start(bf16[1024,128]{1,0:T(8,128)(2,1)S(1)} %add_convert_fusion.refs_0_), channel_id=1, source_target_pairs={{0,4},{1,5},{8,12},{9,13},{16,20},{17,21},{24,28},{25,29}} | collective-permute-start | bytes 786440 | tf_op jit(solution)/shard_map/ppermute | solution.py:329
  27.3 36.8 %collective-permute-start.54 = (bf16[128,2048]{1,0:T(8,128)(2,1)S(1)}, bf16[128,2048]{1,0:T(8,128)(2,1)S(1)}, u32[]{:S(2)}, u32[]{:S(2)}) collective-permute-start(bf16[128,2048]{1,0:T(8,128)(2,1)S(1)} %get-tuple-element.98), channel_id=1, source_target_pairs={{0,2},{1,3},{2,0},{3,1},{4,6},{5,7},{6,4},{7,5},{8,10},{9,11},{10,... | collective-permute-start | bytes 1572872 | tf_op jit(solution)/shard_map/ppermute | solution.py:311
  34.5 33.7 %collective-permute-start.19 = (bf16[128,2048]{1,0:T(8,128)(2,1)S(1)}, bf16[128,2048]{1,0:T(8,128)(2,1)S(1)}, u32[]{:S(2)}, u32[]{:S(2)}) collective-permute-start(bf16[128,2048]{1,0:T(8,128)(2,1)S(1)} %get-tuple-element.98), channel_id=1, source_target_pairs={{0,4},{1,5},{2,6},{3,7},{4,0},{5,1},{6,2},{7,3},{8,12},{9,13},{10,... | collective-permute-start | bytes 1572872 | tf_op jit(solution)/shard_map/ppermute | solution.py:311
  37.9 20.6 %collective-permute-start.21 = (f32[32,128]{1,0:T(8,128)S(1)}, f32[32,128]{1,0:T(8,128)S(1)}, u32[]{:S(2)}, u32[]{:S(2)}) collective-permute-start(f32[32,128]{1,0:T(8,128)S(1)} %select_reduce_fusion.refs_0_), channel_id=1, source_target_pairs={{0,2},{1,3},{2,0},{3,1},{4,6},{5,7},{6,4},{7,5},{8,10},{9,11},{10,... | collective-permute-start | bytes 49160 | tf_op jit(solution)/shard_map/ppermute | solution.py:311
  38.0 32.3 %collective-permute-start.10 = (bf16[40,2048]{1,0:T(8,128)(2,1)S(1)}, bf16[40,2048]{1,0:T(8,128)(2,1)S(1)}, u32[]{:S(2)}, u32[]{:S(2)}) collective-permute-start(bf16[40,2048]{1,0:T(8,128)(2,1)S(1)} %get-tuple-element.86), channel_id=1, source_target_pairs={{0,17},{1,16},{2,19},{3,18},{4,21},{5,20},{6,23},{7,22},{8,25},{9,... | collective-permute-start | bytes 491528 | tf_op jit(solution)/shard_map/ppermute | solution.py:323
  39.0 23.1 %collective-permute-start.22 = (f32[32,128]{1,0:T(8,128)S(1)}, f32[32,128]{1,0:T(8,128)S(1)}, u32[]{:S(2)}, u32[]{:S(2)}) collective-permute-start(f32[32,128]{1,0:T(8,128)S(1)} %select_reduce_fusion.refs_0_), channel_id=1, source_target_pairs={{0,4},{1,5},{2,6},{3,7},{4,0},{5,1},{6,2},{7,3},{8,12},{9,13},{10,... | collective-permute-start | bytes 49160 | tf_op jit(solution)/shard_map/ppermute | solution.py:311
  64.6 7.1 %collective-permute-start.55 = (bf16[40,2048]{1,0:T(8,128)(2,1)S(1)}, bf16[40,2048]{1,0:T(8,128)(2,1)S(1)}, u32[]{:S(2)}, u32[]{:S(2)}) collective-permute-start(bf16[40,2048]{1,0:T(8,128)(2,1)S(1)} %get-tuple-element.134), channel_id=1, source_target_pairs={{0,8},{1,9},{2,10},{3,11},{4,12},{5,13},{6,14},{7,15},{8,0},{9,1},... | collective-permute-start | bytes 491528 | tf_op jit(solution)/shard_map/ppermute | solution.py:323
  66.2 10.0 %collective-permute-start.56 = (bf16[40,2048]{1,0:T(8,128)(2,1)S(1)}, bf16[40,2048]{1,0:T(8,128)(2,1)S(1)}, u32[]{:S(2)}, u32[]{:S(2)}) collective-permute-start(bf16[40,2048]{1,0:T(8,128)(2,1)S(1)} %get-tuple-element.135), channel_id=1, source_target_pairs={{0,16},{1,17},{2,18},{3,19},{4,20},{5,21},{6,22},{7,23},{8,24},{9,... | collective-permute-start | bytes 491528 | tf_op jit(solution)/shard_map/ppermute | solution.py:323
  67.7 8.5 %collective-permute-start.57 = (bf16[40,2048]{1,0:T(8,128)(2,1)S(1)}, bf16[40,2048]{1,0:T(8,128)(2,1)S(1)}, u32[]{:S(2)}, u32[]{:S(2)}) collective-permute-start(bf16[40,2048]{1,0:T(8,128)(2,1)S(1)} %get-tuple-element.136), channel_id=1, source_target_pairs={{0,24},{1,25},{2,26},{3,27},{4,28},{5,29},{6,30},{7,31},{8,16},{9,... | collective-permute-start | bytes 491528 | tf_op jit(solution)/shard_map/ppermute | solution.py:323
  68.7 9.8 %collective-permute-start.38 = (bf16[40,2048]{1,0:T(8,128)(2,1)S(1)}, bf16[40,2048]{1,0:T(8,128)(2,1)S(1)}, u32[]{:S(2)}, u32[]{:S(2)}) collective-permute-start(bf16[40,2048]{1,0:T(8,128)(2,1)S(1)} %get-tuple-element.118), channel_id=1, source_target_pairs={{0,8},{1,9},{2,10},{3,11},{4,12},{5,13},{6,14},{7,15},{8,0},{9,1},... | collective-permute-start | bytes 491528 | tf_op jit(solution)/shard_map/ppermute | solution.py:323
  70.2 10.6 %collective-permute-start.39 = (bf16[40,2048]{1,0:T(8,128)(2,1)S(1)}, bf16[40,2048]{1,0:T(8,128)(2,1)S(1)}, u32[]{:S(2)}, u32[]{:S(2)}) collective-permute-start(bf16[40,2048]{1,0:T(8,128)(2,1)S(1)} %get-tuple-element.119), channel_id=1, source_target_pairs={{0,16},{1,17},{2,18},{3,19},{4,20},{5,21},{6,22},{7,23},{8,24},{9,... | collective-permute-start | bytes 491528 | tf_op jit(solution)/shard_map/ppermute | solution.py:323
  71.8 11.2 %collective-permute-start.40 = (bf16[40,2048]{1,0:T(8,128)(2,1)S(1)}, bf16[40,2048]{1,0:T(8,128)(2,1)S(1)}, u32[]{:S(2)}, u32[]{:S(2)}) collective-permute-start(bf16[40,2048]{1,0:T(8,128)(2,1)S(1)} %get-tuple-element.120), channel_id=1, source_target_pairs={{0,24},{1,25},{2,26},{3,27},{4,28},{5,29},{6,30},{7,31},{8,16},{9,... | collective-permute-start | bytes 491528 | tf_op jit(solution)/shard_map/ppermute | solution.py:323
  76.2 6.8 %collective-permute-start.41 = (bf16[40,2048]{1,0:T(8,128)(2,1)S(1)}, bf16[40,2048]{1,0:T(8,128)(2,1)S(1)}, u32[]{:S(2)}, u32[]{:S(2)}) collective-permute-start(bf16[40,2048]{1,0:T(8,128)(2,1)S(1)} %get-tuple-element.121), channel_id=1, source_target_pairs={{0,1},{1,0},{2,3},{3,2},{4,5},{5,4},{6,7},{7,6},{8,9},{9,8},{10,11... | collective-permute-start | bytes 491528 | tf_op jit(solution)/shard_map/ppermute | solution.py:323
  76.2 7.3 %collective-permute-start.42 = (bf16[40,2048]{1,0:T(8,128)(2,1)S(1)}, bf16[40,2048]{1,0:T(8,128)(2,1)S(1)}, u32[]{:S(2)}, u32[]{:S(2)}) collective-permute-start(bf16[40,2048]{1,0:T(8,128)(2,1)S(1)} %get-tuple-element.122), channel_id=1, source_target_pairs={{0,9},{1,8},{2,11},{3,10},{4,13},{5,12},{6,15},{7,14},{8,1},{9,0},... | collective-permute-start | bytes 491528 | tf_op jit(solution)/shard_map/ppermute | solution.py:323
  78.5 10.7 %collective-permute-start.43 = (bf16[40,2048]{1,0:T(8,128)(2,1)S(1)}, bf16[40,2048]{1,0:T(8,128)(2,1)S(1)}, u32[]{:S(2)}, u32[]{:S(2)}) collective-permute-start(bf16[40,2048]{1,0:T(8,128)(2,1)S(1)} %get-tuple-element.123), channel_id=1, source_target_pairs={{0,17},{1,16},{2,19},{3,18},{4,21},{5,20},{6,23},{7,22},{8,25},{9,... | collective-permute-start | bytes 491528 | tf_op jit(solution)/shard_map/ppermute | solution.py:323
  80.8 33.1 %collective-permute-start.20 = (bf16[128,2048]{1,0:T(8,128)(2,1)S(1)}, bf16[128,2048]{1,0:T(8,128)(2,1)S(1)}, u32[]{:S(2)}, u32[]{:S(2)}) collective-permute-start(bf16[128,2048]{1,0:T(8,128)(2,1)S(1)} %collective-permute-done.19.own_ref), channel_id=1, source_target_pairs={{0,2},{1,3},{2,0},{3,1},{4,6},{5,7},{6,4},{7,5},{8,10},{9,11},{10,... | collective-permute-start | bytes 1572872 | tf_op jit(solution)/shard_map/ppermute | solution.py:311
  83.0 6.2 %collective-permute-start.44 = (bf16[40,2048]{1,0:T(8,128)(2,1)S(1)}, bf16[40,2048]{1,0:T(8,128)(2,1)S(1)}, u32[]{:S(2)}, u32[]{:S(2)}) collective-permute-start(bf16[40,2048]{1,0:T(8,128)(2,1)S(1)} %get-tuple-element.124), channel_id=1, source_target_pairs={{0,25},{1,24},{2,27},{3,26},{4,29},{5,28},{6,31},{7,30},{8,17},{9,... | collective-permute-start | bytes 491528 | tf_op jit(solution)/shard_map/ppermute | solution.py:323
  83.0 11.9 %collective-permute-start.58 = (bf16[40,2048]{1,0:T(8,128)(2,1)S(1)}, bf16[40,2048]{1,0:T(8,128)(2,1)S(1)}, u32[]{:S(2)}, u32[]{:S(2)}) collective-permute-start(bf16[40,2048]{1,0:T(8,128)(2,1)S(1)} %get-tuple-element.137), channel_id=1, source_target_pairs={{0,1},{1,0},{2,3},{3,2},{4,5},{5,4},{6,7},{7,6},{8,9},{9,8},{10,11... | collective-permute-start | bytes 491528 | tf_op jit(solution)/shard_map/ppermute | solution.py:323
  83.5 12.3 %collective-permute-start.59 = (bf16[40,2048]{1,0:T(8,128)(2,1)S(1)}, bf16[40,2048]{1,0:T(8,128)(2,1)S(1)}, u32[]{:S(2)}, u32[]{:S(2)}) collective-permute-start(bf16[40,2048]{1,0:T(8,128)(2,1)S(1)} %get-tuple-element.138), channel_id=1, source_target_pairs={{0,9},{1,8},{2,11},{3,10},{4,13},{5,12},{6,15},{7,14},{8,1},{9,0},... | collective-permute-start | bytes 491528 | tf_op jit(solution)/shard_map/ppermute | solution.py:323
  89.2 9.7 %collective-permute-start.60 = (bf16[40,2048]{1,0:T(8,128)(2,1)S(1)}, bf16[40,2048]{1,0:T(8,128)(2,1)S(1)}, u32[]{:S(2)}, u32[]{:S(2)}) collective-permute-start(bf16[40,2048]{1,0:T(8,128)(2,1)S(1)} %get-tuple-element.139), channel_id=1, source_target_pairs={{0,17},{1,16},{2,19},{3,18},{4,21},{5,20},{6,23},{7,22},{8,25},{9,... | collective-permute-start | bytes 491528 | tf_op jit(solution)/shard_map/ppermute | solution.py:323
  89.2 10.6 %collective-permute-start.61 = (bf16[40,2048]{1,0:T(8,128)(2,1)S(1)}, bf16[40,2048]{1,0:T(8,128)(2,1)S(1)}, u32[]{:S(2)}, u32[]{:S(2)}) collective-permute-start(bf16[40,2048]{1,0:T(8,128)(2,1)S(1)} %get-tuple-element.140), channel_id=1, source_target_pairs={{0,25},{1,24},{2,27},{3,26},{4,29},{5,28},{6,31},{7,30},{8,17},{9,... | collective-permute-start | bytes 491528 | tf_op jit(solution)/shard_map/ppermute | solution.py:323
  94.9 6.5 %collective-permute-start.45 = (bf16[40,2048]{1,0:T(8,128)(2,1)S(1)}, bf16[40,2048]{1,0:T(8,128)(2,1)S(1)}, u32[]{:S(2)}, u32[]{:S(2)}) collective-permute-start(bf16[40,2048]{1,0:T(8,128)(2,1)S(1)} %get-tuple-element.126), channel_id=1, source_target_pairs={{0,8},{1,9},{2,10},{3,11},{4,12},{5,13},{6,14},{7,15},{8,0},{9,1},... | collective-permute-start | bytes 491528 | tf_op jit(solution)/shard_map/ppermute | solution.py:323
  95.8 6.9 %collective-permute-start.46 = (bf16[40,2048]{1,0:T(8,128)(2,1)S(1)}, bf16[40,2048]{1,0:T(8,128)(2,1)S(1)}, u32[]{:S(2)}, u32[]{:S(2)}) collective-permute-start(bf16[40,2048]{1,0:T(8,128)(2,1)S(1)} %get-tuple-element.127), channel_id=1, source_target_pairs={{0,16},{1,17},{2,18},{3,19},{4,20},{5,21},{6,22},{7,23},{8,24},{9,... | collective-permute-start | bytes 491528 | tf_op jit(solution)/shard_map/ppermute | solution.py:323
  98.9 8.0 %collective-permute-start.47 = (bf16[40,2048]{1,0:T(8,128)(2,1)S(1)}, bf16[40,2048]{1,0:T(8,128)(2,1)S(1)}, u32[]{:S(2)}, u32[]{:S(2)}) collective-permute-start(bf16[40,2048]{1,0:T(8,128)(2,1)S(1)} %get-tuple-element.128), channel_id=1, source_target_pairs={{0,24},{1,25},{2,26},{3,27},{4,28},{5,29},{6,30},{7,31},{8,16},{9,... | collective-permute-start | bytes 491528 | tf_op jit(solution)/shard_map/ppermute | solution.py:323
  99.9 7.1 %collective-permute-start.48 = (bf16[40,2048]{1,0:T(8,128)(2,1)S(1)}, bf16[40,2048]{1,0:T(8,128)(2,1)S(1)}, u32[]{:S(2)}, u32[]{:S(2)}) collective-permute-start(bf16[40,2048]{1,0:T(8,128)(2,1)S(1)} %get-tuple-element.129), channel_id=1, source_target_pairs={{0,1},{1,0},{2,3},{3,2},{4,5},{5,4},{6,7},{7,6},{8,9},{9,8},{10,11... | collective-permute-start | bytes 491528 | tf_op jit(solution)/shard_map/ppermute | solution.py:323
  101.4 11.4 %collective-permute-start.49 = (bf16[40,2048]{1,0:T(8,128)(2,1)S(1)}, bf16[40,2048]{1,0:T(8,128)(2,1)S(1)}, u32[]{:S(2)}, u32[]{:S(2)}) collective-permute-start(bf16[40,2048]{1,0:T(8,128)(2,1)S(1)} %get-tuple-element.130), channel_id=1, source_target_pairs={{0,9},{1,8},{2,11},{3,10},{4,13},{5,12},{6,15},{7,14},{8,1},{9,0},... | collective-permute-start | bytes 491528 | tf_op jit(solution)/shard_map/ppermute | solution.py:323
  102.8 12.2 %collective-permute-start.50 = (bf16[40,2048]{1,0:T(8,128)(2,1)S(1)}, bf16[40,2048]{1,0:T(8,128)(2,1)S(1)}, u32[]{:S(2)}, u32[]{:S(2)}) collective-permute-start(bf16[40,2048]{1,0:T(8,128)(2,1)S(1)} %get-tuple-element.131), channel_id=1, source_target_pairs={{0,17},{1,16},{2,19},{3,18},{4,21},{5,20},{6,23},{7,22},{8,25},{9,... | collective-permute-start | bytes 491528 | tf_op jit(solution)/shard_map/ppermute | solution.py:323
  106.9 10.1 %collective-permute-start.51 = (bf16[40,2048]{1,0:T(8,128)(2,1)S(1)}, bf16[40,2048]{1,0:T(8,128)(2,1)S(1)}, u32[]{:S(2)}, u32[]{:S(2)}) collective-permute-start(bf16[40,2048]{1,0:T(8,128)(2,1)S(1)} %get-tuple-element.132), channel_id=1, source_target_pairs={{0,25},{1,24},{2,27},{3,26},{4,29},{5,28},{6,31},{7,30},{8,17},{9,... | collective-permute-start | bytes 491528 | tf_op jit(solution)/shard_map/ppermute | solution.py:323
  107.0 11.5 %collective-permute-start.11 = (bf16[40,2048]{1,0:T(8,128)(2,1)S(1)}, bf16[40,2048]{1,0:T(8,128)(2,1)S(1)}, u32[]{:S(2)}, u32[]{:S(2)}) collective-permute-start(bf16[40,2048]{1,0:T(8,128)(2,1)S(1)} %get-tuple-element.87), channel_id=1, source_target_pairs={{0,25},{1,24},{2,27},{3,26},{4,29},{5,28},{6,31},{7,30},{8,17},{9,... | collective-permute-start | bytes 491528 | tf_op jit(solution)/shard_map/ppermute | solution.py:323
  112.8 7.2 %collective-permute-start.62 = (bf16[40,2048]{1,0:T(8,128)(2,1)S(1)}, bf16[40,2048]{1,0:T(8,128)(2,1)S(1)}, u32[]{:S(2)}, u32[]{:S(2)}) collective-permute-start(bf16[40,2048]{1,0:T(8,128)(2,1)S(1)} %get-tuple-element.142), channel_id=1, source_target_pairs={{0,8},{1,9},{2,10},{3,11},{4,12},{5,13},{6,14},{7,15},{8,0},{9,1},... | collective-permute-start | bytes 491528 | tf_op jit(solution)/shard_map/ppermute | solution.py:323
  113.9 7.8 %collective-permute-start.63 = (bf16[40,2048]{1,0:T(8,128)(2,1)S(1)}, bf16[40,2048]{1,0:T(8,128)(2,1)S(1)}, u32[]{:S(2)}, u32[]{:S(2)}) collective-permute-start(bf16[40,2048]{1,0:T(8,128)(2,1)S(1)} %get-tuple-element.143), channel_id=1, source_target_pairs={{0,16},{1,17},{2,18},{3,19},{4,20},{5,21},{6,22},{7,23},{8,24},{9,... | collective-permute-start | bytes 491528 | tf_op jit(solution)/shard_map/ppermute | solution.py:323
  114.9 9.8 %collective-permute-start.64 = (bf16[40,2048]{1,0:T(8,128)(2,1)S(1)}, bf16[40,2048]{1,0:T(8,128)(2,1)S(1)}, u32[]{:S(2)}, u32[]{:S(2)}) collective-permute-start(bf16[40,2048]{1,0:T(8,128)(2,1)S(1)} %get-tuple-element.144), channel_id=1, source_target_pairs={{0,24},{1,25},{2,26},{3,27},{4,28},{5,29},{6,30},{7,31},{8,16},{9,... | collective-permute-start | bytes 491528 | tf_op jit(solution)/shard_map/ppermute | solution.py:323
  117.0 10.1 %collective-permute-start.24 = (bf16[40,2048]{1,0:T(8,128)(2,1)S(1)}, bf16[40,2048]{1,0:T(8,128)(2,1)S(1)}, u32[]{:S(2)}, u32[]{:S(2)}) collective-permute-start(bf16[40,2048]{1,0:T(8,128)(2,1)S(1)} %get-tuple-element.101), channel_id=1, source_target_pairs={{0,8},{1,9},{2,10},{3,11},{4,12},{5,13},{6,14},{7,15},{8,0},{9,1},... | collective-permute-start | bytes 491528 | tf_op jit(solution)/shard_map/ppermute | solution.py:323
  118.5 30.1 %collective-permute-start.52 = (bf16[128,2048]{1,0:T(8,128)(2,1)S(1)}, bf16[128,2048]{1,0:T(8,128)(2,1)S(1)}, u32[]{:S(2)}, u32[]{:S(2)}) collective-permute-start(bf16[128,2048]{1,0:T(8,128)(2,1)S(1)} %shard_map.130), channel_id=1, source_target_pairs={{0,2},{1,3},{2,0},{3,1},{4,6},{5,7},{6,4},{7,5},{8,10},{9,11},{10,... | collective-permute-start | bytes 1572872 | tf_op jit(solution)/shard_map/ppermute | solution.py:311
  120.0 8.3 %collective-permute-start.25 = (bf16[40,2048]{1,0:T(8,128)(2,1)S(1)}, bf16[40,2048]{1,0:T(8,128)(2,1)S(1)}, u32[]{:S(2)}, u32[]{:S(2)}) collective-permute-start(bf16[40,2048]{1,0:T(8,128)(2,1)S(1)} %get-tuple-element.102), channel_id=1, source_target_pairs={{0,16},{1,17},{2,18},{3,19},{4,20},{5,21},{6,22},{7,23},{8,24},{9,... | collective-permute-start | bytes 491528 | tf_op jit(solution)/shard_map/ppermute | solution.py:323
  121.7 10.0 %collective-permute-start.26 = (bf16[40,2048]{1,0:T(8,128)(2,1)S(1)}, bf16[40,2048]{1,0:T(8,128)(2,1)S(1)}, u32[]{:S(2)}, u32[]{:S(2)}) collective-permute-start(bf16[40,2048]{1,0:T(8,128)(2,1)S(1)} %get-tuple-element.103), channel_id=1, source_target_pairs={{0,24},{1,25},{2,26},{3,27},{4,28},{5,29},{6,30},{7,31},{8,16},{9,... | collective-permute-start | bytes 491528 | tf_op jit(solution)/shard_map/ppermute | solution.py:323
  124.7 7.4 %collective-permute-start.27 = (bf16[40,2048]{1,0:T(8,128)(2,1)S(1)}, bf16[40,2048]{1,0:T(8,128)(2,1)S(1)}, u32[]{:S(2)}, u32[]{:S(2)}) collective-permute-start(bf16[40,2048]{1,0:T(8,128)(2,1)S(1)} %get-tuple-element.104), channel_id=1, source_target_pairs={{0,1},{1,0},{2,3},{3,2},{4,5},{5,4},{6,7},{7,6},{8,9},{9,8},{10,11... | collective-permute-start | bytes 491528 | tf_op jit(solution)/shard_map/ppermute | solution.py:323
  127.0 7.0 %collective-permute-start.28 = (bf16[40,2048]{1,0:T(8,128)(2,1)S(1)}, bf16[40,2048]{1,0:T(8,128)(2,1)S(1)}, u32[]{:S(2)}, u32[]{:S(2)}) collective-permute-start(bf16[40,2048]{1,0:T(8,128)(2,1)S(1)} %get-tuple-element.105), channel_id=1, source_target_pairs={{0,9},{1,8},{2,11},{3,10},{4,13},{5,12},{6,15},{7,14},{8,1},{9,0},... | collective-permute-start | bytes 491528 | tf_op jit(solution)/shard_map/ppermute | solution.py:323
  128.3 7.0 %collective-permute-start.29 = (bf16[40,2048]{1,0:T(8,128)(2,1)S(1)}, bf16[40,2048]{1,0:T(8,128)(2,1)S(1)}, u32[]{:S(2)}, u32[]{:S(2)}) collective-permute-start(bf16[40,2048]{1,0:T(8,128)(2,1)S(1)} %get-tuple-element.106), channel_id=1, source_target_pairs={{0,17},{1,16},{2,19},{3,18},{4,21},{5,20},{6,23},{7,22},{8,25},{9,... | collective-permute-start | bytes 491528 | tf_op jit(solution)/shard_map/ppermute | solution.py:323
  131.8 7.2 %collective-permute-start.30 = (bf16[40,2048]{1,0:T(8,128)(2,1)S(1)}, bf16[40,2048]{1,0:T(8,128)(2,1)S(1)}, u32[]{:S(2)}, u32[]{:S(2)}) collective-permute-start(bf16[40,2048]{1,0:T(8,128)(2,1)S(1)} %get-tuple-element.107), channel_id=1, source_target_pairs={{0,25},{1,24},{2,27},{3,26},{4,29},{5,28},{6,31},{7,30},{8,17},{9,... | collective-permute-start | bytes 491528 | tf_op jit(solution)/shard_map/ppermute | solution.py:323
  132.2 11.1 %collective-permute-start.65 = (bf16[40,2048]{1,0:T(8,128)(2,1)S(1)}, bf16[40,2048]{1,0:T(8,128)(2,1)S(1)}, u32[]{:S(2)}, u32[]{:S(2)}) collective-permute-start(bf16[40,2048]{1,0:T(8,128)(2,1)S(1)} %get-tuple-element.145), channel_id=1, source_target_pairs={{0,1},{1,0},{2,3},{3,2},{4,5},{5,4},{6,7},{7,6},{8,9},{9,8},{10,11... | collective-permute-start | bytes 491528 | tf_op jit(solution)/shard_map/ppermute | solution.py:323
  134.1 9.9 %collective-permute-start.66 = (bf16[40,2048]{1,0:T(8,128)(2,1)S(1)}, bf16[40,2048]{1,0:T(8,128)(2,1)S(1)}, u32[]{:S(2)}, u32[]{:S(2)}) collective-permute-start(bf16[40,2048]{1,0:T(8,128)(2,1)S(1)} %get-tuple-element.146), channel_id=1, source_target_pairs={{0,9},{1,8},{2,11},{3,10},{4,13},{5,12},{6,15},{7,14},{8,1},{9,0},... | collective-permute-start | bytes 491528 | tf_op jit(solution)/shard_map/ppermute | solution.py:323
  135.3 10.4 %collective-permute-start.67 = (bf16[40,2048]{1,0:T(8,128)(2,1)S(1)}, bf16[40,2048]{1,0:T(8,128)(2,1)S(1)}, u32[]{:S(2)}, u32[]{:S(2)}) collective-permute-start(bf16[40,2048]{1,0:T(8,128)(2,1)S(1)} %get-tuple-element.147), channel_id=1, source_target_pairs={{0,17},{1,16},{2,19},{3,18},{4,21},{5,20},{6,23},{7,22},{8,25},{9,... | collective-permute-start | bytes 491528 | tf_op jit(solution)/shard_map/ppermute | solution.py:323
  139.0 7.8 %collective-permute-start.68 = (bf16[40,2048]{1,0:T(8,128)(2,1)S(1)}, bf16[40,2048]{1,0:T(8,128)(2,1)S(1)}, u32[]{:S(2)}, u32[]{:S(2)}) collective-permute-start(bf16[40,2048]{1,0:T(8,128)(2,1)S(1)} %get-tuple-element.148), channel_id=1, source_target_pairs={{0,25},{1,24},{2,27},{3,26},{4,29},{5,28},{6,31},{7,30},{8,17},{9,... | collective-permute-start | bytes 491528 | tf_op jit(solution)/shard_map/ppermute | solution.py:323
  143.2 6.6 %collective-permute-start.31 = (bf16[40,2048]{1,0:T(8,128)(2,1)S(1)}, bf16[40,2048]{1,0:T(8,128)(2,1)S(1)}, u32[]{:S(2)}, u32[]{:S(2)}) collective-permute-start(bf16[40,2048]{1,0:T(8,128)(2,1)S(1)} %get-tuple-element.109), channel_id=1, source_target_pairs={{0,8},{1,9},{2,10},{3,11},{4,12},{5,13},{6,14},{7,15},{8,0},{9,1},... | collective-permute-start | bytes 491528 | tf_op jit(solution)/shard_map/ppermute | solution.py:323
  144.0 9.0 %collective-permute-start.32 = (bf16[40,2048]{1,0:T(8,128)(2,1)S(1)}, bf16[40,2048]{1,0:T(8,128)(2,1)S(1)}, u32[]{:S(2)}, u32[]{:S(2)}) collective-permute-start(bf16[40,2048]{1,0:T(8,128)(2,1)S(1)} %get-tuple-element.110), channel_id=1, source_target_pairs={{0,16},{1,17},{2,18},{3,19},{4,20},{5,21},{6,22},{7,23},{8,24},{9,... | collective-permute-start | bytes 491528 | tf_op jit(solution)/shard_map/ppermute | solution.py:323
  145.7 9.3 %collective-permute-start.33 = (bf16[40,2048]{1,0:T(8,128)(2,1)S(1)}, bf16[40,2048]{1,0:T(8,128)(2,1)S(1)}, u32[]{:S(2)}, u32[]{:S(2)}) collective-permute-start(bf16[40,2048]{1,0:T(8,128)(2,1)S(1)} %get-tuple-element.111), channel_id=1, source_target_pairs={{0,24},{1,25},{2,26},{3,27},{4,28},{5,29},{6,30},{7,31},{8,16},{9,... | collective-permute-start | bytes 491528 | tf_op jit(solution)/shard_map/ppermute | solution.py:323
  146.8 8.9 %collective-permute-start.34 = (bf16[40,2048]{1,0:T(8,128)(2,1)S(1)}, bf16[40,2048]{1,0:T(8,128)(2,1)S(1)}, u32[]{:S(2)}, u32[]{:S(2)}) collective-permute-start(bf16[40,2048]{1,0:T(8,128)(2,1)S(1)} %get-tuple-element.112), channel_id=1, source_target_pairs={{0,1},{1,0},{2,3},{3,2},{4,5},{5,4},{6,7},{7,6},{8,9},{9,8},{10,11... | collective-permute-start | bytes 491528 | tf_op jit(solution)/shard_map/ppermute | solution.py:323
  148.6 8.9 %collective-permute-start.35 = (bf16[40,2048]{1,0:T(8,128)(2,1)S(1)}, bf16[40,2048]{1,0:T(8,128)(2,1)S(1)}, u32[]{:S(2)}, u32[]{:S(2)}) collective-permute-start(bf16[40,2048]{1,0:T(8,128)(2,1)S(1)} %get-tuple-element.113), channel_id=1, source_target_pairs={{0,9},{1,8},{2,11},{3,10},{4,13},{5,12},{6,15},{7,14},{8,1},{9,0},... | collective-permute-start | bytes 491528 | tf_op jit(solution)/shard_map/ppermute | solution.py:323
  149.9 9.4 %collective-permute-start.36 = (bf16[40,2048]{1,0:T(8,128)(2,1)S(1)}, bf16[40,2048]{1,0:T(8,128)(2,1)S(1)}, u32[]{:S(2)}, u32[]{:S(2)}) collective-permute-start(bf16[40,2048]{1,0:T(8,128)(2,1)S(1)} %get-tuple-element.114), channel_id=1, source_target_pairs={{0,17},{1,16},{2,19},{3,18},{4,21},{5,20},{6,23},{7,22},{8,25},{9,... | collective-permute-start | bytes 491528 | tf_op jit(solution)/shard_map/ppermute | solution.py:323
  153.0 8.1 %collective-permute-start.37 = (bf16[40,2048]{1,0:T(8,128)(2,1)S(1)}, bf16[40,2048]{1,0:T(8,128)(2,1)S(1)}, u32[]{:S(2)}, u32[]{:S(2)}) collective-permute-start(bf16[40,2048]{1,0:T(8,128)(2,1)S(1)} %get-tuple-element.115), channel_id=1, source_target_pairs={{0,25},{1,24},{2,27},{3,26},{4,29},{5,28},{6,31},{7,30},{8,17},{9,... | collective-permute-start | bytes 491528 | tf_op jit(solution)/shard_map/ppermute | solution.py:323
  155.0 7.6 %collective-permute-start.5 = (bf16[40,2048]{1,0:T(8,128)(2,1)S(1)}, bf16[40,2048]{1,0:T(8,128)(2,1)S(1)}, u32[]{:S(2)}, u32[]{:S(2)}) collective-permute-start(bf16[40,2048]{1,0:T(8,128)(2,1)S(1)} %get-tuple-element.81), channel_id=1, source_target_pairs={{0,8},{1,9},{2,10},{3,11},{4,12},{5,13},{6,14},{7,15},{8,0},{9,1},... | collective-permute-start | bytes 491528 | tf_op jit(solution)/shard_map/ppermute | solution.py:323
  155.7 13.7 %collective-permute-start.6 = (bf16[40,2048]{1,0:T(8,128)(2,1)S(1)}, bf16[40,2048]{1,0:T(8,128)(2,1)S(1)}, u32[]{:S(2)}, u32[]{:S(2)}) collective-permute-start(bf16[40,2048]{1,0:T(8,128)(2,1)S(1)} %get-tuple-element.82), channel_id=1, source_target_pairs={{0,16},{1,17},{2,18},{3,19},{4,20},{5,21},{6,22},{7,23},{8,24},{9,... | collective-permute-start | bytes 491528 | tf_op jit(solution)/shard_map/ppermute | solution.py:323
  157.5 12.2 %collective-permute-start.7 = (bf16[40,2048]{1,0:T(8,128)(2,1)S(1)}, bf16[40,2048]{1,0:T(8,128)(2,1)S(1)}, u32[]{:S(2)}, u32[]{:S(2)}) collective-permute-start(bf16[40,2048]{1,0:T(8,128)(2,1)S(1)} %get-tuple-element.83), channel_id=1, source_target_pairs={{0,24},{1,25},{2,26},{3,27},{4,28},{5,29},{6,30},{7,31},{8,16},{9,... | collective-permute-start | bytes 491528 | tf_op jit(solution)/shard_map/ppermute | solution.py:323
  159.3 10.4 %collective-permute-start.8 = (bf16[40,2048]{1,0:T(8,128)(2,1)S(1)}, bf16[40,2048]{1,0:T(8,128)(2,1)S(1)}, u32[]{:S(2)}, u32[]{:S(2)}) collective-permute-start(bf16[40,2048]{1,0:T(8,128)(2,1)S(1)} %get-tuple-element.84), channel_id=1, source_target_pairs={{0,1},{1,0},{2,3},{3,2},{4,5},{5,4},{6,7},{7,6},{8,9},{9,8},{10,11... | collective-permute-start | bytes 491528 | tf_op jit(solution)/shard_map/ppermute | solution.py:323
  161.2 9.5 %collective-permute-start.9 = (bf16[40,2048]{1,0:T(8,128)(2,1)S(1)}, bf16[40,2048]{1,0:T(8,128)(2,1)S(1)}, u32[]{:S(2)}, u32[]{:S(2)}) collective-permute-start(bf16[40,2048]{1,0:T(8,128)(2,1)S(1)} %get-tuple-element.85), channel_id=1, source_target_pairs={{0,9},{1,8},{2,11},{3,10},{4,13},{5,12},{6,15},{7,14},{8,1},{9,0},... | collective-permute-start | bytes 491528 | tf_op jit(solution)/shard_map/ppermute | solution.py:323
  162.6 32.6 %collective-permute-start.69 = (bf16[128,2048]{1,0:T(8,128)(2,1)S(1)}, bf16[128,2048]{1,0:T(8,128)(2,1)S(1)}, u32[]{:S(2)}, u32[]{:S(2)}) collective-permute-start(bf16[128,2048]{1,0:T(8,128)(2,1)S(1)} %shard_map.134), channel_id=1, source_target_pairs={{0,2},{1,3},{2,0},{3,1},{4,6},{5,7},{6,4},{7,5},{8,10},{9,11},{10,... | collective-permute-start | bytes 1572872 | tf_op jit(solution)/shard_map/ppermute | solution.py:311
  169.4 25.8 %collective-permute-start.53 = (bf16[128,2048]{1,0:T(8,128)(2,1)S(1)}, bf16[128,2048]{1,0:T(8,128)(2,1)S(1)}, u32[]{:S(2)}, u32[]{:S(2)}) collective-permute-start(bf16[128,2048]{1,0:T(8,128)(2,1)S(1)} %shard_map.131), channel_id=1, source_target_pairs={{0,6},{1,7},{2,4},{3,5},{4,2},{5,3},{6,0},{7,1},{8,14},{9,15},{10,... | collective-permute-start | bytes 1572872 | tf_op jit(solution)/shard_map/ppermute | solution.py:311
  173.9 7.1 %collective-permute-start.12 = (bf16[40,2048]{1,0:T(8,128)(2,1)S(1)}, bf16[40,2048]{1,0:T(8,128)(2,1)S(1)}, u32[]{:S(2)}, u32[]{:S(2)}) collective-permute-start(bf16[40,2048]{1,0:T(8,128)(2,1)S(1)} %get-tuple-element.89), channel_id=1, source_target_pairs={{0,8},{1,9},{2,10},{3,11},{4,12},{5,13},{6,14},{7,15},{8,0},{9,1},... | collective-permute-start | bytes 491528 | tf_op jit(solution)/shard_map/ppermute | solution.py:323
  176.0 7.4 %collective-permute-start.13 = (bf16[40,2048]{1,0:T(8,128)(2,1)S(1)}, bf16[40,2048]{1,0:T(8,128)(2,1)S(1)}, u32[]{:S(2)}, u32[]{:S(2)}) collective-permute-start(bf16[40,2048]{1,0:T(8,128)(2,1)S(1)} %get-tuple-element.90), channel_id=1, source_target_pairs={{0,16},{1,17},{2,18},{3,19},{4,20},{5,21},{6,22},{7,23},{8,24},{9,... | collective-permute-start | bytes 491528 | tf_op jit(solution)/shard_map/ppermute | solution.py:323
  176.6 8.6 %collective-permute-start.14 = (bf16[40,2048]{1,0:T(8,128)(2,1)S(1)}, bf16[40,2048]{1,0:T(8,128)(2,1)S(1)}, u32[]{:S(2)}, u32[]{:S(2)}) collective-permute-start(bf16[40,2048]{1,0:T(8,128)(2,1)S(1)} %get-tuple-element.91), channel_id=1, source_target_pairs={{0,24},{1,25},{2,26},{3,27},{4,28},{5,29},{6,30},{7,31},{8,16},{9,... | collective-permute-start | bytes 491528 | tf_op jit(solution)/shard_map/ppermute | solution.py:323
  185.2 8.9 %collective-permute-start.17 = (bf16[40,2048]{1,0:T(8,128)(2,1)S(1)}, bf16[40,2048]{1,0:T(8,128)(2,1)S(1)}, u32[]{:S(2)}, u32[]{:S(2)}) collective-permute-start(bf16[40,2048]{1,0:T(8,128)(2,1)S(1)} %get-tuple-element.94), channel_id=1, source_target_pairs={{0,17},{1,16},{2,19},{3,18},{4,21},{5,20},{6,23},{7,22},{8,25},{9,... | collective-permute-start | bytes 491528 | tf_op jit(solution)/shard_map/ppermute | solution.py:323
  187.2 8.0 %collective-permute-start.18 = (bf16[40,2048]{1,0:T(8,128)(2,1)S(1)}, bf16[40,2048]{1,0:T(8,128)(2,1)S(1)}, u32[]{:S(2)}, u32[]{:S(2)}) collective-permute-start(bf16[40,2048]{1,0:T(8,128)(2,1)S(1)} %get-tuple-element.95), channel_id=1, source_target_pairs={{0,25},{1,24},{2,27},{3,26},{4,29},{5,28},{6,31},{7,30},{8,17},{9,... | collective-permute-start | bytes 491528 | tf_op jit(solution)/shard_map/ppermute | solution.py:323
  (15 other events, 282.4 us)
